TPU v7x, 128 devices: a whole 4x4x4 slice. The times are simulated.
128 devices in a mesh: section: 2 (over core), blk: 16 (over y, x), mp: 4 (over z).
Axes of the slice: x: 4, y: 4, z: 4, core: 2. Of those that a mesh axis runs over, the one named last changes fastest.
Arguments:
- patches: bfloat16 [256, 5120], P('section'), may hold values from -6 to 6
- merge_gain: float32 [1280], replicated, may hold values from 0.25 to 1.75
- merge_first: bfloat16 [5120, 5120], P(None, ('blk', 'mp')), may hold values from -0.078125 to 0.078125
- merge_second: bfloat16 [5120, 4096], P(('blk', 'mp')), may hold values from -0.078125 to 0.078125
- text_embeds: bfloat16 [4, 1024, 4096], P(None, 'blk', 'mp'), may hold values from -7 to 14
- positions: int32 [256], replicated, may hold values from 0 to 4095, as said below
- segments: int32 [4096], replicated, may hold values from 0 to 2, never falling along the last dimension, each value on 1 to 2048 neighbouring positions
- norm_gain: float32 [2, 4096], P('section'), may hold values from 0.25 to 1.75
- query_weight: bfloat16 [2, 4096, 4096], P('section', 'blk', 'mp'), may hold values from -1 to 1
- keyval_weight: bfloat16 [2, 4096, 4, 2, 128], P('section', 'blk', 'mp'), may hold values from -1 to 1
- out_weight: bfloat16 [2, 4096, 4096], P('section', 'mp', 'blk'), may hold values from -0.09375 to 0.09375
Outputs:
- hidden: bfloat16 [2, 4, 1024, 4096], P('section', None, 'blk', 'mp')
Inputs may be any that keep to these rules, and one draw needn't show every extreme that they name: `positions`: distinct and increasing.
All inputs are finite; a program needn't handle non-finite values.
Results may differ from a plain program's by a relative error of at most 0.015.
Values may be sent and summed in bfloat16 or wider, within the bound.
No kernel may reach another device: no remote copies, remote signals or barrier semaphores. Data moves between devices by JAX's collectives and lax.ppermute only.
A program may use at most 128 MiB of HBM per device.

v0:
```python
import functools
import math

import jax
import jax.numpy as jnp
from jax import lax
from jax.experimental import pallas as pl
from jax.experimental.pallas import tpu as pltpu
from jax.sharding import PartitionSpec as P

epsilon = 1e-06
rope_base = 1000000.0
lane = 128


def moved(value, axis, by):
    size = lax.axis_size(axis)
    return lax.ppermute(value, axis, [(i, (i + by) % size) for i in range(size)])


def swapped(value):
    return lax.ppermute(value, "section", [(0, 1), (1, 0)])


def rope_tables(where_at, head_size):
    steps_half = jnp.arange(head_size // 2).astype(jnp.float32)
    inverse = jnp.exp(-jnp.log(rope_base) * 2.0 * steps_half / head_size)
    angles = where_at.astype(jnp.float32)[:, None] * inverse[None, :]
    return (jnp.cos(angles), jnp.sin(angles))


def rotate(values, cosine, sine):
    half = values.shape[-1] // 2
    first = values[..., :half]
    second = values[..., half:]
    return jnp.concatenate(
        [first * cosine - second * sine, second * cosine + first * sine], axis=-1
    )


def my_half(value, axis, section_index):
    shape = value.shape
    runs = shape[axis] // (2 * lane)
    split = value.reshape(shape[:axis] + (runs, 2, lane) + shape[axis + 1 :])
    index = [slice(None)] * split.ndim
    index[axis + 1] = 0
    even = split[tuple(index)]
    index[axis + 1] = 1
    odd = split[tuple(index)]
    picked = jnp.where(section_index == 0, even, odd)
    return picked.reshape(shape[:axis] + (runs * lane,) + shape[axis + 1 :])


def scatter_sum(term, model_index):
    size = lax.axis_size("mp")
    width = term.shape[1] // size

    def piece(by):
        return lax.dynamic_slice_in_dim(term, ((model_index + by) % size) * width, width, 1)

    total = piece(0)
    arrived = [moved(piece(by).astype(jnp.bfloat16), "mp", by) for by in (1, 3, 2)]
    for part in arrived:
        total = total + part.astype(jnp.float32)
    return total


def spread(value):
    size = lax.axis_size("blk")
    copies = jnp.broadcast_to(value[None], (size,) + value.shape)
    return lax.all_to_all(copies, "blk", 0, 0, tiled=True)


def attention_kernel(scalars, query_ref, mine_ref, other_ref, out_ref, *, chunk_runs):
    runs, blocks, run, head_size = mine_ref.shape
    heads = query_ref.shape[1] // head_size
    rows = heads * run
    chunk = chunk_runs * run
    per_block = runs // chunk_runs
    block_len = runs * run
    start_one, start_two, cycle, section = scalars[0], scalars[1], scalars[2], scalars[3]
    factor = 1.0 / head_size**0.5 * math.log2(math.e)

    def stripes(key_ref, value_ref):
        def stripe(block, carry):
            row_from = pl.multiple_of(block * run, run)
            first = block * block_len + cycle * run
            here = query_ref[pl.ds(row_from, run), :]
            stacked = jnp.concatenate(
                [here[:, h * head_size : (h + 1) * head_size] for h in range(heads)], axis=0
            )
            row_at = lax.broadcasted_iota(jnp.int32, (rows, 1), 0) % run + first
            row_start = jnp.where(
                row_at >= start_two, start_two, jnp.where(row_at >= start_one, start_one, 0)
            )
            stripe_start = jnp.where(
                first >= start_two, start_two, jnp.where(first >= start_one, start_one, 0)
            )

            def step(index, state):
                top, total, mixed = state
                in_block = index // per_block
                from_run = (index % per_block) * chunk_runs
                key = key_ref[pl.ds(from_run, chunk_runs), in_block].reshape(chunk, head_size)
                value = value_ref[pl.ds(from_run, chunk_runs), in_block].reshape(chunk, head_size)
                scores = lax.dot_general(
                    stacked, key, (((1,), (1,)), ((), ())), preferred_element_type=jnp.float32
                )
                key_at = lax.broadcasted_iota(jnp.int32, (1, chunk), 1) + index * chunk
                allowed = (key_at <= row_at) & (key_at >= row_start)
                scores = jnp.where(allowed, scores * factor, -1e30)
                new_top = jnp.maximum(top, jnp.max(scores, axis=1, keepdims=True))
                fade = jnp.exp2(top - new_top)
                weights = jnp.exp2(scores - new_top)
                total = total * fade + jnp.sum(weights, axis=1, keepdims=True)
                mixed = mixed * fade + jnp.dot(
                    weights.astype(jnp.bfloat16), value, preferred_element_type=jnp.float32
                )
                return new_top, total, mixed

            state = (
                jnp.full((rows, 1), -1e30, jnp.float32),
                jnp.zeros((rows, 1), jnp.float32),
                jnp.zeros((rows, head_size), jnp.float32),
            )
            _, total, mixed = lax.fori_loop(
                stripe_start // chunk, (first + run - 1) // chunk + 1, step, state
            )
            result = (mixed / total).astype(out_ref.dtype)
            for h in range(heads):
                out_ref[pl.ds(row_from, run), h * head_size : (h + 1) * head_size] = result[
                    h * run : (h + 1) * run
                ]
            return carry

        lax.fori_loop(0, blocks, stripe, 0)

    @pl.when(section == 0)
    def _():
        stripes(mine_ref, other_ref)

    @pl.when(section != 0)
    def _():
        stripes(other_ref, mine_ref)


def attention(scalars, query, mine, other):
    whole = pl.BlockSpec(memory_space=pltpu.VMEM)
    return pl.pallas_call(
        functools.partial(attention_kernel, chunk_runs=mine.shape[0] // 2),
        out_shape=jax.ShapeDtypeStruct(query.shape, query.dtype),
        in_specs=[pl.BlockSpec(memory_space=pltpu.SMEM), whole, whole, whole],
        out_specs=whole,
        cost_estimate=pl.CostEstimate(
            flops=4 * query.size * mine.size // query.shape[1] // 4,
            bytes_accessed=2 * (2 * query.size + 2 * mine.size),
            transcendentals=0,
        ),
        name="attention",
    )(scalars, query, mine, other)


def local(
    patches,
    merge_gain,
    merge_first,
    merge_second,
    text_embeds,
    positions,
    segments,
    norm_gain,
    query_weight,
    keyval_weight,
    out_weight,
):
    count = patches.shape[0]
    width = merge_gain.shape[0]
    blocks, rows_here, slice_width = text_embeds.shape
    seq_len = segments.shape[0]
    block_len = seq_len // blocks
    section_index = lax.axis_index("section")
    cycle_index = lax.axis_index("blk")
    model_index = lax.axis_index("mp")
    n_mp = lax.axis_size("mp")
    n_blk = lax.axis_size("blk")
    first_core = section_index == 0
    head_size = keyval_weight.shape[4]
    rows = blocks * rows_here
    layers = 2

    query_own = query_weight[0]
    keyval_own = keyval_weight[0].reshape(keyval_weight.shape[1], 2 * head_size)
    out_own = out_weight[0]
    heads_half = query_own.shape[1] // 2
    weight_half = query_own.shape[0] // 2
    proj_width = query_own.shape[1] + 2 * head_size

    def packed(core):
        keep_rows = slice(core * weight_half, (core + 1) * weight_half)
        query_rows, keyval_rows = query_own[keep_rows], keyval_own[keep_rows]
        out_rows = out_own[:, keep_rows].T
        parts = []
        for half in (core, 1 - core):
            parts.append(query_rows[:, half * heads_half : (half + 1) * heads_half])
            parts.append(keyval_rows[:, half * head_size : (half + 1) * head_size])
        for half in (core, 1 - core):
            parts.append(out_rows[:, half * heads_half : (half + 1) * heads_half])
        return jnp.concatenate(parts, axis=1)

    for_first, for_second = packed(0), packed(1)
    weight_keep = jnp.where(first_core, for_first, for_second)
    weight_other = swapped(jnp.where(first_core, for_second, for_first))
    weight_layers = [
        jnp.where(first_core, weight_keep, weight_other),
        jnp.where(first_core, weight_other, weight_keep),
    ]
    gain_half = norm_gain[0].reshape(-1, 2, lane)
    gain_keep = jnp.where(first_core, gain_half[:, 0], gain_half[:, 1])
    gain_send = jnp.where(first_core, gain_half[:, 1], gain_half[:, 0])
    gain_other = swapped(gain_send)
    gain_layers = [
        jnp.where(first_core, gain_keep, gain_other).reshape(n_mp, -1),
        jnp.where(first_core, gain_other, gain_keep).reshape(n_mp, -1),
    ]
    weight_full = [
        lax.all_gather(weight_layers[layer_index], "blk", axis=0, tiled=True)
        for layer_index in range(layers)
    ]

    pieces = patches.astype(jnp.float32).reshape(count, -1, width)
    centered = pieces - jnp.mean(pieces, axis=-1, keepdims=True)
    variance = jnp.mean(centered * centered, axis=-1, keepdims=True)
    normed = (
        (centered * lax.rsqrt(variance + epsilon) * merge_gain)
        .reshape(count, -1)
        .astype(jnp.bfloat16)
    )
    inner = jax.nn.gelu(
        jnp.dot(normed, merge_first, preferred_element_type=jnp.float32), approximate=False
    ).astype(jnp.bfloat16)
    inner_other = swapped(inner)
    inner_all = jnp.concatenate(
        [
            jnp.where(first_core, inner, inner_other),
            jnp.where(first_core, inner_other, inner),
        ],
        axis=0,
    )
    second_half = my_half(merge_second, 1, section_index)
    partial_merge = jnp.dot(inner_all, second_half, preferred_element_type=jnp.float32)
    tokens = partial_merge.shape[0]
    merged_part = scatter_sum(partial_merge, model_index).astype(jnp.bfloat16)
    merged_terms = lax.all_to_all(
        merged_part.reshape(n_blk, tokens // n_blk, -1), "blk", 0, 0, tiled=True
    )
    merged_mine = jnp.sum(merged_terms.astype(jnp.float32), axis=0).astype(jnp.bfloat16)
    merged = spread(merged_mine).reshape(tokens, -1)

    row_where = (
        jnp.arange(blocks)[:, None] * block_len
        + cycle_index * rows_here
        + jnp.arange(rows_here)[None, :]
    ).reshape(-1)
    starts = jnp.stack([jnp.sum(segments < 1), jnp.sum(segments < 2)])
    scalars = jnp.concatenate([starts, jnp.stack([cycle_index, section_index])]).astype(jnp.int32)

    is_visual = positions[None, :] == row_where[:, None]
    picked = jnp.dot(
        is_visual.astype(jnp.bfloat16), merged, preferred_element_type=jnp.float32
    ).astype(jnp.bfloat16)
    text_rows = my_half(text_embeds.reshape(rows, slice_width), 1, section_index)
    state = jnp.where(jnp.any(is_visual, axis=1)[:, None], picked, text_rows)

    cosine, sine = rope_tables(row_where, head_size)
    cosine = cosine[:, None, :]
    sine = sine[:, None, :]
    keyval_cosine = jnp.where(first_core, cosine, 1.0)
    keyval_sine = jnp.where(first_core, sine, 0.0)

    results = []
    for layer_index in range(layers):
        weight = weight_full[layer_index]
        gain = gain_layers[layer_index]
        parts = [state] + [moved(state, "mp", by) for by in (1, 3, 2)]
        squares = 0.0
        projected = 0.0
        for part, by in zip(parts, (0, 1, 3, 2)):
            source = (model_index + n_mp - by) % n_mp
            part_f = part.astype(jnp.float32)
            squares = squares + jnp.sum(part_f * part_f, axis=1, keepdims=True)
            scaled = (part_f * lax.dynamic_index_in_dim(gain, source, 0)).astype(jnp.bfloat16)
            depth = part.shape[1]
            projected = projected + jnp.dot(
                scaled,
                lax.dynamic_slice(weight, (source * depth, 0), (depth, proj_width)),
                preferred_element_type=jnp.float32,
            )
        squares = squares + swapped(squares)
        columns = projected.shape[1] // 2
        total = projected[:, :columns] + swapped(projected[:, columns:])
        total = total * lax.rsqrt(squares / (2 * n_mp * slice_width // 2) + epsilon)
        query = total[:, :heads_half].reshape(rows, -1, head_size)
        query = rotate(query, cosine, sine).astype(jnp.bfloat16).reshape(rows, heads_half)
        keyval = total[:, None, heads_half:]
        keyval = rotate(keyval, keyval_cosine, keyval_sine).astype(jnp.bfloat16)[:, 0]
        gathered = spread(keyval).reshape(n_blk, blocks, rows_here, head_size)
        attended = attention(scalars, query, gathered, swapped(gathered))
        attended_other = swapped(attended)
        term = jnp.einsum(
            "pk,nk->pn",
            attended,
            weight[:, proj_width : proj_width + heads_half],
            preferred_element_type=jnp.float32,
        )
        term = term + jnp.einsum(
            "pk,nk->pn",
            attended_other,
            weight[:, proj_width + heads_half :],
            preferred_element_type=jnp.float32,
        )
        state = (state.astype(jnp.float32) + scatter_sum(term, model_index)).astype(jnp.bfloat16)
        results.append(state)

    keep = jnp.where(first_core, results[0], results[1])
    send = jnp.where(first_core, results[1], results[0])
    other = swapped(send)
    even = jnp.where(first_core, keep, other).reshape(rows, -1, 1, lane)
    odd = jnp.where(first_core, other, keep).reshape(rows, -1, 1, lane)
    return jnp.concatenate([even, odd], axis=2).reshape(1, blocks, rows_here, slice_width)


def solution(mesh):
    return jax.shard_map(
        local,
        mesh=mesh,
        in_specs=(
            P("section", None),
            P(),
            P(None, ("blk", "mp")),
            P(("blk", "mp"), None),
            P(None, "blk", "mp"),
            P(),
            P(),
            P("section", None),
            P("section", "blk", "mp"),
            P("section", "blk", "mp", None, None),
            P("section", "mp", "blk"),
        ),
        out_specs=P("section", None, "blk", "mp"),
        check_vma=False,
    )
```

profile of v0, /device:TPU:1, one launch (start us, length us, event | category | flops | bytes accessed | tf_op | source)
XLA Modules:
  0.0 275.8 jit_solution(6480905707978513394)
XLA Ops:
  14.7 2.9 %reshape.367 = f32[128,4,1280]{2,1,0:T(4,128)S(1)} reshape(bf16[128,5120]{1,0:T(8,128)(2,1)} %param.11) | data formatting | bytes 3932160 | tf_op jit(solution)/shard_map/reshape | solution.py:230
  20.1 2.0 copy.56
  22.2 2.8 %fusion.95 = bf16[128,80]{0,1:T(8,128)(2,1)S(1)} fusion(bf16[5120,80]{0,1:T(8,128)(2,1)S(1)} %copy-done, f32[128,5120]{1,0:T(8,128)S(1)} %bitcast.81, f32[128,5120]{1,0:T(8,128)} %bitcast.82, f32[5120]{0:T(1024)S(1)} %mul.329, bf16[128,5120]{1,0:T(8,128)(2,1)} %param.11), kind=kOutput, calls=%fused_computation.162 | convolution fusion | flops 108800000 | bytes 7413760 | tf_op jit(solution)/shard_map/dot_general | solution.py:239
  25.7 2.4 reshape.368
  32.2 2.1 collective-permute-start.2
  36.2 4.8 %collective-permute-done.1 = bf16[256,512]{1,0:T(8,128)(2,1)} collective-permute-done((bf16[256,512]{1,0:T(8,128)(2,1)}, bf16[256,512]{1,0:T(8,128)(2,1)}, u32[]{:S(2)}, u32[]{:S(2)}) %collective-permute-start.1) | collective-permute-done | bytes 262176 | tf_op jit(solution)/shard_map/ppermute | solution.py:18
  41.0 6.5 %collective-permute-done.3 = bf16[256,512]{1,0:T(8,128)(2,1)} collective-permute-done((bf16[256,512]{1,0:T(8,128)(2,1)S(1)}, bf16[256,512]{1,0:T(8,128)(2,1)}, u32[]{:S(2)}, u32[]{:S(2)}) %collective-permute-start.3) | collective-permute-done | bytes 262176 | tf_op jit(solution)/shard_map/ppermute | solution.py:18
  47.5 1.9 add_convert_fusion.2
  49.4 6.9 %all-to-all-start = ((bf16[16,16,512]{2,1,0:T(8,128)(2,1)}), bf16[16,16,512]{2,1,0:T(8,128)(2,1)S(1)}, u32[]{:S(2)}, u32[]{:S(2)}) async-start(bf16[16,16,512]{2,1,0:T(8,128)(2,1)} %bitcast), calls=%async_computation | async-start | bytes 524288 | tf_op jit(solution)/shard_map/all_to_all | solution.py:253
  57.1 10.3 %all-to-all-done = bf16[16,16,512]{2,1,0:T(8,128)(2,1)S(1)} async-done(((bf16[16,16,512]{2,1,0:T(8,128)(2,1)}), bf16[16,16,512]{2,1,0:T(8,128)(2,1)S(1)}, u32[]{:S(2)}, u32[]{:S(2)}) %all-to-all-start) | async-done | bytes 262176 | tf_op jit(solution)/shard_map/all_to_all | solution.py:253
  68.2 3.5 %all-to-all-start.1 = ((bf16[16,16,512]{2,1,0:T(8,128)(2,1)}), bf16[16,16,512]{2,1,0:T(8,128)(2,1)S(1)}, u32[]{:S(2)}, u32[]{:S(2)}) async-start(bf16[16,16,512]{2,1,0:T(8,128)(2,1)} %broadcast_in_dim.26), calls=%async_computation.1 | async-start | bytes 524288 | tf_op jit(solution)/shard_map/all_to_all | solution.py:71
  72.1 10.3 %all-to-all-done.1 = bf16[16,16,512]{2,1,0:T(8,128)(2,1)S(1)} async-done(((bf16[16,16,512]{2,1,0:T(8,128)(2,1)}), bf16[16,16,512]{2,1,0:T(8,128)(2,1)S(1)}, u32[]{:S(2)}, u32[]{:S(2)}) %all-to-all-start.1) | async-done | bytes 262176 | tf_op jit(solution)/shard_map/all_to_all | solution.py:71
  83.0 2.5 collective-permute-start.7
  85.7 4.0 %collective-permute-done.6 = bf16[256,512]{1,0:T(8,128)(2,1)S(1)} collective-permute-done((bf16[256,512]{1,0:T(8,128)(2,1)S(1)}, bf16[256,512]{1,0:T(8,128)(2,1)S(1)}, u32[]{:S(2)}, u32[]{:S(2)}) %collective-permute-start.6) | collective-permute-done | bytes 262176 | tf_op jit(solution)/shard_map/ppermute | solution.py:18
  89.8 2.5 collective-permute-done.7
  92.5 12.9 %all-gather.3.cloned.1.call-done = bf16[2048,2304]{0,1:T(8,128)(2,1)} async-done(((bf16[128,2304]{0,1:T(8,128)(2,1)}), bf16[2048,2304]{0,1:T(8,128)(2,1)}) %all-gather.3.cloned.1.call-update) | async-done | bytes 9437200 | tf_op jit(solution)/shard_map/all_gather | solution.py:226
  111.0 1.9 fusion.3
  116.9 26.8 %all_to_all.20 = bf16[16,256,128]{2,1,0:T(8,128)(2,1)S(1)} all-to-all(bf16[16,256,128]{2,1,0:T(8,128)(2,1)S(1)} %broadcast_in_dim.30), channel_id=1, replica_groups=mesh['section'=2,'blk'=16,'mp'=4] {'blk'}, dimensions={0} | all-to-all | bytes 2097152 | tf_op jit(solution)/shard_map/all_to_all | solution.py:71
  145.9 1.9 pad_add_fusion.scalars
  150.2 6.9 %attention.2 = bf16[256,512]{1,0:T(8,128)(2,1)} custom-call(s32[4]{0:T(128)} %pad_add_fusion.scalars, bf16[256,512]{1,0:T(8,128)(2,1)} %bitcast.97, bf16[16,4,64,128]{3,2,1,0:T(8,128)(2,1)} %bitcast.86, bf16[16,4,64,128]{3,2,1,0:T(8,128)(2,1)} %collective-permute-done.11.other_ref), custom_call_target="tpu_custom_call" | custom-call | flops 134217728 | bytes 2621440 | tf_op jit(solution)/shard_map/attention/pallas_call | solution.py:149
  158.9 2.3 fusion.7
  161.2 2.4 convolution_add_fusion.3
  167.0 5.8 %collective-permute-done.13 = bf16[256,512]{1,0:T(8,128)(2,1)S(1)} collective-permute-done((bf16[256,512]{1,0:T(8,128)(2,1)S(1)}, bf16[256,512]{1,0:T(8,128)(2,1)S(1)}, u32[]{:S(2)}, u32[]{:S(2)}) %collective-permute-start.13) | collective-permute-done | bytes 262176 | tf_op jit(solution)/shard_map/ppermute | solution.py:18
  172.8 5.7 %collective-permute-done.15 = bf16[256,512]{1,0:T(8,128)(2,1)S(1)} collective-permute-done((bf16[256,512]{1,0:T(8,128)(2,1)S(1)}, bf16[256,512]{1,0:T(8,128)(2,1)S(1)}, u32[]{:S(2)}, u32[]{:S(2)}) %collective-permute-start.15) | collective-permute-done | bytes 262176 | tf_op jit(solution)/shard_map/ppermute | solution.py:18
  179.5 2.0 collective-permute-start.17
  181.7 16.1 %all-gather.5.cloned.1.call-done = bf16[2048,2304]{0,1:T(8,128)(2,1)} async-done(((bf16[128,2304]{0,1:T(8,128)(2,1)}), bf16[2048,2304]{0,1:T(8,128)(2,1)}) %all-gather.5.cloned.1.call-update) | async-done | bytes 9437200 | tf_op jit(solution)/shard_map/all_gather | solution.py:226
  209.7 20.8 %all_to_all.21 = bf16[16,256,128]{2,1,0:T(8,128)(2,1)S(1)} all-to-all(bf16[16,256,128]{2,1,0:T(8,128)(2,1)S(1)} %broadcast_in_dim.32), channel_id=1, replica_groups=mesh['section'=2,'blk'=16,'mp'=4] {'blk'}, dimensions={0} | all-to-all | bytes 2097152 | tf_op jit(solution)/shard_map/all_to_all | solution.py:71
  234.7 6.9 %attention.3 = bf16[256,512]{1,0:T(8,128)(2,1)} custom-call(s32[4]{0:T(128)} %pad_add_fusion.scalars, bf16[256,512]{1,0:T(8,128)(2,1)} %bitcast.96, bf16[16,4,64,128]{3,2,1,0:T(8,128)(2,1)} %bitcast.88, bf16[16,4,64,128]{3,2,1,0:T(8,128)(2,1)} %collective-permute-done.21.other_ref), custom_call_target="tpu_custom_call" | custom-call | flops 134217728 | bytes 2621440 | tf_op jit(solution)/shard_map/attention/pallas_call | solution.py:149
  243.4 2.3 fusion.4
  245.7 2.4 convolution_add_fusion.2
  252.6 4.4 %collective-permute-done.23 = bf16[256,512]{1,0:T(8,128)(2,1)S(1)} collective-permute-done((bf16[256,512]{1,0:T(8,128)(2,1)S(1)}, bf16[256,512]{1,0:T(8,128)(2,1)S(1)}, u32[]{:S(2)}, u32[]{:S(2)}) %collective-permute-start.23) | collective-permute-done | bytes 262176 | tf_op jit(solution)/shard_map/ppermute | solution.py:18
  257.0 6.8 %collective-permute-done.25 = bf16[256,512]{1,0:T(8,128)(2,1)S(1)} collective-permute-done((bf16[256,512]{1,0:T(8,128)(2,1)S(1)}, bf16[256,512]{1,0:T(8,128)(2,1)S(1)}, u32[]{:S(2)}, u32[]{:S(2)}) %collective-permute-start.25) | collective-permute-done | bytes 262176 | tf_op jit(solution)/shard_map/ppermute | solution.py:18
  (173 shorter events, 68.0 us)
Async XLA Ops:
  6.5 98.8 %all-gather.3.cloned.1.call-start = ((), (), s32[]{:S(2)}) async-start(), calls=%async_computation.4 | async-start | bytes 10027008 | tf_op jit(solution)/shard_map/all_gather | solution.py:226
  9.7 3.1 %collective-permute-start.5 = (bf16[128,2304]{0,1:T(8,128)(2,1)S(1)}, bf16[128,2304]{0,1:T(8,128)(2,1)S(1)}, u32[]{:S(2)}, u32[]{:S(2)}) collective-permute-start(bf16[128,2304]{0,1:T(8,128)(2,1)S(1)} %broadcast_select_fusion.2), channel_id=1, source_target_pairs={{0,64},{64,0},{1,65},{65,1},{2,66},{66,2},{3,67},{67,3},{4,68},{68... | collective-permute-start | bytes 1769480 | tf_op jit(solution)/shard_map/ppermute | solution.py:22
  14.0 183.8 %all-gather.5.cloned.1.call-start = ((), (), s32[]{:S(2)}) async-start(), calls=%async_computation.5 | async-start | bytes 10027008 | tf_op jit(solution)/shard_map/all_gather | solution.py:226
  25.0 4.1 %collective-permute-start = (bf16[128,80]{0,1:T(8,128)(2,1)S(1)}, bf16[128,80]{0,1:T(8,128)(2,1)S(1)}, u32[]{:S(2)}, u32[]{:S(2)}) collective-permute-start(bf16[128,80]{0,1:T(8,128)(2,1)S(1)} %fusion.95), channel_id=1, source_target_pairs={{0,64},{64,0},{1,65},{65,1},{2,66},{66,2},{3,67},{67,3},{4,68},{68... | collective-permute-start | bytes 61448 | tf_op jit(solution)/shard_map/ppermute | solution.py:22
  25.5 60.1 %collective-permute-start.4 = (f32[16,128]{1,0:T(8,128)S(1)}, f32[16,128]{1,0:T(8,128)S(1)}, u32[]{:S(2)}, u32[]{:S(2)}) collective-permute-start(f32[16,128]{1,0:T(8,128)S(1)} %bitcast.111), channel_id=1, source_target_pairs={{0,64},{64,0},{1,65},{65,1},{2,66},{66,2},{3,67},{67,3},{4,68},{68... | collective-permute-start | bytes 24584 | tf_op jit(solution)/shard_map/ppermute | solution.py:22
  30.5 10.5 %collective-permute-start.1 = (bf16[256,512]{1,0:T(8,128)(2,1)}, bf16[256,512]{1,0:T(8,128)(2,1)}, u32[]{:S(2)}, u32[]{:S(2)}) collective-permute-start(bf16[256,512]{1,0:T(8,128)(2,1)} %get-tuple-element.17), channel_id=1, source_target_pairs={{0,1},{1,2},{2,3},{3,0},{4,5},{5,6},{6,7},{7,4},{8,9},{9,10},{10,1... | collective-permute-start | bytes 786440 | tf_op jit(solution)/shard_map/ppermute | solution.py:18
  32.2 8.8 %collective-permute-start.2 = (bf16[256,512]{1,0:T(8,128)(2,1)}, bf16[256,512]{1,0:T(8,128)(2,1)}, u32[]{:S(2)}, u32[]{:S(2)}) collective-permute-start(bf16[256,512]{1,0:T(8,128)(2,1)} %get-tuple-element.19), channel_id=1, source_target_pairs={{0,3},{1,0},{2,1},{3,2},{4,7},{5,4},{6,5},{7,6},{8,11},{9,8},{10,9... | collective-permute-start | bytes 786440 | tf_op jit(solution)/shard_map/ppermute | solution.py:18
  34.3 13.2 %collective-permute-start.3 = (bf16[256,512]{1,0:T(8,128)(2,1)S(1)}, bf16[256,512]{1,0:T(8,128)(2,1)}, u32[]{:S(2)}, u32[]{:S(2)}) collective-permute-start(bf16[256,512]{1,0:T(8,128)(2,1)S(1)} %get-tuple-element.18), channel_id=1, source_target_pairs={{0,2},{1,3},{2,0},{3,1},{4,6},{5,7},{6,4},{7,5},{8,10},{9,11},{10,... | collective-permute-start | bytes 786440 | tf_op jit(solution)/shard_map/ppermute | solution.py:18
  49.4 18.0 %all-to-all-start = ((bf16[16,16,512]{2,1,0:T(8,128)(2,1)}), bf16[16,16,512]{2,1,0:T(8,128)(2,1)S(1)}, u32[]{:S(2)}, u32[]{:S(2)}) async-start(bf16[16,16,512]{2,1,0:T(8,128)(2,1)} %bitcast), calls=%async_computation | async-start | bytes 524288 | tf_op jit(solution)/shard_map/all_to_all | solution.py:253
  68.2 14.3 %all-to-all-start.1 = ((bf16[16,16,512]{2,1,0:T(8,128)(2,1)}), bf16[16,16,512]{2,1,0:T(8,128)(2,1)S(1)}, u32[]{:S(2)}, u32[]{:S(2)}) async-start(bf16[16,16,512]{2,1,0:T(8,128)(2,1)} %broadcast_in_dim.26), calls=%async_computation.1 | async-start | bytes 524288 | tf_op jit(solution)/shard_map/all_to_all | solution.py:71
  82.8 6.9 %collective-permute-start.6 = (bf16[256,512]{1,0:T(8,128)(2,1)S(1)}, bf16[256,512]{1,0:T(8,128)(2,1)S(1)}, u32[]{:S(2)}, u32[]{:S(2)}) collective-permute-start(bf16[256,512]{1,0:T(8,128)(2,1)S(1)} %get-tuple-element.58), channel_id=1, source_target_pairs={{0,1},{1,2},{2,3},{3,0},{4,5},{5,6},{6,7},{7,4},{8,9},{9,10},{10,1... | collective-permute-start | bytes 786440 | tf_op jit(solution)/shard_map/ppermute | solution.py:18
  83.0 9.3 %collective-permute-start.7 = (bf16[256,512]{1,0:T(8,128)(2,1)S(1)}, bf16[256,512]{1,0:T(8,128)(2,1)S(1)}, u32[]{:S(2)}, u32[]{:S(2)}) collective-permute-start(bf16[256,512]{1,0:T(8,128)(2,1)S(1)} %get-tuple-element.58), channel_id=1, source_target_pairs={{0,3},{1,0},{2,1},{3,2},{4,7},{5,4},{6,5},{7,6},{8,11},{9,8},{10,9... | collective-permute-start | bytes 786440 | tf_op jit(solution)/shard_map/ppermute | solution.py:18
  85.6 23.5 %collective-permute-start.8 = (bf16[256,512]{1,0:T(8,128)(2,1)S(1)}, bf16[256,512]{1,0:T(8,128)(2,1)S(1)}, u32[]{:S(2)}, u32[]{:S(2)}) collective-permute-start(bf16[256,512]{1,0:T(8,128)(2,1)S(1)} %get-tuple-element.58), channel_id=1, source_target_pairs={{0,2},{1,3},{2,0},{3,1},{4,6},{5,7},{6,4},{7,5},{8,10},{9,11},{10,... | collective-permute-start | bytes 786440 | tf_op jit(solution)/shard_map/ppermute | solution.py:18
  112.9 2.9 %collective-permute-start.9 = (f32[256,640]{1,0:T(8,128)S(1)}, f32[256,640]{1,0:T(8,128)S(1)}, u32[]{:S(2)}, u32[]{:S(2)}) collective-permute-start(f32[256,640]{1,0:T(8,128)S(1)} %slice.208), channel_id=1, source_target_pairs={{0,64},{64,0},{1,65},{65,1},{2,66},{66,2},{3,67},{67,3},{4,68},{68... | collective-permute-start | bytes 1966088 | tf_op jit(solution)/shard_map/ppermute | solution.py:22
  114.2 1.6 collective-permute-start.10
  116.0 29.2 %copy-start.8 = (s32[4096]{0:T(1024)S(1)}, s32[4096]{0:T(1024)}, u32[]{:S(2)}) copy-start(s32[4096]{0:T(1024)} %param.17) | copy-start | bytes 49156
  143.7 6.5 %collective-permute-start.11 = (bf16[16,4,64,128]{3,2,1,0:T(8,128)(2,1)S(1)}, bf16[16,4,64,128]{3,2,1,0:T(8,128)(2,1)}, u32[]{:S(2)}, u32[]{:S(2)}) collective-permute-start(bf16[16,4,64,128]{3,2,1,0:T(8,128)(2,1)S(1)} %bitcast.85), channel_id=1, source_target_pairs={{0,64},{64,0},{1,65},{65,1},{2,66},{66,2},{3,67},{67,3},{4,68},{68... | collective-permute-start | bytes 3145736 | tf_op jit(solution)/shard_map/ppermute | solution.py:22
  157.1 1.7 collective-permute-start.12
  163.7 9.2 %collective-permute-start.13 = (bf16[256,512]{1,0:T(8,128)(2,1)S(1)}, bf16[256,512]{1,0:T(8,128)(2,1)S(1)}, u32[]{:S(2)}, u32[]{:S(2)}) collective-permute-start(bf16[256,512]{1,0:T(8,128)(2,1)S(1)} %get-tuple-element.14), channel_id=1, source_target_pairs={{0,1},{1,2},{2,3},{3,0},{4,5},{5,6},{6,7},{7,4},{8,9},{9,10},{10,1... | collective-permute-start | bytes 786440 | tf_op jit(solution)/shard_map/ppermute | solution.py:18
  164.6 8.2 %collective-permute-start.14 = (bf16[256,512]{1,0:T(8,128)(2,1)S(1)}, bf16[256,512]{1,0:T(8,128)(2,1)S(1)}, u32[]{:S(2)}, u32[]{:S(2)}) collective-permute-start(bf16[256,512]{1,0:T(8,128)(2,1)S(1)} %get-tuple-element.16), channel_id=1, source_target_pairs={{0,3},{1,0},{2,1},{3,2},{4,7},{5,4},{6,5},{7,6},{8,11},{9,8},{10,9... | collective-permute-start | bytes 786440 | tf_op jit(solution)/shard_map/ppermute | solution.py:18
  166.4 12.1 %collective-permute-start.15 = (bf16[256,512]{1,0:T(8,128)(2,1)S(1)}, bf16[256,512]{1,0:T(8,128)(2,1)S(1)}, u32[]{:S(2)}, u32[]{:S(2)}) collective-permute-start(bf16[256,512]{1,0:T(8,128)(2,1)S(1)} %get-tuple-element.15), channel_id=1, source_target_pairs={{0,2},{1,3},{2,0},{3,1},{4,6},{5,7},{6,4},{7,5},{8,10},{9,11},{10,... | collective-permute-start | bytes 786440 | tf_op jit(solution)/shard_map/ppermute | solution.py:18
  178.8 19.0 %collective-permute-start.16 = (bf16[256,512]{1,0:T(8,128)(2,1)S(1)}, bf16[256,512]{1,0:T(8,128)(2,1)S(1)}, u32[]{:S(2)}, u32[]{:S(2)}) collective-permute-start(bf16[256,512]{1,0:T(8,128)(2,1)S(1)} %get-tuple-element.10), channel_id=1, source_target_pairs={{0,1},{1,2},{2,3},{3,0},{4,5},{5,6},{6,7},{7,4},{8,9},{9,10},{10,1... | collective-permute-start | bytes 786440 | tf_op jit(solution)/shard_map/ppermute | solution.py:18
  179.5 20.1 %collective-permute-start.17 = (bf16[256,512]{1,0:T(8,128)(2,1)S(1)}, bf16[256,512]{1,0:T(8,128)(2,1)S(1)}, u32[]{:S(2)}, u32[]{:S(2)}) collective-permute-start(bf16[256,512]{1,0:T(8,128)(2,1)S(1)} %get-tuple-element.10), channel_id=1, source_target_pairs={{0,3},{1,0},{2,1},{3,2},{4,7},{5,4},{6,5},{7,6},{8,11},{9,8},{10,9... | collective-permute-start | bytes 786440 | tf_op jit(solution)/shard_map/ppermute | solution.py:18
  181.5 20.0 %collective-permute-start.18 = (bf16[256,512]{1,0:T(8,128)(2,1)S(1)}, bf16[256,512]{1,0:T(8,128)(2,1)S(1)}, u32[]{:S(2)}, u32[]{:S(2)}) collective-permute-start(bf16[256,512]{1,0:T(8,128)(2,1)S(1)} %get-tuple-element.10), channel_id=1, source_target_pairs={{0,2},{1,3},{2,0},{3,1},{4,6},{5,7},{6,4},{7,5},{8,10},{9,11},{10,... | collective-permute-start | bytes 786440 | tf_op jit(solution)/shard_map/ppermute | solution.py:18
  205.3 3.4 %collective-permute-start.19 = (f32[256,640]{1,0:T(8,128)S(1)}, f32[256,640]{1,0:T(8,128)S(1)}, u32[]{:S(2)}, u32[]{:S(2)}) collective-permute-start(f32[256,640]{1,0:T(8,128)S(1)} %slice.218), channel_id=1, source_target_pairs={{0,64},{64,0},{1,65},{65,1},{2,66},{66,2},{3,67},{67,3},{4,68},{68... | collective-permute-start | bytes 1966088 | tf_op jit(solution)/shard_map/ppermute | solution.py:22
  207.3 1.3 collective-permute-start.20
  230.6 4.2 %collective-permute-start.21 = (bf16[16,4,64,128]{3,2,1,0:T(8,128)(2,1)S(1)}, bf16[16,4,64,128]{3,2,1,0:T(8,128)(2,1)}, u32[]{:S(2)}, u32[]{:S(2)}) collective-permute-start(bf16[16,4,64,128]{3,2,1,0:T(8,128)(2,1)S(1)} %bitcast.87), channel_id=1, source_target_pairs={{0,64},{64,0},{1,65},{65,1},{2,66},{66,2},{3,67},{67,3},{4,68},{68... | collective-permute-start | bytes 3145736 | tf_op jit(solution)/shard_map/ppermute | solution.py:22
  241.6 1.7 collective-permute-start.22
  248.2 8.8 %collective-permute-start.23 = (bf16[256,512]{1,0:T(8,128)(2,1)S(1)}, bf16[256,512]{1,0:T(8,128)(2,1)S(1)}, u32[]{:S(2)}, u32[]{:S(2)}) collective-permute-start(bf16[256,512]{1,0:T(8,128)(2,1)S(1)} %get-tuple-element.11), channel_id=1, source_target_pairs={{0,1},{1,2},{2,3},{3,0},{4,5},{5,6},{6,7},{7,4},{8,9},{9,10},{10,1... | collective-permute-start | bytes 786440 | tf_op jit(solution)/shard_map/ppermute | solution.py:18
  249.5 7.5 %collective-permute-start.24 = (bf16[256,512]{1,0:T(8,128)(2,1)S(1)}, bf16[256,512]{1,0:T(8,128)(2,1)S(1)}, u32[]{:S(2)}, u32[]{:S(2)}) collective-permute-start(bf16[256,512]{1,0:T(8,128)(2,1)S(1)} %get-tuple-element.13), channel_id=1, source_target_pairs={{0,3},{1,0},{2,1},{3,2},{4,7},{5,4},{6,5},{7,6},{8,11},{9,8},{10,9... | collective-permute-start | bytes 786440 | tf_op jit(solution)/shard_map/ppermute | solution.py:18
  251.0 12.8 %collective-permute-start.25 = (bf16[256,512]{1,0:T(8,128)(2,1)S(1)}, bf16[256,512]{1,0:T(8,128)(2,1)S(1)}, u32[]{:S(2)}, u32[]{:S(2)}) collective-permute-start(bf16[256,512]{1,0:T(8,128)(2,1)S(1)} %get-tuple-element.12), channel_id=1, source_target_pairs={{0,2},{1,3},{2,0},{3,1},{4,6},{5,7},{6,4},{7,5},{8,10},{9,11},{10,... | collective-permute-start | bytes 786440 | tf_op jit(solution)/shard_map/ppermute | solution.py:18
  264.0 2.4 collective-permute-start.26
  (11 other events, 71.2 us)
Sparse Core Ops, SparseCore 0:
  14.1 91.2 all-gather.2
  107.5 90.2 all-gather.4
where the time goes:
time: 277 us; the launch traced here: 276 us
  waiting for transfers between devices  99.9 us (36%)
  blocking collectives  47.6 us (17%)
  starting transfers between devices  39.2 us (14%)
  matrix products  27.9 us (10%)
  local copies, waits for them, and re-layouts  20 us (7%)
  between operations  14.2 us (5%)
  Pallas kernels  13.8 us (5%)
  other arithmetic  13.2 us (5%)
    all_to_all x2, blocking collectives, spread(): return lax.all_to_all(copies, 'blk', 0, 0, tiled=True)  47.6 us
    ppermute x15, waiting for transfers between devices, moved(): lax.ppermute(value, axis, [(i, (i + by) % size) for i in range(size)])  40.5 us
    all_gather x2, waiting for transfers between devices, local(): lax.all_gather(weight_layers[layer_index], 'blk', axis=0, tiled=True)  29 us
    ppermute x15, starting transfers between devices, moved(): lax.ppermute(value, axis, [(i, (i + by) % size) for i in range(size)])  18.6 us
    dot_general x8, matrix products, local(): jnp.dot(scaled, lax.dynamic_slice(weight, (source * depth, 0), (depth, pr...  14.9 us
    pallas_call x2, Pallas kernels, attention(): pl.pallas_call(functools.partial(attention_kernel, chunk_runs=mine.shape[...  13.8 us
    all_to_all x1, waiting for transfers between devices, local(): lax.all_to_all(merged_part.reshape(n_blk, tokens // n_blk, -1), 'blk', 0,...  10.3 us
    all_to_all x1, waiting for transfers between devices, spread(): return lax.all_to_all(copies, 'blk', 0, 0, tiled=True)  10.3 us
  transfers between devices with their start and end apart: 31, of which 19 were waited for; matrix products, arithmetic and copies ran while one was open for 16% of the time, Pallas kernels for 2%

commit v1 on v0

--- a/solution.py
+++ b/solution.py
@@ -49,20 +49,6 @@
     odd = split[tuple(index)]
     picked = jnp.where(section_index == 0, even, odd)
     return picked.reshape(shape[:axis] + (runs * lane,) + shape[axis + 1 :])
-
-
-def scatter_sum(term, model_index):
-    size = lax.axis_size("mp")
-    width = term.shape[1] // size
-
-    def piece(by):
-        return lax.dynamic_slice_in_dim(term, ((model_index + by) % size) * width, width, 1)
-
-    total = piece(0)
-    arrived = [moved(piece(by).astype(jnp.bfloat16), "mp", by) for by in (1, 3, 2)]
-    for part in arrived:
-        total = total + part.astype(jnp.float32)
-    return total
 
 
 def spread(value):
@@ -158,6 +144,161 @@
         ),
         name="attention",
     )(scalars, query, mine, other)
+
+
+def merger_kernel(patches_ref, gain_ref, weight_ref, out_ref):
+    width = gain_ref.shape[1]
+    total = jnp.zeros(out_ref.shape, jnp.float32)
+    for at in range(0, patches_ref.shape[1], width):
+        piece = patches_ref[:, at : at + width].astype(jnp.float32)
+        centered = piece - jnp.mean(piece, axis=1, keepdims=True)
+        variance = jnp.mean(centered * centered, axis=1, keepdims=True)
+        normed = (centered * lax.rsqrt(variance + epsilon) * gain_ref[...]).astype(jnp.bfloat16)
+        total = total + jnp.dot(
+            normed, weight_ref[at : at + width, :], preferred_element_type=jnp.float32
+        )
+    out_ref[...] = (0.5 * total * (1.0 + lax.erf(total * math.sqrt(0.5)))).astype(out_ref.dtype)
+
+
+def merger_inner(patches, merge_gain, merge_first):
+    whole = pl.BlockSpec(memory_space=pltpu.VMEM)
+    rows, units = patches.shape[0], merge_first.shape[1]
+    return pl.pallas_call(
+        merger_kernel,
+        out_shape=jax.ShapeDtypeStruct((rows, units), jnp.bfloat16),
+        in_specs=[whole, whole, whole],
+        out_specs=whole,
+        cost_estimate=pl.CostEstimate(
+            flops=2 * rows * merge_first.size,
+            bytes_accessed=2 * (patches.size + merge_first.size),
+            transcendentals=0,
+        ),
+        name="merger_inner",
+    )(patches, merge_gain.reshape(1, -1), merge_first)
+
+
+def project_in_kernel(
+    place, own_ref, from_one, from_two, from_three, gain_ref, weight_ref, kept_ref, sent_ref, rows_ref
+):
+    step = pl.program_id(0)
+    count = pl.num_programs(0)
+    pieces, _, depth = gain_ref.shape
+    columns = weight_ref.shape[1]
+    queries = (count - 1) * columns // 2
+
+    @pl.when(step == 0)
+    def _():
+        squares = jnp.zeros((own_ref.shape[0], 1), jnp.float32)
+        for by, part_ref in enumerate((own_ref, from_one, from_two, from_three)):
+            source = (place[0] + pieces - by) % pieces
+            part = part_ref[...].astype(jnp.float32)
+            squares = squares + jnp.sum(part * part, axis=1, keepdims=True)
+            rows_ref[source] = (part * gain_ref[source]).astype(jnp.bfloat16)
+        spread_squares = jnp.broadcast_to(squares, (squares.shape[0], lane))
+        kept_ref[:, queries + lane :] = spread_squares
+        sent_ref[:, queries + lane :] = spread_squares
+
+    result = jnp.dot(rows_ref[0], weight_ref[:depth, :], preferred_element_type=jnp.float32)
+    for piece in range(1, pieces):
+        result = result + jnp.dot(
+            rows_ref[piece],
+            weight_ref[piece * depth : (piece + 1) * depth, :],
+            preferred_element_type=jnp.float32,
+        )
+
+    for block in range((5 - 1) // 2):
+
+        @pl.when(step == block)
+        def _():
+            kept_ref[:, block * columns : (block + 1) * columns] = result
+
+        @pl.when(step == block + (5 - 1) // 2)
+        def _():
+            sent_ref[:, block * columns : (block + 1) * columns] = result
+
+    @pl.when(step == count - 1)
+    def _():
+        kept_ref[:, queries : queries + lane] = result[:, :lane]
+        sent_ref[:, queries : queries + lane] = result[:, lane:]
+
+
+def project_in(place, parts, gain, weight):
+    rows, depth = parts[0].shape
+    columns = 2 * lane
+    skipped = 2 * depth // columns
+    steps = weight.shape[1] // columns - skipped
+    assert steps == 5
+    out = jax.ShapeDtypeStruct((rows, (steps - 1) * columns // 2 + 2 * lane), jnp.float32)
+    part_spec = pl.BlockSpec((rows, depth), lambda step, place: (0, 0))
+    out_spec = pl.BlockSpec(out.shape, lambda step, place: (0, 0))
+    return pl.pallas_call(
+        project_in_kernel,
+        out_shape=(out, out),
+        grid_spec=pltpu.PrefetchScalarGridSpec(
+            num_scalar_prefetch=1,
+            grid=(steps,),
+            in_specs=[part_spec] * 4
+            + [
+                pl.BlockSpec(gain.shape, lambda step, place: (0, 0, 0)),
+                pl.BlockSpec((weight.shape[0], columns), lambda step, place: (0, step + skipped)),
+            ],
+            out_specs=[out_spec, out_spec],
+            scratch_shapes=[pltpu.VMEM((len(parts), rows, depth), jnp.bfloat16)],
+        ),
+        cost_estimate=pl.CostEstimate(
+            flops=2 * rows * weight.shape[0] * steps * columns,
+            bytes_accessed=2 * weight.shape[0] * steps * columns + 8 * rows * out.shape[1],
+            transcendentals=0,
+        ),
+        name="project_in",
+    )(place.reshape(1), *parts, gain, weight)
+
+
+def project_out_kernel(place, mine_ref, other_ref, weight_ref, own_ref, one_ref, two_ref, three_ref):
+    half = mine_ref.shape[1]
+    over_last = (((1,), (1,)), ((), ()))
+    result = lax.dot_general(
+        mine_ref[...], weight_ref[:, :half], over_last, preferred_element_type=jnp.float32
+    ) + lax.dot_general(
+        other_ref[...], weight_ref[:, half:], over_last, preferred_element_type=jnp.float32
+    )
+    for by, out_ref in enumerate((own_ref, one_ref, two_ref, three_ref)):
+
+        @pl.when(pl.program_id(0) == by)
+        def _():
+            out_ref[...] = result.astype(out_ref.dtype)
+
+
+def project_out(place, mine, other, weight):
+    rows, half = mine.shape
+    pieces = lax.axis_size("mp")
+    depth = weight.shape[0] // pieces
+    shape = (rows, depth)
+    part_spec = pl.BlockSpec((rows, half), lambda step, place: (0, 0))
+    out_spec = pl.BlockSpec(shape, lambda step, place: (0, 0))
+    return pl.pallas_call(
+        project_out_kernel,
+        out_shape=[jax.ShapeDtypeStruct(shape, jnp.float32)]
+        + [jax.ShapeDtypeStruct(shape, jnp.bfloat16)] * (pieces - 1),
+        grid_spec=pltpu.PrefetchScalarGridSpec(
+            num_scalar_prefetch=1,
+            grid=(pieces,),
+            in_specs=[
+                part_spec,
+                part_spec,
+                pl.BlockSpec(
+                    (depth, 2 * half), lambda step, place: ((place[0] + step) % pieces, 0)
+                ),
+            ],
+            out_specs=[out_spec] * pieces,
+        ),
+        cost_estimate=pl.CostEstimate(
+            flops=4 * rows * half * weight.shape[0],
+            bytes_accessed=4 * half * weight.shape[0] + 2 * rows * weight.shape[0],
+            transcendentals=0,
+        ),
+        name="project_out",
+    )(place.reshape(1), mine, other, weight)
 
 
 def local(
@@ -193,18 +334,15 @@
     out_own = out_weight[0]
     heads_half = query_own.shape[1] // 2
     weight_half = query_own.shape[0] // 2
-    proj_width = query_own.shape[1] + 2 * head_size
 
     def packed(core):
         keep_rows = slice(core * weight_half, (core + 1) * weight_half)
         query_rows, keyval_rows = query_own[keep_rows], keyval_own[keep_rows]
         out_rows = out_own[:, keep_rows].T
-        parts = []
-        for half in (core, 1 - core):
-            parts.append(query_rows[:, half * heads_half : (half + 1) * heads_half])
-            parts.append(keyval_rows[:, half * head_size : (half + 1) * head_size])
-        for half in (core, 1 - core):
-            parts.append(out_rows[:, half * heads_half : (half + 1) * heads_half])
+        halves = (core, 1 - core)
+        parts = [out_rows[:, half * heads_half : (half + 1) * heads_half] for half in halves]
+        parts += [query_rows[:, half * heads_half : (half + 1) * heads_half] for half in halves]
+        parts += [keyval_rows[:, half * head_size : (half + 1) * head_size] for half in halves]
         return jnp.concatenate(parts, axis=1)
 
     for_first, for_second = packed(0), packed(1)
@@ -219,25 +357,15 @@
     gain_send = jnp.where(first_core, gain_half[:, 1], gain_half[:, 0])
     gain_other = swapped(gain_send)
     gain_layers = [
-        jnp.where(first_core, gain_keep, gain_other).reshape(n_mp, -1),
-        jnp.where(first_core, gain_other, gain_keep).reshape(n_mp, -1),
+        jnp.where(first_core, gain_keep, gain_other).reshape(n_mp, 1, -1),
+        jnp.where(first_core, gain_other, gain_keep).reshape(n_mp, 1, -1),
     ]
     weight_full = [
         lax.all_gather(weight_layers[layer_index], "blk", axis=0, tiled=True)
         for layer_index in range(layers)
     ]
 
-    pieces = patches.astype(jnp.float32).reshape(count, -1, width)
-    centered = pieces - jnp.mean(pieces, axis=-1, keepdims=True)
-    variance = jnp.mean(centered * centered, axis=-1, keepdims=True)
-    normed = (
-        (centered * lax.rsqrt(variance + epsilon) * merge_gain)
-        .reshape(count, -1)
-        .astype(jnp.bfloat16)
-    )
-    inner = jax.nn.gelu(
-        jnp.dot(normed, merge_first, preferred_element_type=jnp.float32), approximate=False
-    ).astype(jnp.bfloat16)
+    inner = merger_inner(patches, merge_gain, merge_first)
     inner_other = swapped(inner)
     inner_all = jnp.concatenate(
         [
@@ -249,9 +377,16 @@
     second_half = my_half(merge_second, 1, section_index)
     partial_merge = jnp.dot(inner_all, second_half, preferred_element_type=jnp.float32)
     tokens = partial_merge.shape[0]
-    merged_part = scatter_sum(partial_merge, model_index).astype(jnp.bfloat16)
+    share = tokens // n_blk
     merged_terms = lax.all_to_all(
-        merged_part.reshape(n_blk, tokens // n_blk, -1), "blk", 0, 0, tiled=True
+        partial_merge.astype(jnp.bfloat16)
+        .reshape(n_blk, share, n_mp, -1)
+        .transpose(0, 2, 1, 3)
+        .reshape(n_blk * n_mp, share, -1),
+        ("blk", "mp"),
+        0,
+        0,
+        tiled=True,
     )
     merged_mine = jnp.sum(merged_terms.astype(jnp.float32), axis=0).astype(jnp.bfloat16)
     merged = spread(merged_mine).reshape(tokens, -1)
@@ -280,25 +415,13 @@
     results = []
     for layer_index in range(layers):
         weight = weight_full[layer_index]
-        gain = gain_layers[layer_index]
-        parts = [state] + [moved(state, "mp", by) for by in (1, 3, 2)]
-        squares = 0.0
-        projected = 0.0
-        for part, by in zip(parts, (0, 1, 3, 2)):
-            source = (model_index + n_mp - by) % n_mp
-            part_f = part.astype(jnp.float32)
-            squares = squares + jnp.sum(part_f * part_f, axis=1, keepdims=True)
-            scaled = (part_f * lax.dynamic_index_in_dim(gain, source, 0)).astype(jnp.bfloat16)
-            depth = part.shape[1]
-            projected = projected + jnp.dot(
-                scaled,
-                lax.dynamic_slice(weight, (source * depth, 0), (depth, proj_width)),
-                preferred_element_type=jnp.float32,
-            )
-        squares = squares + swapped(squares)
-        columns = projected.shape[1] // 2
-        total = projected[:, :columns] + swapped(projected[:, columns:])
-        total = total * lax.rsqrt(squares / (2 * n_mp * slice_width // 2) + epsilon)
+        parts = [state] + [moved(state, "mp", by) for by in (1, 2, 3)]
+        kept, sent = project_in(model_index, parts, gain_layers[layer_index], weight)
+        total = kept + swapped(sent)
+        squares = total[:, heads_half + head_size :][:, :1]
+        total = total[:, : heads_half + head_size] * lax.rsqrt(
+            squares / (n_mp * slice_width) + epsilon
+        )
         query = total[:, :heads_half].reshape(rows, -1, head_size)
         query = rotate(query, cosine, sine).astype(jnp.bfloat16).reshape(rows, heads_half)
         keyval = total[:, None, heads_half:]
@@ -306,19 +429,12 @@
         gathered = spread(keyval).reshape(n_blk, blocks, rows_here, head_size)
         attended = attention(scalars, query, gathered, swapped(gathered))
         attended_other = swapped(attended)
-        term = jnp.einsum(
-            "pk,nk->pn",
-            attended,
-            weight[:, proj_width : proj_width + heads_half],
-            preferred_element_type=jnp.float32,
-        )
-        term = term + jnp.einsum(
-            "pk,nk->pn",
-            attended_other,
-            weight[:, proj_width + heads_half :],
-            preferred_element_type=jnp.float32,
-        )
-        state = (state.astype(jnp.float32) + scatter_sum(term, model_index)).astype(jnp.bfloat16)
+        total, *terms = project_out(model_index, attended, attended_other, weight)
+        arrived = [moved(terms[by - 1], "mp", by) for by in (2, 1, 3)]
+        total = state.astype(jnp.float32) + total
+        for part in arrived:
+            total = total + part.astype(jnp.float32)
+        state = total.astype(jnp.bfloat16)
         results.append(state)
 
     keep = jnp.where(first_core, results[0], results[1])

time: 277 us -> 285 us (1.029)
  Pallas kernels: 13.8 us -> 44.6 us
  matrix products: 27.9 us -> 0.69 us
    pallas_call x0 -> x5, Pallas kernels: none -> 28.1 us  [the longest x2 13.9 us: project_in(): pl.pallas_call(project_in_kernel, out_shape=(out, out), grid_spec=pltpu.P...]
    dot_general x13 -> x0, matrix products: 27 us -> none  [the longest x8 14.9 us: local(): jnp.dot(scaled, lax.dynamic_slice(weight, (source * depth, 0), (depth, pr...]
    all_to_all x1, waiting for transfers between devices: 10.3 us -> 18.2 us  [local(): lax.all_to_all(partial_merge.astype(jnp.bfloat16).reshape(n_blk, share, n...]
    all_gather x2, waiting for transfers between devices: 29 us -> 22.5 us  [local(): lax.all_gather(weight_layers[layer_index], 'blk', axis=0, tiled=True)]
    unnamed x39 -> x63, local copies, waits for them, and re-layouts: 4.44 us -> 9.84 us
    all_to_all x1, starting transfers between devices: 6.88 us -> 11.3 us  [local(): lax.all_to_all(partial_merge.astype(jnp.bfloat16).reshape(n_blk, share, n...]
    ppermute x15 -> x12, starting transfers between devices: 18.6 us -> 14.7 us  [moved(): lax.ppermute(value, axis, [(i, (i + by) % size) for i in range(size)])]
    ppermute x15 -> x12, waiting for transfers between devices: 40.5 us -> 38.4 us  [moved(): lax.ppermute(value, axis, [(i, (i + by) % size) for i in range(size)])]
  transfers between devices with their start and end apart: 31 -> 26, of which waited for: 19 -> 20; matrix products, arithmetic and copies ran while one was open for 16% -> 7% of each run, Pallas kernels for 2% -> 9%
where the time goes in v1:
time: 285 us; the launch traced here: 284 us
  waiting for transfers between devices  101 us (35%)
  blocking collectives  47.8 us (17%)
  Pallas kernels  44.6 us (16%)
  starting transfers between devices  41.9 us (15%)
  local copies, waits for them, and re-layouts  18.9 us (7%)
  other arithmetic  14.8 us (5%)
  between operations  13.9 us (5%)
    all_to_all x2, blocking collectives, spread(): return lax.all_to_all(copies, 'blk', 0, 0, tiled=True)  47.8 us
    ppermute x12, waiting for transfers between devices, moved(): lax.ppermute(value, axis, [(i, (i + by) % size) for i in range(size)])  38.4 us
    all_gather x2, waiting for transfers between devices, local(): lax.all_gather(weight_layers[layer_index], 'blk', axis=0, tiled=True)  22.5 us
    all_to_all x1, waiting for transfers between devices, local(): lax.all_to_all(partial_merge.astype(jnp.bfloat16).reshape(n_blk, share, n...  18.2 us
    pallas_call x2, Pallas kernels, attention(): pl.pallas_call(functools.partial(attention_kernel, chunk_runs=mine.shape[...  16.5 us
    ppermute x12, starting transfers between devices, moved(): lax.ppermute(value, axis, [(i, (i + by) % size) for i in range(size)])  14.7 us
    pallas_call x2, Pallas kernels, project_in(): pl.pallas_call(project_in_kernel, out_shape=(out, out), grid_spec=pltpu.P...  13.9 us
    ppermute x10, starting transfers between devices, swapped(): return lax.ppermute(value, 'section', [(0, 1), (1, 0)])  12.1 us
  transfers between devices with their start and end apart: 26, of which 20 were waited for; matrix products, arithmetic and copies ran while one was open for 7% of the time, Pallas kernels for 9%

profile of v1, /device:TPU:1, one launch (start us, length us, event | category | flops | bytes accessed | tf_op | source)
XLA Modules:
  0.0 284.1 jit_solution(8984153169223198444)
XLA Ops:
  16.3 3.6 %merger_inner.1 = bf16[128,80]{1,0:T(8,128)(2,1)} custom-call(bf16[128,5120]{1,0:T(8,128)(2,1)} %patches_ref.1, f32[1,1280]{1,0:T(1,128)} %reshape.297.gain_ref, bf16[5120,80]{1,0:T(8,128)(2,1)} %copy.29.weight_ref), custom_call_target="tpu_custom_call" | custom-call | flops 104857600 | bytes 2129920 | tf_op jit(solution)/shard_map/merger_inner/pallas_call | solution.py:166
  24.9 11.3 %all-to-all-start = ((bf16[64,16,512]{2,1,0:T(8,128)(2,1)}), bf16[64,16,512]{2,1,0:T(8,128)(2,1)S(1)}, u32[]{:S(2)}, u32[]{:S(2)}) async-start(bf16[64,16,512]{2,1,0:T(8,128)(2,1)} %bitcast.1), calls=%async_computation | async-start | bytes 2097152 | tf_op jit(solution)/shard_map/all_to_all | solution.py:381
  37.6 18.2 %all-to-all-done = bf16[64,16,512]{2,1,0:T(8,128)(2,1)S(1)} async-done(((bf16[64,16,512]{2,1,0:T(8,128)(2,1)}), bf16[64,16,512]{2,1,0:T(8,128)(2,1)S(1)}, u32[]{:S(2)}, u32[]{:S(2)}) %all-to-all-start) | async-done | bytes 1048608 | tf_op jit(solution)/shard_map/all_to_all | solution.py:381
  56.7 3.7 %all-to-all-start.1 = ((bf16[16,16,512]{2,1,0:T(8,128)(2,1)}), bf16[16,16,512]{2,1,0:T(8,128)(2,1)S(1)}, u32[]{:S(2)}, u32[]{:S(2)}) async-start(bf16[16,16,512]{2,1,0:T(8,128)(2,1)} %broadcast_in_dim.26), calls=%async_computation.1 | async-start | bytes 524288 | tf_op jit(solution)/shard_map/all_to_all | solution.py:57
  60.8 10.5 %all-to-all-done.1 = bf16[16,16,512]{2,1,0:T(8,128)(2,1)S(1)} async-done(((bf16[16,16,512]{2,1,0:T(8,128)(2,1)}), bf16[16,16,512]{2,1,0:T(8,128)(2,1)S(1)}, u32[]{:S(2)}, u32[]{:S(2)}) %all-to-all-start.1) | async-done | bytes 262176 | tf_op jit(solution)/shard_map/all_to_all | solution.py:57
  72.3 2.5 collective-permute-start.3
  74.7 3.0 %collective-permute-start.4 = (f32[16,128]{1,0:T(8,128)S(1)}, f32[16,128]{1,0:T(8,128)S(1)}, u32[]{:S(2)}, u32[]{:S(2)}) collective-permute-start(f32[16,128]{1,0:T(8,128)S(1)} %select_bitcast_fusion), channel_id=1, source_target_pairs={{0,64},{64,0},{1,65},{65,1},{2,66},{66,2},{3,67},{67,3},{4,68},{68... | collective-permute-start | bytes 24584 | tf_op jit(solution)/shard_map/ppermute | solution.py:22
  79.2 3.1 %collective-permute-done.1.from_one = bf16[256,512]{1,0:T(8,128)(2,1)S(1)} collective-permute-done((bf16[256,512]{1,0:T(8,128)(2,1)S(1)}, bf16[256,512]{1,0:T(8,128)(2,1)S(1)}, u32[]{:S(2)}, u32[]{:S(2)}) %collective-permute-start.1) | collective-permute-done | bytes 262176 | tf_op jit(solution)/shard_map/ppermute | solution.py:18
  82.3 3.4 %collective-permute-done.3.from_three = bf16[256,512]{1,0:T(8,128)(2,1)S(1)} collective-permute-done((bf16[256,512]{1,0:T(8,128)(2,1)S(1)}, bf16[256,512]{1,0:T(8,128)(2,1)S(1)}, u32[]{:S(2)}, u32[]{:S(2)}) %collective-permute-start.3) | collective-permute-done | bytes 262176 | tf_op jit(solution)/shard_map/ppermute | solution.py:18
  85.7 18.6 %all-gather.3.cloned.1.call-done.weight_ref = bf16[2048,2304]{1,0:T(8,128)(2,1)} async-done(((bf16[128,2304]{1,0:T(8,128)(2,1)}), bf16[2048,2304]{1,0:T(8,128)(2,1)}) %all-gather.3.cloned.1.call-update) | async-done | bytes 9437200 | tf_op jit(solution)/shard_map/all_gather | solution.py:364
  104.4 7.0 %project_in.2 = (f32[256,768]{1,0:T(8,128)}, f32[256,768]{1,0:T(8,128)}) custom-call(s32[1]{0:T(128)} %bitcast.3.place, bf16[256,512]{1,0:T(8,128)(2,1)} %copy-done.4, bf16[256,512]{1,0:T(8,128)(2,1)} %copy-done.12, bf16[256,512]{1,0:T(8,128)(2,1)} %copy-done.13, bf16[256,512]{1,0:T(8,128)(2,1)} %copy-done.14, f32[4,1,512]{2,1,0:T(1,128)} %bitcast.95, ...), custom_call_target="tpu_custom_call" | custom-call | flops 1342177280 | bytes 6815744 | tf_op jit(solution)/shard_map/project_in/pallas_call | solution.py:234
  112.0 2.1 collective-permute-done.6
  116.6 25.8 %all_to_all.20 = bf16[16,256,128]{2,1,0:T(8,128)(2,1)S(1)} all-to-all(bf16[16,256,128]{2,1,0:T(8,128)(2,1)S(1)} %broadcast_in_dim.50), channel_id=1, replica_groups=mesh['section'=2,'blk'=16,'mp'=4] {'blk'}, dimensions={0} | all-to-all | bytes 2097152 | tf_op jit(solution)/shard_map/all_to_all | solution.py:57
  144.2 1.9 pad_add_fusion.scalars
  149.5 8.3 %attention.2.mine_ref = bf16[256,512]{1,0:T(8,128)(2,1)} custom-call(s32[4]{0:T(128)} %pad_add_fusion.scalars, bf16[256,512]{1,0:T(8,128)(2,1)} %bitcast.81, bf16[16,4,64,128]{3,2,1,0:T(8,128)(2,1)} %bitcast.73, bf16[16,4,64,128]{3,2,1,0:T(8,128)(2,1)} %copy-done.6), custom_call_target="tpu_custom_call" | custom-call | flops 134217728 | bytes 2621440 | tf_op jit(solution)/shard_map/attention/pallas_call | solution.py:135
  160.3 5.4 %project_out.2 = (f32[256,512]{1,0:T(8,128)}, bf16[256,512]{1,0:T(8,128)(2,1)}, bf16[256,512]{1,0:T(8,128)(2,1)}, bf16[256,512]{1,0:T(8,128)(2,1)}) custom-call(s32[1]{0:T(128)} %bitcast.3.place, bf16[256,512]{1,0:T(8,128)(2,1)} %attention.2.mine_ref, bf16[256,512]{1,0:T(8,128)(2,1)} %copy-done.19, bf16[2048,2304]{1,0:T(8,128)(2,1)} %all-gather.3.cloned.1.call-done.weight_ref), custom_call_target="tpu_custom_call" | custom-call | flops 1073741824 | bytes 5242880 | tf_op jit(solution)/shard_map/project_out/pallas_call | solution.py:279
  165.6 2.8 collective-permute-start.11
  168.4 1.7 collective-permute-start.9
  170.1 9.6 %collective-permute-done.11 = bf16[256,512]{1,0:T(8,128)(2,1)S(1)} collective-permute-done((bf16[256,512]{1,0:T(8,128)(2,1)}, bf16[256,512]{1,0:T(8,128)(2,1)S(1)}, u32[]{:S(2)}, u32[]{:S(2)}) %collective-permute-start.11) | collective-permute-done | bytes 262176 | tf_op jit(solution)/shard_map/ppermute | solution.py:18
  179.6 2.2 collective-permute-done.9
  183.1 2.6 collective-permute-start.13
  186.9 3.9 %all-gather.5.cloned.1.call-done.weight_ref = bf16[2048,2304]{1,0:T(8,128)(2,1)} async-done(((bf16[128,2304]{1,0:T(8,128)(2,1)}), bf16[2048,2304]{1,0:T(8,128)(2,1)}) %all-gather.5.cloned.1.call-update) | async-done | bytes 9437200 | tf_op jit(solution)/shard_map/all_gather | solution.py:364
  190.7 6.0 %collective-permute-done.13.from_two = bf16[256,512]{1,0:T(8,128)(2,1)S(1)} collective-permute-done((bf16[256,512]{1,0:T(8,128)(2,1)S(1)}, bf16[256,512]{1,0:T(8,128)(2,1)S(1)}, u32[]{:S(2)}, u32[]{:S(2)}) %collective-permute-start.13) | collective-permute-done | bytes 262176 | tf_op jit(solution)/shard_map/ppermute | solution.py:18
  198.4 6.9 %project_in.3 = (f32[256,768]{1,0:T(8,128)}, f32[256,768]{1,0:T(8,128)}) custom-call(s32[1]{0:T(128)} %bitcast.3.place, bf16[256,512]{1,0:T(8,128)(2,1)} %copy-done, bf16[256,512]{1,0:T(8,128)(2,1)} %copy-done.15, bf16[256,512]{1,0:T(8,128)(2,1)} %copy-done.16, bf16[256,512]{1,0:T(8,128)(2,1)} %copy-done.17, f32[4,1,512]{2,1,0:T(1,128)} %bitcast.94, ...), custom_call_target="tpu_custom_call" | custom-call | flops 1342177280 | bytes 6815744 | tf_op jit(solution)/shard_map/project_in/pallas_call | solution.py:234
  206.9 2.1 collective-permute-done.15
  211.4 22.0 %all_to_all.21 = bf16[16,256,128]{2,1,0:T(8,128)(2,1)S(1)} all-to-all(bf16[16,256,128]{2,1,0:T(8,128)(2,1)S(1)} %broadcast_in_dim.52), channel_id=1, replica_groups=mesh['section'=2,'blk'=16,'mp'=4] {'blk'}, dimensions={0} | all-to-all | bytes 2097152 | tf_op jit(solution)/shard_map/all_to_all | solution.py:57
  233.5 1.8 collective-permute-start.16
  238.5 8.2 %attention.3.mine_ref = bf16[256,512]{1,0:T(8,128)(2,1)} custom-call(s32[4]{0:T(128)} %pad_add_fusion.scalars, bf16[256,512]{1,0:T(8,128)(2,1)} %bitcast.80, bf16[16,4,64,128]{3,2,1,0:T(8,128)(2,1)} %bitcast.75, bf16[16,4,64,128]{3,2,1,0:T(8,128)(2,1)} %copy-done.7), custom_call_target="tpu_custom_call" | custom-call | flops 134217728 | bytes 2621440 | tf_op jit(solution)/shard_map/attention/pallas_call | solution.py:135
  249.1 5.3 %project_out.3 = (f32[256,512]{1,0:T(8,128)}, bf16[256,512]{1,0:T(8,128)(2,1)}, bf16[256,512]{1,0:T(8,128)(2,1)}, bf16[256,512]{1,0:T(8,128)(2,1)}) custom-call(s32[1]{0:T(128)} %bitcast.3.place, bf16[256,512]{1,0:T(8,128)(2,1)} %attention.3.mine_ref, bf16[256,512]{1,0:T(8,128)(2,1)} %copy-done.18, bf16[2048,2304]{1,0:T(8,128)(2,1)} %all-gather.5.cloned.1.call-done.weight_ref), custom_call_target="tpu_custom_call" | custom-call | flops 1073741824 | bytes 5242880 | tf_op jit(solution)/shard_map/project_out/pallas_call | solution.py:279
  254.4 2.1 collective-permute-start.20
  257.7 4.9 %collective-permute-done.20 = bf16[256,512]{1,0:T(8,128)(2,1)S(1)} collective-permute-done((bf16[256,512]{1,0:T(8,128)(2,1)}, bf16[256,512]{1,0:T(8,128)(2,1)S(1)}, u32[]{:S(2)}, u32[]{:S(2)}) %collective-permute-start.20) | collective-permute-done | bytes 262176 | tf_op jit(solution)/shard_map/ppermute | solution.py:18
  262.5 8.2 %collective-permute-done.19 = bf16[256,512]{1,0:T(8,128)(2,1)S(1)} collective-permute-done((bf16[256,512]{1,0:T(8,128)(2,1)}, bf16[256,512]{1,0:T(8,128)(2,1)S(1)}, u32[]{:S(2)}, u32[]{:S(2)}) %collective-permute-start.19) | collective-permute-done | bytes 262176 | tf_op jit(solution)/shard_map/ppermute | solution.py:18
  (156 shorter events, 51.7 us)
Async XLA Ops:
  6.5 97.8 %all-gather.3.cloned.1.call-start = ((), (), s32[]{:S(2)}) async-start(), calls=%async_computation.4 | async-start | bytes 10027008 | tf_op jit(solution)/shard_map/all_gather | solution.py:364
  9.1 3.1 %collective-permute-start.5 = (bf16[128,2304]{1,0:T(8,128)(2,1)S(1)}, bf16[128,2304]{1,0:T(8,128)(2,1)S(1)}, u32[]{:S(2)}, u32[]{:S(2)}) collective-permute-start(bf16[128,2304]{1,0:T(8,128)(2,1)S(1)} %broadcast_select_fusion.2), channel_id=1, source_target_pairs={{0,64},{64,0},{1,65},{65,1},{2,66},{66,2},{3,67},{67,3},{4,68},{68... | collective-permute-start | bytes 1769480 | tf_op jit(solution)/shard_map/ppermute | solution.py:22
  13.6 177.1 %all-gather.5.cloned.1.call-start = ((), (), s32[]{:S(2)}) async-start(), calls=%async_computation.5 | async-start | bytes 10027008 | tf_op jit(solution)/shard_map/all_gather | solution.py:364
  19.9 1.9 collective-permute-start
  24.9 30.9 %all-to-all-start = ((bf16[64,16,512]{2,1,0:T(8,128)(2,1)}), bf16[64,16,512]{2,1,0:T(8,128)(2,1)S(1)}, u32[]{:S(2)}, u32[]{:S(2)}) async-start(bf16[64,16,512]{2,1,0:T(8,128)(2,1)} %bitcast.1), calls=%async_computation | async-start | bytes 2097152 | tf_op jit(solution)/shard_map/all_to_all | solution.py:381
  37.6 22.8 %copy-start.25 = (s32[256]{0:T(256)S(1)}, s32[256]{0:T(256)}, u32[]{:S(2)}) copy-start(s32[256]{0:T(256)} %param.16) | copy-start | bytes 3076
  56.7 14.6 %all-to-all-start.1 = ((bf16[16,16,512]{2,1,0:T(8,128)(2,1)}), bf16[16,16,512]{2,1,0:T(8,128)(2,1)S(1)}, u32[]{:S(2)}, u32[]{:S(2)}) async-start(bf16[16,16,512]{2,1,0:T(8,128)(2,1)} %broadcast_in_dim.26), calls=%async_computation.1 | async-start | bytes 524288 | tf_op jit(solution)/shard_map/all_to_all | solution.py:57
  71.5 32.9 %copy-start.4 = (bf16[256,512]{1,0:T(8,128)(2,1)}, bf16[256,512]{1,0:T(8,128)(2,1)S(1)}, u32[]{:S(2)}) copy-start(bf16[256,512]{1,0:T(8,128)(2,1)S(1)} %fusion.own_ref) | copy-start | bytes 786436
  71.5 10.8 %collective-permute-start.1 = (bf16[256,512]{1,0:T(8,128)(2,1)S(1)}, bf16[256,512]{1,0:T(8,128)(2,1)S(1)}, u32[]{:S(2)}, u32[]{:S(2)}) collective-permute-start(bf16[256,512]{1,0:T(8,128)(2,1)S(1)} %fusion.own_ref), channel_id=1, source_target_pairs={{0,1},{1,2},{2,3},{3,0},{4,5},{5,6},{6,7},{7,4},{8,9},{9,10},{10,1... | collective-permute-start | bytes 786440 | tf_op jit(solution)/shard_map/ppermute | solution.py:18
  72.2 10.1 %collective-permute-start.2 = (bf16[256,512]{1,0:T(8,128)(2,1)S(1)}, bf16[256,512]{1,0:T(8,128)(2,1)S(1)}, u32[]{:S(2)}, u32[]{:S(2)}) collective-permute-start(bf16[256,512]{1,0:T(8,128)(2,1)S(1)} %fusion.own_ref), channel_id=1, source_target_pairs={{0,2},{1,3},{2,0},{3,1},{4,6},{5,7},{6,4},{7,5},{8,10},{9,11},{10,... | collective-permute-start | bytes 786440 | tf_op jit(solution)/shard_map/ppermute | solution.py:18
  72.3 13.5 %collective-permute-start.3 = (bf16[256,512]{1,0:T(8,128)(2,1)S(1)}, bf16[256,512]{1,0:T(8,128)(2,1)S(1)}, u32[]{:S(2)}, u32[]{:S(2)}) collective-permute-start(bf16[256,512]{1,0:T(8,128)(2,1)S(1)} %fusion.own_ref), channel_id=1, source_target_pairs={{0,3},{1,0},{2,1},{3,2},{4,7},{5,4},{6,5},{7,6},{8,11},{9,8},{10,9... | collective-permute-start | bytes 786440 | tf_op jit(solution)/shard_map/ppermute | solution.py:18
  74.7 3.8 %collective-permute-start.4 = (f32[16,128]{1,0:T(8,128)S(1)}, f32[16,128]{1,0:T(8,128)S(1)}, u32[]{:S(2)}, u32[]{:S(2)}) collective-permute-start(f32[16,128]{1,0:T(8,128)S(1)} %select_bitcast_fusion), channel_id=1, source_target_pairs={{0,64},{64,0},{1,65},{65,1},{2,66},{66,2},{3,67},{67,3},{4,68},{68... | collective-permute-start | bytes 24584 | tf_op jit(solution)/shard_map/ppermute | solution.py:22
  82.3 22.1 %copy-start.12 = (bf16[256,512]{1,0:T(8,128)(2,1)}, bf16[256,512]{1,0:T(8,128)(2,1)S(1)}, u32[]{:S(2)}) copy-start(bf16[256,512]{1,0:T(8,128)(2,1)S(1)} %collective-permute-done.1.from_one) | copy-start | bytes 786436
  111.4 2.8 collective-permute-start.6
  116.6 26.9 %copy-start.23 = (s32[4096]{0:T(1024)S(1)}, s32[4096]{0:T(1024)}, u32[]{:S(2)}) copy-start(s32[4096]{0:T(1024)} %param.17) | copy-start | bytes 49156
  142.4 6.1 %collective-permute-start.7 = (bf16[16,4,64,128]{3,2,1,0:T(8,128)(2,1)S(1)}, bf16[16,4,64,128]{3,2,1,0:T(8,128)(2,1)S(1)}, u32[]{:S(2)}, u32[]{:S(2)}) collective-permute-start(bf16[16,4,64,128]{3,2,1,0:T(8,128)(2,1)S(1)} %bitcast.72), channel_id=1, source_target_pairs={{0,64},{64,0},{1,65},{65,1},{2,66},{66,2},{3,67},{67,3},{4,68},{68... | collective-permute-start | bytes 3145736 | tf_op jit(solution)/shard_map/ppermute | solution.py:22
  157.8 24.0 %copy-start.5 = (bf16[256,512]{1,0:T(8,128)(2,1)S(1)}, bf16[256,512]{1,0:T(8,128)(2,1)}, u32[]{:S(2)}) copy-start(bf16[256,512]{1,0:T(8,128)(2,1)} %copy-done.4) | copy-start | bytes 786436
  157.8 1.7 collective-permute-start.8
  165.6 14.0 %collective-permute-start.11 = (bf16[256,512]{1,0:T(8,128)(2,1)}, bf16[256,512]{1,0:T(8,128)(2,1)S(1)}, u32[]{:S(2)}, u32[]{:S(2)}) collective-permute-start(bf16[256,512]{1,0:T(8,128)(2,1)} %get-tuple-element.22), channel_id=1, source_target_pairs={{0,3},{1,0},{2,1},{3,2},{4,7},{5,4},{6,5},{7,6},{8,11},{9,8},{10,9... | collective-permute-start | bytes 786440 | tf_op jit(solution)/shard_map/ppermute | solution.py:18
  168.4 11.3 %collective-permute-start.10 = (bf16[256,512]{1,0:T(8,128)(2,1)}, bf16[256,512]{1,0:T(8,128)(2,1)S(1)}, u32[]{:S(2)}, u32[]{:S(2)}) collective-permute-start(bf16[256,512]{1,0:T(8,128)(2,1)} %get-tuple-element.21), channel_id=1, source_target_pairs={{0,1},{1,2},{2,3},{3,0},{4,5},{5,6},{6,7},{7,4},{8,9},{9,10},{10,1... | collective-permute-start | bytes 786440 | tf_op jit(solution)/shard_map/ppermute | solution.py:18
  168.4 13.4 %collective-permute-start.9 = (bf16[256,512]{1,0:T(8,128)(2,1)}, bf16[256,512]{1,0:T(8,128)(2,1)S(1)}, u32[]{:S(2)}, u32[]{:S(2)}) collective-permute-start(bf16[256,512]{1,0:T(8,128)(2,1)} %get-tuple-element.20), channel_id=1, source_target_pairs={{0,2},{1,3},{2,0},{3,1},{4,6},{5,7},{6,4},{7,5},{8,10},{9,11},{10,... | collective-permute-start | bytes 786440 | tf_op jit(solution)/shard_map/ppermute | solution.py:18
  183.1 7.7 %collective-permute-start.12 = (bf16[256,512]{1,0:T(8,128)(2,1)S(1)}, bf16[256,512]{1,0:T(8,128)(2,1)S(1)}, u32[]{:S(2)}, u32[]{:S(2)}) collective-permute-start(bf16[256,512]{1,0:T(8,128)(2,1)S(1)} %add_convert_fusion.2.own_ref), channel_id=1, source_target_pairs={{0,1},{1,2},{2,3},{3,0},{4,5},{5,6},{6,7},{7,4},{8,9},{9,10},{10,1... | collective-permute-start | bytes 786440 | tf_op jit(solution)/shard_map/ppermute | solution.py:18
  183.1 13.6 %collective-permute-start.13 = (bf16[256,512]{1,0:T(8,128)(2,1)S(1)}, bf16[256,512]{1,0:T(8,128)(2,1)S(1)}, u32[]{:S(2)}, u32[]{:S(2)}) collective-permute-start(bf16[256,512]{1,0:T(8,128)(2,1)S(1)} %add_convert_fusion.2.own_ref), channel_id=1, source_target_pairs={{0,2},{1,3},{2,0},{3,1},{4,6},{5,7},{6,4},{7,5},{8,10},{9,11},{10,... | collective-permute-start | bytes 786440 | tf_op jit(solution)/shard_map/ppermute | solution.py:18
  185.7 12.0 %collective-permute-start.14 = (bf16[256,512]{1,0:T(8,128)(2,1)S(1)}, bf16[256,512]{1,0:T(8,128)(2,1)S(1)}, u32[]{:S(2)}, u32[]{:S(2)}) collective-permute-start(bf16[256,512]{1,0:T(8,128)(2,1)S(1)} %add_convert_fusion.2.own_ref), channel_id=1, source_target_pairs={{0,3},{1,0},{2,1},{3,2},{4,7},{5,4},{6,5},{7,6},{8,11},{9,8},{10,9... | collective-permute-start | bytes 786440 | tf_op jit(solution)/shard_map/ppermute | solution.py:18
  205.4 3.7 %collective-permute-start.15 = (f32[256,768]{1,0:T(8,128)}, f32[256,768]{1,0:T(8,128)S(1)}, u32[]{:S(2)}, u32[]{:S(2)}) collective-permute-start(f32[256,768]{1,0:T(8,128)} %get-tuple-element.24), channel_id=1, source_target_pairs={{0,64},{64,0},{1,65},{65,1},{2,66},{66,2},{3,67},{67,3},{4,68},{68... | collective-permute-start | bytes 2359304 | tf_op jit(solution)/shard_map/ppermute | solution.py:22
  233.5 4.1 %collective-permute-start.16 = (bf16[16,4,64,128]{3,2,1,0:T(8,128)(2,1)S(1)}, bf16[16,4,64,128]{3,2,1,0:T(8,128)(2,1)S(1)}, u32[]{:S(2)}, u32[]{:S(2)}) collective-permute-start(bf16[16,4,64,128]{3,2,1,0:T(8,128)(2,1)S(1)} %bitcast.74), channel_id=1, source_target_pairs={{0,64},{64,0},{1,65},{65,1},{2,66},{66,2},{3,67},{67,3},{4,68},{68... | collective-permute-start | bytes 3145736 | tf_op jit(solution)/shard_map/ppermute | solution.py:22
  246.7 24.1 %copy-start.1 = (bf16[256,512]{1,0:T(8,128)(2,1)S(1)}, bf16[256,512]{1,0:T(8,128)(2,1)}, u32[]{:S(2)}) copy-start(bf16[256,512]{1,0:T(8,128)(2,1)} %copy-done) | copy-start | bytes 786436
  246.7 1.7 collective-permute-start.17
  254.4 8.1 %collective-permute-start.20 = (bf16[256,512]{1,0:T(8,128)(2,1)}, bf16[256,512]{1,0:T(8,128)(2,1)S(1)}, u32[]{:S(2)}, u32[]{:S(2)}) collective-permute-start(bf16[256,512]{1,0:T(8,128)(2,1)} %get-tuple-element.28), channel_id=1, source_target_pairs={{0,3},{1,0},{2,1},{3,2},{4,7},{5,4},{6,5},{7,6},{8,11},{9,8},{10,9... | collective-permute-start | bytes 786440 | tf_op jit(solution)/shard_map/ppermute | solution.py:18
  256.5 14.3 %collective-permute-start.19 = (bf16[256,512]{1,0:T(8,128)(2,1)}, bf16[256,512]{1,0:T(8,128)(2,1)S(1)}, u32[]{:S(2)}, u32[]{:S(2)}) collective-permute-start(bf16[256,512]{1,0:T(8,128)(2,1)} %get-tuple-element.27), channel_id=1, source_target_pairs={{0,1},{1,2},{2,3},{3,0},{4,5},{5,6},{6,7},{7,4},{8,9},{9,10},{10,1... | collective-permute-start | bytes 786440 | tf_op jit(solution)/shard_map/ppermute | solution.py:18
  256.5 14.3 %collective-permute-start.18 = (bf16[256,512]{1,0:T(8,128)(2,1)}, bf16[256,512]{1,0:T(8,128)(2,1)S(1)}, u32[]{:S(2)}, u32[]{:S(2)}) collective-permute-start(bf16[256,512]{1,0:T(8,128)(2,1)} %get-tuple-element.26), channel_id=1, source_target_pairs={{0,2},{1,3},{2,0},{3,1},{4,6},{5,7},{6,4},{7,5},{8,10},{9,11},{10,... | collective-permute-start | bytes 786440 | tf_op jit(solution)/shard_map/ppermute | solution.py:18
  272.0 2.7 collective-permute-start.21
  (20 other events, 107.1 us)
Sparse Core Ops, SparseCore 0:
  13.7 90.6 all-gather.2
  106.5 84.1 all-gather.4

commit v2 on v1

--- a/solution.py
+++ b/solution.py
@@ -20,6 +20,16 @@
 
 def swapped(value):
     return lax.ppermute(value, "section", [(0, 1), (1, 0)])
+
+
+def ringed(value, stride, by):
+    size = lax.axis_size("blk")
+    side = 4
+    span = stride * side
+    pairs = [
+        (i, i // span * span + (i % span + by * stride) % span) for i in range(size)
+    ]
+    return lax.ppermute(value, "blk", pairs)
 
 
 def rope_tables(where_at, head_size):
@@ -177,128 +187,226 @@
     )(patches, merge_gain.reshape(1, -1), merge_first)
 
 
+def merger_outer_kernel(place, mine_ref, other_ref, weight_ref, out_ref):
+    section = place[0]
+    pieces, share, depth = out_ref.shape
+    tokens = mine_ref.shape[0]
+    runs = weight_ref.shape[1] // (2 * lane)
+    slices = runs * lane // depth
+    weight = jnp.concatenate(
+        [
+            weight_ref[:, pl.ds(pl.multiple_of((2 * run + section) * lane, lane), lane)]
+            for run in range(runs)
+        ],
+        axis=1,
+    )
+    for inner_ref, core in ((mine_ref, section), (other_ref, 1 - section)):
+        result = jnp.dot(inner_ref[...], weight, preferred_element_type=jnp.float32)
+        result = result.astype(out_ref.dtype)
+        for owner in range(tokens // share):
+            for piece in range(slices):
+                out_ref[(core * (tokens // share) + owner) * slices + piece] = result[
+                    owner * share : (owner + 1) * share, piece * depth : (piece + 1) * depth
+                ]
+
+
+def merger_outer(place, mine, other, merge_second, n_blk, n_mp):
+    whole = pl.BlockSpec(memory_space=pltpu.VMEM)
+    share = 2 * mine.shape[0] // n_blk
+    depth = merge_second.shape[1] // 2 // n_mp
+    return pl.pallas_call(
+        merger_outer_kernel,
+        out_shape=jax.ShapeDtypeStruct((n_blk * n_mp, share, depth), jnp.bfloat16),
+        in_specs=[pl.BlockSpec(memory_space=pltpu.SMEM), whole, whole, whole],
+        out_specs=whole,
+        name="merger_outer",
+    )(place, mine, other, merge_second)
+
+
 def project_in_kernel(
-    place, own_ref, from_one, from_two, from_three, gain_ref, weight_ref, kept_ref, sent_ref, rows_ref
+    place,
+    own_ref,
+    from_one,
+    from_two,
+    from_three,
+    gain_ref,
+    weight_hbm,
+    kept_ref,
+    sent_ref,
+    rows_ref,
+    weight_ref,
+    sums_ref,
+    semaphores,
 ):
-    step = pl.program_id(0)
-    count = pl.num_programs(0)
     pieces, _, depth = gain_ref.shape
-    columns = weight_ref.shape[1]
-    queries = (count - 1) * columns // 2
-
-    @pl.when(step == 0)
-    def _():
-        squares = jnp.zeros((own_ref.shape[0], 1), jnp.float32)
-        for by, part_ref in enumerate((own_ref, from_one, from_two, from_three)):
-            source = (place[0] + pieces - by) % pieces
-            part = part_ref[...].astype(jnp.float32)
-            squares = squares + jnp.sum(part * part, axis=1, keepdims=True)
-            rows_ref[source] = (part * gain_ref[source]).astype(jnp.bfloat16)
-        spread_squares = jnp.broadcast_to(squares, (squares.shape[0], lane))
-        kept_ref[:, queries + lane :] = spread_squares
-        sent_ref[:, queries + lane :] = spread_squares
-
-    result = jnp.dot(rows_ref[0], weight_ref[:depth, :], preferred_element_type=jnp.float32)
-    for piece in range(1, pieces):
-        result = result + jnp.dot(
+    width = weight_ref.shape[1]
+    queries = width // 2 - lane
+    copies = []
+    for piece in range(pieces):
+        span = (pl.ds(piece * depth, depth), pl.ds(0, width))
+        copies.append(
+            pltpu.make_async_copy(
+                weight_hbm.at[span], weight_ref.at[span], semaphores.at[piece]
+            )
+        )
+        copies[-1].start()
+    squares = jnp.zeros((own_ref.shape[0], 1), jnp.float32)
+    for by, part_ref in enumerate((own_ref, from_one, from_two, from_three)):
+        source = (place[2] + pieces - by) % pieces
+        part = part_ref[...].astype(jnp.float32)
+        squares = squares + jnp.sum(part * part, axis=1, keepdims=True)
+        rows_ref[source] = (part * gain_ref[source]).astype(jnp.bfloat16)
+    squares = jnp.broadcast_to(squares, (squares.shape[0], lane))
+    kept_ref[:, queries + lane :] = squares
+    sent_ref[:, queries + lane :] = squares
+    for piece in range(pieces):
+        copies[piece].wait()
+        result = jnp.dot(
             rows_ref[piece],
             weight_ref[piece * depth : (piece + 1) * depth, :],
             preferred_element_type=jnp.float32,
         )
-
-    for block in range((5 - 1) // 2):
-
-        @pl.when(step == block)
-        def _():
-            kept_ref[:, block * columns : (block + 1) * columns] = result
-
-        @pl.when(step == block + (5 - 1) // 2)
-        def _():
-            sent_ref[:, block * columns : (block + 1) * columns] = result
-
-    @pl.when(step == count - 1)
-    def _():
-        kept_ref[:, queries : queries + lane] = result[:, :lane]
-        sent_ref[:, queries : queries + lane] = result[:, lane:]
+        if piece > 0:
+            result = result + sums_ref[...]
+        if piece < pieces - 1:
+            sums_ref[...] = result
+    kept_ref[:, :queries] = result[:, :queries]
+    sent_ref[:, :queries] = result[:, queries : 2 * queries]
+    kept_ref[:, queries : queries + lane] = result[:, 2 * queries : 2 * queries + lane]
+    sent_ref[:, queries : queries + lane] = result[:, 2 * queries + lane :]
 
 
 def project_in(place, parts, gain, weight):
     rows, depth = parts[0].shape
-    columns = 2 * lane
-    skipped = 2 * depth // columns
-    steps = weight.shape[1] // columns - skipped
-    assert steps == 5
-    out = jax.ShapeDtypeStruct((rows, (steps - 1) * columns // 2 + 2 * lane), jnp.float32)
-    part_spec = pl.BlockSpec((rows, depth), lambda step, place: (0, 0))
-    out_spec = pl.BlockSpec(out.shape, lambda step, place: (0, 0))
+    width = 2 * (depth + lane)
+    out = jax.ShapeDtypeStruct((rows, width // 2 + lane), jnp.float32)
+    whole = pl.BlockSpec(memory_space=pltpu.VMEM)
     return pl.pallas_call(
         project_in_kernel,
         out_shape=(out, out),
-        grid_spec=pltpu.PrefetchScalarGridSpec(
-            num_scalar_prefetch=1,
-            grid=(steps,),
-            in_specs=[part_spec] * 4
-            + [
-                pl.BlockSpec(gain.shape, lambda step, place: (0, 0, 0)),
-                pl.BlockSpec((weight.shape[0], columns), lambda step, place: (0, step + skipped)),
-            ],
-            out_specs=[out_spec, out_spec],
-            scratch_shapes=[pltpu.VMEM((len(parts), rows, depth), jnp.bfloat16)],
-        ),
+        in_specs=[pl.BlockSpec(memory_space=pltpu.SMEM)]
+        + [whole] * 5
+        + [pl.BlockSpec(memory_space=pl.ANY)],
+        out_specs=(whole, whole),
+        scratch_shapes=[
+            pltpu.VMEM((len(parts), rows, depth), jnp.bfloat16),
+            pltpu.VMEM((weight.shape[0], width), jnp.bfloat16),
+            pltpu.VMEM((rows, width), jnp.float32),
+            pltpu.SemaphoreType.DMA((len(parts),)),
+        ],
         cost_estimate=pl.CostEstimate(
-            flops=2 * rows * weight.shape[0] * steps * columns,
-            bytes_accessed=2 * weight.shape[0] * steps * columns + 8 * rows * out.shape[1],
+            flops=2 * rows * weight.shape[0] * width,
+            bytes_accessed=2 * weight.shape[0] * width + 8 * rows * out.shape[1],
             transcendentals=0,
         ),
+        compiler_params=pltpu.CompilerParams(vmem_limit_bytes=24 << 20),
         name="project_in",
-    )(place.reshape(1), *parts, gain, weight)
-
-
-def project_out_kernel(place, mine_ref, other_ref, weight_ref, own_ref, one_ref, two_ref, three_ref):
+    )(place, *parts, gain, weight)
+
+
+def project_out_kernel(
+    place, mine_ref, other_ref, weight_hbm, own_ref, one_ref, two_ref, three_ref, weight_ref, semaphores
+):
     half = mine_ref.shape[1]
+    depth = own_ref.shape[1]
     over_last = (((1,), (1,)), ((), ()))
-    result = lax.dot_general(
-        mine_ref[...], weight_ref[:, :half], over_last, preferred_element_type=jnp.float32
-    ) + lax.dot_general(
-        other_ref[...], weight_ref[:, half:], over_last, preferred_element_type=jnp.float32
-    )
-    for by, out_ref in enumerate((own_ref, one_ref, two_ref, three_ref)):
-
-        @pl.when(pl.program_id(0) == by)
-        def _():
-            out_ref[...] = result.astype(out_ref.dtype)
+    outs = (own_ref, one_ref, two_ref, three_ref)
+    copies = []
+    for by in range(len(outs)):
+        source = (place[2] + by) % len(outs)
+        copies.append(
+            pltpu.make_async_copy(
+                weight_hbm.at[
+                    pl.ds(source * depth, depth), pl.ds(weight_hbm.shape[1] - 2 * half, 2 * half)
+                ],
+                weight_ref.at[by],
+                semaphores.at[by],
+            )
+        )
+        copies[-1].start()
+    for by, out_ref in enumerate(outs):
+        copies[by].wait()
+        result = lax.dot_general(
+            mine_ref[...], weight_ref[by, :, :half], over_last, preferred_element_type=jnp.float32
+        ) + lax.dot_general(
+            other_ref[...], weight_ref[by, :, half:], over_last, preferred_element_type=jnp.float32
+        )
+        out_ref[...] = result.astype(out_ref.dtype)
 
 
 def project_out(place, mine, other, weight):
     rows, half = mine.shape
     pieces = lax.axis_size("mp")
     depth = weight.shape[0] // pieces
-    shape = (rows, depth)
-    part_spec = pl.BlockSpec((rows, half), lambda step, place: (0, 0))
-    out_spec = pl.BlockSpec(shape, lambda step, place: (0, 0))
+    shape = jax.ShapeDtypeStruct((rows, depth), jnp.bfloat16)
+    whole = pl.BlockSpec(memory_space=pltpu.VMEM)
     return pl.pallas_call(
         project_out_kernel,
-        out_shape=[jax.ShapeDtypeStruct(shape, jnp.float32)]
-        + [jax.ShapeDtypeStruct(shape, jnp.bfloat16)] * (pieces - 1),
-        grid_spec=pltpu.PrefetchScalarGridSpec(
-            num_scalar_prefetch=1,
-            grid=(pieces,),
-            in_specs=[
-                part_spec,
-                part_spec,
-                pl.BlockSpec(
-                    (depth, 2 * half), lambda step, place: ((place[0] + step) % pieces, 0)
-                ),
-            ],
-            out_specs=[out_spec] * pieces,
-        ),
+        out_shape=[shape] * pieces,
+        in_specs=[
+            pl.BlockSpec(memory_space=pltpu.SMEM),
+            whole,
+            whole,
+            pl.BlockSpec(memory_space=pl.ANY),
+        ],
+        out_specs=[whole] * pieces,
+        scratch_shapes=[
+            pltpu.VMEM((pieces, depth, 2 * half), jnp.bfloat16),
+            pltpu.SemaphoreType.DMA((pieces,)),
+        ],
         cost_estimate=pl.CostEstimate(
             flops=4 * rows * half * weight.shape[0],
             bytes_accessed=4 * half * weight.shape[0] + 2 * rows * weight.shape[0],
             transcendentals=0,
         ),
+        compiler_params=pltpu.CompilerParams(vmem_limit_bytes=24 << 20),
         name="project_out",
-    )(place.reshape(1), mine, other, weight)
+    )(place, mine, other, weight)
+
+
+def project_out_ring_kernel(place, mine_ref, other_ref, *refs):
+    weights, outs = refs[:4], refs[4:]
+    side = len(weights)
+    half = mine_ref.shape[1]
+    over_last = (((1,), (1,)), ((), ()))
+    row, column = place[1] // side, place[1] % side
+    for back, weight_ref in enumerate(weights):
+        weight = weight_ref[...].reshape(-1, 2 * half)
+        result = lax.dot_general(
+            mine_ref[...], weight[:, :half], over_last, preferred_element_type=jnp.float32
+        ) + lax.dot_general(
+            other_ref[...], weight[:, half:], over_last, preferred_element_type=jnp.float32
+        )
+        result = result.astype(jnp.bfloat16)
+        ahead = (row + 2 * side - back - place[2]) % side
+        for by, out_ref in enumerate(outs):
+
+            @pl.when(ahead == by)
+            def _():
+                for run in range(side):
+                    at = pl.multiple_of(((column + side - run) % side) * lane, lane)
+                    out_ref[:, pl.ds(at, lane)] = result[:, run * lane : (run + 1) * lane]
+
+
+def project_out_ring(place, mine, other, weights):
+    rows, half = mine.shape
+    depth = weights[0].shape[0] * weights[0].shape[1]
+    shape = jax.ShapeDtypeStruct((rows, depth), jnp.bfloat16)
+    whole = pl.BlockSpec(memory_space=pltpu.VMEM)
+    total = depth * len(weights)
+    return pl.pallas_call(
+        project_out_ring_kernel,
+        out_shape=[shape] * len(weights),
+        in_specs=[pl.BlockSpec(memory_space=pltpu.SMEM)] + [whole] * (2 + len(weights)),
+        out_specs=[whole] * len(weights),
+        cost_estimate=pl.CostEstimate(
+            flops=4 * rows * half * total,
+            bytes_accessed=4 * half * total + 2 * rows * total,
+            transcendentals=0,
+        ),
+        compiler_params=pltpu.CompilerParams(vmem_limit_bytes=24 << 20),
+        name="project_out_ring",
+    )(place, mine, other, *weights)
 
 
 def local(
@@ -340,18 +448,18 @@
         query_rows, keyval_rows = query_own[keep_rows], keyval_own[keep_rows]
         out_rows = out_own[:, keep_rows].T
         halves = (core, 1 - core)
-        parts = [out_rows[:, half * heads_half : (half + 1) * heads_half] for half in halves]
-        parts += [query_rows[:, half * heads_half : (half + 1) * heads_half] for half in halves]
+        parts = [query_rows[:, half * heads_half : (half + 1) * heads_half] for half in halves]
         parts += [keyval_rows[:, half * head_size : (half + 1) * head_size] for half in halves]
+        parts += [out_rows[:, half * heads_half : (half + 1) * heads_half] for half in halves]
         return jnp.concatenate(parts, axis=1)
 
     for_first, for_second = packed(0), packed(1)
     weight_keep = jnp.where(first_core, for_first, for_second)
     weight_other = swapped(jnp.where(first_core, for_second, for_first))
-    weight_layers = [
-        jnp.where(first_core, weight_keep, weight_other),
-        jnp.where(first_core, weight_other, weight_keep),
-    ]
+    proj_width = 2 * (heads_half + head_size)
+    proj_first = jnp.where(first_core, weight_keep[:, :proj_width], weight_other[:, :proj_width])
+    out_first = jnp.where(first_core, weight_keep[:, proj_width:], weight_other[:, proj_width:])
+    weight_second = jnp.where(first_core, weight_other, weight_keep)
     gain_half = norm_gain[0].reshape(-1, 2, lane)
     gain_keep = jnp.where(first_core, gain_half[:, 0], gain_half[:, 1])
     gain_send = jnp.where(first_core, gain_half[:, 1], gain_half[:, 0])
@@ -360,36 +468,14 @@
         jnp.where(first_core, gain_keep, gain_other).reshape(n_mp, 1, -1),
         jnp.where(first_core, gain_other, gain_keep).reshape(n_mp, 1, -1),
     ]
-    weight_full = [
-        lax.all_gather(weight_layers[layer_index], "blk", axis=0, tiled=True)
-        for layer_index in range(layers)
-    ]
+    proj_full = lax.all_gather(proj_first, "blk", axis=0, tiled=True)
+    second_full = lax.all_gather(weight_second, "blk", axis=0, tiled=True)
+    out_near = jnp.stack([out_first] + [ringed(out_first, 1, by) for by in (1, 2, 3)])
 
     inner = merger_inner(patches, merge_gain, merge_first)
-    inner_other = swapped(inner)
-    inner_all = jnp.concatenate(
-        [
-            jnp.where(first_core, inner, inner_other),
-            jnp.where(first_core, inner_other, inner),
-        ],
-        axis=0,
-    )
-    second_half = my_half(merge_second, 1, section_index)
-    partial_merge = jnp.dot(inner_all, second_half, preferred_element_type=jnp.float32)
-    tokens = partial_merge.shape[0]
-    share = tokens // n_blk
-    merged_terms = lax.all_to_all(
-        partial_merge.astype(jnp.bfloat16)
-        .reshape(n_blk, share, n_mp, -1)
-        .transpose(0, 2, 1, 3)
-        .reshape(n_blk * n_mp, share, -1),
-        ("blk", "mp"),
-        0,
-        0,
-        tiled=True,
-    )
-    merged_mine = jnp.sum(merged_terms.astype(jnp.float32), axis=0).astype(jnp.bfloat16)
-    merged = spread(merged_mine).reshape(tokens, -1)
+    place = jnp.stack([section_index, cycle_index, model_index]).astype(jnp.int32)
+    merged_pieces = merger_outer(place, inner, swapped(inner), merge_second, n_blk, n_mp)
+    merged_terms = lax.all_to_all(merged_pieces, ("blk", "mp"), 0, 0, tiled=True)
 
     row_where = (
         jnp.arange(blocks)[:, None] * block_len
@@ -398,15 +484,21 @@
     ).reshape(-1)
     starts = jnp.stack([jnp.sum(segments < 1), jnp.sum(segments < 2)])
     scalars = jnp.concatenate([starts, jnp.stack([cycle_index, section_index])]).astype(jnp.int32)
-
-    is_visual = positions[None, :] == row_where[:, None]
-    picked = jnp.dot(
-        is_visual.astype(jnp.bfloat16), merged, preferred_element_type=jnp.float32
-    ).astype(jnp.bfloat16)
+    is_visual = (positions[None, :] == row_where[:, None]).astype(jnp.bfloat16)
+    has_visual = jnp.max(is_visual, axis=1, keepdims=True)
     text_rows = my_half(text_embeds.reshape(rows, slice_width), 1, section_index)
-    state = jnp.where(jnp.any(is_visual, axis=1)[:, None], picked, text_rows)
-
     cosine, sine = rope_tables(row_where, head_size)
+    merged_terms, scalars, is_visual, has_visual, text_rows, cosine, sine, out_near = (
+        lax.optimization_barrier(
+            (merged_terms, scalars, is_visual, has_visual, text_rows, cosine, sine, out_near)
+        )
+    )
+    out_far = [out_near] + [ringed(out_near, n_blk // 4, by) for by in (1, 2, 3)]
+    merged_mine = jnp.sum(merged_terms.astype(jnp.float32), axis=0).astype(jnp.bfloat16)
+    merged = spread(merged_mine).reshape(n_blk * merged_mine.shape[0], -1)
+    picked = jnp.dot(is_visual, merged, preferred_element_type=jnp.float32).astype(jnp.bfloat16)
+    state = jnp.where(has_visual > 0, picked, text_rows)
+
     cosine = cosine[:, None, :]
     sine = sine[:, None, :]
     keyval_cosine = jnp.where(first_core, cosine, 1.0)
@@ -414,9 +506,9 @@
 
     results = []
     for layer_index in range(layers):
-        weight = weight_full[layer_index]
         parts = [state] + [moved(state, "mp", by) for by in (1, 2, 3)]
-        kept, sent = project_in(model_index, parts, gain_layers[layer_index], weight)
+        weight = proj_full if layer_index == 0 else second_full
+        kept, sent = project_in(place, parts, gain_layers[layer_index], weight)
         total = kept + swapped(sent)
         squares = total[:, heads_half + head_size :][:, :1]
         total = total[:, : heads_half + head_size] * lax.rsqrt(
@@ -429,9 +521,12 @@
         gathered = spread(keyval).reshape(n_blk, blocks, rows_here, head_size)
         attended = attention(scalars, query, gathered, swapped(gathered))
         attended_other = swapped(attended)
-        total, *terms = project_out(model_index, attended, attended_other, weight)
+        if layer_index == 0:
+            own, *terms = project_out_ring(place, attended, attended_other, out_far)
+        else:
+            own, *terms = project_out(place, attended, attended_other, second_full)
         arrived = [moved(terms[by - 1], "mp", by) for by in (2, 1, 3)]
-        total = state.astype(jnp.float32) + total
+        total = state.astype(jnp.float32) + own.astype(jnp.float32)
         for part in arrived:
             total = total + part.astype(jnp.float32)
         state = total.astype(jnp.bfloat16)

time: 285 us -> 334 us (1.17)
  waiting for transfers between devices: 101 us -> 135 us
  starting transfers between devices: 41.9 us -> 64 us
  Pallas kernels: 44.6 us -> 33 us
  local copies, waits for them, and re-layouts: 18.9 us -> 26.5 us
    ppermute x0 -> x6, waiting for transfers between devices: none -> 82.9 us  [ringed(): return lax.ppermute(value, 'blk', pairs)]
    all_gather x2, waiting for transfers between devices: 22.5 us -> 0.02 us  [the longest x1 0.02 us: local(): proj_full = lax.all_gather(proj_first, 'blk', axis=0, tiled=True)]
    all_to_all x1, waiting for transfers between devices: 18.2 us -> 0.01 us  [local(): lax.all_to_all(merged_pieces, ('blk', 'mp'), 0, 0, tiled=True)]
    ppermute x10, starting transfers between devices: 12.1 us -> 22.2 us  [swapped(): return lax.ppermute(value, 'section', [(0, 1), (1, 0)])]
    pallas_call x4 -> x5, Pallas kernels: 24.5 us -> 15.6 us  [the longest x2 6.65 us: project_in(): pl.pallas_call(project_in_kernel, out_shape=(out, out), in_specs=[pl.Bloc...]
    unnamed x63 -> x50, local copies, waits for them, and re-layouts: 9.84 us -> 16.3 us
    ppermute x0 -> x6, starting transfers between devices: none -> 6.13 us  [ringed(): return lax.ppermute(value, 'blk', pairs)]
    all_to_all x1, starting transfers between devices: 3.7 us -> 8.14 us  [spread(): return lax.all_to_all(copies, 'blk', 0, 0, tiled=True)]
  transfers between devices with their start and end apart: 26 -> 32, of which waited for: 20 -> 21; matrix products, arithmetic and copies ran while one was open for 7% -> 5% of each run, Pallas kernels for 9% -> 6%
where the time goes in v2:
time: 334 us; the launch traced here: 333 us
  waiting for transfers between devices  135 us (40%)
  starting transfers between devices  64 us (19%)
  blocking collectives  48.5 us (15%)
  Pallas kernels  33 us (10%)
  local copies, waits for them, and re-layouts  26.5 us (8%)
  between operations  14 us (4%)
  other arithmetic  11.6 us (3%)
    ppermute x6, waiting for transfers between devices, ringed(): return lax.ppermute(value, 'blk', pairs)  82.9 us
    all_to_all x2, blocking collectives, spread(): return lax.all_to_all(copies, 'blk', 0, 0, tiled=True)  48.5 us
    ppermute x12, waiting for transfers between devices, moved(): lax.ppermute(value, axis, [(i, (i + by) % size) for i in range(size)])  34.8 us
    ppermute x10, starting transfers between devices, swapped(): return lax.ppermute(value, 'section', [(0, 1), (1, 0)])  22.2 us
    unnamed x50, local copies, waits for them, and re-layouts  16.3 us
    ppermute x12, starting transfers between devices, moved(): lax.ppermute(value, axis, [(i, (i + by) % size) for i in range(size)])  16.1 us
    pallas_call x2, Pallas kernels, attention(): pl.pallas_call(functools.partial(attention_kernel, chunk_runs=mine.shape[...  13.8 us
    all_to_all x1, starting transfers between devices, local(): lax.all_to_all(merged_pieces, ('blk', 'mp'), 0, 0, tiled=True)  11.3 us
  transfers between devices with their start and end apart: 32, of which 21 were waited for; matrix products, arithmetic and copies ran while one was open for 5% of the time, Pallas kernels for 6%

profile of v2, /device:TPU:1, one launch (start us, length us, event | category | flops | bytes accessed | tf_op | source)
XLA Modules:
  0.0 333.0 jit_solution(271445709557826328)
XLA Ops:
  16.2 3.6 %merger_inner.1.mine_ref = bf16[128,80]{1,0:T(8,128)(2,1)} custom-call(bf16[128,5120]{1,0:T(8,128)(2,1)} %patches_ref.1, f32[1,1280]{1,0:T(1,128)} %reshape.147.gain_ref, bf16[5120,80]{1,0:T(8,128)(2,1)} %copy.26.weight_ref), custom_call_target="tpu_custom_call" | custom-call | flops 104857600 | bytes 2129920 | tf_op jit(solution)/shard_map/merger_inner/pallas_call | solution.py:176
  24.4 2.6 merger_outer.1
  27.0 11.3 %all-to-all-start = ((bf16[64,16,512]{2,1,0:T(8,128)(2,1)}), bf16[64,16,512]{2,1,0:T(8,128)(2,1)S(1)}, u32[]{:S(2)}, u32[]{:S(2)}) async-start(bf16[64,16,512]{2,1,0:T(8,128)(2,1)} %merger_outer.1), calls=%async_computation | async-start | bytes 2097152 | tf_op jit(solution)/shard_map/all_to_all | solution.py:478
  44.5 18.9 %collective-permute-done.4 = bf16[128,1024]{1,0:T(8,128)(2,1)S(1)} collective-permute-done((bf16[128,1024]{1,0:T(8,128)(2,1)S(1)}, bf16[128,1024]{1,0:T(8,128)(2,1)S(1)}, u32[]{:S(2)}, u32[]{:S(2)}) %collective-permute-start.4) | collective-permute-done | bytes 262176 | tf_op jit(solution)/shard_map/ppermute | solution.py:32
  64.9 8.0 %collective-permute-done.2 = bf16[128,1024]{1,0:T(8,128)(2,1)S(1)} collective-permute-done((bf16[128,1024]{1,0:T(8,128)(2,1)S(1)}, bf16[128,1024]{1,0:T(8,128)(2,1)S(1)}, u32[]{:S(2)}, u32[]{:S(2)}) %collective-permute-start.2) | collective-permute-done | bytes 262176 | tf_op jit(solution)/shard_map/ppermute | solution.py:32
  73.9 8.1 %all-to-all-start.1 = ((bf16[16,16,512]{2,1,0:T(8,128)(2,1)}), bf16[16,16,512]{2,1,0:T(8,128)(2,1)S(1)}, u32[]{:S(2)}, u32[]{:S(2)}) async-start(bf16[16,16,512]{2,1,0:T(8,128)(2,1)} %broadcast_in_dim.52), calls=%async_computation.1 | async-start | bytes 524288 | tf_op jit(solution)/shard_map/all_to_all | solution.py:67
  82.1 7.5 %all-to-all-done.1 = bf16[16,16,512]{2,1,0:T(8,128)(2,1)S(1)} async-done(((bf16[16,16,512]{2,1,0:T(8,128)(2,1)}), bf16[16,16,512]{2,1,0:T(8,128)(2,1)S(1)}, u32[]{:S(2)}, u32[]{:S(2)}) %all-to-all-start.1) | async-done | bytes 262176 | tf_op jit(solution)/shard_map/all_to_all | solution.py:67
  94.6 5.4 %collective-permute-start.8 = (f32[16,128]{1,0:T(8,128)S(1)}, f32[16,128]{1,0:T(8,128)S(1)}, u32[]{:S(2)}, u32[]{:S(2)}) collective-permute-start(f32[16,128]{1,0:T(8,128)S(1)} %select_bitcast_fusion), channel_id=1, source_target_pairs={{0,64},{64,0},{1,65},{65,1},{2,66},{66,2},{3,67},{67,3},{4,68},{68... | collective-permute-start | bytes 24584 | tf_op jit(solution)/shard_map/ppermute | solution.py:22
  100.9 2.5 copy-done.2
  103.4 3.3 project_in.2
  106.7 5.7 %collective-permute-start.9 = (f32[256,768]{1,0:T(8,128)S(1)}, f32[256,768]{1,0:T(8,128)S(1)}, u32[]{:S(2)}, u32[]{:S(2)}) collective-permute-start(f32[256,768]{1,0:T(8,128)S(1)} %get-tuple-element.31), channel_id=1, source_target_pairs={{0,64},{64,0},{1,65},{65,1},{2,66},{66,2},{3,67},{67,3},{4,68},{68... | collective-permute-start | bytes 2359304 | tf_op jit(solution)/shard_map/ppermute | solution.py:22
  115.1 27.7 %all_to_all.20 = bf16[16,256,128]{2,1,0:T(8,128)(2,1)} all-to-all(bf16[16,256,128]{2,1,0:T(8,128)(2,1)S(1)} %broadcast_in_dim.56), channel_id=1, replica_groups=mesh['section'=2,'blk'=16,'mp'=4] {'blk'}, dimensions={0} | all-to-all | bytes 2097152 | tf_op jit(solution)/shard_map/all_to_all | solution.py:67
  142.8 3.1 collective-permute-start.10
  154.3 6.9 %attention.2.mine_ref = bf16[256,512]{1,0:T(8,128)(2,1)} custom-call(s32[4]{0:T(128)} %pad_add_fusion.1.scalars, bf16[256,512]{1,0:T(8,128)(2,1)} %bitcast.130, bf16[16,4,64,128]{3,2,1,0:T(8,128)(2,1)} %bitcast.24.mine_ref, bf16[16,4,64,128]{3,2,1,0:T(8,128)(2,1)} %collective-permute-done.10.other_ref), custom_call_target="tpu_custom_call" | custom-call | flops 134217728 | bytes 2621440 | tf_op jit(solution)/shard_map/attention/pallas_call | solution.py:145
  161.9 31.8 %collective-permute-done.12.refs_1_ = bf16[4,128,1024]{2,1,0:T(8,128)(2,1)S(1)} collective-permute-done((bf16[4,128,1024]{2,1,0:T(8,128)(2,1)S(1)}, bf16[4,128,1024]{2,1,0:T(8,128)(2,1)S(1)}, u32[]{:S(2)}, u32[]{:S(2)}) %collective-permute-start.12) | collective-permute-done | bytes 1048608 | tf_op jit(solution)/shard_map/ppermute | solution.py:32
  193.8 22.7 %collective-permute-done.13.refs_2_ = bf16[4,128,1024]{2,1,0:T(8,128)(2,1)S(1)} collective-permute-done((bf16[4,128,1024]{2,1,0:T(8,128)(2,1)S(1)}, bf16[4,128,1024]{2,1,0:T(8,128)(2,1)S(1)}, u32[]{:S(2)}, u32[]{:S(2)}) %collective-permute-start.13) | collective-permute-done | bytes 1048608 | tf_op jit(solution)/shard_map/ppermute | solution.py:32
  217.4 3.3 project_out_ring.1
  224.9 4.1 %collective-permute-done.17 = bf16[256,512]{1,0:T(8,128)(2,1)S(1)} collective-permute-done((bf16[256,512]{1,0:T(8,128)(2,1)S(1)}, bf16[256,512]{1,0:T(8,128)(2,1)S(1)}, u32[]{:S(2)}, u32[]{:S(2)}) %collective-permute-start.17) | collective-permute-done | bytes 262176 | tf_op jit(solution)/shard_map/ppermute | solution.py:18
  228.9 3.4 %collective-permute-done.16 = bf16[256,512]{1,0:T(8,128)(2,1)S(1)} collective-permute-done((bf16[256,512]{1,0:T(8,128)(2,1)S(1)}, bf16[256,512]{1,0:T(8,128)(2,1)S(1)}, u32[]{:S(2)}, u32[]{:S(2)}) %collective-permute-start.16) | collective-permute-done | bytes 262176 | tf_op jit(solution)/shard_map/ppermute | solution.py:18
  232.3 3.7 %collective-permute-done.15 = bf16[256,512]{1,0:T(8,128)(2,1)S(1)} collective-permute-done((bf16[256,512]{1,0:T(8,128)(2,1)S(1)}, bf16[256,512]{1,0:T(8,128)(2,1)S(1)}, u32[]{:S(2)}, u32[]{:S(2)}) %collective-permute-start.15) | collective-permute-done | bytes 262176 | tf_op jit(solution)/shard_map/ppermute | solution.py:18
  236.3 2.4 collective-permute-start.19
  239.9 2.8 collective-permute-done.18.from_one
  242.7 6.6 %collective-permute-done.19.from_two = bf16[256,512]{1,0:T(8,128)(2,1)S(1)} collective-permute-done((bf16[256,512]{1,0:T(8,128)(2,1)S(1)}, bf16[256,512]{1,0:T(8,128)(2,1)S(1)}, u32[]{:S(2)}, u32[]{:S(2)}) %collective-permute-start.19) | collective-permute-done | bytes 262176 | tf_op jit(solution)/shard_map/ppermute | solution.py:18
  250.7 3.7 %copy-done = bf16[2048,2304]{1,0:T(8,128)(2,1)S(1)} copy-done((bf16[2048,2304]{1,0:T(8,128)(2,1)S(1)}, bf16[2048,2304]{1,0:T(8,128)(2,1)}, u32[]{:S(2)}) %copy-start) | copy-done | bytes 9437208
  254.4 3.3 project_in.3
  262.9 20.7 %all_to_all.21 = bf16[16,256,128]{2,1,0:T(8,128)(2,1)S(1)} all-to-all(bf16[16,256,128]{2,1,0:T(8,128)(2,1)S(1)} %broadcast_in_dim.58), channel_id=1, replica_groups=mesh['section'=2,'blk'=16,'mp'=4] {'blk'}, dimensions={0} | all-to-all | bytes 2097152 | tf_op jit(solution)/shard_map/all_to_all | solution.py:67
  287.8 6.9 %attention.3.mine_ref = bf16[256,512]{1,0:T(8,128)(2,1)} custom-call(s32[4]{0:T(128)} %pad_add_fusion.1.scalars, bf16[256,512]{1,0:T(8,128)(2,1)} %bitcast.129, bf16[16,4,64,128]{3,2,1,0:T(8,128)(2,1)} %bitcast.122, bf16[16,4,64,128]{3,2,1,0:T(8,128)(2,1)} %collective-permute-done.22.other_ref), custom_call_target="tpu_custom_call" | custom-call | flops 134217728 | bytes 2621440 | tf_op jit(solution)/shard_map/attention/pallas_call | solution.py:145
  296.5 3.7 %copy-done.1 = bf16[2048,2304]{1,0:T(8,128)(2,1)S(1)} copy-done((bf16[2048,2304]{1,0:T(8,128)(2,1)S(1)}, bf16[2048,2304]{1,0:T(8,128)(2,1)}, u32[]{:S(2)}) %copy-start.1) | copy-done | bytes 9437208
  301.1 3.0 project_out.1
  304.2 2.4 collective-permute-start.26
  307.9 4.7 %collective-permute-done.26 = bf16[256,512]{1,0:T(8,128)(2,1)S(1)} collective-permute-done((bf16[256,512]{1,0:T(8,128)(2,1)S(1)}, bf16[256,512]{1,0:T(8,128)(2,1)S(1)}, u32[]{:S(2)}, u32[]{:S(2)}) %collective-permute-start.26) | collective-permute-done | bytes 262176 | tf_op jit(solution)/shard_map/ppermute | solution.py:18
  312.6 8.1 %collective-permute-done.25 = bf16[256,512]{1,0:T(8,128)(2,1)S(1)} collective-permute-done((bf16[256,512]{1,0:T(8,128)(2,1)S(1)}, bf16[256,512]{1,0:T(8,128)(2,1)S(1)}, u32[]{:S(2)}, u32[]{:S(2)}) %collective-permute-start.25) | collective-permute-done | bytes 262176 | tf_op jit(solution)/shard_map/ppermute | solution.py:18
  (157 shorter events, 66.9 us)
Async XLA Ops:
  6.5 94.3 %all-gather.3.cloned.1.call-start = ((), (), s32[]{:S(2)}) async-start(), calls=%async_computation.4 | async-start | bytes 5570560 | tf_op jit(solution)/shard_map/all_gather | solution.py:471
  8.4 3.1 collective-permute-start.1
  13.4 237.4 %all-gather.5.cloned.1.call-start = ((), (), s32[]{:S(2)}) async-start(), calls=%async_computation.5 | async-start | bytes 10027008 | tf_op jit(solution)/shard_map/all_gather | solution.py:472
  19.7 4.1 %collective-permute-start = (bf16[128,80]{1,0:T(8,128)(2,1)}, bf16[128,80]{1,0:T(8,128)(2,1)S(1)}, u32[]{:S(2)}, u32[]{:S(2)}) collective-permute-start(bf16[128,80]{1,0:T(8,128)(2,1)} %merger_inner.1.mine_ref), channel_id=1, source_target_pairs={{0,64},{64,0},{1,65},{65,1},{2,66},{66,2},{3,67},{67,3},{4,68},{68... | collective-permute-start | bytes 61448 | tf_op jit(solution)/shard_map/ppermute | solution.py:22
  27.0 45.9 %all-to-all-start = ((bf16[64,16,512]{2,1,0:T(8,128)(2,1)}), bf16[64,16,512]{2,1,0:T(8,128)(2,1)S(1)}, u32[]{:S(2)}, u32[]{:S(2)}) async-start(bf16[64,16,512]{2,1,0:T(8,128)(2,1)} %merger_outer.1), calls=%async_computation | async-start | bytes 2097152 | tf_op jit(solution)/shard_map/all_to_all | solution.py:478
  38.6 24.8 %collective-permute-start.4 = (bf16[128,1024]{1,0:T(8,128)(2,1)S(1)}, bf16[128,1024]{1,0:T(8,128)(2,1)S(1)}, u32[]{:S(2)}, u32[]{:S(2)}) collective-permute-start(bf16[128,1024]{1,0:T(8,128)(2,1)S(1)} %slice_select_fusion.1), channel_id=1, source_target_pairs={{0,12},{4,0},{8,4},{12,8},{16,28},{20,16},{24,20},{28,24},{32,44},... | collective-permute-start | bytes 786440 | tf_op jit(solution)/shard_map/ppermute | solution.py:32
  40.9 23.9 %collective-permute-start.3 = (bf16[128,1024]{1,0:T(8,128)(2,1)S(1)}, bf16[128,1024]{1,0:T(8,128)(2,1)S(1)}, u32[]{:S(2)}, u32[]{:S(2)}) collective-permute-start(bf16[128,1024]{1,0:T(8,128)(2,1)S(1)} %slice_select_fusion.1), channel_id=1, source_target_pairs={{0,8},{4,12},{8,0},{12,4},{16,24},{20,28},{24,16},{28,20},{32,40},... | collective-permute-start | bytes 786440 | tf_op jit(solution)/shard_map/ppermute | solution.py:32
  41.5 31.3 %collective-permute-start.2 = (bf16[128,1024]{1,0:T(8,128)(2,1)S(1)}, bf16[128,1024]{1,0:T(8,128)(2,1)S(1)}, u32[]{:S(2)}, u32[]{:S(2)}) collective-permute-start(bf16[128,1024]{1,0:T(8,128)(2,1)S(1)} %slice_select_fusion.1), channel_id=1, source_target_pairs={{0,4},{4,8},{8,12},{12,0},{16,20},{20,24},{24,28},{28,16},{32,36},... | collective-permute-start | bytes 786440 | tf_op jit(solution)/shard_map/ppermute | solution.py:32
  73.9 15.7 %all-to-all-start.1 = ((bf16[16,16,512]{2,1,0:T(8,128)(2,1)}), bf16[16,16,512]{2,1,0:T(8,128)(2,1)S(1)}, u32[]{:S(2)}, u32[]{:S(2)}) async-start(bf16[16,16,512]{2,1,0:T(8,128)(2,1)} %broadcast_in_dim.52), calls=%async_computation.1 | async-start | bytes 524288 | tf_op jit(solution)/shard_map/all_to_all | solution.py:67
  89.9 10.9 %collective-permute-start.5 = (bf16[256,512]{1,0:T(8,128)(2,1)S(1)}, bf16[256,512]{1,0:T(8,128)(2,1)S(1)}, u32[]{:S(2)}, u32[]{:S(2)}) collective-permute-start(bf16[256,512]{1,0:T(8,128)(2,1)S(1)} %broadcast_select_fusion.3.own_ref), channel_id=1, source_target_pairs={{0,1},{1,2},{2,3},{3,0},{4,5},{5,6},{6,7},{7,4},{8,9},{9,10},{10,1... | collective-permute-start | bytes 786440 | tf_op jit(solution)/shard_map/ppermute | solution.py:18
  91.1 9.7 %collective-permute-start.6 = (bf16[256,512]{1,0:T(8,128)(2,1)S(1)}, bf16[256,512]{1,0:T(8,128)(2,1)S(1)}, u32[]{:S(2)}, u32[]{:S(2)}) collective-permute-start(bf16[256,512]{1,0:T(8,128)(2,1)S(1)} %broadcast_select_fusion.3.own_ref), channel_id=1, source_target_pairs={{0,2},{1,3},{2,0},{3,1},{4,6},{5,7},{6,4},{7,5},{8,10},{9,11},{10,... | collective-permute-start | bytes 786440 | tf_op jit(solution)/shard_map/ppermute | solution.py:18
  93.3 7.5 %collective-permute-start.7 = (bf16[256,512]{1,0:T(8,128)(2,1)S(1)}, bf16[256,512]{1,0:T(8,128)(2,1)S(1)}, u32[]{:S(2)}, u32[]{:S(2)}) collective-permute-start(bf16[256,512]{1,0:T(8,128)(2,1)S(1)} %broadcast_select_fusion.3.own_ref), channel_id=1, source_target_pairs={{0,3},{1,0},{2,1},{3,2},{4,7},{5,4},{6,5},{7,6},{8,11},{9,8},{10,9... | collective-permute-start | bytes 786440 | tf_op jit(solution)/shard_map/ppermute | solution.py:18
  94.6 6.2 %collective-permute-start.8 = (f32[16,128]{1,0:T(8,128)S(1)}, f32[16,128]{1,0:T(8,128)S(1)}, u32[]{:S(2)}, u32[]{:S(2)}) collective-permute-start(f32[16,128]{1,0:T(8,128)S(1)} %select_bitcast_fusion), channel_id=1, source_target_pairs={{0,64},{64,0},{1,65},{65,1},{2,66},{66,2},{3,67},{67,3},{4,68},{68... | collective-permute-start | bytes 24584 | tf_op jit(solution)/shard_map/ppermute | solution.py:22
  106.7 7.6 %collective-permute-start.9 = (f32[256,768]{1,0:T(8,128)S(1)}, f32[256,768]{1,0:T(8,128)S(1)}, u32[]{:S(2)}, u32[]{:S(2)}) collective-permute-start(f32[256,768]{1,0:T(8,128)S(1)} %get-tuple-element.31), channel_id=1, source_target_pairs={{0,64},{64,0},{1,65},{65,1},{2,66},{66,2},{3,67},{67,3},{4,68},{68... | collective-permute-start | bytes 2359304 | tf_op jit(solution)/shard_map/ppermute | solution.py:22
  142.8 11.5 %collective-permute-start.10 = (bf16[16,4,64,128]{3,2,1,0:T(8,128)(2,1)}, bf16[16,4,64,128]{3,2,1,0:T(8,128)(2,1)}, u32[]{:S(2)}, u32[]{:S(2)}) collective-permute-start(bf16[16,4,64,128]{3,2,1,0:T(8,128)(2,1)} %bitcast.24.mine_ref), channel_id=1, source_target_pairs={{0,64},{64,0},{1,65},{65,1},{2,66},{66,2},{3,67},{67,3},{4,68},{68... | collective-permute-start | bytes 3145736 | tf_op jit(solution)/shard_map/ppermute | solution.py:22
  145.9 47.8 %collective-permute-start.12 = (bf16[4,128,1024]{2,1,0:T(8,128)(2,1)S(1)}, bf16[4,128,1024]{2,1,0:T(8,128)(2,1)S(1)}, u32[]{:S(2)}, u32[]{:S(2)}) collective-permute-start(bf16[4,128,1024]{2,1,0:T(8,128)(2,1)S(1)} %pad_maximum_fusion.refs_0_), channel_id=1, source_target_pairs={{0,16},{4,20},{8,24},{12,28},{16,32},{20,36},{24,40},{28,44},{32,4... | collective-permute-start | bytes 3145736 | tf_op jit(solution)/shard_map/ppermute | solution.py:32
  145.9 70.6 %collective-permute-start.13 = (bf16[4,128,1024]{2,1,0:T(8,128)(2,1)S(1)}, bf16[4,128,1024]{2,1,0:T(8,128)(2,1)S(1)}, u32[]{:S(2)}, u32[]{:S(2)}) collective-permute-start(bf16[4,128,1024]{2,1,0:T(8,128)(2,1)S(1)} %pad_maximum_fusion.refs_0_), channel_id=1, source_target_pairs={{0,32},{4,36},{8,40},{12,44},{16,48},{20,52},{24,56},{28,60},{32,0... | collective-permute-start | bytes 3145736 | tf_op jit(solution)/shard_map/ppermute | solution.py:32
  147.6 68.8 %collective-permute-start.14 = (bf16[4,128,1024]{2,1,0:T(8,128)(2,1)S(1)}, bf16[4,128,1024]{2,1,0:T(8,128)(2,1)}, u32[]{:S(2)}, u32[]{:S(2)}) collective-permute-start(bf16[4,128,1024]{2,1,0:T(8,128)(2,1)S(1)} %pad_maximum_fusion.refs_0_), channel_id=1, source_target_pairs={{0,48},{4,52},{8,56},{12,60},{16,0},{20,4},{24,8},{28,12},{32,16},... | collective-permute-start | bytes 3145736 | tf_op jit(solution)/shard_map/ppermute | solution.py:32
  161.2 55.3 %collective-permute-start.11 = (bf16[256,512]{1,0:T(8,128)(2,1)}, bf16[256,512]{1,0:T(8,128)(2,1)S(1)}, u32[]{:S(2)}, u32[]{:S(2)}) collective-permute-start(bf16[256,512]{1,0:T(8,128)(2,1)} %attention.2.mine_ref), channel_id=1, source_target_pairs={{0,64},{64,0},{1,65},{65,1},{2,66},{66,2},{3,67},{67,3},{4,68},{68... | collective-permute-start | bytes 786440 | tf_op jit(solution)/shard_map/ppermute | solution.py:22
  220.7 8.2 %collective-permute-start.17 = (bf16[256,512]{1,0:T(8,128)(2,1)S(1)}, bf16[256,512]{1,0:T(8,128)(2,1)S(1)}, u32[]{:S(2)}, u32[]{:S(2)}) collective-permute-start(bf16[256,512]{1,0:T(8,128)(2,1)S(1)} %get-tuple-element.38), channel_id=1, source_target_pairs={{0,3},{1,0},{2,1},{3,2},{4,7},{5,4},{6,5},{7,6},{8,11},{9,8},{10,9... | collective-permute-start | bytes 786440 | tf_op jit(solution)/shard_map/ppermute | solution.py:18
  223.1 9.2 %collective-permute-start.16 = (bf16[256,512]{1,0:T(8,128)(2,1)S(1)}, bf16[256,512]{1,0:T(8,128)(2,1)S(1)}, u32[]{:S(2)}, u32[]{:S(2)}) collective-permute-start(bf16[256,512]{1,0:T(8,128)(2,1)S(1)} %get-tuple-element.37), channel_id=1, source_target_pairs={{0,1},{1,2},{2,3},{3,0},{4,5},{5,6},{6,7},{7,4},{8,9},{9,10},{10,1... | collective-permute-start | bytes 786440 | tf_op jit(solution)/shard_map/ppermute | solution.py:18
  223.1 12.9 %collective-permute-start.15 = (bf16[256,512]{1,0:T(8,128)(2,1)S(1)}, bf16[256,512]{1,0:T(8,128)(2,1)S(1)}, u32[]{:S(2)}, u32[]{:S(2)}) collective-permute-start(bf16[256,512]{1,0:T(8,128)(2,1)S(1)} %get-tuple-element.36), channel_id=1, source_target_pairs={{0,2},{1,3},{2,0},{3,1},{4,6},{5,7},{6,4},{7,5},{8,10},{9,11},{10,... | collective-permute-start | bytes 786440 | tf_op jit(solution)/shard_map/ppermute | solution.py:18
  236.2 6.5 %collective-permute-start.18 = (bf16[256,512]{1,0:T(8,128)(2,1)S(1)}, bf16[256,512]{1,0:T(8,128)(2,1)S(1)}, u32[]{:S(2)}, u32[]{:S(2)}) collective-permute-start(bf16[256,512]{1,0:T(8,128)(2,1)S(1)} %add_convert_fusion.2.own_ref), channel_id=1, source_target_pairs={{0,1},{1,2},{2,3},{3,0},{4,5},{5,6},{6,7},{7,4},{8,9},{9,10},{10,1... | collective-permute-start | bytes 786440 | tf_op jit(solution)/shard_map/ppermute | solution.py:18
  236.3 13.0 %collective-permute-start.19 = (bf16[256,512]{1,0:T(8,128)(2,1)S(1)}, bf16[256,512]{1,0:T(8,128)(2,1)S(1)}, u32[]{:S(2)}, u32[]{:S(2)}) collective-permute-start(bf16[256,512]{1,0:T(8,128)(2,1)S(1)} %add_convert_fusion.2.own_ref), channel_id=1, source_target_pairs={{0,2},{1,3},{2,0},{3,1},{4,6},{5,7},{6,4},{7,5},{8,10},{9,11},{10,... | collective-permute-start | bytes 786440 | tf_op jit(solution)/shard_map/ppermute | solution.py:18
  238.7 12.0 %collective-permute-start.20 = (bf16[256,512]{1,0:T(8,128)(2,1)S(1)}, bf16[256,512]{1,0:T(8,128)(2,1)S(1)}, u32[]{:S(2)}, u32[]{:S(2)}) collective-permute-start(bf16[256,512]{1,0:T(8,128)(2,1)S(1)} %add_convert_fusion.2.own_ref), channel_id=1, source_target_pairs={{0,3},{1,0},{2,1},{3,2},{4,7},{5,4},{6,5},{7,6},{8,11},{9,8},{10,9... | collective-permute-start | bytes 786440 | tf_op jit(solution)/shard_map/ppermute | solution.py:18
  257.7 3.7 %collective-permute-start.21 = (f32[256,768]{1,0:T(8,128)S(1)}, f32[256,768]{1,0:T(8,128)S(1)}, u32[]{:S(2)}, u32[]{:S(2)}) collective-permute-start(f32[256,768]{1,0:T(8,128)S(1)} %get-tuple-element.40), channel_id=1, source_target_pairs={{0,64},{64,0},{1,65},{65,1},{2,66},{66,2},{3,67},{67,3},{4,68},{68... | collective-permute-start | bytes 2359304 | tf_op jit(solution)/shard_map/ppermute | solution.py:22
  283.7 4.2 %collective-permute-start.22 = (bf16[16,4,64,128]{3,2,1,0:T(8,128)(2,1)S(1)}, bf16[16,4,64,128]{3,2,1,0:T(8,128)(2,1)}, u32[]{:S(2)}, u32[]{:S(2)}) collective-permute-start(bf16[16,4,64,128]{3,2,1,0:T(8,128)(2,1)S(1)} %bitcast.121), channel_id=1, source_target_pairs={{0,64},{64,0},{1,65},{65,1},{2,66},{66,2},{3,67},{67,3},{4,68},{68... | collective-permute-start | bytes 3145736 | tf_op jit(solution)/shard_map/ppermute | solution.py:22
  294.7 1.7 collective-permute-start.23
  304.2 8.4 %collective-permute-start.26 = (bf16[256,512]{1,0:T(8,128)(2,1)S(1)}, bf16[256,512]{1,0:T(8,128)(2,1)S(1)}, u32[]{:S(2)}, u32[]{:S(2)}) collective-permute-start(bf16[256,512]{1,0:T(8,128)(2,1)S(1)} %get-tuple-element.44), channel_id=1, source_target_pairs={{0,3},{1,0},{2,1},{3,2},{4,7},{5,4},{6,5},{7,6},{8,11},{9,8},{10,9... | collective-permute-start | bytes 786440 | tf_op jit(solution)/shard_map/ppermute | solution.py:18
  306.6 14.1 %collective-permute-start.25 = (bf16[256,512]{1,0:T(8,128)(2,1)S(1)}, bf16[256,512]{1,0:T(8,128)(2,1)S(1)}, u32[]{:S(2)}, u32[]{:S(2)}) collective-permute-start(bf16[256,512]{1,0:T(8,128)(2,1)S(1)} %get-tuple-element.43), channel_id=1, source_target_pairs={{0,1},{1,2},{2,3},{3,0},{4,5},{5,6},{6,7},{7,4},{8,9},{9,10},{10,1... | collective-permute-start | bytes 786440 | tf_op jit(solution)/shard_map/ppermute | solution.py:18
  306.6 14.1 %collective-permute-start.24 = (bf16[256,512]{1,0:T(8,128)(2,1)S(1)}, bf16[256,512]{1,0:T(8,128)(2,1)S(1)}, u32[]{:S(2)}, u32[]{:S(2)}) collective-permute-start(bf16[256,512]{1,0:T(8,128)(2,1)S(1)} %get-tuple-element.42), channel_id=1, source_target_pairs={{0,2},{1,3},{2,0},{3,1},{4,6},{5,7},{6,4},{7,5},{8,10},{9,11},{10,... | collective-permute-start | bytes 786440 | tf_op jit(solution)/shard_map/ppermute | solution.py:18
  320.8 2.7 collective-permute-start.27
  (19 other events, 154.1 us)
Sparse Core Ops, SparseCore 0:
  13.5 72.1 all-gather.2
  87.8 121.0 all-gather.4

commit v3 on v2

--- a/solution.py
+++ b/solution.py
@@ -20,16 +20,6 @@
 
 def swapped(value):
     return lax.ppermute(value, "section", [(0, 1), (1, 0)])
-
-
-def ringed(value, stride, by):
-    size = lax.axis_size("blk")
-    side = 4
-    span = stride * side
-    pairs = [
-        (i, i // span * span + (i % span + by * stride) % span) for i in range(size)
-    ]
-    return lax.ppermute(value, "blk", pairs)
 
 
 def rope_tables(where_at, head_size):
@@ -239,11 +229,10 @@
     semaphores,
 ):
     pieces, _, depth = gain_ref.shape
-    width = weight_ref.shape[1]
-    queries = width // 2 - lane
+    half = weight_ref.shape[1] // 2
     copies = []
     for piece in range(pieces):
-        span = (pl.ds(piece * depth, depth), pl.ds(0, width))
+        span = (pl.ds(piece * depth, depth), pl.ds(0, 2 * half))
         copies.append(
             pltpu.make_async_copy(
                 weight_hbm.at[span], weight_ref.at[span], semaphores.at[piece]
@@ -254,11 +243,13 @@
     for by, part_ref in enumerate((own_ref, from_one, from_two, from_three)):
         source = (place[2] + pieces - by) % pieces
         part = part_ref[...].astype(jnp.float32)
-        squares = squares + jnp.sum(part * part, axis=1, keepdims=True)
+        if kept_ref.shape[1] > half:
+            squares = squares + jnp.sum(part * part, axis=1, keepdims=True)
         rows_ref[source] = (part * gain_ref[source]).astype(jnp.bfloat16)
-    squares = jnp.broadcast_to(squares, (squares.shape[0], lane))
-    kept_ref[:, queries + lane :] = squares
-    sent_ref[:, queries + lane :] = squares
+    if kept_ref.shape[1] > half:
+        squares = jnp.broadcast_to(squares, (squares.shape[0], lane))
+        kept_ref[:, half:] = squares
+        sent_ref[:, half:] = squares
     for piece in range(pieces):
         copies[piece].wait()
         result = jnp.dot(
@@ -270,16 +261,14 @@
             result = result + sums_ref[...]
         if piece < pieces - 1:
             sums_ref[...] = result
-    kept_ref[:, :queries] = result[:, :queries]
-    sent_ref[:, :queries] = result[:, queries : 2 * queries]
-    kept_ref[:, queries : queries + lane] = result[:, 2 * queries : 2 * queries + lane]
-    sent_ref[:, queries : queries + lane] = result[:, 2 * queries + lane :]
-
-
-def project_in(place, parts, gain, weight):
+    kept_ref[:, :half] = result[:, :half]
+    sent_ref[:, :half] = result[:, half:]
+
+
+def project_in(place, parts, gain, weight, width, with_squares):
     rows, depth = parts[0].shape
-    width = 2 * (depth + lane)
-    out = jax.ShapeDtypeStruct((rows, width // 2 + lane), jnp.float32)
+    spare = lane if with_squares else 0
+    out = jax.ShapeDtypeStruct((rows, width // 2 + spare), jnp.float32)
     whole = pl.BlockSpec(memory_space=pltpu.VMEM)
     return pl.pallas_call(
         project_in_kernel,
@@ -300,7 +289,7 @@
             transcendentals=0,
         ),
         compiler_params=pltpu.CompilerParams(vmem_limit_bytes=24 << 20),
-        name="project_in",
+        name="project_kv" if with_squares else "project_q",
     )(place, *parts, gain, weight)
 
 
@@ -364,51 +353,6 @@
     )(place, mine, other, weight)
 
 
-def project_out_ring_kernel(place, mine_ref, other_ref, *refs):
-    weights, outs = refs[:4], refs[4:]
-    side = len(weights)
-    half = mine_ref.shape[1]
-    over_last = (((1,), (1,)), ((), ()))
-    row, column = place[1] // side, place[1] % side
-    for back, weight_ref in enumerate(weights):
-        weight = weight_ref[...].reshape(-1, 2 * half)
-        result = lax.dot_general(
-            mine_ref[...], weight[:, :half], over_last, preferred_element_type=jnp.float32
-        ) + lax.dot_general(
-            other_ref[...], weight[:, half:], over_last, preferred_element_type=jnp.float32
-        )
-        result = result.astype(jnp.bfloat16)
-        ahead = (row + 2 * side - back - place[2]) % side
-        for by, out_ref in enumerate(outs):
-
-            @pl.when(ahead == by)
-            def _():
-                for run in range(side):
-                    at = pl.multiple_of(((column + side - run) % side) * lane, lane)
-                    out_ref[:, pl.ds(at, lane)] = result[:, run * lane : (run + 1) * lane]
-
-
-def project_out_ring(place, mine, other, weights):
-    rows, half = mine.shape
-    depth = weights[0].shape[0] * weights[0].shape[1]
-    shape = jax.ShapeDtypeStruct((rows, depth), jnp.bfloat16)
-    whole = pl.BlockSpec(memory_space=pltpu.VMEM)
-    total = depth * len(weights)
-    return pl.pallas_call(
-        project_out_ring_kernel,
-        out_shape=[shape] * len(weights),
-        in_specs=[pl.BlockSpec(memory_space=pltpu.SMEM)] + [whole] * (2 + len(weights)),
-        out_specs=[whole] * len(weights),
-        cost_estimate=pl.CostEstimate(
-            flops=4 * rows * half * total,
-            bytes_accessed=4 * half * total + 2 * rows * total,
-            transcendentals=0,
-        ),
-        compiler_params=pltpu.CompilerParams(vmem_limit_bytes=24 << 20),
-        name="project_out_ring",
-    )(place, mine, other, *weights)
-
-
 def local(
     patches,
     merge_gain,
@@ -448,18 +392,20 @@
         query_rows, keyval_rows = query_own[keep_rows], keyval_own[keep_rows]
         out_rows = out_own[:, keep_rows].T
         halves = (core, 1 - core)
-        parts = [query_rows[:, half * heads_half : (half + 1) * heads_half] for half in halves]
-        parts += [keyval_rows[:, half * head_size : (half + 1) * head_size] for half in halves]
+        parts = [keyval_rows[:, half * head_size : (half + 1) * head_size] for half in halves]
+        parts += [query_rows[:, half * heads_half : (half + 1) * heads_half] for half in halves]
         parts += [out_rows[:, half * heads_half : (half + 1) * heads_half] for half in halves]
         return jnp.concatenate(parts, axis=1)
 
     for_first, for_second = packed(0), packed(1)
     weight_keep = jnp.where(first_core, for_first, for_second)
     weight_other = swapped(jnp.where(first_core, for_second, for_first))
-    proj_width = 2 * (heads_half + head_size)
-    proj_first = jnp.where(first_core, weight_keep[:, :proj_width], weight_other[:, :proj_width])
-    out_first = jnp.where(first_core, weight_keep[:, proj_width:], weight_other[:, proj_width:])
-    weight_second = jnp.where(first_core, weight_other, weight_keep)
+    keyval_width = 2 * head_size
+    keyval_shards, weight_full = [], []
+    for home in range(layers):
+        mine = jnp.where(section_index == home, weight_keep, weight_other)
+        keyval_shards.append(mine[:, :keyval_width])
+        weight_full.append(lax.all_gather(mine[:, keyval_width:], "blk", axis=0, tiled=True))
     gain_half = norm_gain[0].reshape(-1, 2, lane)
     gain_keep = jnp.where(first_core, gain_half[:, 0], gain_half[:, 1])
     gain_send = jnp.where(first_core, gain_half[:, 1], gain_half[:, 0])
@@ -468,13 +414,14 @@
         jnp.where(first_core, gain_keep, gain_other).reshape(n_mp, 1, -1),
         jnp.where(first_core, gain_other, gain_keep).reshape(n_mp, 1, -1),
     ]
-    proj_full = lax.all_gather(proj_first, "blk", axis=0, tiled=True)
-    second_full = lax.all_gather(weight_second, "blk", axis=0, tiled=True)
-    out_near = jnp.stack([out_first] + [ringed(out_first, 1, by) for by in (1, 2, 3)])
+    keyval_weight_full = spread(keyval_shards[0])
 
     inner = merger_inner(patches, merge_gain, merge_first)
     place = jnp.stack([section_index, cycle_index, model_index]).astype(jnp.int32)
     merged_pieces = merger_outer(place, inner, swapped(inner), merge_second, n_blk, n_mp)
+    merged_pieces, keyval_weight_full = lax.optimization_barrier(
+        (merged_pieces, keyval_weight_full)
+    )
     merged_terms = lax.all_to_all(merged_pieces, ("blk", "mp"), 0, 0, tiled=True)
 
     row_where = (
@@ -488,43 +435,42 @@
     has_visual = jnp.max(is_visual, axis=1, keepdims=True)
     text_rows = my_half(text_embeds.reshape(rows, slice_width), 1, section_index)
     cosine, sine = rope_tables(row_where, head_size)
-    merged_terms, scalars, is_visual, has_visual, text_rows, cosine, sine, out_near = (
+    merged_terms, scalars, is_visual, has_visual, text_rows, cosine, sine = (
         lax.optimization_barrier(
-            (merged_terms, scalars, is_visual, has_visual, text_rows, cosine, sine, out_near)
+            (merged_terms, scalars, is_visual, has_visual, text_rows, cosine, sine)
         )
     )
-    out_far = [out_near] + [ringed(out_near, n_blk // 4, by) for by in (1, 2, 3)]
     merged_mine = jnp.sum(merged_terms.astype(jnp.float32), axis=0).astype(jnp.bfloat16)
     merged = spread(merged_mine).reshape(n_blk * merged_mine.shape[0], -1)
     picked = jnp.dot(is_visual, merged, preferred_element_type=jnp.float32).astype(jnp.bfloat16)
     state = jnp.where(has_visual > 0, picked, text_rows)
 
-    cosine = cosine[:, None, :]
-    sine = sine[:, None, :]
     keyval_cosine = jnp.where(first_core, cosine, 1.0)
     keyval_sine = jnp.where(first_core, sine, 0.0)
 
     results = []
     for layer_index in range(layers):
         parts = [state] + [moved(state, "mp", by) for by in (1, 2, 3)]
-        weight = proj_full if layer_index == 0 else second_full
-        kept, sent = project_in(place, parts, gain_layers[layer_index], weight)
+        gain = gain_layers[layer_index]
+        weight = weight_full[layer_index]
+        kept, sent = project_in(
+            place, parts, gain, keyval_weight_full.reshape(-1, keyval_width), keyval_width, True
+        )
         total = kept + swapped(sent)
-        squares = total[:, heads_half + head_size :][:, :1]
-        total = total[:, : heads_half + head_size] * lax.rsqrt(
-            squares / (n_mp * slice_width) + epsilon
-        )
-        query = total[:, :heads_half].reshape(rows, -1, head_size)
-        query = rotate(query, cosine, sine).astype(jnp.bfloat16).reshape(rows, heads_half)
-        keyval = total[:, None, heads_half:]
-        keyval = rotate(keyval, keyval_cosine, keyval_sine).astype(jnp.bfloat16)[:, 0]
+        shrink = lax.rsqrt(total[:, head_size : head_size + 1] / (n_mp * slice_width) + epsilon)
+        keyval = rotate(total[:, :head_size] * shrink, keyval_cosine, keyval_sine).astype(jnp.bfloat16)
+        keyval, parts = lax.optimization_barrier((keyval, parts))
+        kept, sent = project_in(place, parts, gain, weight, 2 * heads_half, False)
+        query = ((kept + swapped(sent)) * shrink).reshape(rows, -1, head_size)
+        query = rotate(query, cosine[:, None, :], sine[:, None, :])
+        query = query.astype(jnp.bfloat16).reshape(rows, heads_half)
         gathered = spread(keyval).reshape(n_blk, blocks, rows_here, head_size)
         attended = attention(scalars, query, gathered, swapped(gathered))
+        if layer_index + 1 < layers:
+            attended, shard = lax.optimization_barrier((attended, keyval_shards[layer_index + 1]))
+            keyval_weight_full = spread(shard)
         attended_other = swapped(attended)
-        if layer_index == 0:
-            own, *terms = project_out_ring(place, attended, attended_other, out_far)
-        else:
-            own, *terms = project_out(place, attended, attended_other, second_full)
+        own, *terms = project_out(place, attended, attended_other, weight)
         arrived = [moved(terms[by - 1], "mp", by) for by in (2, 1, 3)]
         total = state.astype(jnp.float32) + own.astype(jnp.float32)
         for part in arrived:

time: 334 us -> 273 us (0.82)
  blocking collectives: 48.5 us -> 0 us
  waiting for transfers between devices: 135 us -> 99.2 us
  starting transfers between devices: 64 us -> 81.3 us
  local copies, waits for them, and re-layouts: 26.5 us -> 32.9 us
  Pallas kernels: 33 us -> 36.4 us
    ppermute x6 -> x0, waiting for transfers between devices: 82.9 us -> none  [ringed(): return lax.ppermute(value, 'blk', pairs)]
    all_to_all x2 -> x0, blocking collectives: 48.5 us -> none  [spread(): return lax.all_to_all(copies, 'blk', 0, 0, tiled=True)]
    all_to_all x1 -> x5, waiting for transfers between devices: 7.49 us -> 45.3 us  [spread(): return lax.all_to_all(copies, 'blk', 0, 0, tiled=True)]
    all_to_all x1 -> x5, starting transfers between devices: 8.14 us -> 25.5 us  [spread(): return lax.all_to_all(copies, 'blk', 0, 0, tiled=True)]
    all_to_all x1, waiting for transfers between devices: 0.01 us -> 12.4 us  [local(): lax.all_to_all(merged_pieces, ('blk', 'mp'), 0, 0, tiled=True)]
    ppermute x10 -> x12, starting transfers between devices: 22.2 us -> 29.9 us  [swapped(): return lax.ppermute(value, 'section', [(0, 1), (1, 0)])]
    ppermute x6 -> x0, starting transfers between devices: 6.13 us -> none  [ringed(): return lax.ppermute(value, 'blk', pairs)]
    broadcast_in_dim x3 -> x5, local copies, waits for them, and re-layouts: 1.12 us -> 5.31 us  [spread(): copies = jnp.broadcast_to(value[None], (size,) + value.shape)]
  transfers between devices with their start and end apart: 32 -> 32, of which waited for: 21 -> 18; matrix products, arithmetic and copies ran while one was open for 5% -> 7% of each run, Pallas kernels for 6% -> 10%
where the time goes in v3:
time: 273 us
  waiting for transfers between devices  99.2 us (36%)
  starting transfers between devices  81.3 us (30%)
  Pallas kernels  36.4 us (13%)
  local copies, waits for them, and re-layouts  32.9 us (12%)
  between operations  14 us (5%)
  other arithmetic  8.71 us (3%)
    all_to_all x5, waiting for transfers between devices, spread(): return lax.all_to_all(copies, 'blk', 0, 0, tiled=True)  45.3 us
    ppermute x12, waiting for transfers between devices, moved(): lax.ppermute(value, axis, [(i, (i + by) % size) for i in range(size)])  33.5 us
    ppermute x12, starting transfers between devices, swapped(): return lax.ppermute(value, 'section', [(0, 1), (1, 0)])  29.9 us
    all_to_all x5, starting transfers between devices, spread(): return lax.all_to_all(copies, 'blk', 0, 0, tiled=True)  25.5 us
    unnamed x48, local copies, waits for them, and re-layouts  18.5 us
    ppermute x12, starting transfers between devices, moved(): lax.ppermute(value, axis, [(i, (i + by) % size) for i in range(size)])  16.8 us
    pallas_call x2, Pallas kernels, attention(): pl.pallas_call(functools.partial(attention_kernel, chunk_runs=mine.shape[...  13.8 us
    all_to_all x1, waiting for transfers between devices, local(): lax.all_to_all(merged_pieces, ('blk', 'mp'), 0, 0, tiled=True)  12.4 us
  transfers between devices with their start and end apart: 32, of which 18 were waited for; matrix products, arithmetic and copies ran while one was open for 7% of the time, Pallas kernels for 10%

profile of v3, /device:TPU:1, one launch (start us, length us, event | category | flops | bytes accessed | tf_op | source)
XLA Modules:
  0.0 272.7 jit_solution(15244204587952301159)
XLA Ops:
  15.6 7.0 %all-to-all-start = ((bf16[16,128,256]{2,1,0:T(8,128)(2,1)}), bf16[16,128,256]{2,1,0:T(8,128)(2,1)S(1)}, u32[]{:S(2)}, u32[]{:S(2)}) async-start(bf16[16,128,256]{2,1,0:T(8,128)(2,1)} %broadcast_in_dim.29), calls=%async_computation | async-start | bytes 2097152 | tf_op jit(solution)/shard_map/all_to_all | solution.py:57
  24.6 3.7 %merger_inner.1.mine_ref = bf16[128,80]{1,0:T(8,128)(2,1)} custom-call(bf16[128,5120]{1,0:T(8,128)(2,1)} %patches_ref.1, f32[1,1280]{1,0:T(1,128)} %reshape.103.gain_ref, bf16[5120,80]{1,0:T(8,128)(2,1)} %copy.26.weight_ref), custom_call_target="tpu_custom_call" | custom-call | flops 104857600 | bytes 2129920 | tf_op jit(solution)/shard_map/merger_inner/pallas_call | solution.py:166
  31.7 2.6 merger_outer.1
  34.3 8.9 %all-to-all-done = bf16[16,128,256]{2,1,0:T(8,128)(2,1)S(1)} async-done(((bf16[16,128,256]{2,1,0:T(8,128)(2,1)}), bf16[16,128,256]{2,1,0:T(8,128)(2,1)S(1)}, u32[]{:S(2)}, u32[]{:S(2)}) %all-to-all-start) | async-done | bytes 1048608 | tf_op jit(solution)/shard_map/all_to_all | solution.py:57
  43.2 9.1 %all-to-all-start.1 = ((bf16[64,16,512]{2,1,0:T(8,128)(2,1)}), bf16[64,16,512]{2,1,0:T(8,128)(2,1)S(1)}, u32[]{:S(2)}, u32[]{:S(2)}) async-start(bf16[64,16,512]{2,1,0:T(8,128)(2,1)} %merger_outer.1), calls=%async_computation.1 | async-start | bytes 2097152 | tf_op jit(solution)/shard_map/all_to_all | solution.py:425
  55.9 12.4 %all-to-all-done.1 = bf16[64,16,512]{2,1,0:T(8,128)(2,1)S(1)} async-done(((bf16[64,16,512]{2,1,0:T(8,128)(2,1)}), bf16[64,16,512]{2,1,0:T(8,128)(2,1)S(1)}, u32[]{:S(2)}, u32[]{:S(2)}) %all-to-all-start.1) | async-done | bytes 1048608 | tf_op jit(solution)/shard_map/all_to_all | solution.py:425
  69.3 3.6 %all-to-all-start.2 = ((bf16[16,16,512]{2,1,0:T(8,128)(2,1)}), bf16[16,16,512]{2,1,0:T(8,128)(2,1)S(1)}, u32[]{:S(2)}, u32[]{:S(2)}) async-start(bf16[16,16,512]{2,1,0:T(8,128)(2,1)} %broadcast_in_dim.33), calls=%async_computation.2 | async-start | bytes 524288 | tf_op jit(solution)/shard_map/all_to_all | solution.py:57
  72.9 10.4 %all-to-all-done.2 = bf16[16,16,512]{2,1,0:T(8,128)(2,1)S(1)} async-done(((bf16[16,16,512]{2,1,0:T(8,128)(2,1)}), bf16[16,16,512]{2,1,0:T(8,128)(2,1)S(1)}, u32[]{:S(2)}, u32[]{:S(2)}) %all-to-all-start.2) | async-done | bytes 262176 | tf_op jit(solution)/shard_map/all_to_all | solution.py:57
  87.3 14.5 %collective-permute-start.5 = (f32[16,128]{1,0:T(8,128)S(1)}, f32[16,128]{1,0:T(8,128)S(1)}, u32[]{:S(2)}, u32[]{:S(2)}) collective-permute-start(f32[16,128]{1,0:T(8,128)S(1)} %select_bitcast_fusion), channel_id=1, source_target_pairs={{0,64},{64,0},{1,65},{65,1},{2,66},{66,2},{3,67},{67,3},{4,68},{68... | collective-permute-start | bytes 24584 | tf_op jit(solution)/shard_map/ppermute | solution.py:22
  104.7 6.2 %collective-permute-start.6 = (f32[256,256]{1,0:T(8,128)S(1)}, f32[256,256]{1,0:T(8,128)S(1)}, u32[]{:S(2)}, u32[]{:S(2)}) collective-permute-start(f32[256,256]{1,0:T(8,128)S(1)} %get-tuple-element.50), channel_id=1, source_target_pairs={{0,64},{64,0},{1,65},{65,1},{2,66},{66,2},{3,67},{67,3},{4,68},{68... | collective-permute-start | bytes 786440 | tf_op jit(solution)/shard_map/ppermute | solution.py:22
  113.8 3.8 %all-to-all-start.3 = ((bf16[16,256,128]{2,1,0:T(8,128)(2,1)}), bf16[16,256,128]{2,1,0:T(8,128)(2,1)S(1)}, u32[]{:S(2)}, u32[]{:S(2)}) async-start(bf16[16,256,128]{2,1,0:T(8,128)(2,1)} %broadcast_in_dim.36), calls=%async_computation.3 | async-start | bytes 2097152 | tf_op jit(solution)/shard_map/all_to_all | solution.py:57
  117.7 3.4 %copy-done.2 = bf16[2048,2048]{1,0:T(8,128)(2,1)S(1)} copy-done((bf16[2048,2048]{1,0:T(8,128)(2,1)S(1)}, bf16[2048,2048]{1,0:T(8,128)(2,1)}, u32[]{:S(2)}) %copy-start.2) | copy-done | bytes 8388632
  121.1 2.9 %project_q.2 = (f32[256,512]{1,0:T(8,128)S(1)}, f32[256,512]{1,0:T(8,128)S(1)}) custom-call(s32[3]{0:T(128)S(1)} %copy-done.6, bf16[256,512]{1,0:T(8,128)(2,1)S(1)} %fusion.own_ref, bf16[256,512]{1,0:T(8,128)(2,1)S(1)} %collective-permute-done.2.from_one, bf16[256,512]{1,0:T(8,128)(2,1)S(1)} %collective-permute-done.3.from_two, ...), custom_call_target="tpu_custom_call" | custom-call | flops 1073741824 | bytes 5242880 | tf_op jit(solution)/shard_map/project_q/pallas_call | solution.py:273
  124.5 16.8 %all-to-all-done.3 = bf16[16,256,128]{2,1,0:T(8,128)(2,1)S(1)} async-done(((bf16[16,256,128]{2,1,0:T(8,128)(2,1)}), bf16[16,256,128]{2,1,0:T(8,128)(2,1)S(1)}, u32[]{:S(2)}, u32[]{:S(2)}) %all-to-all-start.3) | async-done | bytes 1048608 | tf_op jit(solution)/shard_map/all_to_all | solution.py:57
  145.5 6.9 %attention.2.mine_ref = bf16[256,512]{1,0:T(8,128)(2,1)} custom-call(s32[4]{0:T(128)} %pad_add_fusion.1.scalars, bf16[256,512]{1,0:T(8,128)(2,1)} %bitcast.72, bf16[16,4,64,128]{3,2,1,0:T(8,128)(2,1)} %bitcast.64, bf16[16,4,64,128]{3,2,1,0:T(8,128)(2,1)} %collective-permute-done.8.other_ref), custom_call_target="tpu_custom_call" | custom-call | flops 134217728 | bytes 2621440 | tf_op jit(solution)/shard_map/attention/pallas_call | solution.py:135
  153.5 4.6 %all-to-all-start.4 = ((bf16[16,128,256]{2,1,0:T(8,128)(2,1)}), bf16[16,128,256]{2,1,0:T(8,128)(2,1)S(1)}, u32[]{:S(2)}, u32[]{:S(2)}) async-start(bf16[16,128,256]{2,1,0:T(8,128)(2,1)} %broadcast_in_dim.37), calls=%async_computation.4 | async-start | bytes 2097152 | tf_op jit(solution)/shard_map/all_to_all | solution.py:57
  158.1 3.5 %copy-done.3 = bf16[2048,2048]{1,0:T(8,128)(2,1)S(1)} copy-done((bf16[2048,2048]{1,0:T(8,128)(2,1)S(1)}, bf16[2048,2048]{1,0:T(8,128)(2,1)}, u32[]{:S(2)}) %copy-start.3) | copy-done | bytes 8388632
  161.7 3.3 %project_out.2 = (bf16[256,512]{1,0:T(8,128)(2,1)S(1)}, bf16[256,512]{1,0:T(8,128)(2,1)S(1)}, bf16[256,512]{1,0:T(8,128)(2,1)S(1)}, bf16[256,512]{1,0:T(8,128)(2,1)S(1)}) custom-call(s32[3]{0:T(128)S(1)} %copy-done.6, bf16[256,512]{1,0:T(8,128)(2,1)S(1)} %copy-done.4, bf16[256,512]{1,0:T(8,128)(2,1)S(1)} %collective-permute-done.9.other_ref, ...), custom_call_target="tpu_custom_call" | custom-call | flops 1073741824 | bytes 5242880 | tf_op jit(solution)/shard_map/project_out/pallas_call | solution.py:332
  170.0 3.6 %collective-permute-done.10 = bf16[256,512]{1,0:T(8,128)(2,1)S(1)} collective-permute-done((bf16[256,512]{1,0:T(8,128)(2,1)S(1)}, bf16[256,512]{1,0:T(8,128)(2,1)S(1)}, u32[]{:S(2)}, u32[]{:S(2)}) %collective-permute-start.10) | collective-permute-done | bytes 262176 | tf_op jit(solution)/shard_map/ppermute | solution.py:18
  173.7 6.8 %collective-permute-done.11 = bf16[256,512]{1,0:T(8,128)(2,1)S(1)} collective-permute-done((bf16[256,512]{1,0:T(8,128)(2,1)S(1)}, bf16[256,512]{1,0:T(8,128)(2,1)S(1)}, u32[]{:S(2)}, u32[]{:S(2)}) %collective-permute-start.11) | collective-permute-done | bytes 262176 | tf_op jit(solution)/shard_map/ppermute | solution.py:18
  182.0 2.6 collective-permute-start.14
  184.6 4.6 %collective-permute-done.13.from_one = bf16[256,512]{1,0:T(8,128)(2,1)S(1)} collective-permute-done((bf16[256,512]{1,0:T(8,128)(2,1)S(1)}, bf16[256,512]{1,0:T(8,128)(2,1)S(1)}, u32[]{:S(2)}, u32[]{:S(2)}) %collective-permute-start.13) | collective-permute-done | bytes 262176 | tf_op jit(solution)/shard_map/ppermute | solution.py:18
  189.2 7.0 %collective-permute-done.14.from_two = bf16[256,512]{1,0:T(8,128)(2,1)S(1)} collective-permute-done((bf16[256,512]{1,0:T(8,128)(2,1)S(1)}, bf16[256,512]{1,0:T(8,128)(2,1)S(1)}, u32[]{:S(2)}, u32[]{:S(2)}) %collective-permute-start.14) | collective-permute-done | bytes 262176 | tf_op jit(solution)/shard_map/ppermute | solution.py:18
  202.3 6.5 %all-to-all-start.5 = ((bf16[16,256,128]{2,1,0:T(8,128)(2,1)}), bf16[16,256,128]{2,1,0:T(8,128)(2,1)S(1)}, u32[]{:S(2)}, u32[]{:S(2)}) async-start(bf16[16,256,128]{2,1,0:T(8,128)(2,1)} %broadcast_in_dim.68), calls=%async_computation.5 | async-start | bytes 2097152 | tf_op jit(solution)/shard_map/all_to_all | solution.py:57
  208.8 3.4 %copy-done = bf16[2048,2048]{1,0:T(8,128)(2,1)S(1)} copy-done((bf16[2048,2048]{1,0:T(8,128)(2,1)S(1)}, bf16[2048,2048]{1,0:T(8,128)(2,1)}, u32[]{:S(2)}) %copy-start) | copy-done | bytes 8388632
  212.2 2.9 %project_q.3 = (f32[256,512]{1,0:T(8,128)S(1)}, f32[256,512]{1,0:T(8,128)S(1)}) custom-call(s32[3]{0:T(128)S(1)} %copy-done.6, bf16[256,512]{1,0:T(8,128)(2,1)S(1)} %add_convert_fusion.2.own_ref, bf16[256,512]{1,0:T(8,128)(2,1)S(1)} %collective-permute-done.13.from_one, bf16[256,512]{1,0:T(8,128)(2,1)S(1)} %collective-permute-done.14.from_two, ...), custom_call_target="tpu_custom_call" | custom-call | flops 1073741824 | bytes 5242880 | tf_op jit(solution)/shard_map/project_q/pallas_call | solution.py:273
  215.9 9.2 %all-to-all-done.5 = bf16[16,256,128]{2,1,0:T(8,128)(2,1)S(1)} async-done(((bf16[16,256,128]{2,1,0:T(8,128)(2,1)}), bf16[16,256,128]{2,1,0:T(8,128)(2,1)S(1)}, u32[]{:S(2)}, u32[]{:S(2)}) %all-to-all-start.5) | async-done | bytes 1048608 | tf_op jit(solution)/shard_map/all_to_all | solution.py:57
  229.7 6.9 %attention.3.mine_ref = bf16[256,512]{1,0:T(8,128)(2,1)} custom-call(s32[4]{0:T(128)} %pad_add_fusion.1.scalars, bf16[256,512]{1,0:T(8,128)(2,1)} %bitcast.71, bf16[16,4,64,128]{3,2,1,0:T(8,128)(2,1)} %bitcast.62, bf16[16,4,64,128]{3,2,1,0:T(8,128)(2,1)} %collective-permute-done.18.other_ref), custom_call_target="tpu_custom_call" | custom-call | flops 134217728 | bytes 2621440 | tf_op jit(solution)/shard_map/attention/pallas_call | solution.py:135
  238.3 3.4 %copy-done.1 = bf16[2048,2048]{1,0:T(8,128)(2,1)S(1)} copy-done((bf16[2048,2048]{1,0:T(8,128)(2,1)S(1)}, bf16[2048,2048]{1,0:T(8,128)(2,1)}, u32[]{:S(2)}) %copy-start.1) | copy-done | bytes 8388632
  242.6 3.3 %project_out.3 = (bf16[256,512]{1,0:T(8,128)(2,1)S(1)}, bf16[256,512]{1,0:T(8,128)(2,1)S(1)}, bf16[256,512]{1,0:T(8,128)(2,1)S(1)}, bf16[256,512]{1,0:T(8,128)(2,1)S(1)}) custom-call(s32[3]{0:T(128)S(1)} %copy-done.6, bf16[256,512]{1,0:T(8,128)(2,1)S(1)} %copy-done.5, bf16[256,512]{1,0:T(8,128)(2,1)S(1)} %collective-permute-done.19.other_ref, ...), custom_call_target="tpu_custom_call" | custom-call | flops 1073741824 | bytes 5242880 | tf_op jit(solution)/shard_map/project_out/pallas_call | solution.py:332
  249.9 5.2 %collective-permute-done.20 = bf16[256,512]{1,0:T(8,128)(2,1)S(1)} collective-permute-done((bf16[256,512]{1,0:T(8,128)(2,1)S(1)}, bf16[256,512]{1,0:T(8,128)(2,1)S(1)}, u32[]{:S(2)}, u32[]{:S(2)}) %collective-permute-start.20) | collective-permute-done | bytes 262176 | tf_op jit(solution)/shard_map/ppermute | solution.py:18
  255.1 6.2 %collective-permute-done.21 = bf16[256,512]{1,0:T(8,128)(2,1)S(1)} collective-permute-done((bf16[256,512]{1,0:T(8,128)(2,1)S(1)}, bf16[256,512]{1,0:T(8,128)(2,1)S(1)}, u32[]{:S(2)}, u32[]{:S(2)}) %collective-permute-start.21) | collective-permute-done | bytes 262176 | tf_op jit(solution)/shard_map/ppermute | solution.py:18
  (155 shorter events, 63.3 us)
Async XLA Ops:
  6.5 111.1 %all-gather.3.cloned.1.call-start = ((), (), s32[]{:S(2)}) async-start(), calls=%async_computation.6 | async-start | bytes 8912896 | tf_op jit(solution)/shard_map/all_gather | solution.py:408
  9.2 3.1 %collective-permute-start.1 = (bf16[128,2304]{1,0:T(8,128)(2,1)S(1)}, bf16[128,2304]{1,0:T(8,128)(2,1)S(1)}, u32[]{:S(2)}, u32[]{:S(2)}) collective-permute-start(bf16[128,2304]{1,0:T(8,128)(2,1)S(1)} %broadcast_select_fusion.2), channel_id=1, source_target_pairs={{0,64},{64,0},{1,65},{65,1},{2,66},{66,2},{3,67},{67,3},{4,68},{68... | collective-permute-start | bytes 1769480 | tf_op jit(solution)/shard_map/ppermute | solution.py:22
  13.6 195.3 %all-gather.5.cloned.1.call-start = ((), (), s32[]{:S(2)}) async-start(), calls=%async_computation.7 | async-start | bytes 8912896 | tf_op jit(solution)/shard_map/all_gather | solution.py:408
  15.6 27.6 %all-to-all-start = ((bf16[16,128,256]{2,1,0:T(8,128)(2,1)}), bf16[16,128,256]{2,1,0:T(8,128)(2,1)S(1)}, u32[]{:S(2)}, u32[]{:S(2)}) async-start(bf16[16,128,256]{2,1,0:T(8,128)(2,1)} %broadcast_in_dim.29), calls=%async_computation | async-start | bytes 2097152 | tf_op jit(solution)/shard_map/all_to_all | solution.py:57
  28.4 2.7 collective-permute-start
  43.2 25.2 %all-to-all-start.1 = ((bf16[64,16,512]{2,1,0:T(8,128)(2,1)}), bf16[64,16,512]{2,1,0:T(8,128)(2,1)S(1)}, u32[]{:S(2)}, u32[]{:S(2)}) async-start(bf16[64,16,512]{2,1,0:T(8,128)(2,1)} %merger_outer.1), calls=%async_computation.1 | async-start | bytes 2097152 | tf_op jit(solution)/shard_map/all_to_all | solution.py:425
  69.3 14.1 %all-to-all-start.2 = ((bf16[16,16,512]{2,1,0:T(8,128)(2,1)}), bf16[16,16,512]{2,1,0:T(8,128)(2,1)S(1)}, u32[]{:S(2)}, u32[]{:S(2)}) async-start(bf16[16,16,512]{2,1,0:T(8,128)(2,1)} %broadcast_in_dim.33), calls=%async_computation.2 | async-start | bytes 524288 | tf_op jit(solution)/shard_map/all_to_all | solution.py:57
  83.6 19.2 %collective-permute-start.2 = (bf16[256,512]{1,0:T(8,128)(2,1)S(1)}, bf16[256,512]{1,0:T(8,128)(2,1)S(1)}, u32[]{:S(2)}, u32[]{:S(2)}) collective-permute-start(bf16[256,512]{1,0:T(8,128)(2,1)S(1)} %fusion.own_ref), channel_id=1, source_target_pairs={{0,1},{1,2},{2,3},{3,0},{4,5},{5,6},{6,7},{7,4},{8,9},{9,10},{10,1... | collective-permute-start | bytes 786440 | tf_op jit(solution)/shard_map/ppermute | solution.py:18
  84.7 18.1 %collective-permute-start.3 = (bf16[256,512]{1,0:T(8,128)(2,1)S(1)}, bf16[256,512]{1,0:T(8,128)(2,1)S(1)}, u32[]{:S(2)}, u32[]{:S(2)}) collective-permute-start(bf16[256,512]{1,0:T(8,128)(2,1)S(1)} %fusion.own_ref), channel_id=1, source_target_pairs={{0,2},{1,3},{2,0},{3,1},{4,6},{5,7},{6,4},{7,5},{8,10},{9,11},{10,... | collective-permute-start | bytes 786440 | tf_op jit(solution)/shard_map/ppermute | solution.py:18
  86.4 16.3 %collective-permute-start.4 = (bf16[256,512]{1,0:T(8,128)(2,1)S(1)}, bf16[256,512]{1,0:T(8,128)(2,1)S(1)}, u32[]{:S(2)}, u32[]{:S(2)}) collective-permute-start(bf16[256,512]{1,0:T(8,128)(2,1)S(1)} %fusion.own_ref), channel_id=1, source_target_pairs={{0,3},{1,0},{2,1},{3,2},{4,7},{5,4},{6,5},{7,6},{8,11},{9,8},{10,9... | collective-permute-start | bytes 786440 | tf_op jit(solution)/shard_map/ppermute | solution.py:18
  87.3 15.4 %collective-permute-start.5 = (f32[16,128]{1,0:T(8,128)S(1)}, f32[16,128]{1,0:T(8,128)S(1)}, u32[]{:S(2)}, u32[]{:S(2)}) collective-permute-start(f32[16,128]{1,0:T(8,128)S(1)} %select_bitcast_fusion), channel_id=1, source_target_pairs={{0,64},{64,0},{1,65},{65,1},{2,66},{66,2},{3,67},{67,3},{4,68},{68... | collective-permute-start | bytes 24584 | tf_op jit(solution)/shard_map/ppermute | solution.py:22
  104.7 7.4 %collective-permute-start.6 = (f32[256,256]{1,0:T(8,128)S(1)}, f32[256,256]{1,0:T(8,128)S(1)}, u32[]{:S(2)}, u32[]{:S(2)}) collective-permute-start(f32[256,256]{1,0:T(8,128)S(1)} %get-tuple-element.50), channel_id=1, source_target_pairs={{0,64},{64,0},{1,65},{65,1},{2,66},{66,2},{3,67},{67,3},{4,68},{68... | collective-permute-start | bytes 786440 | tf_op jit(solution)/shard_map/ppermute | solution.py:22
  113.8 27.5 %all-to-all-start.3 = ((bf16[16,256,128]{2,1,0:T(8,128)(2,1)}), bf16[16,256,128]{2,1,0:T(8,128)(2,1)S(1)}, u32[]{:S(2)}, u32[]{:S(2)}) async-start(bf16[16,256,128]{2,1,0:T(8,128)(2,1)} %broadcast_in_dim.36), calls=%async_computation.3 | async-start | bytes 2097152 | tf_op jit(solution)/shard_map/all_to_all | solution.py:57
  124.0 19.5 %collective-permute-start.7 = (f32[256,512]{1,0:T(8,128)S(1)}, f32[256,512]{1,0:T(8,128)S(1)}, u32[]{:S(2)}, u32[]{:S(2)}) collective-permute-start(f32[256,512]{1,0:T(8,128)S(1)} %get-tuple-element.58), channel_id=1, source_target_pairs={{0,64},{64,0},{1,65},{65,1},{2,66},{66,2},{3,67},{67,3},{4,68},{68... | collective-permute-start | bytes 1572872 | tf_op jit(solution)/shard_map/ppermute | solution.py:22
  141.2 4.2 %collective-permute-start.8 = (bf16[16,4,64,128]{3,2,1,0:T(8,128)(2,1)S(1)}, bf16[16,4,64,128]{3,2,1,0:T(8,128)(2,1)}, u32[]{:S(2)}, u32[]{:S(2)}) collective-permute-start(bf16[16,4,64,128]{3,2,1,0:T(8,128)(2,1)S(1)} %bitcast.63), channel_id=1, source_target_pairs={{0,64},{64,0},{1,65},{65,1},{2,66},{66,2},{3,67},{67,3},{4,68},{68... | collective-permute-start | bytes 3145736 | tf_op jit(solution)/shard_map/ppermute | solution.py:22
  152.4 5.7 %collective-permute-start.9 = (bf16[256,512]{1,0:T(8,128)(2,1)}, bf16[256,512]{1,0:T(8,128)(2,1)S(1)}, u32[]{:S(2)}, u32[]{:S(2)}) collective-permute-start(bf16[256,512]{1,0:T(8,128)(2,1)} %attention.2.mine_ref), channel_id=1, source_target_pairs={{0,64},{64,0},{1,65},{65,1},{2,66},{66,2},{3,67},{67,3},{4,68},{68... | collective-permute-start | bytes 786440 | tf_op jit(solution)/shard_map/ppermute | solution.py:22
  153.5 42.7 %all-to-all-start.4 = ((bf16[16,128,256]{2,1,0:T(8,128)(2,1)}), bf16[16,128,256]{2,1,0:T(8,128)(2,1)S(1)}, u32[]{:S(2)}, u32[]{:S(2)}) async-start(bf16[16,128,256]{2,1,0:T(8,128)(2,1)} %broadcast_in_dim.37), calls=%async_computation.4 | async-start | bytes 2097152 | tf_op jit(solution)/shard_map/all_to_all | solution.py:57
  165.0 8.7 %collective-permute-start.10 = (bf16[256,512]{1,0:T(8,128)(2,1)S(1)}, bf16[256,512]{1,0:T(8,128)(2,1)S(1)}, u32[]{:S(2)}, u32[]{:S(2)}) collective-permute-start(bf16[256,512]{1,0:T(8,128)(2,1)S(1)} %get-tuple-element.62), channel_id=1, source_target_pairs={{0,2},{1,3},{2,0},{3,1},{4,6},{5,7},{6,4},{7,5},{8,10},{9,11},{10,... | collective-permute-start | bytes 786440 | tf_op jit(solution)/shard_map/ppermute | solution.py:18
  167.4 13.1 %collective-permute-start.11 = (bf16[256,512]{1,0:T(8,128)(2,1)S(1)}, bf16[256,512]{1,0:T(8,128)(2,1)S(1)}, u32[]{:S(2)}, u32[]{:S(2)}) collective-permute-start(bf16[256,512]{1,0:T(8,128)(2,1)S(1)} %get-tuple-element.63), channel_id=1, source_target_pairs={{0,1},{1,2},{2,3},{3,0},{4,5},{5,6},{6,7},{7,4},{8,9},{9,10},{10,1... | collective-permute-start | bytes 786440 | tf_op jit(solution)/shard_map/ppermute | solution.py:18
  168.3 12.2 %collective-permute-start.12 = (bf16[256,512]{1,0:T(8,128)(2,1)S(1)}, bf16[256,512]{1,0:T(8,128)(2,1)S(1)}, u32[]{:S(2)}, u32[]{:S(2)}) collective-permute-start(bf16[256,512]{1,0:T(8,128)(2,1)S(1)} %get-tuple-element.64), channel_id=1, source_target_pairs={{0,3},{1,0},{2,1},{3,2},{4,7},{5,4},{6,5},{7,6},{8,11},{9,8},{10,9... | collective-permute-start | bytes 786440 | tf_op jit(solution)/shard_map/ppermute | solution.py:18
  180.7 8.5 %collective-permute-start.13 = (bf16[256,512]{1,0:T(8,128)(2,1)S(1)}, bf16[256,512]{1,0:T(8,128)(2,1)S(1)}, u32[]{:S(2)}, u32[]{:S(2)}) collective-permute-start(bf16[256,512]{1,0:T(8,128)(2,1)S(1)} %add_convert_fusion.2.own_ref), channel_id=1, source_target_pairs={{0,1},{1,2},{2,3},{3,0},{4,5},{5,6},{6,7},{7,4},{8,9},{9,10},{10,1... | collective-permute-start | bytes 786440 | tf_op jit(solution)/shard_map/ppermute | solution.py:18
  182.0 14.2 %collective-permute-start.14 = (bf16[256,512]{1,0:T(8,128)(2,1)S(1)}, bf16[256,512]{1,0:T(8,128)(2,1)S(1)}, u32[]{:S(2)}, u32[]{:S(2)}) collective-permute-start(bf16[256,512]{1,0:T(8,128)(2,1)S(1)} %add_convert_fusion.2.own_ref), channel_id=1, source_target_pairs={{0,2},{1,3},{2,0},{3,1},{4,6},{5,7},{6,4},{7,5},{8,10},{9,11},{10,... | collective-permute-start | bytes 786440 | tf_op jit(solution)/shard_map/ppermute | solution.py:18
  184.6 11.7 %collective-permute-start.15 = (bf16[256,512]{1,0:T(8,128)(2,1)S(1)}, bf16[256,512]{1,0:T(8,128)(2,1)S(1)}, u32[]{:S(2)}, u32[]{:S(2)}) collective-permute-start(bf16[256,512]{1,0:T(8,128)(2,1)S(1)} %add_convert_fusion.2.own_ref), channel_id=1, source_target_pairs={{0,3},{1,0},{2,1},{3,2},{4,7},{5,4},{6,5},{7,6},{8,11},{9,8},{10,9... | collective-permute-start | bytes 786440 | tf_op jit(solution)/shard_map/ppermute | solution.py:18
  198.2 2.5 collective-permute-start.16
  202.3 22.9 %all-to-all-start.5 = ((bf16[16,256,128]{2,1,0:T(8,128)(2,1)}), bf16[16,256,128]{2,1,0:T(8,128)(2,1)S(1)}, u32[]{:S(2)}, u32[]{:S(2)}) async-start(bf16[16,256,128]{2,1,0:T(8,128)(2,1)} %broadcast_in_dim.68), calls=%async_computation.5 | async-start | bytes 2097152 | tf_op jit(solution)/shard_map/all_to_all | solution.py:57
  215.2 12.1 %collective-permute-start.17 = (f32[256,512]{1,0:T(8,128)S(1)}, f32[256,512]{1,0:T(8,128)S(1)}, u32[]{:S(2)}, u32[]{:S(2)}) collective-permute-start(f32[256,512]{1,0:T(8,128)S(1)} %get-tuple-element.73), channel_id=1, source_target_pairs={{0,64},{64,0},{1,65},{65,1},{2,66},{66,2},{3,67},{67,3},{4,68},{68... | collective-permute-start | bytes 1572872 | tf_op jit(solution)/shard_map/ppermute | solution.py:22
  225.1 4.5 %collective-permute-start.18 = (bf16[16,4,64,128]{3,2,1,0:T(8,128)(2,1)S(1)}, bf16[16,4,64,128]{3,2,1,0:T(8,128)(2,1)}, u32[]{:S(2)}, u32[]{:S(2)}) collective-permute-start(bf16[16,4,64,128]{3,2,1,0:T(8,128)(2,1)S(1)} %bitcast.61), channel_id=1, source_target_pairs={{0,64},{64,0},{1,65},{65,1},{2,66},{66,2},{3,67},{67,3},{4,68},{68... | collective-permute-start | bytes 3145736 | tf_op jit(solution)/shard_map/ppermute | solution.py:22
  236.6 1.7 collective-permute-start.19
  245.9 9.2 %collective-permute-start.20 = (bf16[256,512]{1,0:T(8,128)(2,1)S(1)}, bf16[256,512]{1,0:T(8,128)(2,1)S(1)}, u32[]{:S(2)}, u32[]{:S(2)}) collective-permute-start(bf16[256,512]{1,0:T(8,128)(2,1)S(1)} %get-tuple-element.76), channel_id=1, source_target_pairs={{0,2},{1,3},{2,0},{3,1},{4,6},{5,7},{6,4},{7,5},{8,10},{9,11},{10,... | collective-permute-start | bytes 786440 | tf_op jit(solution)/shard_map/ppermute | solution.py:18
  247.3 14.1 %collective-permute-start.21 = (bf16[256,512]{1,0:T(8,128)(2,1)S(1)}, bf16[256,512]{1,0:T(8,128)(2,1)S(1)}, u32[]{:S(2)}, u32[]{:S(2)}) collective-permute-start(bf16[256,512]{1,0:T(8,128)(2,1)S(1)} %get-tuple-element.77), channel_id=1, source_target_pairs={{0,1},{1,2},{2,3},{3,0},{4,5},{5,6},{6,7},{7,4},{8,9},{9,10},{10,1... | collective-permute-start | bytes 786440 | tf_op jit(solution)/shard_map/ppermute | solution.py:18
  248.4 12.9 %collective-permute-start.22 = (bf16[256,512]{1,0:T(8,128)(2,1)S(1)}, bf16[256,512]{1,0:T(8,128)(2,1)S(1)}, u32[]{:S(2)}, u32[]{:S(2)}) collective-permute-start(bf16[256,512]{1,0:T(8,128)(2,1)S(1)} %get-tuple-element.78), channel_id=1, source_target_pairs={{0,3},{1,0},{2,1},{3,2},{4,7},{5,4},{6,5},{7,6},{8,11},{9,8},{10,9... | collective-permute-start | bytes 786440 | tf_op jit(solution)/shard_map/ppermute | solution.py:18
  261.5 1.7 collective-permute-start.23
  (18 other events, 133.2 us)
Sparse Core Ops, SparseCore 0:
  13.7 91.3 all-gather.2
  107.2 90.9 all-gather.4

commit v4 on v3

--- a/solution.py
+++ b/solution.py
@@ -227,15 +227,17 @@
     weight_ref,
     sums_ref,
     semaphores,
+    *,
+    at,
 ):
     pieces, _, depth = gain_ref.shape
     half = weight_ref.shape[1] // 2
     copies = []
     for piece in range(pieces):
-        span = (pl.ds(piece * depth, depth), pl.ds(0, 2 * half))
+        deep = pl.ds(piece * depth, depth)
         copies.append(
             pltpu.make_async_copy(
-                weight_hbm.at[span], weight_ref.at[span], semaphores.at[piece]
+                weight_hbm.at[deep, pl.ds(at, 2 * half)], weight_ref.at[deep], semaphores.at[piece]
             )
         )
         copies[-1].start()
@@ -265,17 +267,17 @@
     sent_ref[:, :half] = result[:, half:]
 
 
-def project_in(place, parts, gain, weight, width, with_squares):
+def project_in(place, parts, gain, weight, at, width, with_squares):
     rows, depth = parts[0].shape
     spare = lane if with_squares else 0
     out = jax.ShapeDtypeStruct((rows, width // 2 + spare), jnp.float32)
     whole = pl.BlockSpec(memory_space=pltpu.VMEM)
     return pl.pallas_call(
-        project_in_kernel,
+        functools.partial(project_in_kernel, at=at),
         out_shape=(out, out),
         in_specs=[pl.BlockSpec(memory_space=pltpu.SMEM)]
         + [whole] * 5
-        + [pl.BlockSpec(memory_space=pl.ANY)],
+        + [pl.BlockSpec(memory_space=pltpu.HBM)],
         out_specs=(whole, whole),
         scratch_shapes=[
             pltpu.VMEM((len(parts), rows, depth), jnp.bfloat16),
@@ -336,7 +338,7 @@
             pl.BlockSpec(memory_space=pltpu.SMEM),
             whole,
             whole,
-            pl.BlockSpec(memory_space=pl.ANY),
+            pl.BlockSpec(memory_space=pltpu.HBM),
         ],
         out_specs=[whole] * pieces,
         scratch_shapes=[
@@ -351,6 +353,35 @@
         compiler_params=pltpu.CompilerParams(vmem_limit_bytes=24 << 20),
         name="project_out",
     )(place, mine, other, weight)
+
+
+def joined_kernel(place, first_ref, first_other_ref, second_ref, second_other_ref, out_ref):
+    runs = first_ref.shape[1] // lane
+
+    def write(even_ref, odd_ref):
+        for run in range(runs):
+            here = slice(run * lane, (run + 1) * lane)
+            out_ref[:, 2 * run * lane : (2 * run + 1) * lane] = even_ref[:, here]
+            out_ref[:, (2 * run + 1) * lane : (2 * run + 2) * lane] = odd_ref[:, here]
+
+    @pl.when(place[0] == 0)
+    def _():
+        write(first_ref, first_other_ref)
+
+    @pl.when(place[0] != 0)
+    def _():
+        write(second_other_ref, second_ref)
+
+
+def joined(place, first, first_other, second, second_other):
+    whole = pl.BlockSpec(memory_space=pltpu.VMEM)
+    return pl.pallas_call(
+        joined_kernel,
+        out_shape=jax.ShapeDtypeStruct((first.shape[0], 2 * first.shape[1]), first.dtype),
+        in_specs=[pl.BlockSpec(memory_space=pltpu.SMEM)] + [whole] * 4,
+        out_specs=whole,
+        name="joined",
+    )(place, first, first_other, second, second_other)
 
 
 def local(
@@ -405,7 +436,8 @@
     for home in range(layers):
         mine = jnp.where(section_index == home, weight_keep, weight_other)
         keyval_shards.append(mine[:, :keyval_width])
-        weight_full.append(lax.all_gather(mine[:, keyval_width:], "blk", axis=0, tiled=True))
+        sent_off = mine if home == 0 else mine[:, keyval_width:]
+        weight_full.append(lax.all_gather(sent_off, "blk", axis=0, tiled=True))
     gain_half = norm_gain[0].reshape(-1, 2, lane)
     gain_keep = jnp.where(first_core, gain_half[:, 0], gain_half[:, 1])
     gain_send = jnp.where(first_core, gain_half[:, 1], gain_half[:, 0])
@@ -414,14 +446,10 @@
         jnp.where(first_core, gain_keep, gain_other).reshape(n_mp, 1, -1),
         jnp.where(first_core, gain_other, gain_keep).reshape(n_mp, 1, -1),
     ]
-    keyval_weight_full = spread(keyval_shards[0])
 
     inner = merger_inner(patches, merge_gain, merge_first)
     place = jnp.stack([section_index, cycle_index, model_index]).astype(jnp.int32)
     merged_pieces = merger_outer(place, inner, swapped(inner), merge_second, n_blk, n_mp)
-    merged_pieces, keyval_weight_full = lax.optimization_barrier(
-        (merged_pieces, keyval_weight_full)
-    )
     merged_terms = lax.all_to_all(merged_pieces, ("blk", "mp"), 0, 0, tiled=True)
 
     row_where = (
@@ -453,24 +481,26 @@
         parts = [state] + [moved(state, "mp", by) for by in (1, 2, 3)]
         gain = gain_layers[layer_index]
         weight = weight_full[layer_index]
-        kept, sent = project_in(
-            place, parts, gain, keyval_weight_full.reshape(-1, keyval_width), keyval_width, True
-        )
+        if layer_index == 0:
+            keyval_from, query_at = weight, keyval_width
+        else:
+            keyval_from, query_at = keyval_weight_full.reshape(-1, keyval_width), 0
+        kept, sent = project_in(place, parts, gain, keyval_from, 0, keyval_width, True)
         total = kept + swapped(sent)
         shrink = lax.rsqrt(total[:, head_size : head_size + 1] / (n_mp * slice_width) + epsilon)
         keyval = rotate(total[:, :head_size] * shrink, keyval_cosine, keyval_sine).astype(jnp.bfloat16)
         keyval, parts = lax.optimization_barrier((keyval, parts))
-        kept, sent = project_in(place, parts, gain, weight, 2 * heads_half, False)
+        kept, sent = project_in(place, parts, gain, weight, query_at, 2 * heads_half, False)
         query = ((kept + swapped(sent)) * shrink).reshape(rows, -1, head_size)
         query = rotate(query, cosine[:, None, :], sine[:, None, :])
         query = query.astype(jnp.bfloat16).reshape(rows, heads_half)
         gathered = spread(keyval).reshape(n_blk, blocks, rows_here, head_size)
         attended = attention(scalars, query, gathered, swapped(gathered))
-        if layer_index + 1 < layers:
-            attended, shard = lax.optimization_barrier((attended, keyval_shards[layer_index + 1]))
-            keyval_weight_full = spread(shard)
         attended_other = swapped(attended)
         own, *terms = project_out(place, attended, attended_other, weight)
+        if layer_index + 1 < layers:
+            own, shard = lax.optimization_barrier((own, keyval_shards[layer_index + 1]))
+            keyval_weight_full = spread(shard)
         arrived = [moved(terms[by - 1], "mp", by) for by in (2, 1, 3)]
         total = state.astype(jnp.float32) + own.astype(jnp.float32)
         for part in arrived:
@@ -478,12 +508,10 @@
         state = total.astype(jnp.bfloat16)
         results.append(state)
 
-    keep = jnp.where(first_core, results[0], results[1])
-    send = jnp.where(first_core, results[1], results[0])
-    other = swapped(send)
-    even = jnp.where(first_core, keep, other).reshape(rows, -1, 1, lane)
-    odd = jnp.where(first_core, other, keep).reshape(rows, -1, 1, lane)
-    return jnp.concatenate([even, odd], axis=2).reshape(1, blocks, rows_here, slice_width)
+    first_other = swapped(results[0])
+    second_other = swapped(results[1])
+    hidden = joined(place, results[0], first_other, results[1], second_other)
+    return hidden.reshape(1, blocks, rows_here, slice_width)
 
 
 def solution(mesh):

time: 273 us -> 278 us (1.018)
  starting transfers between devices: 81.3 us -> 62.5 us
  waiting for transfers between devices: 99.2 us -> 116 us
    all_gather x2, waiting for transfers between devices: 0.04 us -> 16.2 us  [local(): weight_full.append(lax.all_gather(sent_off, 'blk', axis=0, tiled=True))]
    ppermute x12 -> x13, starting transfers between devices: 29.9 us -> 14.4 us  [swapped(): return lax.ppermute(value, 'section', [(0, 1), (1, 0)])]
    all_to_all x5 -> x4, waiting for transfers between devices: 45.3 us -> 36.8 us  [spread(): return lax.all_to_all(copies, 'blk', 0, 0, tiled=True)]
    unnamed x48 -> x54, local copies, waits for them, and re-layouts: 18.5 us -> 24.9 us
    all_to_all x5 -> x4, starting transfers between devices: 25.5 us -> 19.6 us  [spread(): return lax.all_to_all(copies, 'blk', 0, 0, tiled=True)]
    ppermute x12, waiting for transfers between devices: 33.5 us -> 38.5 us  [moved(): lax.ppermute(value, axis, [(i, (i + by) % size) for i in range(size)])]
    ppermute x12 -> x13, waiting for transfers between devices: 7.81 us -> 9.84 us  [swapped(): return lax.ppermute(value, 'section', [(0, 1), (1, 0)])]
    pallas_call x4 -> x5, Pallas kernels: 9.74 us -> 11.7 us  [the longest x4 9.53 us: project_in(): pl.pallas_call(functools.partial(project_in_kernel, at=at), out_shape=(ou...]
  transfers between devices with their start and end apart: 32 -> 32, of which waited for: 18 -> 23; matrix products, arithmetic and copies ran while one was open for 7% -> 7% of each run, Pallas kernels for 10% -> 9%
where the time goes in v4:
time: 278 us; the launch traced here: 275 us
  waiting for transfers between devices  116 us (42%)
  starting transfers between devices  62.5 us (22%)
  Pallas kernels  39.1 us (14%)
  local copies, waits for them, and re-layouts  34.3 us (12%)
  between operations  13.9 us (5%)
  other arithmetic  9.08 us (3%)
    ppermute x12, waiting for transfers between devices, moved(): lax.ppermute(value, axis, [(i, (i + by) % size) for i in range(size)])  38.5 us
    all_to_all x4, waiting for transfers between devices, spread(): return lax.all_to_all(copies, 'blk', 0, 0, tiled=True)  36.8 us
    unnamed x54, local copies, waits for them, and re-layouts  24.9 us
    all_to_all x4, starting transfers between devices, spread(): return lax.all_to_all(copies, 'blk', 0, 0, tiled=True)  19.6 us
    ppermute x12, starting transfers between devices, moved(): lax.ppermute(value, axis, [(i, (i + by) % size) for i in range(size)])  17.1 us
    all_gather x2, waiting for transfers between devices, local(): weight_full.append(lax.all_gather(sent_off, 'blk', axis=0, tiled=True))  16.2 us
    pallas_call x2, Pallas kernels, attention(): pl.pallas_call(functools.partial(attention_kernel, chunk_runs=mine.shape[...  15 us
    all_to_all x1, waiting for transfers between devices, local(): lax.all_to_all(merged_pieces, ('blk', 'mp'), 0, 0, tiled=True)  14.8 us
  transfers between devices with their start and end apart: 32, of which 23 were waited for; matrix products, arithmetic and copies ran while one was open for 7% of the time, Pallas kernels for 9%

profile of v4, /device:TPU:1, one launch (start us, length us, event | category | flops | bytes accessed | tf_op | source)
XLA Modules:
  0.0 275.3 jit_solution(2572047334446298285)
XLA Ops:
  16.8 3.6 %merger_inner.1.mine_ref = bf16[128,80]{1,0:T(8,128)(2,1)} custom-call(bf16[128,5120]{1,0:T(8,128)(2,1)} %patches_ref.1, f32[1,1280]{1,0:T(1,128)} %reshape.93.gain_ref, bf16[5120,80]{1,0:T(8,128)(2,1)} %copy.24.weight_ref), custom_call_target="tpu_custom_call" | custom-call | flops 104857600 | bytes 2129920 | tf_op jit(solution)/shard_map/merger_inner/pallas_call | solution.py:166
  25.9 11.4 %all-to-all-start = ((bf16[64,16,512]{2,1,0:T(8,128)(2,1)}), bf16[64,16,512]{2,1,0:T(8,128)(2,1)S(1)}, u32[]{:S(2)}, u32[]{:S(2)}) async-start(bf16[64,16,512]{2,1,0:T(8,128)(2,1)} %merger_outer.1), calls=%async_computation | async-start | bytes 2097152 | tf_op jit(solution)/shard_map/all_to_all | solution.py:453
  40.9 14.8 %all-to-all-done = bf16[64,16,512]{2,1,0:T(8,128)(2,1)S(1)} async-done(((bf16[64,16,512]{2,1,0:T(8,128)(2,1)}), bf16[64,16,512]{2,1,0:T(8,128)(2,1)S(1)}, u32[]{:S(2)}, u32[]{:S(2)}) %all-to-all-start) | async-done | bytes 1048608 | tf_op jit(solution)/shard_map/all_to_all | solution.py:453
  56.6 4.2 %all-to-all-start.1 = ((bf16[16,16,512]{2,1,0:T(8,128)(2,1)}), bf16[16,16,512]{2,1,0:T(8,128)(2,1)S(1)}, u32[]{:S(2)}, u32[]{:S(2)}) async-start(bf16[16,16,512]{2,1,0:T(8,128)(2,1)} %broadcast_in_dim.30), calls=%async_computation.1 | async-start | bytes 524288 | tf_op jit(solution)/shard_map/all_to_all | solution.py:57
  60.8 11.1 %all-to-all-done.1 = bf16[16,16,512]{2,1,0:T(8,128)(2,1)S(1)} async-done(((bf16[16,16,512]{2,1,0:T(8,128)(2,1)}), bf16[16,16,512]{2,1,0:T(8,128)(2,1)S(1)}, u32[]{:S(2)}, u32[]{:S(2)}) %all-to-all-start.1) | async-done | bytes 262176 | tf_op jit(solution)/shard_map/all_to_all | solution.py:57
  75.8 3.0 %collective-permute-start.4 = (f32[16,128]{1,0:T(8,128)S(1)}, f32[16,128]{1,0:T(8,128)S(1)}, u32[]{:S(2)}, u32[]{:S(2)}) collective-permute-start(f32[16,128]{1,0:T(8,128)S(1)} %select_bitcast_fusion), channel_id=1, source_target_pairs={{0,64},{64,0},{1,65},{65,1},{2,66},{66,2},{3,67},{67,3},{4,68},{68... | collective-permute-start | bytes 24584 | tf_op jit(solution)/shard_map/ppermute | solution.py:22
  79.7 2.9 %collective-permute-done.1.from_one = bf16[256,512]{1,0:T(8,128)(2,1)S(1)} collective-permute-done((bf16[256,512]{1,0:T(8,128)(2,1)S(1)}, bf16[256,512]{1,0:T(8,128)(2,1)S(1)}, u32[]{:S(2)}, u32[]{:S(2)}) %collective-permute-start.1) | collective-permute-done | bytes 262176 | tf_op jit(solution)/shard_map/ppermute | solution.py:18
  82.8 3.7 %collective-permute-done.3.from_three = bf16[256,512]{1,0:T(8,128)(2,1)S(1)} collective-permute-done((bf16[256,512]{1,0:T(8,128)(2,1)S(1)}, bf16[256,512]{1,0:T(8,128)(2,1)S(1)}, u32[]{:S(2)}, u32[]{:S(2)}) %collective-permute-start.3) | collective-permute-done | bytes 262176 | tf_op jit(solution)/shard_map/ppermute | solution.py:18
  86.4 16.1 %all-gather.3.cloned.1.call-done.weight_hbm = bf16[2048,2304]{1,0:T(8,128)(2,1)} async-done(((bf16[128,2304]{1,0:T(8,128)(2,1)}), bf16[2048,2304]{1,0:T(8,128)(2,1)}) %all-gather.3.cloned.1.call-update) | async-done | bytes 9437200 | tf_op jit(solution)/shard_map/all_gather | solution.py:440
  102.6 3.7 %copy-done = bf16[2048,2304]{1,0:T(8,128)(2,1)S(1)} copy-done((bf16[2048,2304]{1,0:T(8,128)(2,1)S(1)}, bf16[2048,2304]{1,0:T(8,128)(2,1)}, u32[]{:S(2)}) %copy-start) | copy-done | bytes 9437208
  111.8 5.0 %all-to-all-start.2 = ((bf16[16,256,128]{2,1,0:T(8,128)(2,1)}), bf16[16,256,128]{2,1,0:T(8,128)(2,1)}, u32[]{:S(2)}, u32[]{:S(2)}) async-start(bf16[16,256,128]{2,1,0:T(8,128)(2,1)} %broadcast_in_dim.33), calls=%async_computation.2 | async-start | bytes 2097152 | tf_op jit(solution)/shard_map/all_to_all | solution.py:57
  116.8 3.7 %copy-done.1 = bf16[2048,2304]{1,0:T(8,128)(2,1)S(1)} copy-done((bf16[2048,2304]{1,0:T(8,128)(2,1)S(1)}, bf16[2048,2304]{1,0:T(8,128)(2,1)}, u32[]{:S(2)}) %copy-start.1) | copy-done | bytes 9437208
  120.5 2.7 project_q.2
  124.2 16.5 %all-to-all-done.2 = bf16[16,256,128]{2,1,0:T(8,128)(2,1)} async-done(((bf16[16,256,128]{2,1,0:T(8,128)(2,1)}), bf16[16,256,128]{2,1,0:T(8,128)(2,1)}, u32[]{:S(2)}, u32[]{:S(2)}) %all-to-all-start.2) | async-done | bytes 1048608 | tf_op jit(solution)/shard_map/all_to_all | solution.py:57
  144.5 7.4 %attention.2.mine_ref = bf16[256,512]{1,0:T(8,128)(2,1)} custom-call(s32[4]{0:T(128)} %pad_add_fusion.1.scalars, bf16[256,512]{1,0:T(8,128)(2,1)} %bitcast.69, bf16[16,4,64,128]{3,2,1,0:T(8,128)(2,1)} %bitcast.15.mine_ref, bf16[16,4,64,128]{3,2,1,0:T(8,128)(2,1)} %collective-permute-done.8.other_ref), custom_call_target="tpu_custom_call" | custom-call | flops 134217728 | bytes 2621440 | tf_op jit(solution)/shard_map/attention/pallas_call | solution.py:135
  153.6 3.9 %copy-done.2 = bf16[2048,2304]{1,0:T(8,128)(2,1)S(1)} copy-done((bf16[2048,2304]{1,0:T(8,128)(2,1)S(1)}, bf16[2048,2304]{1,0:T(8,128)(2,1)}, u32[]{:S(2)}) %copy-start.2) | copy-done | bytes 9437208
  158.5 3.0 %project_out.2 = (bf16[256,512]{1,0:T(8,128)(2,1)S(1)}, bf16[256,512]{1,0:T(8,128)(2,1)S(1)}, bf16[256,512]{1,0:T(8,128)(2,1)S(1)}, bf16[256,512]{1,0:T(8,128)(2,1)S(1)}) custom-call(s32[3]{0:T(128)S(1)} %copy-done.8, bf16[256,512]{1,0:T(8,128)(2,1)S(1)} %copy-done.6, bf16[256,512]{1,0:T(8,128)(2,1)S(1)} %collective-permute-done.9.other_ref, ...), custom_call_target="tpu_custom_call" | custom-call | flops 1073741824 | bytes 5242880 | tf_op jit(solution)/shard_map/project_out/pallas_call | solution.py:334
  162.6 4.0 %all-to-all-start.3 = ((bf16[16,128,256]{2,1,0:T(8,128)(2,1)}), bf16[16,128,256]{2,1,0:T(8,128)(2,1)S(1)}, u32[]{:S(2)}, u32[]{:S(2)}) async-start(bf16[16,128,256]{2,1,0:T(8,128)(2,1)} %broadcast_in_dim.60), calls=%async_computation.3 | async-start | bytes 2097152 | tf_op jit(solution)/shard_map/all_to_all | solution.py:57
  166.6 3.0 %collective-permute-start.10 = (bf16[256,512]{1,0:T(8,128)(2,1)S(1)}, bf16[256,512]{1,0:T(8,128)(2,1)S(1)}, u32[]{:S(2)}, u32[]{:S(2)}) collective-permute-start(bf16[256,512]{1,0:T(8,128)(2,1)S(1)} %get-tuple-element.58), channel_id=1, source_target_pairs={{0,2},{1,3},{2,0},{3,1},{4,6},{5,7},{6,4},{7,5},{8,10},{9,11},{10,... | collective-permute-start | bytes 786440 | tf_op jit(solution)/shard_map/ppermute | solution.py:18
  172.2 3.2 %collective-permute-done.10 = bf16[256,512]{1,0:T(8,128)(2,1)S(1)} collective-permute-done((bf16[256,512]{1,0:T(8,128)(2,1)S(1)}, bf16[256,512]{1,0:T(8,128)(2,1)S(1)}, u32[]{:S(2)}, u32[]{:S(2)}) %collective-permute-start.10) | collective-permute-done | bytes 262176 | tf_op jit(solution)/shard_map/ppermute | solution.py:18
  175.5 6.7 %collective-permute-done.11 = bf16[256,512]{1,0:T(8,128)(2,1)S(1)} collective-permute-done((bf16[256,512]{1,0:T(8,128)(2,1)S(1)}, bf16[256,512]{1,0:T(8,128)(2,1)S(1)}, u32[]{:S(2)}, u32[]{:S(2)}) %collective-permute-start.11) | collective-permute-done | bytes 262176 | tf_op jit(solution)/shard_map/ppermute | solution.py:18
  186.2 4.6 %collective-permute-done.14.from_one = bf16[256,512]{1,0:T(8,128)(2,1)S(1)} collective-permute-done((bf16[256,512]{1,0:T(8,128)(2,1)S(1)}, bf16[256,512]{1,0:T(8,128)(2,1)S(1)}, u32[]{:S(2)}, u32[]{:S(2)}) %collective-permute-start.14) | collective-permute-done | bytes 262176 | tf_op jit(solution)/shard_map/ppermute | solution.py:18
  190.8 7.1 %collective-permute-done.15.from_two = bf16[256,512]{1,0:T(8,128)(2,1)S(1)} collective-permute-done((bf16[256,512]{1,0:T(8,128)(2,1)S(1)}, bf16[256,512]{1,0:T(8,128)(2,1)S(1)}, u32[]{:S(2)}, u32[]{:S(2)}) %collective-permute-start.15) | collective-permute-done | bytes 262176 | tf_op jit(solution)/shard_map/ppermute | solution.py:18
  204.0 6.4 %all-to-all-start.4 = ((bf16[16,256,128]{2,1,0:T(8,128)(2,1)}), bf16[16,256,128]{2,1,0:T(8,128)(2,1)S(1)}, u32[]{:S(2)}, u32[]{:S(2)}) async-start(bf16[16,256,128]{2,1,0:T(8,128)(2,1)} %broadcast_in_dim.61), calls=%async_computation.4 | async-start | bytes 2097152 | tf_op jit(solution)/shard_map/all_to_all | solution.py:57
  210.5 3.4 %copy-done.3 = bf16[2048,2048]{1,0:T(8,128)(2,1)S(1)} copy-done((bf16[2048,2048]{1,0:T(8,128)(2,1)S(1)}, bf16[2048,2048]{1,0:T(8,128)(2,1)}, u32[]{:S(2)}) %copy-start.3) | copy-done | bytes 8388632
  213.9 2.9 %project_q.3 = (f32[256,512]{1,0:T(8,128)S(1)}, f32[256,512]{1,0:T(8,128)S(1)}) custom-call(s32[3]{0:T(128)S(1)} %copy-done.8, bf16[256,512]{1,0:T(8,128)(2,1)S(1)} %add_convert_fusion.2.own_ref.first_ref, bf16[256,512]{1,0:T(8,128)(2,1)S(1)} %collective-permute-done.14.from_one, bf16[256,512]{1,0:T(8,128)(2,1)S(1)} %collective-permute-done.15.from_two, ...), custom_call_target="tpu_custom_call" | custom-call | flops 1073741824 | bytes 5242880 | tf_op jit(solution)/shard_map/project_q/pallas_call | solution.py:275
  217.5 9.2 %all-to-all-done.4 = bf16[16,256,128]{2,1,0:T(8,128)(2,1)S(1)} async-done(((bf16[16,256,128]{2,1,0:T(8,128)(2,1)}), bf16[16,256,128]{2,1,0:T(8,128)(2,1)S(1)}, u32[]{:S(2)}, u32[]{:S(2)}) %all-to-all-start.4) | async-done | bytes 1048608 | tf_op jit(solution)/shard_map/all_to_all | solution.py:57
  231.3 7.6 %attention.3.mine_ref = bf16[256,512]{1,0:T(8,128)(2,1)} custom-call(s32[4]{0:T(128)} %pad_add_fusion.1.scalars, bf16[256,512]{1,0:T(8,128)(2,1)} %bitcast.68, bf16[16,4,64,128]{3,2,1,0:T(8,128)(2,1)} %bitcast.61, bf16[16,4,64,128]{3,2,1,0:T(8,128)(2,1)} %collective-permute-done.19.other_ref), custom_call_target="tpu_custom_call" | custom-call | flops 134217728 | bytes 2621440 | tf_op jit(solution)/shard_map/attention/pallas_call | solution.py:135
  240.7 3.4 %copy-done.4 = bf16[2048,2048]{1,0:T(8,128)(2,1)S(1)} copy-done((bf16[2048,2048]{1,0:T(8,128)(2,1)S(1)}, bf16[2048,2048]{1,0:T(8,128)(2,1)}, u32[]{:S(2)}) %copy-start.4) | copy-done | bytes 8388632
  245.0 3.3 %project_out.3 = (bf16[256,512]{1,0:T(8,128)(2,1)S(1)}, bf16[256,512]{1,0:T(8,128)(2,1)S(1)}, bf16[256,512]{1,0:T(8,128)(2,1)S(1)}, bf16[256,512]{1,0:T(8,128)(2,1)S(1)}) custom-call(s32[3]{0:T(128)S(1)} %copy-done.8, bf16[256,512]{1,0:T(8,128)(2,1)S(1)} %copy-done.7, bf16[256,512]{1,0:T(8,128)(2,1)S(1)} %collective-permute-done.20.other_ref, ...), custom_call_target="tpu_custom_call" | custom-call | flops 1073741824 | bytes 5242880 | tf_op jit(solution)/shard_map/project_out/pallas_call | solution.py:334
  253.5 4.0 %collective-permute-done.21 = bf16[256,512]{1,0:T(8,128)(2,1)S(1)} collective-permute-done((bf16[256,512]{1,0:T(8,128)(2,1)S(1)}, bf16[256,512]{1,0:T(8,128)(2,1)S(1)}, u32[]{:S(2)}, u32[]{:S(2)}) %collective-permute-start.21) | collective-permute-done | bytes 262176 | tf_op jit(solution)/shard_map/ppermute | solution.py:18
  257.5 6.2 %collective-permute-done.22 = bf16[256,512]{1,0:T(8,128)(2,1)S(1)} collective-permute-done((bf16[256,512]{1,0:T(8,128)(2,1)S(1)}, bf16[256,512]{1,0:T(8,128)(2,1)S(1)}, u32[]{:S(2)}, u32[]{:S(2)}) %collective-permute-start.22) | collective-permute-done | bytes 262176 | tf_op jit(solution)/shard_map/ppermute | solution.py:18
  (154 shorter events, 69.8 us)
Async XLA Ops:
  6.5 96.1 %all-gather.3.cloned.1.call-start = ((), (), s32[]{:S(2)}) async-start(), calls=%async_computation.5 | async-start | bytes 10027008 | tf_op jit(solution)/shard_map/all_gather | solution.py:440
  9.2 3.1 %collective-permute-start.5 = (bf16[128,2304]{1,0:T(8,128)(2,1)S(1)}, bf16[128,2304]{1,0:T(8,128)(2,1)S(1)}, u32[]{:S(2)}, u32[]{:S(2)}) collective-permute-start(bf16[128,2304]{1,0:T(8,128)(2,1)S(1)} %broadcast_select_fusion.2), channel_id=1, source_target_pairs={{0,64},{64,0},{1,65},{65,1},{2,66},{66,2},{3,67},{67,3},{4,68},{68... | collective-permute-start | bytes 1769480 | tf_op jit(solution)/shard_map/ppermute | solution.py:22
  13.4 197.0 %all-gather.5.cloned.1.call-start = ((), (), s32[]{:S(2)}) async-start(), calls=%async_computation.6 | async-start | bytes 8912896 | tf_op jit(solution)/shard_map/all_gather | solution.py:440
  20.4 2.4 collective-permute-start
  25.9 29.8 %all-to-all-start = ((bf16[64,16,512]{2,1,0:T(8,128)(2,1)}), bf16[64,16,512]{2,1,0:T(8,128)(2,1)S(1)}, u32[]{:S(2)}, u32[]{:S(2)}) async-start(bf16[64,16,512]{2,1,0:T(8,128)(2,1)} %merger_outer.1), calls=%async_computation | async-start | bytes 2097152 | tf_op jit(solution)/shard_map/all_to_all | solution.py:453
  56.6 15.4 %all-to-all-start.1 = ((bf16[16,16,512]{2,1,0:T(8,128)(2,1)}), bf16[16,16,512]{2,1,0:T(8,128)(2,1)S(1)}, u32[]{:S(2)}, u32[]{:S(2)}) async-start(bf16[16,16,512]{2,1,0:T(8,128)(2,1)} %broadcast_in_dim.30), calls=%async_computation.1 | async-start | bytes 524288 | tf_op jit(solution)/shard_map/all_to_all | solution.py:57
  72.3 10.2 %collective-permute-start.1 = (bf16[256,512]{1,0:T(8,128)(2,1)S(1)}, bf16[256,512]{1,0:T(8,128)(2,1)S(1)}, u32[]{:S(2)}, u32[]{:S(2)}) collective-permute-start(bf16[256,512]{1,0:T(8,128)(2,1)S(1)} %broadcast_select_fusion.4.own_ref), channel_id=1, source_target_pairs={{0,1},{1,2},{2,3},{3,0},{4,5},{5,6},{6,7},{7,4},{8,9},{9,10},{10,1... | collective-permute-start | bytes 786440 | tf_op jit(solution)/shard_map/ppermute | solution.py:18
  72.7 10.1 %collective-permute-start.2 = (bf16[256,512]{1,0:T(8,128)(2,1)S(1)}, bf16[256,512]{1,0:T(8,128)(2,1)S(1)}, u32[]{:S(2)}, u32[]{:S(2)}) collective-permute-start(bf16[256,512]{1,0:T(8,128)(2,1)S(1)} %broadcast_select_fusion.4.own_ref), channel_id=1, source_target_pairs={{0,2},{1,3},{2,0},{3,1},{4,6},{5,7},{6,4},{7,5},{8,10},{9,11},{10,... | collective-permute-start | bytes 786440 | tf_op jit(solution)/shard_map/ppermute | solution.py:18
  73.8 12.6 %collective-permute-start.3 = (bf16[256,512]{1,0:T(8,128)(2,1)S(1)}, bf16[256,512]{1,0:T(8,128)(2,1)S(1)}, u32[]{:S(2)}, u32[]{:S(2)}) collective-permute-start(bf16[256,512]{1,0:T(8,128)(2,1)S(1)} %broadcast_select_fusion.4.own_ref), channel_id=1, source_target_pairs={{0,3},{1,0},{2,1},{3,2},{4,7},{5,4},{6,5},{7,6},{8,11},{9,8},{10,9... | collective-permute-start | bytes 786440 | tf_op jit(solution)/shard_map/ppermute | solution.py:18
  75.8 3.8 %collective-permute-start.4 = (f32[16,128]{1,0:T(8,128)S(1)}, f32[16,128]{1,0:T(8,128)S(1)}, u32[]{:S(2)}, u32[]{:S(2)}) collective-permute-start(f32[16,128]{1,0:T(8,128)S(1)} %select_bitcast_fusion), channel_id=1, source_target_pairs={{0,64},{64,0},{1,65},{65,1},{2,66},{66,2},{3,67},{67,3},{4,68},{68... | collective-permute-start | bytes 24584 | tf_op jit(solution)/shard_map/ppermute | solution.py:22
  108.2 1.9 collective-permute-start.6
  111.8 28.9 %all-to-all-start.2 = ((bf16[16,256,128]{2,1,0:T(8,128)(2,1)}), bf16[16,256,128]{2,1,0:T(8,128)(2,1)}, u32[]{:S(2)}, u32[]{:S(2)}) async-start(bf16[16,256,128]{2,1,0:T(8,128)(2,1)} %broadcast_in_dim.33), calls=%async_computation.2 | async-start | bytes 2097152 | tf_op jit(solution)/shard_map/all_to_all | solution.py:57
  123.3 18.6 %collective-permute-start.7 = (f32[256,512]{1,0:T(8,128)S(1)}, f32[256,512]{1,0:T(8,128)S(1)}, u32[]{:S(2)}, u32[]{:S(2)}) collective-permute-start(f32[256,512]{1,0:T(8,128)S(1)} %get-tuple-element.54), channel_id=1, source_target_pairs={{0,64},{64,0},{1,65},{65,1},{2,66},{66,2},{3,67},{67,3},{4,68},{68... | collective-permute-start | bytes 1572872 | tf_op jit(solution)/shard_map/ppermute | solution.py:22
  140.6 3.9 %collective-permute-start.8 = (bf16[16,4,64,128]{3,2,1,0:T(8,128)(2,1)}, bf16[16,4,64,128]{3,2,1,0:T(8,128)(2,1)}, u32[]{:S(2)}, u32[]{:S(2)}) collective-permute-start(bf16[16,4,64,128]{3,2,1,0:T(8,128)(2,1)} %bitcast.15.mine_ref), channel_id=1, source_target_pairs={{0,64},{64,0},{1,65},{65,1},{2,66},{66,2},{3,67},{67,3},{4,68},{68... | collective-permute-start | bytes 3145736 | tf_op jit(solution)/shard_map/ppermute | solution.py:22
  151.9 1.7 collective-permute-start.9
  162.6 35.3 %all-to-all-start.3 = ((bf16[16,128,256]{2,1,0:T(8,128)(2,1)}), bf16[16,128,256]{2,1,0:T(8,128)(2,1)S(1)}, u32[]{:S(2)}, u32[]{:S(2)}) async-start(bf16[16,128,256]{2,1,0:T(8,128)(2,1)} %broadcast_in_dim.60), calls=%async_computation.3 | async-start | bytes 2097152 | tf_op jit(solution)/shard_map/all_to_all | solution.py:57
  166.6 8.9 %collective-permute-start.10 = (bf16[256,512]{1,0:T(8,128)(2,1)S(1)}, bf16[256,512]{1,0:T(8,128)(2,1)S(1)}, u32[]{:S(2)}, u32[]{:S(2)}) collective-permute-start(bf16[256,512]{1,0:T(8,128)(2,1)S(1)} %get-tuple-element.58), channel_id=1, source_target_pairs={{0,2},{1,3},{2,0},{3,1},{4,6},{5,7},{6,4},{7,5},{8,10},{9,11},{10,... | collective-permute-start | bytes 786440 | tf_op jit(solution)/shard_map/ppermute | solution.py:18
  169.6 12.6 %collective-permute-start.11 = (bf16[256,512]{1,0:T(8,128)(2,1)S(1)}, bf16[256,512]{1,0:T(8,128)(2,1)S(1)}, u32[]{:S(2)}, u32[]{:S(2)}) collective-permute-start(bf16[256,512]{1,0:T(8,128)(2,1)S(1)} %get-tuple-element.59), channel_id=1, source_target_pairs={{0,1},{1,2},{2,3},{3,0},{4,5},{5,6},{6,7},{7,4},{8,9},{9,10},{10,1... | collective-permute-start | bytes 786440 | tf_op jit(solution)/shard_map/ppermute | solution.py:18
  169.9 12.2 %collective-permute-start.12 = (bf16[256,512]{1,0:T(8,128)(2,1)S(1)}, bf16[256,512]{1,0:T(8,128)(2,1)S(1)}, u32[]{:S(2)}, u32[]{:S(2)}) collective-permute-start(bf16[256,512]{1,0:T(8,128)(2,1)S(1)} %get-tuple-element.60), channel_id=1, source_target_pairs={{0,3},{1,0},{2,1},{3,2},{4,7},{5,4},{6,5},{7,6},{8,11},{9,8},{10,9... | collective-permute-start | bytes 786440 | tf_op jit(solution)/shard_map/ppermute | solution.py:18
  182.3 8.5 %collective-permute-start.14 = (bf16[256,512]{1,0:T(8,128)(2,1)S(1)}, bf16[256,512]{1,0:T(8,128)(2,1)S(1)}, u32[]{:S(2)}, u32[]{:S(2)}) collective-permute-start(bf16[256,512]{1,0:T(8,128)(2,1)S(1)} %add_convert_fusion.2.own_ref.first_ref), channel_id=1, source_target_pairs={{0,1},{1,2},{2,3},{3,0},{4,5},{5,6},{6,7},{7,4},{8,9},{9,10},{10,1... | collective-permute-start | bytes 786440 | tf_op jit(solution)/shard_map/ppermute | solution.py:18
  183.7 14.2 %collective-permute-start.15 = (bf16[256,512]{1,0:T(8,128)(2,1)S(1)}, bf16[256,512]{1,0:T(8,128)(2,1)S(1)}, u32[]{:S(2)}, u32[]{:S(2)}) collective-permute-start(bf16[256,512]{1,0:T(8,128)(2,1)S(1)} %add_convert_fusion.2.own_ref.first_ref), channel_id=1, source_target_pairs={{0,2},{1,3},{2,0},{3,1},{4,6},{5,7},{6,4},{7,5},{8,10},{9,11},{10,... | collective-permute-start | bytes 786440 | tf_op jit(solution)/shard_map/ppermute | solution.py:18
  186.2 11.7 %collective-permute-start.16 = (bf16[256,512]{1,0:T(8,128)(2,1)S(1)}, bf16[256,512]{1,0:T(8,128)(2,1)S(1)}, u32[]{:S(2)}, u32[]{:S(2)}) collective-permute-start(bf16[256,512]{1,0:T(8,128)(2,1)S(1)} %add_convert_fusion.2.own_ref.first_ref), channel_id=1, source_target_pairs={{0,3},{1,0},{2,1},{3,2},{4,7},{5,4},{6,5},{7,6},{8,11},{9,8},{10,9... | collective-permute-start | bytes 786440 | tf_op jit(solution)/shard_map/ppermute | solution.py:18
  199.8 2.5 collective-permute-start.17
  204.0 22.8 %all-to-all-start.4 = ((bf16[16,256,128]{2,1,0:T(8,128)(2,1)}), bf16[16,256,128]{2,1,0:T(8,128)(2,1)S(1)}, u32[]{:S(2)}, u32[]{:S(2)}) async-start(bf16[16,256,128]{2,1,0:T(8,128)(2,1)} %broadcast_in_dim.61), calls=%async_computation.4 | async-start | bytes 2097152 | tf_op jit(solution)/shard_map/all_to_all | solution.py:57
  216.8 12.1 %collective-permute-start.18 = (f32[256,512]{1,0:T(8,128)S(1)}, f32[256,512]{1,0:T(8,128)S(1)}, u32[]{:S(2)}, u32[]{:S(2)}) collective-permute-start(f32[256,512]{1,0:T(8,128)S(1)} %get-tuple-element.69), channel_id=1, source_target_pairs={{0,64},{64,0},{1,65},{65,1},{2,66},{66,2},{3,67},{67,3},{4,68},{68... | collective-permute-start | bytes 1572872 | tf_op jit(solution)/shard_map/ppermute | solution.py:22
  226.8 4.5 %collective-permute-start.19 = (bf16[16,4,64,128]{3,2,1,0:T(8,128)(2,1)S(1)}, bf16[16,4,64,128]{3,2,1,0:T(8,128)(2,1)}, u32[]{:S(2)}, u32[]{:S(2)}) collective-permute-start(bf16[16,4,64,128]{3,2,1,0:T(8,128)(2,1)S(1)} %bitcast.60), channel_id=1, source_target_pairs={{0,64},{64,0},{1,65},{65,1},{2,66},{66,2},{3,67},{67,3},{4,68},{68... | collective-permute-start | bytes 3145736 | tf_op jit(solution)/shard_map/ppermute | solution.py:22
  238.9 1.7 collective-permute-start.20
  248.3 9.2 %collective-permute-start.21 = (bf16[256,512]{1,0:T(8,128)(2,1)S(1)}, bf16[256,512]{1,0:T(8,128)(2,1)S(1)}, u32[]{:S(2)}, u32[]{:S(2)}) collective-permute-start(bf16[256,512]{1,0:T(8,128)(2,1)S(1)} %get-tuple-element.72), channel_id=1, source_target_pairs={{0,2},{1,3},{2,0},{3,1},{4,6},{5,7},{6,4},{7,5},{8,10},{9,11},{10,... | collective-permute-start | bytes 786440 | tf_op jit(solution)/shard_map/ppermute | solution.py:18
  249.7 14.1 %collective-permute-start.22 = (bf16[256,512]{1,0:T(8,128)(2,1)S(1)}, bf16[256,512]{1,0:T(8,128)(2,1)S(1)}, u32[]{:S(2)}, u32[]{:S(2)}) collective-permute-start(bf16[256,512]{1,0:T(8,128)(2,1)S(1)} %get-tuple-element.73), channel_id=1, source_target_pairs={{0,1},{1,2},{2,3},{3,0},{4,5},{5,6},{6,7},{7,4},{8,9},{9,10},{10,1... | collective-permute-start | bytes 786440 | tf_op jit(solution)/shard_map/ppermute | solution.py:18
  250.8 12.9 %collective-permute-start.23 = (bf16[256,512]{1,0:T(8,128)(2,1)S(1)}, bf16[256,512]{1,0:T(8,128)(2,1)S(1)}, u32[]{:S(2)}, u32[]{:S(2)}) collective-permute-start(bf16[256,512]{1,0:T(8,128)(2,1)S(1)} %get-tuple-element.74), channel_id=1, source_target_pairs={{0,3},{1,0},{2,1},{3,2},{4,7},{5,4},{6,5},{7,6},{8,11},{9,8},{10,9... | collective-permute-start | bytes 786440 | tf_op jit(solution)/shard_map/ppermute | solution.py:18
  252.3 12.2 %collective-permute-start.13 = (bf16[256,512]{1,0:T(8,128)(2,1)S(1)}, bf16[256,512]{1,0:T(8,128)(2,1)S(1)}, u32[]{:S(2)}, u32[]{:S(2)}) collective-permute-start(bf16[256,512]{1,0:T(8,128)(2,1)S(1)} %add_convert_fusion.2.own_ref.first_ref), channel_id=1, source_target_pairs={{0,64},{64,0},{1,65},{65,1},{2,66},{66,2},{3,67},{67,3},{4,68},{68... | collective-permute-start | bytes 786440 | tf_op jit(solution)/shard_map/ppermute | solution.py:22
  263.9 1.7 collective-permute-start.24
  (21 other events, 210.5 us)
Sparse Core Ops, SparseCore 0:
  13.6 88.9 all-gather.2
  104.7 91.7 all-gather.4

commit v5 on v4

--- a/solution.py
+++ b/solution.py
@@ -133,7 +133,7 @@
 def attention(scalars, query, mine, other):
     whole = pl.BlockSpec(memory_space=pltpu.VMEM)
     return pl.pallas_call(
-        functools.partial(attention_kernel, chunk_runs=mine.shape[0] // 2),
+        functools.partial(attention_kernel, chunk_runs=mine.shape[0]),
         out_shape=jax.ShapeDtypeStruct(query.shape, query.dtype),
         in_specs=[pl.BlockSpec(memory_space=pltpu.SMEM), whole, whole, whole],
         out_specs=whole,
@@ -290,7 +290,7 @@
             bytes_accessed=2 * weight.shape[0] * width + 8 * rows * out.shape[1],
             transcendentals=0,
         ),
-        compiler_params=pltpu.CompilerParams(vmem_limit_bytes=24 << 20),
+        compiler_params=pltpu.CompilerParams(vmem_limit_bytes=48 << 20),
         name="project_kv" if with_squares else "project_q",
     )(place, *parts, gain, weight)
 
@@ -350,7 +350,7 @@
             bytes_accessed=4 * half * weight.shape[0] + 2 * rows * weight.shape[0],
             transcendentals=0,
         ),
-        compiler_params=pltpu.CompilerParams(vmem_limit_bytes=24 << 20),
+        compiler_params=pltpu.CompilerParams(vmem_limit_bytes=48 << 20),
         name="project_out",
     )(place, mine, other, weight)
 

time: 278 us -> 267 us (0.960)
  local copies, waits for them, and re-layouts: 34.3 us -> 16.2 us
  waiting for transfers between devices: 116 us -> 121 us
    unnamed x54 -> x44, local copies, waits for them, and re-layouts: 24.9 us -> 6.83 us
    all_to_all x4, waiting for transfers between devices: 36.8 us -> 41.5 us  [spread(): return lax.all_to_all(copies, 'blk', 0, 0, tiled=True)]
  transfers between devices with their start and end apart: 32 -> 32, of which waited for: 23 -> 22; matrix products, arithmetic and copies ran while one was open for 7% -> 7% of each run, Pallas kernels for 9% -> 11%
where the time goes in v5:
time: 267 us; the launch traced here: 266 us
  waiting for transfers between devices  121 us (45%)
  starting transfers between devices  64 us (24%)
  Pallas kernels  41.8 us (16%)
  local copies, waits for them, and re-layouts  16.2 us (6%)
  between operations  13.9 us (5%)
  other arithmetic  9.01 us (3%)
    all_to_all x4, waiting for transfers between devices, spread(): return lax.all_to_all(copies, 'blk', 0, 0, tiled=True)  41.5 us
    ppermute x12, waiting for transfers between devices, moved(): lax.ppermute(value, axis, [(i, (i + by) % size) for i in range(size)])  38.5 us
    all_to_all x4, starting transfers between devices, spread(): return lax.all_to_all(copies, 'blk', 0, 0, tiled=True)  19.7 us
    ppermute x12, starting transfers between devices, moved(): lax.ppermute(value, axis, [(i, (i + by) % size) for i in range(size)])  17.1 us
    all_gather x2, waiting for transfers between devices, local(): weight_full.append(lax.all_gather(sent_off, 'blk', axis=0, tiled=True))  16.5 us
    ppermute x13, starting transfers between devices, swapped(): return lax.ppermute(value, 'section', [(0, 1), (1, 0)])  15.8 us
    all_to_all x1, waiting for transfers between devices, local(): lax.all_to_all(merged_pieces, ('blk', 'mp'), 0, 0, tiled=True)  15.1 us
    pallas_call x2, Pallas kernels, attention(): pl.pallas_call(functools.partial(attention_kernel, chunk_runs=mine.shape[...  14.9 us
  transfers between devices with their start and end apart: 32, of which 22 were waited for; matrix products, arithmetic and copies ran while one was open for 7% of the time, Pallas kernels for 11%

profile of v5, /device:TPU:1, one launch (start us, length us, event | category | flops | bytes accessed | tf_op | source)
XLA Modules:
  0.0 266.5 jit_solution(17099353926085716378)
XLA Ops:
  16.8 3.6 %merger_inner.1.mine_ref = bf16[128,80]{1,0:T(8,128)(2,1)} custom-call(bf16[128,5120]{1,0:T(8,128)(2,1)} %patches_ref.1, f32[1,1280]{1,0:T(1,128)} %reshape.93.gain_ref, bf16[5120,80]{1,0:T(8,128)(2,1)} %copy.24.weight_ref), custom_call_target="tpu_custom_call" | custom-call | flops 104857600 | bytes 2129920 | tf_op jit(solution)/shard_map/merger_inner/pallas_call | solution.py:166
  23.4 2.5 merger_outer.1
  25.9 11.4 %all-to-all-start = ((bf16[64,16,512]{2,1,0:T(8,128)(2,1)}), bf16[64,16,512]{2,1,0:T(8,128)(2,1)S(1)}, u32[]{:S(2)}, u32[]{:S(2)}) async-start(bf16[64,16,512]{2,1,0:T(8,128)(2,1)} %merger_outer.1), calls=%async_computation | async-start | bytes 2097152 | tf_op jit(solution)/shard_map/all_to_all | solution.py:453
  40.7 15.1 %all-to-all-done = bf16[64,16,512]{2,1,0:T(8,128)(2,1)S(1)} async-done(((bf16[64,16,512]{2,1,0:T(8,128)(2,1)}), bf16[64,16,512]{2,1,0:T(8,128)(2,1)S(1)}, u32[]{:S(2)}, u32[]{:S(2)}) %all-to-all-start) | async-done | bytes 1048608 | tf_op jit(solution)/shard_map/all_to_all | solution.py:453
  56.7 4.1 %all-to-all-start.1 = ((bf16[16,16,512]{2,1,0:T(8,128)(2,1)}), bf16[16,16,512]{2,1,0:T(8,128)(2,1)S(1)}, u32[]{:S(2)}, u32[]{:S(2)}) async-start(bf16[16,16,512]{2,1,0:T(8,128)(2,1)} %broadcast_in_dim.30), calls=%async_computation.1 | async-start | bytes 524288 | tf_op jit(solution)/shard_map/all_to_all | solution.py:57
  60.8 11.1 %all-to-all-done.1 = bf16[16,16,512]{2,1,0:T(8,128)(2,1)S(1)} async-done(((bf16[16,16,512]{2,1,0:T(8,128)(2,1)}), bf16[16,16,512]{2,1,0:T(8,128)(2,1)S(1)}, u32[]{:S(2)}, u32[]{:S(2)}) %all-to-all-start.1) | async-done | bytes 262176 | tf_op jit(solution)/shard_map/all_to_all | solution.py:57
  75.5 3.2 %collective-permute-start.4 = (f32[16,128]{1,0:T(8,128)S(1)}, f32[16,128]{1,0:T(8,128)S(1)}, u32[]{:S(2)}, u32[]{:S(2)}) collective-permute-start(f32[16,128]{1,0:T(8,128)S(1)} %select_bitcast_fusion), channel_id=1, source_target_pairs={{0,64},{64,0},{1,65},{65,1},{2,66},{66,2},{3,67},{67,3},{4,68},{68... | collective-permute-start | bytes 24584 | tf_op jit(solution)/shard_map/ppermute | solution.py:22
  79.6 3.4 %collective-permute-done.1.from_one = bf16[256,512]{1,0:T(8,128)(2,1)S(1)} collective-permute-done((bf16[256,512]{1,0:T(8,128)(2,1)S(1)}, bf16[256,512]{1,0:T(8,128)(2,1)S(1)}, u32[]{:S(2)}, u32[]{:S(2)}) %collective-permute-start.1) | collective-permute-done | bytes 262176 | tf_op jit(solution)/shard_map/ppermute | solution.py:18
  83.0 3.5 %collective-permute-done.3.from_three = bf16[256,512]{1,0:T(8,128)(2,1)S(1)} collective-permute-done((bf16[256,512]{1,0:T(8,128)(2,1)S(1)}, bf16[256,512]{1,0:T(8,128)(2,1)S(1)}, u32[]{:S(2)}, u32[]{:S(2)}) %collective-permute-start.3) | collective-permute-done | bytes 262176 | tf_op jit(solution)/shard_map/ppermute | solution.py:18
  86.5 16.5 %all-gather.3.cloned.1.call-done.weight_hbm = bf16[2048,2304]{1,0:T(8,128)(2,1)} async-done(((bf16[128,2304]{1,0:T(8,128)(2,1)}), bf16[2048,2304]{1,0:T(8,128)(2,1)}) %all-gather.3.cloned.1.call-update) | async-done | bytes 9437200 | tf_op jit(solution)/shard_map/all_gather | solution.py:440
  103.0 2.6 project_kv.2
  109.2 5.0 %all-to-all-start.2 = ((bf16[16,256,128]{2,1,0:T(8,128)(2,1)}), bf16[16,256,128]{2,1,0:T(8,128)(2,1)}, u32[]{:S(2)}, u32[]{:S(2)}) async-start(bf16[16,256,128]{2,1,0:T(8,128)(2,1)} %broadcast_in_dim.33), calls=%async_computation.2 | async-start | bytes 2097152 | tf_op jit(solution)/shard_map/all_to_all | solution.py:57
  114.2 3.5 %project_q.2 = (f32[256,512]{1,0:T(8,128)S(1)}, f32[256,512]{1,0:T(8,128)S(1)}) custom-call(s32[3]{0:T(128)S(1)} %copy-done.3, bf16[256,512]{1,0:T(8,128)(2,1)S(1)} %broadcast_select_fusion.4.own_ref, bf16[256,512]{1,0:T(8,128)(2,1)S(1)} %collective-permute-done.1.from_one, bf16[256,512]{1,0:T(8,128)(2,1)S(1)} %collective-permute-done.2.from_two, ...), custom_call_target="tpu_custom_call" | custom-call | flops 1073741824 | bytes 5242880 | tf_op jit(solution)/shard_map/project_q/pallas_call | solution.py:275
  118.4 18.0 %all-to-all-done.2 = bf16[16,256,128]{2,1,0:T(8,128)(2,1)} async-done(((bf16[16,256,128]{2,1,0:T(8,128)(2,1)}), bf16[16,256,128]{2,1,0:T(8,128)(2,1)}, u32[]{:S(2)}, u32[]{:S(2)}) %all-to-all-start.2) | async-done | bytes 1048608 | tf_op jit(solution)/shard_map/all_to_all | solution.py:57
  136.4 2.6 collective-permute-start.8
  141.6 7.3 %attention.2.mine_ref = bf16[256,512]{1,0:T(8,128)(2,1)} custom-call(s32[4]{0:T(128)} %pad_add_fusion.1.scalars, bf16[256,512]{1,0:T(8,128)(2,1)} %bitcast.69, bf16[16,4,64,128]{3,2,1,0:T(8,128)(2,1)} %bitcast.15.mine_ref, bf16[16,4,64,128]{3,2,1,0:T(8,128)(2,1)} %collective-permute-done.8.other_ref), custom_call_target="tpu_custom_call" | custom-call | flops 134217728 | bytes 2621440 | tf_op jit(solution)/shard_map/attention/pallas_call | solution.py:135
  151.6 3.7 %project_out.2 = (bf16[256,512]{1,0:T(8,128)(2,1)S(1)}, bf16[256,512]{1,0:T(8,128)(2,1)S(1)}, bf16[256,512]{1,0:T(8,128)(2,1)S(1)}, bf16[256,512]{1,0:T(8,128)(2,1)S(1)}) custom-call(s32[3]{0:T(128)S(1)} %copy-done.3, bf16[256,512]{1,0:T(8,128)(2,1)S(1)} %copy-done.1, bf16[256,512]{1,0:T(8,128)(2,1)S(1)} %collective-permute-done.9.other_ref, ...), custom_call_target="tpu_custom_call" | custom-call | flops 1073741824 | bytes 5242880 | tf_op jit(solution)/shard_map/project_out/pallas_call | solution.py:334
  156.4 4.2 %all-to-all-start.3 = ((bf16[16,128,256]{2,1,0:T(8,128)(2,1)}), bf16[16,128,256]{2,1,0:T(8,128)(2,1)S(1)}, u32[]{:S(2)}, u32[]{:S(2)}) async-start(bf16[16,128,256]{2,1,0:T(8,128)(2,1)} %broadcast_in_dim.60), calls=%async_computation.3 | async-start | bytes 2097152 | tf_op jit(solution)/shard_map/all_to_all | solution.py:57
  160.6 3.2 %collective-permute-start.10 = (bf16[256,512]{1,0:T(8,128)(2,1)S(1)}, bf16[256,512]{1,0:T(8,128)(2,1)S(1)}, u32[]{:S(2)}, u32[]{:S(2)}) collective-permute-start(bf16[256,512]{1,0:T(8,128)(2,1)S(1)} %get-tuple-element.58), channel_id=1, source_target_pairs={{0,2},{1,3},{2,0},{3,1},{4,6},{5,7},{6,4},{7,5},{8,10},{9,11},{10,... | collective-permute-start | bytes 786440 | tf_op jit(solution)/shard_map/ppermute | solution.py:18
  164.1 2.3 collective-permute-start.12
  166.4 3.2 %collective-permute-done.10 = bf16[256,512]{1,0:T(8,128)(2,1)S(1)} collective-permute-done((bf16[256,512]{1,0:T(8,128)(2,1)S(1)}, bf16[256,512]{1,0:T(8,128)(2,1)S(1)}, u32[]{:S(2)}, u32[]{:S(2)}) %collective-permute-start.10) | collective-permute-done | bytes 262176 | tf_op jit(solution)/shard_map/ppermute | solution.py:18
  169.7 6.6 %collective-permute-done.11 = bf16[256,512]{1,0:T(8,128)(2,1)S(1)} collective-permute-done((bf16[256,512]{1,0:T(8,128)(2,1)S(1)}, bf16[256,512]{1,0:T(8,128)(2,1)S(1)}, u32[]{:S(2)}, u32[]{:S(2)}) %collective-permute-start.11) | collective-permute-done | bytes 262176 | tf_op jit(solution)/shard_map/ppermute | solution.py:18
  177.9 2.6 collective-permute-start.15
  180.5 4.6 %collective-permute-done.14.from_one = bf16[256,512]{1,0:T(8,128)(2,1)S(1)} collective-permute-done((bf16[256,512]{1,0:T(8,128)(2,1)S(1)}, bf16[256,512]{1,0:T(8,128)(2,1)S(1)}, u32[]{:S(2)}, u32[]{:S(2)}) %collective-permute-start.14) | collective-permute-done | bytes 262176 | tf_op jit(solution)/shard_map/ppermute | solution.py:18
  185.0 7.1 %collective-permute-done.15.from_two = bf16[256,512]{1,0:T(8,128)(2,1)S(1)} collective-permute-done((bf16[256,512]{1,0:T(8,128)(2,1)S(1)}, bf16[256,512]{1,0:T(8,128)(2,1)S(1)}, u32[]{:S(2)}, u32[]{:S(2)}) %collective-permute-start.15) | collective-permute-done | bytes 262176 | tf_op jit(solution)/shard_map/ppermute | solution.py:18
  198.2 6.4 %all-to-all-start.4 = ((bf16[16,256,128]{2,1,0:T(8,128)(2,1)}), bf16[16,256,128]{2,1,0:T(8,128)(2,1)S(1)}, u32[]{:S(2)}, u32[]{:S(2)}) async-start(bf16[16,256,128]{2,1,0:T(8,128)(2,1)} %broadcast_in_dim.61), calls=%async_computation.4 | async-start | bytes 2097152 | tf_op jit(solution)/shard_map/all_to_all | solution.py:57
  204.6 3.2 %project_q.3 = (f32[256,512]{1,0:T(8,128)S(1)}, f32[256,512]{1,0:T(8,128)S(1)}) custom-call(s32[3]{0:T(128)S(1)} %copy-done.3, bf16[256,512]{1,0:T(8,128)(2,1)S(1)} %add_convert_fusion.2.own_ref.first_ref, bf16[256,512]{1,0:T(8,128)(2,1)S(1)} %collective-permute-done.14.from_one, bf16[256,512]{1,0:T(8,128)(2,1)S(1)} %collective-permute-done.15.from_two, ...), custom_call_target="tpu_custom_call" | custom-call | flops 1073741824 | bytes 5242880 | tf_op jit(solution)/shard_map/project_q/pallas_call | solution.py:275
  208.6 12.3 %all-to-all-done.4 = bf16[16,256,128]{2,1,0:T(8,128)(2,1)S(1)} async-done(((bf16[16,256,128]{2,1,0:T(8,128)(2,1)}), bf16[16,256,128]{2,1,0:T(8,128)(2,1)S(1)}, u32[]{:S(2)}, u32[]{:S(2)}) %all-to-all-start.4) | async-done | bytes 1048608 | tf_op jit(solution)/shard_map/all_to_all | solution.py:57
  225.5 7.6 %attention.3.mine_ref = bf16[256,512]{1,0:T(8,128)(2,1)} custom-call(s32[4]{0:T(128)} %pad_add_fusion.1.scalars, bf16[256,512]{1,0:T(8,128)(2,1)} %bitcast.68, bf16[16,4,64,128]{3,2,1,0:T(8,128)(2,1)} %bitcast.61, bf16[16,4,64,128]{3,2,1,0:T(8,128)(2,1)} %collective-permute-done.19.other_ref), custom_call_target="tpu_custom_call" | custom-call | flops 134217728 | bytes 2621440 | tf_op jit(solution)/shard_map/attention/pallas_call | solution.py:135
  235.7 3.7 %project_out.3 = (bf16[256,512]{1,0:T(8,128)(2,1)S(1)}, bf16[256,512]{1,0:T(8,128)(2,1)S(1)}, bf16[256,512]{1,0:T(8,128)(2,1)S(1)}, bf16[256,512]{1,0:T(8,128)(2,1)S(1)}) custom-call(s32[3]{0:T(128)S(1)} %copy-done.3, bf16[256,512]{1,0:T(8,128)(2,1)S(1)} %copy-done.2, bf16[256,512]{1,0:T(8,128)(2,1)S(1)} %collective-permute-done.20.other_ref, ...), custom_call_target="tpu_custom_call" | custom-call | flops 1073741824 | bytes 5242880 | tf_op jit(solution)/shard_map/project_out/pallas_call | solution.py:334
  244.7 3.9 %collective-permute-done.21 = bf16[256,512]{1,0:T(8,128)(2,1)S(1)} collective-permute-done((bf16[256,512]{1,0:T(8,128)(2,1)S(1)}, bf16[256,512]{1,0:T(8,128)(2,1)S(1)}, u32[]{:S(2)}, u32[]{:S(2)}) %collective-permute-start.21) | collective-permute-done | bytes 262176 | tf_op jit(solution)/shard_map/ppermute | solution.py:18
  248.6 6.3 %collective-permute-done.22 = bf16[256,512]{1,0:T(8,128)(2,1)S(1)} collective-permute-done((bf16[256,512]{1,0:T(8,128)(2,1)S(1)}, bf16[256,512]{1,0:T(8,128)(2,1)S(1)}, u32[]{:S(2)}, u32[]{:S(2)}) %collective-permute-start.22) | collective-permute-done | bytes 262176 | tf_op jit(solution)/shard_map/ppermute | solution.py:18
  (144 shorter events, 58.4 us)
Async XLA Ops:
  6.5 96.4 %all-gather.3.cloned.1.call-start = ((), (), s32[]{:S(2)}) async-start(), calls=%async_computation.5 | async-start | bytes 10027008 | tf_op jit(solution)/shard_map/all_gather | solution.py:440
  9.2 3.1 %collective-permute-start.5 = (bf16[128,2304]{1,0:T(8,128)(2,1)S(1)}, bf16[128,2304]{1,0:T(8,128)(2,1)S(1)}, u32[]{:S(2)}, u32[]{:S(2)}) collective-permute-start(bf16[128,2304]{1,0:T(8,128)(2,1)S(1)} %broadcast_select_fusion.2), channel_id=1, source_target_pairs={{0,64},{64,0},{1,65},{65,1},{2,66},{66,2},{3,67},{67,3},{4,68},{68... | collective-permute-start | bytes 1769480 | tf_op jit(solution)/shard_map/ppermute | solution.py:22
  13.5 191.2 %all-gather.5.cloned.1.call-start = ((), (), s32[]{:S(2)}) async-start(), calls=%async_computation.6 | async-start | bytes 8912896 | tf_op jit(solution)/shard_map/all_gather | solution.py:440
  20.4 2.4 collective-permute-start
  25.9 29.9 %all-to-all-start = ((bf16[64,16,512]{2,1,0:T(8,128)(2,1)}), bf16[64,16,512]{2,1,0:T(8,128)(2,1)S(1)}, u32[]{:S(2)}, u32[]{:S(2)}) async-start(bf16[64,16,512]{2,1,0:T(8,128)(2,1)} %merger_outer.1), calls=%async_computation | async-start | bytes 2097152 | tf_op jit(solution)/shard_map/all_to_all | solution.py:453
  56.7 15.2 %all-to-all-start.1 = ((bf16[16,16,512]{2,1,0:T(8,128)(2,1)}), bf16[16,16,512]{2,1,0:T(8,128)(2,1)S(1)}, u32[]{:S(2)}, u32[]{:S(2)}) async-start(bf16[16,16,512]{2,1,0:T(8,128)(2,1)} %broadcast_in_dim.30), calls=%async_computation.1 | async-start | bytes 524288 | tf_op jit(solution)/shard_map/all_to_all | solution.py:57
  72.3 10.7 %collective-permute-start.1 = (bf16[256,512]{1,0:T(8,128)(2,1)S(1)}, bf16[256,512]{1,0:T(8,128)(2,1)S(1)}, u32[]{:S(2)}, u32[]{:S(2)}) collective-permute-start(bf16[256,512]{1,0:T(8,128)(2,1)S(1)} %broadcast_select_fusion.4.own_ref), channel_id=1, source_target_pairs={{0,1},{1,2},{2,3},{3,0},{4,5},{5,6},{6,7},{7,4},{8,9},{9,10},{10,1... | collective-permute-start | bytes 786440 | tf_op jit(solution)/shard_map/ppermute | solution.py:18
  72.4 10.6 %collective-permute-start.2 = (bf16[256,512]{1,0:T(8,128)(2,1)S(1)}, bf16[256,512]{1,0:T(8,128)(2,1)S(1)}, u32[]{:S(2)}, u32[]{:S(2)}) collective-permute-start(bf16[256,512]{1,0:T(8,128)(2,1)S(1)} %broadcast_select_fusion.4.own_ref), channel_id=1, source_target_pairs={{0,2},{1,3},{2,0},{3,1},{4,6},{5,7},{6,4},{7,5},{8,10},{9,11},{10,... | collective-permute-start | bytes 786440 | tf_op jit(solution)/shard_map/ppermute | solution.py:18
  73.5 12.9 %collective-permute-start.3 = (bf16[256,512]{1,0:T(8,128)(2,1)S(1)}, bf16[256,512]{1,0:T(8,128)(2,1)S(1)}, u32[]{:S(2)}, u32[]{:S(2)}) collective-permute-start(bf16[256,512]{1,0:T(8,128)(2,1)S(1)} %broadcast_select_fusion.4.own_ref), channel_id=1, source_target_pairs={{0,3},{1,0},{2,1},{3,2},{4,7},{5,4},{6,5},{7,6},{8,11},{9,8},{10,9... | collective-permute-start | bytes 786440 | tf_op jit(solution)/shard_map/ppermute | solution.py:18
  75.5 4.1 %collective-permute-start.4 = (f32[16,128]{1,0:T(8,128)S(1)}, f32[16,128]{1,0:T(8,128)S(1)}, u32[]{:S(2)}, u32[]{:S(2)}) collective-permute-start(f32[16,128]{1,0:T(8,128)S(1)} %select_bitcast_fusion), channel_id=1, source_target_pairs={{0,64},{64,0},{1,65},{65,1},{2,66},{66,2},{3,67},{67,3},{4,68},{68... | collective-permute-start | bytes 24584 | tf_op jit(solution)/shard_map/ppermute | solution.py:22
  105.6 1.9 collective-permute-start.6
  109.2 27.2 %all-to-all-start.2 = ((bf16[16,256,128]{2,1,0:T(8,128)(2,1)}), bf16[16,256,128]{2,1,0:T(8,128)(2,1)}, u32[]{:S(2)}, u32[]{:S(2)}) async-start(bf16[16,256,128]{2,1,0:T(8,128)(2,1)} %broadcast_in_dim.33), calls=%async_computation.2 | async-start | bytes 2097152 | tf_op jit(solution)/shard_map/all_to_all | solution.py:57
  117.7 21.2 %collective-permute-start.7 = (f32[256,512]{1,0:T(8,128)S(1)}, f32[256,512]{1,0:T(8,128)S(1)}, u32[]{:S(2)}, u32[]{:S(2)}) collective-permute-start(f32[256,512]{1,0:T(8,128)S(1)} %get-tuple-element.54), channel_id=1, source_target_pairs={{0,64},{64,0},{1,65},{65,1},{2,66},{66,2},{3,67},{67,3},{4,68},{68... | collective-permute-start | bytes 1572872 | tf_op jit(solution)/shard_map/ppermute | solution.py:22
  136.4 5.2 %collective-permute-start.8 = (bf16[16,4,64,128]{3,2,1,0:T(8,128)(2,1)}, bf16[16,4,64,128]{3,2,1,0:T(8,128)(2,1)}, u32[]{:S(2)}, u32[]{:S(2)}) collective-permute-start(bf16[16,4,64,128]{3,2,1,0:T(8,128)(2,1)} %bitcast.15.mine_ref), channel_id=1, source_target_pairs={{0,64},{64,0},{1,65},{65,1},{2,66},{66,2},{3,67},{67,3},{4,68},{68... | collective-permute-start | bytes 3145736 | tf_op jit(solution)/shard_map/ppermute | solution.py:22
  148.9 1.7 collective-permute-start.9
  156.4 35.7 %all-to-all-start.3 = ((bf16[16,128,256]{2,1,0:T(8,128)(2,1)}), bf16[16,128,256]{2,1,0:T(8,128)(2,1)S(1)}, u32[]{:S(2)}, u32[]{:S(2)}) async-start(bf16[16,128,256]{2,1,0:T(8,128)(2,1)} %broadcast_in_dim.60), calls=%async_computation.3 | async-start | bytes 2097152 | tf_op jit(solution)/shard_map/all_to_all | solution.py:57
  160.6 9.1 %collective-permute-start.10 = (bf16[256,512]{1,0:T(8,128)(2,1)S(1)}, bf16[256,512]{1,0:T(8,128)(2,1)S(1)}, u32[]{:S(2)}, u32[]{:S(2)}) collective-permute-start(bf16[256,512]{1,0:T(8,128)(2,1)S(1)} %get-tuple-element.58), channel_id=1, source_target_pairs={{0,2},{1,3},{2,0},{3,1},{4,6},{5,7},{6,4},{7,5},{8,10},{9,11},{10,... | collective-permute-start | bytes 786440 | tf_op jit(solution)/shard_map/ppermute | solution.py:18
  163.8 12.5 %collective-permute-start.11 = (bf16[256,512]{1,0:T(8,128)(2,1)S(1)}, bf16[256,512]{1,0:T(8,128)(2,1)S(1)}, u32[]{:S(2)}, u32[]{:S(2)}) collective-permute-start(bf16[256,512]{1,0:T(8,128)(2,1)S(1)} %get-tuple-element.59), channel_id=1, source_target_pairs={{0,1},{1,2},{2,3},{3,0},{4,5},{5,6},{6,7},{7,4},{8,9},{9,10},{10,1... | collective-permute-start | bytes 786440 | tf_op jit(solution)/shard_map/ppermute | solution.py:18
  164.1 12.1 %collective-permute-start.12 = (bf16[256,512]{1,0:T(8,128)(2,1)S(1)}, bf16[256,512]{1,0:T(8,128)(2,1)S(1)}, u32[]{:S(2)}, u32[]{:S(2)}) collective-permute-start(bf16[256,512]{1,0:T(8,128)(2,1)S(1)} %get-tuple-element.60), channel_id=1, source_target_pairs={{0,3},{1,0},{2,1},{3,2},{4,7},{5,4},{6,5},{7,6},{8,11},{9,8},{10,9... | collective-permute-start | bytes 786440 | tf_op jit(solution)/shard_map/ppermute | solution.py:18
  176.4 8.6 %collective-permute-start.14 = (bf16[256,512]{1,0:T(8,128)(2,1)S(1)}, bf16[256,512]{1,0:T(8,128)(2,1)S(1)}, u32[]{:S(2)}, u32[]{:S(2)}) collective-permute-start(bf16[256,512]{1,0:T(8,128)(2,1)S(1)} %add_convert_fusion.2.own_ref.first_ref), channel_id=1, source_target_pairs={{0,1},{1,2},{2,3},{3,0},{4,5},{5,6},{6,7},{7,4},{8,9},{9,10},{10,1... | collective-permute-start | bytes 786440 | tf_op jit(solution)/shard_map/ppermute | solution.py:18
  177.9 14.2 %collective-permute-start.15 = (bf16[256,512]{1,0:T(8,128)(2,1)S(1)}, bf16[256,512]{1,0:T(8,128)(2,1)S(1)}, u32[]{:S(2)}, u32[]{:S(2)}) collective-permute-start(bf16[256,512]{1,0:T(8,128)(2,1)S(1)} %add_convert_fusion.2.own_ref.first_ref), channel_id=1, source_target_pairs={{0,2},{1,3},{2,0},{3,1},{4,6},{5,7},{6,4},{7,5},{8,10},{9,11},{10,... | collective-permute-start | bytes 786440 | tf_op jit(solution)/shard_map/ppermute | solution.py:18
  180.5 11.7 %collective-permute-start.16 = (bf16[256,512]{1,0:T(8,128)(2,1)S(1)}, bf16[256,512]{1,0:T(8,128)(2,1)S(1)}, u32[]{:S(2)}, u32[]{:S(2)}) collective-permute-start(bf16[256,512]{1,0:T(8,128)(2,1)S(1)} %add_convert_fusion.2.own_ref.first_ref), channel_id=1, source_target_pairs={{0,3},{1,0},{2,1},{3,2},{4,7},{5,4},{6,5},{7,6},{8,11},{9,8},{10,9... | collective-permute-start | bytes 786440 | tf_op jit(solution)/shard_map/ppermute | solution.py:18
  194.0 2.5 collective-permute-start.17
  198.2 22.7 %all-to-all-start.4 = ((bf16[16,256,128]{2,1,0:T(8,128)(2,1)}), bf16[16,256,128]{2,1,0:T(8,128)(2,1)S(1)}, u32[]{:S(2)}, u32[]{:S(2)}) async-start(bf16[16,256,128]{2,1,0:T(8,128)(2,1)} %broadcast_in_dim.61), calls=%async_computation.4 | async-start | bytes 2097152 | tf_op jit(solution)/shard_map/all_to_all | solution.py:57
  207.9 15.2 %collective-permute-start.18 = (f32[256,512]{1,0:T(8,128)S(1)}, f32[256,512]{1,0:T(8,128)S(1)}, u32[]{:S(2)}, u32[]{:S(2)}) collective-permute-start(f32[256,512]{1,0:T(8,128)S(1)} %get-tuple-element.69), channel_id=1, source_target_pairs={{0,64},{64,0},{1,65},{65,1},{2,66},{66,2},{3,67},{67,3},{4,68},{68... | collective-permute-start | bytes 1572872 | tf_op jit(solution)/shard_map/ppermute | solution.py:22
  220.9 4.5 %collective-permute-start.19 = (bf16[16,4,64,128]{3,2,1,0:T(8,128)(2,1)S(1)}, bf16[16,4,64,128]{3,2,1,0:T(8,128)(2,1)}, u32[]{:S(2)}, u32[]{:S(2)}) collective-permute-start(bf16[16,4,64,128]{3,2,1,0:T(8,128)(2,1)S(1)} %bitcast.60), channel_id=1, source_target_pairs={{0,64},{64,0},{1,65},{65,1},{2,66},{66,2},{3,67},{67,3},{4,68},{68... | collective-permute-start | bytes 3145736 | tf_op jit(solution)/shard_map/ppermute | solution.py:22
  233.0 1.7 collective-permute-start.20
  239.4 9.1 %collective-permute-start.21 = (bf16[256,512]{1,0:T(8,128)(2,1)S(1)}, bf16[256,512]{1,0:T(8,128)(2,1)S(1)}, u32[]{:S(2)}, u32[]{:S(2)}) collective-permute-start(bf16[256,512]{1,0:T(8,128)(2,1)S(1)} %get-tuple-element.72), channel_id=1, source_target_pairs={{0,2},{1,3},{2,0},{3,1},{4,6},{5,7},{6,4},{7,5},{8,10},{9,11},{10,... | collective-permute-start | bytes 786440 | tf_op jit(solution)/shard_map/ppermute | solution.py:18
  240.8 14.1 %collective-permute-start.22 = (bf16[256,512]{1,0:T(8,128)(2,1)S(1)}, bf16[256,512]{1,0:T(8,128)(2,1)S(1)}, u32[]{:S(2)}, u32[]{:S(2)}) collective-permute-start(bf16[256,512]{1,0:T(8,128)(2,1)S(1)} %get-tuple-element.73), channel_id=1, source_target_pairs={{0,1},{1,2},{2,3},{3,0},{4,5},{5,6},{6,7},{7,4},{8,9},{9,10},{10,1... | collective-permute-start | bytes 786440 | tf_op jit(solution)/shard_map/ppermute | solution.py:18
  242.0 12.9 %collective-permute-start.23 = (bf16[256,512]{1,0:T(8,128)(2,1)S(1)}, bf16[256,512]{1,0:T(8,128)(2,1)S(1)}, u32[]{:S(2)}, u32[]{:S(2)}) collective-permute-start(bf16[256,512]{1,0:T(8,128)(2,1)S(1)} %get-tuple-element.74), channel_id=1, source_target_pairs={{0,3},{1,0},{2,1},{3,2},{4,7},{5,4},{6,5},{7,6},{8,11},{9,8},{10,9... | collective-permute-start | bytes 786440 | tf_op jit(solution)/shard_map/ppermute | solution.py:18
  243.5 12.1 %collective-permute-start.13 = (bf16[256,512]{1,0:T(8,128)(2,1)S(1)}, bf16[256,512]{1,0:T(8,128)(2,1)S(1)}, u32[]{:S(2)}, u32[]{:S(2)}) collective-permute-start(bf16[256,512]{1,0:T(8,128)(2,1)S(1)} %add_convert_fusion.2.own_ref.first_ref), channel_id=1, source_target_pairs={{0,64},{64,0},{1,65},{65,1},{2,66},{66,2},{3,67},{67,3},{4,68},{68... | collective-permute-start | bytes 786440 | tf_op jit(solution)/shard_map/ppermute | solution.py:22
  255.1 1.7 collective-permute-start.24
  (16 other events, 189.7 us)
Sparse Core Ops, SparseCore 0:
  13.6 89.3 all-gather.2
  105.1 91.0 all-gather.4

commit v6 on v5

--- a/solution.py
+++ b/solution.py
@@ -293,6 +293,32 @@
         compiler_params=pltpu.CompilerParams(vmem_limit_bytes=48 << 20),
         name="project_kv" if with_squares else "project_q",
     )(place, *parts, gain, weight)
+
+
+def keyval_rotate_kernel(kept_ref, arrived_ref, cosine_ref, sine_ref, out_ref, shrink_ref, *, features):
+    total = kept_ref[...] + arrived_ref[...]
+    shrink = lax.rsqrt(total[:, lane:] / features + epsilon)
+    shrink_ref[...] = shrink
+    values = total[:, :lane] * shrink
+    turned = pltpu.roll(values, lane // 2, 1)
+    result = (values * cosine_ref[...] + turned * sine_ref[...]).astype(out_ref.dtype)
+    for copy in range(out_ref.shape[0]):
+        out_ref[copy] = result
+
+
+def keyval_rotate(kept, arrived, cosine, sine, copies, features):
+    whole = pl.BlockSpec(memory_space=pltpu.VMEM)
+    rows = kept.shape[0]
+    return pl.pallas_call(
+        functools.partial(keyval_rotate_kernel, features=features),
+        out_shape=(
+            jax.ShapeDtypeStruct((copies, rows, lane), jnp.bfloat16),
+            jax.ShapeDtypeStruct((rows, lane), jnp.float32),
+        ),
+        in_specs=[whole] * 4,
+        out_specs=(whole, whole),
+        name="keyval_rotate",
+    )(kept, arrived, cosine, sine)
 
 
 def project_out_kernel(
@@ -432,12 +458,10 @@
     weight_keep = jnp.where(first_core, for_first, for_second)
     weight_other = swapped(jnp.where(first_core, for_second, for_first))
     keyval_width = 2 * head_size
-    keyval_shards, weight_full = [], []
+    weight_full = []
     for home in range(layers):
         mine = jnp.where(section_index == home, weight_keep, weight_other)
-        keyval_shards.append(mine[:, :keyval_width])
-        sent_off = mine if home == 0 else mine[:, keyval_width:]
-        weight_full.append(lax.all_gather(sent_off, "blk", axis=0, tiled=True))
+        weight_full.append(lax.all_gather(mine, "blk", axis=0, tiled=True))
     gain_half = norm_gain[0].reshape(-1, 2, lane)
     gain_keep = jnp.where(first_core, gain_half[:, 0], gain_half[:, 1])
     gain_send = jnp.where(first_core, gain_half[:, 1], gain_half[:, 0])
@@ -463,44 +487,36 @@
     has_visual = jnp.max(is_visual, axis=1, keepdims=True)
     text_rows = my_half(text_embeds.reshape(rows, slice_width), 1, section_index)
     cosine, sine = rope_tables(row_where, head_size)
-    merged_terms, scalars, is_visual, has_visual, text_rows, cosine, sine = (
-        lax.optimization_barrier(
-            (merged_terms, scalars, is_visual, has_visual, text_rows, cosine, sine)
-        )
-    )
+    keyval_cosine = jnp.where(first_core, jnp.concatenate([cosine, cosine], axis=1), 1.0)
+    keyval_sine = jnp.where(first_core, jnp.concatenate([-sine, sine], axis=1), 0.0)
+    early = (scalars, is_visual, has_visual, text_rows, cosine, sine, keyval_cosine, keyval_sine)
+    merged_terms, early = lax.optimization_barrier((merged_terms, early))
+    scalars, is_visual, has_visual, text_rows, cosine, sine, keyval_cosine, keyval_sine = early
     merged_mine = jnp.sum(merged_terms.astype(jnp.float32), axis=0).astype(jnp.bfloat16)
     merged = spread(merged_mine).reshape(n_blk * merged_mine.shape[0], -1)
     picked = jnp.dot(is_visual, merged, preferred_element_type=jnp.float32).astype(jnp.bfloat16)
     state = jnp.where(has_visual > 0, picked, text_rows)
 
-    keyval_cosine = jnp.where(first_core, cosine, 1.0)
-    keyval_sine = jnp.where(first_core, sine, 0.0)
 
     results = []
     for layer_index in range(layers):
         parts = [state] + [moved(state, "mp", by) for by in (1, 2, 3)]
         gain = gain_layers[layer_index]
         weight = weight_full[layer_index]
-        if layer_index == 0:
-            keyval_from, query_at = weight, keyval_width
-        else:
-            keyval_from, query_at = keyval_weight_full.reshape(-1, keyval_width), 0
-        kept, sent = project_in(place, parts, gain, keyval_from, 0, keyval_width, True)
-        total = kept + swapped(sent)
-        shrink = lax.rsqrt(total[:, head_size : head_size + 1] / (n_mp * slice_width) + epsilon)
-        keyval = rotate(total[:, :head_size] * shrink, keyval_cosine, keyval_sine).astype(jnp.bfloat16)
-        keyval, parts = lax.optimization_barrier((keyval, parts))
-        kept, sent = project_in(place, parts, gain, weight, query_at, 2 * heads_half, False)
-        query = ((kept + swapped(sent)) * shrink).reshape(rows, -1, head_size)
+        kept, sent = project_in(place, parts, gain, weight, 0, keyval_width, True)
+        keyval_copies, shrink = keyval_rotate(
+            kept, swapped(sent), keyval_cosine, keyval_sine, n_blk, n_mp * slice_width
+        )
+        keyval_copies, parts = lax.optimization_barrier((keyval_copies, parts))
+        kept, sent = project_in(place, parts, gain, weight, keyval_width, 2 * heads_half, False)
+        query = (kept + swapped(sent)).reshape(rows, -1, head_size) * shrink[:, None, :]
         query = rotate(query, cosine[:, None, :], sine[:, None, :])
         query = query.astype(jnp.bfloat16).reshape(rows, heads_half)
-        gathered = spread(keyval).reshape(n_blk, blocks, rows_here, head_size)
+        gathered = lax.all_to_all(keyval_copies, "blk", 0, 0, tiled=True)
+        gathered = gathered.reshape(n_blk, blocks, rows_here, head_size)
         attended = attention(scalars, query, gathered, swapped(gathered))
         attended_other = swapped(attended)
         own, *terms = project_out(place, attended, attended_other, weight)
-        if layer_index + 1 < layers:
-            own, shard = lax.optimization_barrier((own, keyval_shards[layer_index + 1]))
-            keyval_weight_full = spread(shard)
         arrived = [moved(terms[by - 1], "mp", by) for by in (2, 1, 3)]
         total = state.astype(jnp.float32) + own.astype(jnp.float32)
         for part in arrived:

time: 267 us -> 268 us (level)
  starting transfers between devices: 64 us -> 57.5 us
  Pallas kernels: 41.8 us -> 46.9 us
    all_to_all x0 -> x2, waiting for transfers between devices: none -> 32.1 us  [local(): gathered = lax.all_to_all(keyval_copies, 'blk', 0, 0, tiled=True)]
    all_to_all x4 -> x1, waiting for transfers between devices: 41.5 us -> 11.1 us  [spread(): return lax.all_to_all(copies, 'blk', 0, 0, tiled=True)]
    all_to_all x4 -> x1, starting transfers between devices: 19.7 us -> 3.69 us  [spread(): return lax.all_to_all(copies, 'blk', 0, 0, tiled=True)]
    all_gather x2, waiting for transfers between devices: 16.5 us -> 29.6 us  [local(): weight_full.append(lax.all_gather(mine, 'blk', axis=0, tiled=True))]
    ppermute x12, waiting for transfers between devices: 38.5 us -> 25.6 us  [moved(): lax.ppermute(value, axis, [(i, (i + by) % size) for i in range(size)])]
    all_to_all x0 -> x2, starting transfers between devices: none -> 9.95 us  [local(): gathered = lax.all_to_all(keyval_copies, 'blk', 0, 0, tiled=True)]
    pallas_call x0 -> x2, Pallas kernels: none -> 4.55 us  [keyval_rotate(): pl.pallas_call(functools.partial(keyval_rotate_kernel, features=features)...]
    unnamed x44 -> x58, local copies, waits for them, and re-layouts: 6.83 us -> 10.8 us
  transfers between devices with their start and end apart: 32 -> 31, of which waited for: 22 -> 19; matrix products, arithmetic and copies ran while one was open for 7% -> 5% of each run, Pallas kernels for 11% -> 11%
where the time goes in v6:
time: 268 us; the launch traced here: 267 us
  waiting for transfers between devices  123 us (46%)
  starting transfers between devices  57.5 us (21%)
  Pallas kernels  46.9 us (18%)
  local copies, waits for them, and re-layouts  15.9 us (6%)
  between operations  13.9 us (5%)
  other arithmetic  9.37 us (3%)
    all_to_all x2, waiting for transfers between devices, local(): gathered = lax.all_to_all(keyval_copies, 'blk', 0, 0, tiled=True)  32.1 us
    all_gather x2, waiting for transfers between devices, local(): weight_full.append(lax.all_gather(mine, 'blk', axis=0, tiled=True))  29.6 us
    ppermute x12, waiting for transfers between devices, moved(): lax.ppermute(value, axis, [(i, (i + by) % size) for i in range(size)])  25.6 us
    ppermute x12, starting transfers between devices, moved(): lax.ppermute(value, axis, [(i, (i + by) % size) for i in range(size)])  18.3 us
    pallas_call x2, Pallas kernels, attention(): pl.pallas_call(functools.partial(attention_kernel, chunk_runs=mine.shape[...  14.9 us
    all_to_all x1, waiting for transfers between devices, local(): lax.all_to_all(merged_pieces, ('blk', 'mp'), 0, 0, tiled=True)  14.6 us
    ppermute x13, starting transfers between devices, swapped(): return lax.ppermute(value, 'section', [(0, 1), (1, 0)])  14.1 us
    pallas_call x4, Pallas kernels, project_in(): pl.pallas_call(functools.partial(project_in_kernel, at=at), out_shape=(ou...  11.7 us
  transfers between devices with their start and end apart: 31, of which 19 were waited for; matrix products, arithmetic and copies ran while one was open for 5% of the time, Pallas kernels for 11%

profile of v6, /device:TPU:1, one launch (start us, length us, event | category | flops | bytes accessed | tf_op | source)
XLA Modules:
  0.0 266.7 jit_solution(7364041472005079305)
XLA Ops:
  16.8 3.6 %merger_inner.1.mine_ref = bf16[128,80]{1,0:T(8,128)(2,1)} custom-call(bf16[128,5120]{1,0:T(8,128)(2,1)} %patches_ref.1, f32[1,1280]{1,0:T(1,128)} %reshape.89.gain_ref, bf16[5120,80]{1,0:T(8,128)(2,1)} %copy.24.weight_ref), custom_call_target="tpu_custom_call" | custom-call | flops 104857600 | bytes 2129920 | tf_op jit(solution)/shard_map/merger_inner/pallas_call | solution.py:166
  23.5 2.6 merger_outer.1
  26.0 11.4 %all-to-all-start = ((bf16[64,16,512]{2,1,0:T(8,128)(2,1)}), bf16[64,16,512]{2,1,0:T(8,128)(2,1)S(1)}, u32[]{:S(2)}, u32[]{:S(2)}) async-start(bf16[64,16,512]{2,1,0:T(8,128)(2,1)} %merger_outer.1), calls=%async_computation | async-start | bytes 2097152 | tf_op jit(solution)/shard_map/all_to_all | solution.py:477
  41.7 14.6 %all-to-all-done = bf16[64,16,512]{2,1,0:T(8,128)(2,1)S(1)} async-done(((bf16[64,16,512]{2,1,0:T(8,128)(2,1)}), bf16[64,16,512]{2,1,0:T(8,128)(2,1)S(1)}, u32[]{:S(2)}, u32[]{:S(2)}) %all-to-all-start) | async-done | bytes 1048608 | tf_op jit(solution)/shard_map/all_to_all | solution.py:477
  57.2 3.7 %all-to-all-start.1 = ((bf16[16,16,512]{2,1,0:T(8,128)(2,1)}), bf16[16,16,512]{2,1,0:T(8,128)(2,1)S(1)}, u32[]{:S(2)}, u32[]{:S(2)}) async-start(bf16[16,16,512]{2,1,0:T(8,128)(2,1)} %broadcast_in_dim.42), calls=%async_computation.1 | async-start | bytes 524288 | tf_op jit(solution)/shard_map/all_to_all | solution.py:57
  61.0 11.1 %all-to-all-done.1 = bf16[16,16,512]{2,1,0:T(8,128)(2,1)S(1)} async-done(((bf16[16,16,512]{2,1,0:T(8,128)(2,1)}), bf16[16,16,512]{2,1,0:T(8,128)(2,1)S(1)}, u32[]{:S(2)}, u32[]{:S(2)}) %all-to-all-start.1) | async-done | bytes 262176 | tf_op jit(solution)/shard_map/all_to_all | solution.py:57
  75.6 3.3 %collective-permute-start.4 = (f32[16,128]{1,0:T(8,128)S(1)}, f32[16,128]{1,0:T(8,128)S(1)}, u32[]{:S(2)}, u32[]{:S(2)}) collective-permute-start(f32[16,128]{1,0:T(8,128)S(1)} %select_bitcast_fusion), channel_id=1, source_target_pairs={{0,64},{64,0},{1,65},{65,1},{2,66},{66,2},{3,67},{67,3},{4,68},{68... | collective-permute-start | bytes 24584 | tf_op jit(solution)/shard_map/ppermute | solution.py:22
  79.7 3.2 %collective-permute-done.1.from_one = bf16[256,512]{1,0:T(8,128)(2,1)S(1)} collective-permute-done((bf16[256,512]{1,0:T(8,128)(2,1)S(1)}, bf16[256,512]{1,0:T(8,128)(2,1)S(1)}, u32[]{:S(2)}, u32[]{:S(2)}) %collective-permute-start.1) | collective-permute-done | bytes 262176 | tf_op jit(solution)/shard_map/ppermute | solution.py:18
  83.0 3.6 %collective-permute-done.3.from_three = bf16[256,512]{1,0:T(8,128)(2,1)S(1)} collective-permute-done((bf16[256,512]{1,0:T(8,128)(2,1)S(1)}, bf16[256,512]{1,0:T(8,128)(2,1)S(1)}, u32[]{:S(2)}, u32[]{:S(2)}) %collective-permute-start.3) | collective-permute-done | bytes 262176 | tf_op jit(solution)/shard_map/ppermute | solution.py:18
  86.6 16.6 %all-gather.3.cloned.1.call-done.weight_hbm = bf16[2048,2304]{1,0:T(8,128)(2,1)} async-done(((bf16[128,2304]{1,0:T(8,128)(2,1)}), bf16[2048,2304]{1,0:T(8,128)(2,1)}) %all-gather.3.cloned.1.call-update) | async-done | bytes 9437200 | tf_op jit(solution)/shard_map/all_gather | solution.py:464
  103.2 2.6 project_kv.2
  111.4 5.0 %all-to-all-start.2 = ((bf16[16,256,128]{2,1,0:T(8,128)(2,1)}), bf16[16,256,128]{2,1,0:T(8,128)(2,1)S(1)}, u32[]{:S(2)}, u32[]{:S(2)}) async-start(bf16[16,256,128]{2,1,0:T(8,128)(2,1)} %get-tuple-element.63), calls=%async_computation.2 | async-start | bytes 2097152 | tf_op jit(solution)/shard_map/all_to_all | solution.py:515
  116.4 3.2 %project_q.2 = (f32[256,512]{1,0:T(8,128)S(1)}, f32[256,512]{1,0:T(8,128)S(1)}) custom-call(s32[3]{0:T(128)S(1)} %copy-done.5, bf16[256,512]{1,0:T(8,128)(2,1)S(1)} %broadcast_select_fusion.4.own_ref, bf16[256,512]{1,0:T(8,128)(2,1)S(1)} %collective-permute-done.1.from_one, bf16[256,512]{1,0:T(8,128)(2,1)S(1)} %collective-permute-done.2.from_two, ...), custom_call_target="tpu_custom_call" | custom-call | flops 1073741824 | bytes 5242880 | tf_op jit(solution)/shard_map/project_q/pallas_call | solution.py:275
  120.3 19.8 %all-to-all-done.2 = bf16[16,256,128]{2,1,0:T(8,128)(2,1)S(1)} async-done(((bf16[16,256,128]{2,1,0:T(8,128)(2,1)}), bf16[16,256,128]{2,1,0:T(8,128)(2,1)S(1)}, u32[]{:S(2)}, u32[]{:S(2)}) %all-to-all-start.2) | async-done | bytes 1048608 | tf_op jit(solution)/shard_map/all_to_all | solution.py:515
  144.6 7.3 %attention.2.mine_ref = bf16[256,512]{1,0:T(8,128)(2,1)} custom-call(s32[4]{0:T(128)} %pad_add_fusion.1.scalars, bf16[256,512]{1,0:T(8,128)(2,1)} %bitcast.69, bf16[16,4,64,128]{3,2,1,0:T(8,128)(2,1)} %bitcast.61, bf16[16,4,64,128]{3,2,1,0:T(8,128)(2,1)} %collective-permute-done.8.other_ref), custom_call_target="tpu_custom_call" | custom-call | flops 134217728 | bytes 2621440 | tf_op jit(solution)/shard_map/attention/pallas_call | solution.py:135
  154.7 3.7 %project_out.2 = (bf16[256,512]{1,0:T(8,128)(2,1)S(1)}, bf16[256,512]{1,0:T(8,128)(2,1)S(1)}, bf16[256,512]{1,0:T(8,128)(2,1)S(1)}, bf16[256,512]{1,0:T(8,128)(2,1)S(1)}) custom-call(s32[3]{0:T(128)S(1)} %copy-done.5, bf16[256,512]{1,0:T(8,128)(2,1)S(1)} %copy-done.2, bf16[256,512]{1,0:T(8,128)(2,1)S(1)} %collective-permute-done.9.other_ref, ...), custom_call_target="tpu_custom_call" | custom-call | flops 1073741824 | bytes 5242880 | tf_op jit(solution)/shard_map/project_out/pallas_call | solution.py:360
  158.4 3.0 %collective-permute-start.10 = (bf16[256,512]{1,0:T(8,128)(2,1)S(1)}, bf16[256,512]{1,0:T(8,128)(2,1)S(1)}, u32[]{:S(2)}, u32[]{:S(2)}) collective-permute-start(bf16[256,512]{1,0:T(8,128)(2,1)S(1)} %get-tuple-element.65), channel_id=1, source_target_pairs={{0,2},{1,3},{2,0},{3,1},{4,6},{5,7},{6,4},{7,5},{8,10},{9,11},{10,... | collective-permute-start | bytes 786440 | tf_op jit(solution)/shard_map/ppermute | solution.py:18
  161.7 2.3 collective-permute-start.12
  164.0 3.8 %collective-permute-done.10 = bf16[256,512]{1,0:T(8,128)(2,1)S(1)} collective-permute-done((bf16[256,512]{1,0:T(8,128)(2,1)S(1)}, bf16[256,512]{1,0:T(8,128)(2,1)S(1)}, u32[]{:S(2)}, u32[]{:S(2)}) %collective-permute-start.10) | collective-permute-done | bytes 262176 | tf_op jit(solution)/shard_map/ppermute | solution.py:18
  167.8 6.2 %collective-permute-done.11 = bf16[256,512]{1,0:T(8,128)(2,1)S(1)} collective-permute-done((bf16[256,512]{1,0:T(8,128)(2,1)S(1)}, bf16[256,512]{1,0:T(8,128)(2,1)S(1)}, u32[]{:S(2)}, u32[]{:S(2)}) %collective-permute-start.11) | collective-permute-done | bytes 262176 | tf_op jit(solution)/shard_map/ppermute | solution.py:18
  175.4 2.6 collective-permute-start.15
  178.0 13.0 %all-gather.5.cloned.1.call-done.weight_hbm = bf16[2048,2304]{1,0:T(8,128)(2,1)} async-done(((bf16[128,2304]{1,0:T(8,128)(2,1)}), bf16[2048,2304]{1,0:T(8,128)(2,1)}) %all-gather.5.cloned.1.call-update) | async-done | bytes 9437200 | tf_op jit(solution)/shard_map/all_gather | solution.py:464
  191.0 2.6 project_kv.3
  199.2 5.0 %all-to-all-start.3 = ((bf16[16,256,128]{2,1,0:T(8,128)(2,1)}), bf16[16,256,128]{2,1,0:T(8,128)(2,1)S(1)}, u32[]{:S(2)}, u32[]{:S(2)}) async-start(bf16[16,256,128]{2,1,0:T(8,128)(2,1)} %get-tuple-element.78), calls=%async_computation.3 | async-start | bytes 2097152 | tf_op jit(solution)/shard_map/all_to_all | solution.py:515
  204.2 3.2 %project_q.3 = (f32[256,512]{1,0:T(8,128)S(1)}, f32[256,512]{1,0:T(8,128)S(1)}) custom-call(s32[3]{0:T(128)S(1)} %copy-done.5, bf16[256,512]{1,0:T(8,128)(2,1)S(1)} %add_convert_fusion.2.own_ref.first_ref, bf16[256,512]{1,0:T(8,128)(2,1)S(1)} %collective-permute-done.14.from_one, bf16[256,512]{1,0:T(8,128)(2,1)S(1)} %collective-permute-done.15.from_two, ...), custom_call_target="tpu_custom_call" | custom-call | flops 1073741824 | bytes 5242880 | tf_op jit(solution)/shard_map/project_q/pallas_call | solution.py:275
  208.1 12.4 %all-to-all-done.3 = bf16[16,256,128]{2,1,0:T(8,128)(2,1)S(1)} async-done(((bf16[16,256,128]{2,1,0:T(8,128)(2,1)}), bf16[16,256,128]{2,1,0:T(8,128)(2,1)S(1)}, u32[]{:S(2)}, u32[]{:S(2)}) %all-to-all-start.3) | async-done | bytes 1048608 | tf_op jit(solution)/shard_map/all_to_all | solution.py:515
  225.3 7.6 %attention.3.mine_ref = bf16[256,512]{1,0:T(8,128)(2,1)} custom-call(s32[4]{0:T(128)} %pad_add_fusion.1.scalars, bf16[256,512]{1,0:T(8,128)(2,1)} %bitcast.68, bf16[16,4,64,128]{3,2,1,0:T(8,128)(2,1)} %bitcast.59, bf16[16,4,64,128]{3,2,1,0:T(8,128)(2,1)} %collective-permute-done.19.other_ref), custom_call_target="tpu_custom_call" | custom-call | flops 134217728 | bytes 2621440 | tf_op jit(solution)/shard_map/attention/pallas_call | solution.py:135
  235.6 3.7 %project_out.3 = (bf16[256,512]{1,0:T(8,128)(2,1)S(1)}, bf16[256,512]{1,0:T(8,128)(2,1)S(1)}, bf16[256,512]{1,0:T(8,128)(2,1)S(1)}, bf16[256,512]{1,0:T(8,128)(2,1)S(1)}) custom-call(s32[3]{0:T(128)S(1)} %copy-done.5, bf16[256,512]{1,0:T(8,128)(2,1)S(1)} %copy-done.1, bf16[256,512]{1,0:T(8,128)(2,1)S(1)} %collective-permute-done.20.other_ref, ...), custom_call_target="tpu_custom_call" | custom-call | flops 1073741824 | bytes 5242880 | tf_op jit(solution)/shard_map/project_out/pallas_call | solution.py:360
  239.3 3.0 %collective-permute-start.21 = (bf16[256,512]{1,0:T(8,128)(2,1)S(1)}, bf16[256,512]{1,0:T(8,128)(2,1)S(1)}, u32[]{:S(2)}, u32[]{:S(2)}) collective-permute-start(bf16[256,512]{1,0:T(8,128)(2,1)S(1)} %get-tuple-element.80), channel_id=1, source_target_pairs={{0,2},{1,3},{2,0},{3,1},{4,6},{5,7},{6,4},{7,5},{8,10},{9,11},{10,... | collective-permute-start | bytes 786440 | tf_op jit(solution)/shard_map/ppermute | solution.py:18
  242.6 2.3 collective-permute-start.23
  245.9 2.8 %collective-permute-done.21 = bf16[256,512]{1,0:T(8,128)(2,1)S(1)} collective-permute-done((bf16[256,512]{1,0:T(8,128)(2,1)S(1)}, bf16[256,512]{1,0:T(8,128)(2,1)S(1)}, u32[]{:S(2)}, u32[]{:S(2)}) %collective-permute-start.21) | collective-permute-done | bytes 262176 | tf_op jit(solution)/shard_map/ppermute | solution.py:18
  248.7 6.0 %collective-permute-done.22 = bf16[256,512]{1,0:T(8,128)(2,1)S(1)} collective-permute-done((bf16[256,512]{1,0:T(8,128)(2,1)S(1)}, bf16[256,512]{1,0:T(8,128)(2,1)S(1)}, u32[]{:S(2)}, u32[]{:S(2)}) %collective-permute-start.22) | collective-permute-done | bytes 262176 | tf_op jit(solution)/shard_map/ppermute | solution.py:18
  (146 shorter events, 58.1 us)
Async XLA Ops:
  6.5 96.7 %all-gather.3.cloned.1.call-start = ((), (), s32[]{:S(2)}) async-start(), calls=%async_computation.4 | async-start | bytes 10027008 | tf_op jit(solution)/shard_map/all_gather | solution.py:464
  9.2 3.1 %collective-permute-start.5 = (bf16[128,2304]{1,0:T(8,128)(2,1)S(1)}, bf16[128,2304]{1,0:T(8,128)(2,1)S(1)}, u32[]{:S(2)}, u32[]{:S(2)}) collective-permute-start(bf16[128,2304]{1,0:T(8,128)(2,1)S(1)} %broadcast_select_fusion.2), channel_id=1, source_target_pairs={{0,64},{64,0},{1,65},{65,1},{2,66},{66,2},{3,67},{67,3},{4,68},{68... | collective-permute-start | bytes 1769480 | tf_op jit(solution)/shard_map/ppermute | solution.py:22
  13.6 177.4 %all-gather.5.cloned.1.call-start = ((), (), s32[]{:S(2)}) async-start(), calls=%async_computation.5 | async-start | bytes 10027008 | tf_op jit(solution)/shard_map/all_gather | solution.py:464
  20.4 2.5 collective-permute-start
  26.0 30.3 %all-to-all-start = ((bf16[64,16,512]{2,1,0:T(8,128)(2,1)}), bf16[64,16,512]{2,1,0:T(8,128)(2,1)S(1)}, u32[]{:S(2)}, u32[]{:S(2)}) async-start(bf16[64,16,512]{2,1,0:T(8,128)(2,1)} %merger_outer.1), calls=%async_computation | async-start | bytes 2097152 | tf_op jit(solution)/shard_map/all_to_all | solution.py:477
  57.2 14.9 %all-to-all-start.1 = ((bf16[16,16,512]{2,1,0:T(8,128)(2,1)}), bf16[16,16,512]{2,1,0:T(8,128)(2,1)S(1)}, u32[]{:S(2)}, u32[]{:S(2)}) async-start(bf16[16,16,512]{2,1,0:T(8,128)(2,1)} %broadcast_in_dim.42), calls=%async_computation.1 | async-start | bytes 524288 | tf_op jit(solution)/shard_map/all_to_all | solution.py:57
  72.4 10.5 %collective-permute-start.1 = (bf16[256,512]{1,0:T(8,128)(2,1)S(1)}, bf16[256,512]{1,0:T(8,128)(2,1)S(1)}, u32[]{:S(2)}, u32[]{:S(2)}) collective-permute-start(bf16[256,512]{1,0:T(8,128)(2,1)S(1)} %broadcast_select_fusion.4.own_ref), channel_id=1, source_target_pairs={{0,1},{1,2},{2,3},{3,0},{4,5},{5,6},{6,7},{7,4},{8,9},{9,10},{10,1... | collective-permute-start | bytes 786440 | tf_op jit(solution)/shard_map/ppermute | solution.py:18
  72.8 10.1 %collective-permute-start.2 = (bf16[256,512]{1,0:T(8,128)(2,1)S(1)}, bf16[256,512]{1,0:T(8,128)(2,1)S(1)}, u32[]{:S(2)}, u32[]{:S(2)}) collective-permute-start(bf16[256,512]{1,0:T(8,128)(2,1)S(1)} %broadcast_select_fusion.4.own_ref), channel_id=1, source_target_pairs={{0,2},{1,3},{2,0},{3,1},{4,6},{5,7},{6,4},{7,5},{8,10},{9,11},{10,... | collective-permute-start | bytes 786440 | tf_op jit(solution)/shard_map/ppermute | solution.py:18
  73.8 12.8 %collective-permute-start.3 = (bf16[256,512]{1,0:T(8,128)(2,1)S(1)}, bf16[256,512]{1,0:T(8,128)(2,1)S(1)}, u32[]{:S(2)}, u32[]{:S(2)}) collective-permute-start(bf16[256,512]{1,0:T(8,128)(2,1)S(1)} %broadcast_select_fusion.4.own_ref), channel_id=1, source_target_pairs={{0,3},{1,0},{2,1},{3,2},{4,7},{5,4},{6,5},{7,6},{8,11},{9,8},{10,9... | collective-permute-start | bytes 786440 | tf_op jit(solution)/shard_map/ppermute | solution.py:18
  75.6 4.1 %collective-permute-start.4 = (f32[16,128]{1,0:T(8,128)S(1)}, f32[16,128]{1,0:T(8,128)S(1)}, u32[]{:S(2)}, u32[]{:S(2)}) collective-permute-start(f32[16,128]{1,0:T(8,128)S(1)} %select_bitcast_fusion), channel_id=1, source_target_pairs={{0,64},{64,0},{1,65},{65,1},{2,66},{66,2},{3,67},{67,3},{4,68},{68... | collective-permute-start | bytes 24584 | tf_op jit(solution)/shard_map/ppermute | solution.py:22
  106.6 1.8 collective-permute-start.6
  111.4 28.7 %all-to-all-start.2 = ((bf16[16,256,128]{2,1,0:T(8,128)(2,1)}), bf16[16,256,128]{2,1,0:T(8,128)(2,1)S(1)}, u32[]{:S(2)}, u32[]{:S(2)}) async-start(bf16[16,256,128]{2,1,0:T(8,128)(2,1)} %get-tuple-element.63), calls=%async_computation.2 | async-start | bytes 2097152 | tf_op jit(solution)/shard_map/all_to_all | solution.py:515
  119.6 22.4 %collective-permute-start.7 = (f32[256,512]{1,0:T(8,128)S(1)}, f32[256,512]{1,0:T(8,128)S(1)}, u32[]{:S(2)}, u32[]{:S(2)}) collective-permute-start(f32[256,512]{1,0:T(8,128)S(1)} %get-tuple-element.59), channel_id=1, source_target_pairs={{0,64},{64,0},{1,65},{65,1},{2,66},{66,2},{3,67},{67,3},{4,68},{68... | collective-permute-start | bytes 1572872 | tf_op jit(solution)/shard_map/ppermute | solution.py:22
  140.1 4.5 %collective-permute-start.8 = (bf16[16,4,64,128]{3,2,1,0:T(8,128)(2,1)S(1)}, bf16[16,4,64,128]{3,2,1,0:T(8,128)(2,1)}, u32[]{:S(2)}, u32[]{:S(2)}) collective-permute-start(bf16[16,4,64,128]{3,2,1,0:T(8,128)(2,1)S(1)} %bitcast.60), channel_id=1, source_target_pairs={{0,64},{64,0},{1,65},{65,1},{2,66},{66,2},{3,67},{67,3},{4,68},{68... | collective-permute-start | bytes 3145736 | tf_op jit(solution)/shard_map/ppermute | solution.py:22
  152.0 1.7 collective-permute-start.9
  158.4 9.4 %collective-permute-start.10 = (bf16[256,512]{1,0:T(8,128)(2,1)S(1)}, bf16[256,512]{1,0:T(8,128)(2,1)S(1)}, u32[]{:S(2)}, u32[]{:S(2)}) collective-permute-start(bf16[256,512]{1,0:T(8,128)(2,1)S(1)} %get-tuple-element.65), channel_id=1, source_target_pairs={{0,2},{1,3},{2,0},{3,1},{4,6},{5,7},{6,4},{7,5},{8,10},{9,11},{10,... | collective-permute-start | bytes 786440 | tf_op jit(solution)/shard_map/ppermute | solution.py:18
  161.3 12.6 %collective-permute-start.11 = (bf16[256,512]{1,0:T(8,128)(2,1)S(1)}, bf16[256,512]{1,0:T(8,128)(2,1)S(1)}, u32[]{:S(2)}, u32[]{:S(2)}) collective-permute-start(bf16[256,512]{1,0:T(8,128)(2,1)S(1)} %get-tuple-element.66), channel_id=1, source_target_pairs={{0,1},{1,2},{2,3},{3,0},{4,5},{5,6},{6,7},{7,4},{8,9},{9,10},{10,1... | collective-permute-start | bytes 786440 | tf_op jit(solution)/shard_map/ppermute | solution.py:18
  161.7 12.2 %collective-permute-start.12 = (bf16[256,512]{1,0:T(8,128)(2,1)S(1)}, bf16[256,512]{1,0:T(8,128)(2,1)S(1)}, u32[]{:S(2)}, u32[]{:S(2)}) collective-permute-start(bf16[256,512]{1,0:T(8,128)(2,1)S(1)} %get-tuple-element.67), channel_id=1, source_target_pairs={{0,3},{1,0},{2,1},{3,2},{4,7},{5,4},{6,5},{7,6},{8,11},{9,8},{10,9... | collective-permute-start | bytes 786440 | tf_op jit(solution)/shard_map/ppermute | solution.py:18
  174.1 80.6 %copy-start = (bf16[256,512]{1,0:T(8,128)(2,1)}, bf16[256,512]{1,0:T(8,128)(2,1)S(1)}, u32[]{:S(2)}) copy-start(bf16[256,512]{1,0:T(8,128)(2,1)S(1)} %add_convert_fusion.2.own_ref.first_ref) | copy-start | bytes 786436
  174.1 16.9 %collective-permute-start.14 = (bf16[256,512]{1,0:T(8,128)(2,1)S(1)}, bf16[256,512]{1,0:T(8,128)(2,1)S(1)}, u32[]{:S(2)}, u32[]{:S(2)}) collective-permute-start(bf16[256,512]{1,0:T(8,128)(2,1)S(1)} %add_convert_fusion.2.own_ref.first_ref), channel_id=1, source_target_pairs={{0,1},{1,2},{2,3},{3,0},{4,5},{5,6},{6,7},{7,4},{8,9},{9,10},{10,1... | collective-permute-start | bytes 786440 | tf_op jit(solution)/shard_map/ppermute | solution.py:18
  175.4 15.6 %collective-permute-start.15 = (bf16[256,512]{1,0:T(8,128)(2,1)S(1)}, bf16[256,512]{1,0:T(8,128)(2,1)S(1)}, u32[]{:S(2)}, u32[]{:S(2)}) collective-permute-start(bf16[256,512]{1,0:T(8,128)(2,1)S(1)} %add_convert_fusion.2.own_ref.first_ref), channel_id=1, source_target_pairs={{0,2},{1,3},{2,0},{3,1},{4,6},{5,7},{6,4},{7,5},{8,10},{9,11},{10,... | collective-permute-start | bytes 786440 | tf_op jit(solution)/shard_map/ppermute | solution.py:18
  178.0 13.0 %collective-permute-start.16 = (bf16[256,512]{1,0:T(8,128)(2,1)S(1)}, bf16[256,512]{1,0:T(8,128)(2,1)S(1)}, u32[]{:S(2)}, u32[]{:S(2)}) collective-permute-start(bf16[256,512]{1,0:T(8,128)(2,1)S(1)} %add_convert_fusion.2.own_ref.first_ref), channel_id=1, source_target_pairs={{0,3},{1,0},{2,1},{3,2},{4,7},{5,4},{6,5},{7,6},{8,11},{9,8},{10,9... | collective-permute-start | bytes 786440 | tf_op jit(solution)/shard_map/ppermute | solution.py:18
  194.4 1.8 collective-permute-start.17
  199.2 21.3 %all-to-all-start.3 = ((bf16[16,256,128]{2,1,0:T(8,128)(2,1)}), bf16[16,256,128]{2,1,0:T(8,128)(2,1)S(1)}, u32[]{:S(2)}, u32[]{:S(2)}) async-start(bf16[16,256,128]{2,1,0:T(8,128)(2,1)} %get-tuple-element.78), calls=%async_computation.3 | async-start | bytes 2097152 | tf_op jit(solution)/shard_map/all_to_all | solution.py:515
  207.4 15.2 %collective-permute-start.18 = (f32[256,512]{1,0:T(8,128)S(1)}, f32[256,512]{1,0:T(8,128)S(1)}, u32[]{:S(2)}, u32[]{:S(2)}) collective-permute-start(f32[256,512]{1,0:T(8,128)S(1)} %get-tuple-element.76), channel_id=1, source_target_pairs={{0,64},{64,0},{1,65},{65,1},{2,66},{66,2},{3,67},{67,3},{4,68},{68... | collective-permute-start | bytes 1572872 | tf_op jit(solution)/shard_map/ppermute | solution.py:22
  220.5 4.8 %collective-permute-start.19 = (bf16[16,4,64,128]{3,2,1,0:T(8,128)(2,1)S(1)}, bf16[16,4,64,128]{3,2,1,0:T(8,128)(2,1)}, u32[]{:S(2)}, u32[]{:S(2)}) collective-permute-start(bf16[16,4,64,128]{3,2,1,0:T(8,128)(2,1)S(1)} %bitcast.58), channel_id=1, source_target_pairs={{0,64},{64,0},{1,65},{65,1},{2,66},{66,2},{3,67},{67,3},{4,68},{68... | collective-permute-start | bytes 3145736 | tf_op jit(solution)/shard_map/ppermute | solution.py:22
  232.9 1.7 collective-permute-start.20
  239.3 9.4 %collective-permute-start.21 = (bf16[256,512]{1,0:T(8,128)(2,1)S(1)}, bf16[256,512]{1,0:T(8,128)(2,1)S(1)}, u32[]{:S(2)}, u32[]{:S(2)}) collective-permute-start(bf16[256,512]{1,0:T(8,128)(2,1)S(1)} %get-tuple-element.80), channel_id=1, source_target_pairs={{0,2},{1,3},{2,0},{3,1},{4,6},{5,7},{6,4},{7,5},{8,10},{9,11},{10,... | collective-permute-start | bytes 786440 | tf_op jit(solution)/shard_map/ppermute | solution.py:18
  242.2 12.5 %collective-permute-start.22 = (bf16[256,512]{1,0:T(8,128)(2,1)S(1)}, bf16[256,512]{1,0:T(8,128)(2,1)S(1)}, u32[]{:S(2)}, u32[]{:S(2)}) collective-permute-start(bf16[256,512]{1,0:T(8,128)(2,1)S(1)} %get-tuple-element.81), channel_id=1, source_target_pairs={{0,1},{1,2},{2,3},{3,0},{4,5},{5,6},{6,7},{7,4},{8,9},{9,10},{10,1... | collective-permute-start | bytes 786440 | tf_op jit(solution)/shard_map/ppermute | solution.py:18
  242.6 12.1 %collective-permute-start.23 = (bf16[256,512]{1,0:T(8,128)(2,1)S(1)}, bf16[256,512]{1,0:T(8,128)(2,1)S(1)}, u32[]{:S(2)}, u32[]{:S(2)}) collective-permute-start(bf16[256,512]{1,0:T(8,128)(2,1)S(1)} %get-tuple-element.82), channel_id=1, source_target_pairs={{0,3},{1,0},{2,1},{3,2},{4,7},{5,4},{6,5},{7,6},{8,11},{9,8},{10,9... | collective-permute-start | bytes 786440 | tf_op jit(solution)/shard_map/ppermute | solution.py:18
  244.9 10.9 %collective-permute-start.13 = (bf16[256,512]{1,0:T(8,128)(2,1)S(1)}, bf16[256,512]{1,0:T(8,128)(2,1)S(1)}, u32[]{:S(2)}, u32[]{:S(2)}) collective-permute-start(bf16[256,512]{1,0:T(8,128)(2,1)S(1)} %add_convert_fusion.2.own_ref.first_ref), channel_id=1, source_target_pairs={{0,64},{64,0},{1,65},{65,1},{2,66},{66,2},{3,67},{67,3},{4,68},{68... | collective-permute-start | bytes 786440 | tf_op jit(solution)/shard_map/ppermute | solution.py:22
  254.9 2.0 collective-permute-start.24
  (22 other events, 114.2 us)
Sparse Core Ops, SparseCore 0:
  13.8 89.4 all-gather.2
  105.4 85.5 all-gather.4

commit v7 on v5

--- a/solution.py
+++ b/solution.py
@@ -177,38 +177,37 @@
     )(patches, merge_gain.reshape(1, -1), merge_first)
 
 
-def merger_outer_kernel(place, mine_ref, other_ref, weight_ref, out_ref):
+def merger_outer_kernel(place, mine_ref, other_ref, weight_ref, *out_refs):
     section = place[0]
-    pieces, share, depth = out_ref.shape
     tokens = mine_ref.shape[0]
-    runs = weight_ref.shape[1] // (2 * lane)
-    slices = runs * lane // depth
-    weight = jnp.concatenate(
-        [
-            weight_ref[:, pl.ds(pl.multiple_of((2 * run + section) * lane, lane), lane)]
-            for run in range(runs)
-        ],
-        axis=1,
+    runs = out_refs[0].shape[1] // lane
+    for by, out_ref in enumerate(out_refs):
+        piece = (place[2] + by) % len(out_refs)
+        weight = jnp.concatenate(
+            [
+                weight_ref[
+                    :, pl.ds(pl.multiple_of((2 * (piece * runs + run) + section) * lane, lane), lane)
+                ]
+                for run in range(runs)
+            ],
+            axis=1,
+        )
+        for inner_ref, core in ((mine_ref, section), (other_ref, 1 - section)):
+            result = jnp.dot(inner_ref[...], weight, preferred_element_type=jnp.float32)
+            at = pl.multiple_of(core * tokens, tokens)
+            out_ref[pl.ds(at, tokens), :] = result.astype(out_ref.dtype)
+
+
+def merger_outer(place, mine, other, merge_second, n_mp):
+    whole = pl.BlockSpec(memory_space=pltpu.VMEM)
+    shape = jax.ShapeDtypeStruct(
+        (2 * mine.shape[0], merge_second.shape[1] // 2 // n_mp), jnp.bfloat16
     )
-    for inner_ref, core in ((mine_ref, section), (other_ref, 1 - section)):
-        result = jnp.dot(inner_ref[...], weight, preferred_element_type=jnp.float32)
-        result = result.astype(out_ref.dtype)
-        for owner in range(tokens // share):
-            for piece in range(slices):
-                out_ref[(core * (tokens // share) + owner) * slices + piece] = result[
-                    owner * share : (owner + 1) * share, piece * depth : (piece + 1) * depth
-                ]
-
-
-def merger_outer(place, mine, other, merge_second, n_blk, n_mp):
-    whole = pl.BlockSpec(memory_space=pltpu.VMEM)
-    share = 2 * mine.shape[0] // n_blk
-    depth = merge_second.shape[1] // 2 // n_mp
     return pl.pallas_call(
         merger_outer_kernel,
-        out_shape=jax.ShapeDtypeStruct((n_blk * n_mp, share, depth), jnp.bfloat16),
+        out_shape=[shape] * n_mp,
         in_specs=[pl.BlockSpec(memory_space=pltpu.SMEM), whole, whole, whole],
-        out_specs=whole,
+        out_specs=[whole] * n_mp,
         name="merger_outer",
     )(place, mine, other, merge_second)
 
@@ -432,12 +431,10 @@
     weight_keep = jnp.where(first_core, for_first, for_second)
     weight_other = swapped(jnp.where(first_core, for_second, for_first))
     keyval_width = 2 * head_size
-    keyval_shards, weight_full = [], []
+    weight_full = []
     for home in range(layers):
         mine = jnp.where(section_index == home, weight_keep, weight_other)
-        keyval_shards.append(mine[:, :keyval_width])
-        sent_off = mine if home == 0 else mine[:, keyval_width:]
-        weight_full.append(lax.all_gather(sent_off, "blk", axis=0, tiled=True))
+        weight_full.append(lax.all_gather(mine, "blk", axis=0, tiled=True))
     gain_half = norm_gain[0].reshape(-1, 2, lane)
     gain_keep = jnp.where(first_core, gain_half[:, 0], gain_half[:, 1])
     gain_send = jnp.where(first_core, gain_half[:, 1], gain_half[:, 0])
@@ -449,8 +446,13 @@
 
     inner = merger_inner(patches, merge_gain, merge_first)
     place = jnp.stack([section_index, cycle_index, model_index]).astype(jnp.int32)
-    merged_pieces = merger_outer(place, inner, swapped(inner), merge_second, n_blk, n_mp)
-    merged_terms = lax.all_to_all(merged_pieces, ("blk", "mp"), 0, 0, tiled=True)
+    own, *terms = merger_outer(place, inner, swapped(inner), merge_second, n_mp)
+    total = own.astype(jnp.float32)
+    for part in [moved(terms[by - 1], "mp", by) for by in (2, 1, 3)]:
+        total = total + part.astype(jnp.float32)
+    merged_terms = lax.all_to_all(
+        total.astype(jnp.bfloat16).reshape(n_blk, -1, total.shape[1]), "blk", 0, 0, tiled=True
+    )
 
     row_where = (
         jnp.arange(blocks)[:, None] * block_len
@@ -463,34 +465,31 @@
     has_visual = jnp.max(is_visual, axis=1, keepdims=True)
     text_rows = my_half(text_embeds.reshape(rows, slice_width), 1, section_index)
     cosine, sine = rope_tables(row_where, head_size)
-    merged_terms, scalars, is_visual, has_visual, text_rows, cosine, sine = (
-        lax.optimization_barrier(
-            (merged_terms, scalars, is_visual, has_visual, text_rows, cosine, sine)
-        )
-    )
+    keyval_cosine = jnp.where(first_core, jnp.concatenate([cosine, cosine], axis=1), 1.0)
+    keyval_sine = jnp.where(first_core, jnp.concatenate([-sine, sine], axis=1), 0.0)
+    early = (scalars, is_visual, has_visual, text_rows, cosine, sine, keyval_cosine, keyval_sine)
+    merged_terms, early = lax.optimization_barrier((merged_terms, early))
+    scalars, is_visual, has_visual, text_rows, cosine, sine, keyval_cosine, keyval_sine = early
     merged_mine = jnp.sum(merged_terms.astype(jnp.float32), axis=0).astype(jnp.bfloat16)
     merged = spread(merged_mine).reshape(n_blk * merged_mine.shape[0], -1)
     picked = jnp.dot(is_visual, merged, preferred_element_type=jnp.float32).astype(jnp.bfloat16)
     state = jnp.where(has_visual > 0, picked, text_rows)
 
-    keyval_cosine = jnp.where(first_core, cosine, 1.0)
-    keyval_sine = jnp.where(first_core, sine, 0.0)
 
     results = []
     for layer_index in range(layers):
         parts = [state] + [moved(state, "mp", by) for by in (1, 2, 3)]
         gain = gain_layers[layer_index]
         weight = weight_full[layer_index]
-        if layer_index == 0:
-            keyval_from, query_at = weight, keyval_width
-        else:
-            keyval_from, query_at = keyval_weight_full.reshape(-1, keyval_width), 0
-        kept, sent = project_in(place, parts, gain, keyval_from, 0, keyval_width, True)
+        kept, sent = project_in(place, parts, gain, weight, 0, keyval_width, True)
         total = kept + swapped(sent)
         shrink = lax.rsqrt(total[:, head_size : head_size + 1] / (n_mp * slice_width) + epsilon)
-        keyval = rotate(total[:, :head_size] * shrink, keyval_cosine, keyval_sine).astype(jnp.bfloat16)
+        keyval = total[:, :head_size] * shrink
+        half = head_size // 2
+        turned = jnp.concatenate([keyval[:, half:], keyval[:, :half]], axis=1)
+        keyval = (keyval * keyval_cosine + turned * keyval_sine).astype(jnp.bfloat16)
         keyval, parts = lax.optimization_barrier((keyval, parts))
-        kept, sent = project_in(place, parts, gain, weight, query_at, 2 * heads_half, False)
+        kept, sent = project_in(place, parts, gain, weight, keyval_width, 2 * heads_half, False)
         query = ((kept + swapped(sent)) * shrink).reshape(rows, -1, head_size)
         query = rotate(query, cosine[:, None, :], sine[:, None, :])
         query = query.astype(jnp.bfloat16).reshape(rows, heads_half)
@@ -498,9 +497,6 @@
         attended = attention(scalars, query, gathered, swapped(gathered))
         attended_other = swapped(attended)
         own, *terms = project_out(place, attended, attended_other, weight)
-        if layer_index + 1 < layers:
-            own, shard = lax.optimization_barrier((own, keyval_shards[layer_index + 1]))
-            keyval_weight_full = spread(shard)
         arrived = [moved(terms[by - 1], "mp", by) for by in (2, 1, 3)]
         total = state.astype(jnp.float32) + own.astype(jnp.float32)
         for part in arrived:

time: 267 us -> 259 us (0.970)
  waiting for transfers between devices: 121 us -> 112 us
  Pallas kernels: 41.8 us -> 45.2 us
    ppermute x12 -> x15, starting transfers between devices: 17.1 us -> 26 us  [moved(): lax.ppermute(value, axis, [(i, (i + by) % size) for i in range(size)])]
    ppermute x12 -> x15, waiting for transfers between devices: 38.5 us -> 32.1 us  [moved(): lax.ppermute(value, axis, [(i, (i + by) % size) for i in range(size)])]
    all_to_all x1, waiting for transfers between devices: 15.1 us -> 8.86 us  [local(): lax.all_to_all(total.astype(jnp.bfloat16).reshape(n_blk, -1, total.shape[...]
    all_to_all x4 -> x3, starting transfers between devices: 19.7 us -> 13.5 us  [spread(): return lax.all_to_all(copies, 'blk', 0, 0, tiled=True)]
    all_to_all x1, starting transfers between devices: 11.4 us -> 6.88 us  [local(): lax.all_to_all(total.astype(jnp.bfloat16).reshape(n_blk, -1, total.shape[...]
    all_gather x2, waiting for transfers between devices: 16.5 us -> 19.5 us  [local(): weight_full.append(lax.all_gather(mine, 'blk', axis=0, tiled=True))]
    pallas_call x2, Pallas kernels: 14.9 us -> 17.8 us  [attention(): pl.pallas_call(functools.partial(attention_kernel, chunk_runs=mine.shape[...]
    all_to_all x4 -> x3, waiting for transfers between devices: 41.5 us -> 41.4 us  [spread(): return lax.all_to_all(copies, 'blk', 0, 0, tiled=True)]
  transfers between devices with their start and end apart: 32 -> 34, of which waited for: 22 -> 24; matrix products, arithmetic and copies ran while one was open for 7% -> 6% of each run, Pallas kernels for 11% -> 11%
where the time goes in v7:
time: 259 us
  waiting for transfers between devices  112 us (43%)
  starting transfers between devices  63.3 us (24%)
  Pallas kernels  45.2 us (17%)
  local copies, waits for them, and re-layouts  14.4 us (6%)
  between operations  13.9 us (5%)
  other arithmetic  9.97 us (4%)
    all_to_all x3, waiting for transfers between devices, spread(): return lax.all_to_all(copies, 'blk', 0, 0, tiled=True)  41.4 us
    ppermute x15, waiting for transfers between devices, moved(): lax.ppermute(value, axis, [(i, (i + by) % size) for i in range(size)])  32.1 us
    ppermute x15, starting transfers between devices, moved(): lax.ppermute(value, axis, [(i, (i + by) % size) for i in range(size)])  26 us
    all_gather x2, waiting for transfers between devices, local(): weight_full.append(lax.all_gather(mine, 'blk', axis=0, tiled=True))  19.5 us
    pallas_call x2, Pallas kernels, attention(): pl.pallas_call(functools.partial(attention_kernel, chunk_runs=mine.shape[...  17.8 us
    ppermute x13, starting transfers between devices, swapped(): return lax.ppermute(value, 'section', [(0, 1), (1, 0)])  16.9 us
    all_to_all x3, starting transfers between devices, spread(): return lax.all_to_all(copies, 'blk', 0, 0, tiled=True)  13.5 us
    pallas_call x4, Pallas kernels, project_in(): pl.pallas_call(functools.partial(project_in_kernel, at=at), out_shape=(ou...  12 us
  transfers between devices with their start and end apart: 34, of which 24 were waited for; matrix products, arithmetic and copies ran while one was open for 6% of the time, Pallas kernels for 11%

profile of v7, /device:TPU:1, one launch (start us, length us, event | category | flops | bytes accessed | tf_op | source)
XLA Modules:
  0.0 259.2 jit_solution(12343185060597781094)
XLA Ops:
  16.8 3.6 %merger_inner.1.mine_ref = bf16[128,80]{1,0:T(8,128)(2,1)} custom-call(bf16[128,5120]{1,0:T(8,128)(2,1)} %patches_ref.1, f32[1,1280]{1,0:T(1,128)} %reshape.92.gain_ref, bf16[5120,80]{1,0:T(8,128)(2,1)} %copy.24.weight_ref), custom_call_target="tpu_custom_call" | custom-call | flops 104857600 | bytes 2129920 | tf_op jit(solution)/shard_map/merger_inner/pallas_call | solution.py:166
  26.5 3.7 %collective-permute-start.1 = (bf16[256,512]{1,0:T(8,128)(2,1)}, bf16[256,512]{1,0:T(8,128)(2,1)S(1)}, u32[]{:S(2)}, u32[]{:S(2)}) collective-permute-start(bf16[256,512]{1,0:T(8,128)(2,1)} %get-tuple-element.45), channel_id=1, source_target_pairs={{0,2},{1,3},{2,0},{3,1},{4,6},{5,7},{6,4},{7,5},{8,10},{9,11},{10,... | collective-permute-start | bytes 786440 | tf_op jit(solution)/shard_map/ppermute | solution.py:18
  33.8 3.2 %collective-permute-done.1 = bf16[256,512]{1,0:T(8,128)(2,1)S(1)} collective-permute-done((bf16[256,512]{1,0:T(8,128)(2,1)}, bf16[256,512]{1,0:T(8,128)(2,1)S(1)}, u32[]{:S(2)}, u32[]{:S(2)}) %collective-permute-start.1) | collective-permute-done | bytes 262176 | tf_op jit(solution)/shard_map/ppermute | solution.py:18
  37.0 5.8 %collective-permute-done.2 = bf16[256,512]{1,0:T(8,128)(2,1)S(1)} collective-permute-done((bf16[256,512]{1,0:T(8,128)(2,1)}, bf16[256,512]{1,0:T(8,128)(2,1)S(1)}, u32[]{:S(2)}, u32[]{:S(2)}) %collective-permute-start.2) | collective-permute-done | bytes 262176 | tf_op jit(solution)/shard_map/ppermute | solution.py:18
  44.0 6.9 %all-to-all-start = ((bf16[16,16,512]{2,1,0:T(8,128)(2,1)}), bf16[16,16,512]{2,1,0:T(8,128)(2,1)S(1)}, u32[]{:S(2)}, u32[]{:S(2)}) async-start(bf16[16,16,512]{2,1,0:T(8,128)(2,1)} %bitcast.3), calls=%async_computation | async-start | bytes 524288 | tf_op jit(solution)/shard_map/all_to_all | solution.py:453
  53.0 8.9 %all-to-all-done = bf16[16,16,512]{2,1,0:T(8,128)(2,1)S(1)} async-done(((bf16[16,16,512]{2,1,0:T(8,128)(2,1)}), bf16[16,16,512]{2,1,0:T(8,128)(2,1)S(1)}, u32[]{:S(2)}, u32[]{:S(2)}) %all-to-all-start) | async-done | bytes 262176 | tf_op jit(solution)/shard_map/all_to_all | solution.py:453
  62.6 3.5 %all-to-all-start.1 = ((bf16[16,16,512]{2,1,0:T(8,128)(2,1)}), bf16[16,16,512]{2,1,0:T(8,128)(2,1)S(1)}, u32[]{:S(2)}, u32[]{:S(2)}) async-start(bf16[16,16,512]{2,1,0:T(8,128)(2,1)} %broadcast_in_dim.52), calls=%async_computation.1 | async-start | bytes 524288 | tf_op jit(solution)/shard_map/all_to_all | solution.py:57
  66.2 10.6 %all-to-all-done.1 = bf16[16,16,512]{2,1,0:T(8,128)(2,1)S(1)} async-done(((bf16[16,16,512]{2,1,0:T(8,128)(2,1)}), bf16[16,16,512]{2,1,0:T(8,128)(2,1)S(1)}, u32[]{:S(2)}, u32[]{:S(2)}) %all-to-all-start.1) | async-done | bytes 262176 | tf_op jit(solution)/shard_map/all_to_all | solution.py:57
  77.9 3.6 %collective-permute-start.5 = (bf16[256,512]{1,0:T(8,128)(2,1)S(1)}, bf16[256,512]{1,0:T(8,128)(2,1)S(1)}, u32[]{:S(2)}, u32[]{:S(2)}) collective-permute-start(bf16[256,512]{1,0:T(8,128)(2,1)S(1)} %fusion.own_ref), channel_id=1, source_target_pairs={{0,2},{1,3},{2,0},{3,1},{4,6},{5,7},{6,4},{7,5},{8,10},{9,11},{10,... | collective-permute-start | bytes 786440 | tf_op jit(solution)/shard_map/ppermute | solution.py:18
  81.5 4.0 %collective-permute-start.7 = (f32[16,128]{1,0:T(8,128)S(1)}, f32[16,128]{1,0:T(8,128)S(1)}, u32[]{:S(2)}, u32[]{:S(2)}) collective-permute-start(f32[16,128]{1,0:T(8,128)S(1)} %select_bitcast_fusion), channel_id=1, source_target_pairs={{0,64},{64,0},{1,65},{65,1},{2,66},{66,2},{3,67},{67,3},{4,68},{68... | collective-permute-start | bytes 24584 | tf_op jit(solution)/shard_map/ppermute | solution.py:22
  86.3 3.6 %collective-permute-done.5.from_two = bf16[256,512]{1,0:T(8,128)(2,1)S(1)} collective-permute-done((bf16[256,512]{1,0:T(8,128)(2,1)S(1)}, bf16[256,512]{1,0:T(8,128)(2,1)S(1)}, u32[]{:S(2)}, u32[]{:S(2)}) %collective-permute-start.5) | collective-permute-done | bytes 262176 | tf_op jit(solution)/shard_map/ppermute | solution.py:18
  90.6 6.6 %all-gather.3.cloned.1.call-done.weight_hbm = bf16[2048,2304]{1,0:T(8,128)(2,1)} async-done(((bf16[128,2304]{1,0:T(8,128)(2,1)}), bf16[2048,2304]{1,0:T(8,128)(2,1)}) %all-gather.3.cloned.1.call-update) | async-done | bytes 9437200 | tf_op jit(solution)/shard_map/all_gather | solution.py:437
  97.2 2.6 %project_kv.2 = (f32[256,256]{1,0:T(8,128)S(1)}, f32[256,256]{1,0:T(8,128)S(1)}) custom-call(s32[3]{0:T(128)S(1)} %copy-done.3, bf16[256,512]{1,0:T(8,128)(2,1)S(1)} %fusion.own_ref, bf16[256,512]{1,0:T(8,128)(2,1)S(1)} %collective-permute-done.4.from_one, bf16[256,512]{1,0:T(8,128)(2,1)S(1)} %collective-permute-done.5.from_two, ...), custom_call_target="tpu_custom_call" | custom-call | flops 268435456 | bytes 1572864 | tf_op jit(solution)/shard_map/project_kv/pallas_call | solution.py:274
  103.5 5.0 %all-to-all-start.2 = ((bf16[16,256,128]{2,1,0:T(8,128)(2,1)}), bf16[16,256,128]{2,1,0:T(8,128)(2,1)S(1)}, u32[]{:S(2)}, u32[]{:S(2)}) async-start(bf16[16,256,128]{2,1,0:T(8,128)(2,1)} %broadcast_in_dim.53), calls=%async_computation.2 | async-start | bytes 2097152 | tf_op jit(solution)/shard_map/all_to_all | solution.py:57
  108.5 3.5 %project_q.2 = (f32[256,512]{1,0:T(8,128)S(1)}, f32[256,512]{1,0:T(8,128)S(1)}) custom-call(s32[3]{0:T(128)S(1)} %copy-done.3, bf16[256,512]{1,0:T(8,128)(2,1)S(1)} %fusion.own_ref, bf16[256,512]{1,0:T(8,128)(2,1)S(1)} %collective-permute-done.4.from_one, bf16[256,512]{1,0:T(8,128)(2,1)S(1)} %collective-permute-done.5.from_two, ...), custom_call_target="tpu_custom_call" | custom-call | flops 1073741824 | bytes 5242880 | tf_op jit(solution)/shard_map/project_q/pallas_call | solution.py:274
  112.7 18.4 %all-to-all-done.2 = bf16[16,256,128]{2,1,0:T(8,128)(2,1)S(1)} async-done(((bf16[16,256,128]{2,1,0:T(8,128)(2,1)}), bf16[16,256,128]{2,1,0:T(8,128)(2,1)S(1)}, u32[]{:S(2)}, u32[]{:S(2)}) %all-to-all-start.2) | async-done | bytes 1048608 | tf_op jit(solution)/shard_map/all_to_all | solution.py:57
  131.0 3.1 %collective-permute-start.11 = (bf16[16,4,64,128]{3,2,1,0:T(8,128)(2,1)S(1)}, bf16[16,4,64,128]{3,2,1,0:T(8,128)(2,1)}, u32[]{:S(2)}, u32[]{:S(2)}) collective-permute-start(bf16[16,4,64,128]{3,2,1,0:T(8,128)(2,1)S(1)} %bitcast.61), channel_id=1, source_target_pairs={{0,64},{64,0},{1,65},{65,1},{2,66},{66,2},{3,67},{67,3},{4,68},{68... | collective-permute-start | bytes 3145736 | tf_op jit(solution)/shard_map/ppermute | solution.py:22
  136.6 8.9 %attention.2.mine_ref = bf16[256,512]{1,0:T(8,128)(2,1)} custom-call(s32[4]{0:T(128)} %pad_add_fusion.1.scalars, bf16[256,512]{1,0:T(8,128)(2,1)} %bitcast.70, bf16[16,4,64,128]{3,2,1,0:T(8,128)(2,1)} %bitcast.62, bf16[16,4,64,128]{3,2,1,0:T(8,128)(2,1)} %collective-permute-done.11.other_ref), custom_call_target="tpu_custom_call" | custom-call | flops 134217728 | bytes 2621440 | tf_op jit(solution)/shard_map/attention/pallas_call | solution.py:135
  148.1 3.7 %project_out.2 = (bf16[256,512]{1,0:T(8,128)(2,1)S(1)}, bf16[256,512]{1,0:T(8,128)(2,1)S(1)}, bf16[256,512]{1,0:T(8,128)(2,1)S(1)}, bf16[256,512]{1,0:T(8,128)(2,1)S(1)}) custom-call(s32[3]{0:T(128)S(1)} %copy-done.3, bf16[256,512]{1,0:T(8,128)(2,1)S(1)} %copy-done.2, bf16[256,512]{1,0:T(8,128)(2,1)S(1)} %collective-permute-done.12.other_ref, ...), custom_call_target="tpu_custom_call" | custom-call | flops 1073741824 | bytes 5242880 | tf_op jit(solution)/shard_map/project_out/pallas_call | solution.py:333
  151.9 3.0 %collective-permute-start.13 = (bf16[256,512]{1,0:T(8,128)(2,1)S(1)}, bf16[256,512]{1,0:T(8,128)(2,1)S(1)}, u32[]{:S(2)}, u32[]{:S(2)}) collective-permute-start(bf16[256,512]{1,0:T(8,128)(2,1)S(1)} %get-tuple-element.67), channel_id=1, source_target_pairs={{0,2},{1,3},{2,0},{3,1},{4,6},{5,7},{6,4},{7,5},{8,10},{9,11},{10,... | collective-permute-start | bytes 786440 | tf_op jit(solution)/shard_map/ppermute | solution.py:18
  157.5 3.5 %collective-permute-done.13 = bf16[256,512]{1,0:T(8,128)(2,1)S(1)} collective-permute-done((bf16[256,512]{1,0:T(8,128)(2,1)S(1)}, bf16[256,512]{1,0:T(8,128)(2,1)S(1)}, u32[]{:S(2)}, u32[]{:S(2)}) %collective-permute-start.13) | collective-permute-done | bytes 262176 | tf_op jit(solution)/shard_map/ppermute | solution.py:18
  161.0 6.4 %collective-permute-done.14 = bf16[256,512]{1,0:T(8,128)(2,1)S(1)} collective-permute-done((bf16[256,512]{1,0:T(8,128)(2,1)S(1)}, bf16[256,512]{1,0:T(8,128)(2,1)S(1)}, u32[]{:S(2)}, u32[]{:S(2)}) %collective-permute-start.14) | collective-permute-done | bytes 262176 | tf_op jit(solution)/shard_map/ppermute | solution.py:18
  168.9 2.6 collective-permute-start.18
  171.5 12.9 %all-gather.5.cloned.1.call-done.weight_hbm = bf16[2048,2304]{1,0:T(8,128)(2,1)} async-done(((bf16[128,2304]{1,0:T(8,128)(2,1)}), bf16[2048,2304]{1,0:T(8,128)(2,1)}) %all-gather.5.cloned.1.call-update) | async-done | bytes 9437200 | tf_op jit(solution)/shard_map/all_gather | solution.py:437
  184.4 2.6 %project_kv.3 = (f32[256,256]{1,0:T(8,128)S(1)}, f32[256,256]{1,0:T(8,128)S(1)}) custom-call(s32[3]{0:T(128)S(1)} %copy-done.3, bf16[256,512]{1,0:T(8,128)(2,1)S(1)} %add_convert_fusion.2.own_ref.first_ref, bf16[256,512]{1,0:T(8,128)(2,1)S(1)} %collective-permute-done.17.from_one, bf16[256,512]{1,0:T(8,128)(2,1)S(1)} %collective-permute-done.18.from_two, ...), custom_call_target="tpu_custom_call" | custom-call | flops 268435456 | bytes 1572864 | tf_op jit(solution)/shard_map/project_kv/pallas_call | solution.py:274
  190.7 5.0 %all-to-all-start.3 = ((bf16[16,256,128]{2,1,0:T(8,128)(2,1)}), bf16[16,256,128]{2,1,0:T(8,128)(2,1)S(1)}, u32[]{:S(2)}, u32[]{:S(2)}) async-start(bf16[16,256,128]{2,1,0:T(8,128)(2,1)} %broadcast_in_dim.54), calls=%async_computation.3 | async-start | bytes 2097152 | tf_op jit(solution)/shard_map/all_to_all | solution.py:57
  195.7 3.2 %project_q.3 = (f32[256,512]{1,0:T(8,128)S(1)}, f32[256,512]{1,0:T(8,128)S(1)}) custom-call(s32[3]{0:T(128)S(1)} %copy-done.3, bf16[256,512]{1,0:T(8,128)(2,1)S(1)} %add_convert_fusion.2.own_ref.first_ref, bf16[256,512]{1,0:T(8,128)(2,1)S(1)} %collective-permute-done.17.from_one, bf16[256,512]{1,0:T(8,128)(2,1)S(1)} %collective-permute-done.18.from_two, ...), custom_call_target="tpu_custom_call" | custom-call | flops 1073741824 | bytes 5242880 | tf_op jit(solution)/shard_map/project_q/pallas_call | solution.py:274
  199.6 12.4 %all-to-all-done.3 = bf16[16,256,128]{2,1,0:T(8,128)(2,1)S(1)} async-done(((bf16[16,256,128]{2,1,0:T(8,128)(2,1)}), bf16[16,256,128]{2,1,0:T(8,128)(2,1)S(1)}, u32[]{:S(2)}, u32[]{:S(2)}) %all-to-all-start.3) | async-done | bytes 1048608 | tf_op jit(solution)/shard_map/all_to_all | solution.py:57
  216.6 8.9 %attention.3.mine_ref = bf16[256,512]{1,0:T(8,128)(2,1)} custom-call(s32[4]{0:T(128)} %pad_add_fusion.1.scalars, bf16[256,512]{1,0:T(8,128)(2,1)} %bitcast.69, bf16[16,4,64,128]{3,2,1,0:T(8,128)(2,1)} %bitcast.60, bf16[16,4,64,128]{3,2,1,0:T(8,128)(2,1)} %collective-permute-done.22.other_ref), custom_call_target="tpu_custom_call" | custom-call | flops 134217728 | bytes 2621440 | tf_op jit(solution)/shard_map/attention/pallas_call | solution.py:135
  228.1 3.7 %project_out.3 = (bf16[256,512]{1,0:T(8,128)(2,1)S(1)}, bf16[256,512]{1,0:T(8,128)(2,1)S(1)}, bf16[256,512]{1,0:T(8,128)(2,1)S(1)}, bf16[256,512]{1,0:T(8,128)(2,1)S(1)}) custom-call(s32[3]{0:T(128)S(1)} %copy-done.3, bf16[256,512]{1,0:T(8,128)(2,1)S(1)} %copy-done.1, bf16[256,512]{1,0:T(8,128)(2,1)S(1)} %collective-permute-done.23.other_ref, ...), custom_call_target="tpu_custom_call" | custom-call | flops 1073741824 | bytes 5242880 | tf_op jit(solution)/shard_map/project_out/pallas_call | solution.py:333
  231.8 3.0 %collective-permute-start.24 = (bf16[256,512]{1,0:T(8,128)(2,1)S(1)}, bf16[256,512]{1,0:T(8,128)(2,1)S(1)}, u32[]{:S(2)}, u32[]{:S(2)}) collective-permute-start(bf16[256,512]{1,0:T(8,128)(2,1)S(1)} %get-tuple-element.80), channel_id=1, source_target_pairs={{0,2},{1,3},{2,0},{3,1},{4,6},{5,7},{6,4},{7,5},{8,10},{9,11},{10,... | collective-permute-start | bytes 786440 | tf_op jit(solution)/shard_map/ppermute | solution.py:18
  241.0 6.3 %collective-permute-done.25 = bf16[256,512]{1,0:T(8,128)(2,1)S(1)} collective-permute-done((bf16[256,512]{1,0:T(8,128)(2,1)S(1)}, bf16[256,512]{1,0:T(8,128)(2,1)S(1)}, u32[]{:S(2)}, u32[]{:S(2)}) %collective-permute-start.25) | collective-permute-done | bytes 262176 | tf_op jit(solution)/shard_map/ppermute | solution.py:18
  (158 shorter events, 62.6 us)
Async XLA Ops:
  6.5 90.6 %all-gather.3.cloned.1.call-start = ((), (), s32[]{:S(2)}) async-start(), calls=%async_computation.4 | async-start | bytes 10027008 | tf_op jit(solution)/shard_map/all_gather | solution.py:437
  9.2 3.1 %collective-permute-start.8 = (bf16[128,2304]{1,0:T(8,128)(2,1)S(1)}, bf16[128,2304]{1,0:T(8,128)(2,1)S(1)}, u32[]{:S(2)}, u32[]{:S(2)}) collective-permute-start(bf16[128,2304]{1,0:T(8,128)(2,1)S(1)} %broadcast_select_fusion.2), channel_id=1, source_target_pairs={{0,64},{64,0},{1,65},{65,1},{2,66},{66,2},{3,67},{67,3},{4,68},{68... | collective-permute-start | bytes 1769480 | tf_op jit(solution)/shard_map/ppermute | solution.py:22
  13.7 170.7 %all-gather.5.cloned.1.call-start = ((), (), s32[]{:S(2)}) async-start(), calls=%async_computation.5 | async-start | bytes 10027008 | tf_op jit(solution)/shard_map/all_gather | solution.py:437
  20.4 3.2 %collective-permute-start = (bf16[128,80]{1,0:T(8,128)(2,1)}, bf16[128,80]{1,0:T(8,128)(2,1)S(1)}, u32[]{:S(2)}, u32[]{:S(2)}) collective-permute-start(bf16[128,80]{1,0:T(8,128)(2,1)} %merger_inner.1.mine_ref), channel_id=1, source_target_pairs={{0,64},{64,0},{1,65},{65,1},{2,66},{66,2},{3,67},{67,3},{4,68},{68... | collective-permute-start | bytes 61448 | tf_op jit(solution)/shard_map/ppermute | solution.py:22
  26.5 10.5 %collective-permute-start.1 = (bf16[256,512]{1,0:T(8,128)(2,1)}, bf16[256,512]{1,0:T(8,128)(2,1)S(1)}, u32[]{:S(2)}, u32[]{:S(2)}) collective-permute-start(bf16[256,512]{1,0:T(8,128)(2,1)} %get-tuple-element.45), channel_id=1, source_target_pairs={{0,2},{1,3},{2,0},{3,1},{4,6},{5,7},{6,4},{7,5},{8,10},{9,11},{10,... | collective-permute-start | bytes 786440 | tf_op jit(solution)/shard_map/ppermute | solution.py:18
  30.2 12.6 %collective-permute-start.2 = (bf16[256,512]{1,0:T(8,128)(2,1)}, bf16[256,512]{1,0:T(8,128)(2,1)S(1)}, u32[]{:S(2)}, u32[]{:S(2)}) collective-permute-start(bf16[256,512]{1,0:T(8,128)(2,1)} %get-tuple-element.46), channel_id=1, source_target_pairs={{0,1},{1,2},{2,3},{3,0},{4,5},{5,6},{6,7},{7,4},{8,9},{9,10},{10,1... | collective-permute-start | bytes 786440 | tf_op jit(solution)/shard_map/ppermute | solution.py:18
  30.9 12.2 %collective-permute-start.3 = (bf16[256,512]{1,0:T(8,128)(2,1)}, bf16[256,512]{1,0:T(8,128)(2,1)S(1)}, u32[]{:S(2)}, u32[]{:S(2)}) collective-permute-start(bf16[256,512]{1,0:T(8,128)(2,1)} %get-tuple-element.47), channel_id=1, source_target_pairs={{0,3},{1,0},{2,1},{3,2},{4,7},{5,4},{6,5},{7,6},{8,11},{9,8},{10,9... | collective-permute-start | bytes 786440 | tf_op jit(solution)/shard_map/ppermute | solution.py:18
  44.0 17.8 %all-to-all-start = ((bf16[16,16,512]{2,1,0:T(8,128)(2,1)}), bf16[16,16,512]{2,1,0:T(8,128)(2,1)S(1)}, u32[]{:S(2)}, u32[]{:S(2)}) async-start(bf16[16,16,512]{2,1,0:T(8,128)(2,1)} %bitcast.3), calls=%async_computation | async-start | bytes 524288 | tf_op jit(solution)/shard_map/all_to_all | solution.py:453
  62.6 14.2 %all-to-all-start.1 = ((bf16[16,16,512]{2,1,0:T(8,128)(2,1)}), bf16[16,16,512]{2,1,0:T(8,128)(2,1)S(1)}, u32[]{:S(2)}, u32[]{:S(2)}) async-start(bf16[16,16,512]{2,1,0:T(8,128)(2,1)} %broadcast_in_dim.52), calls=%async_computation.1 | async-start | bytes 524288 | tf_op jit(solution)/shard_map/all_to_all | solution.py:57
  77.1 9.3 %collective-permute-start.4 = (bf16[256,512]{1,0:T(8,128)(2,1)S(1)}, bf16[256,512]{1,0:T(8,128)(2,1)S(1)}, u32[]{:S(2)}, u32[]{:S(2)}) collective-permute-start(bf16[256,512]{1,0:T(8,128)(2,1)S(1)} %fusion.own_ref), channel_id=1, source_target_pairs={{0,1},{1,2},{2,3},{3,0},{4,5},{5,6},{6,7},{7,4},{8,9},{9,10},{10,1... | collective-permute-start | bytes 786440 | tf_op jit(solution)/shard_map/ppermute | solution.py:18
  77.9 12.1 %collective-permute-start.5 = (bf16[256,512]{1,0:T(8,128)(2,1)S(1)}, bf16[256,512]{1,0:T(8,128)(2,1)S(1)}, u32[]{:S(2)}, u32[]{:S(2)}) collective-permute-start(bf16[256,512]{1,0:T(8,128)(2,1)S(1)} %fusion.own_ref), channel_id=1, source_target_pairs={{0,2},{1,3},{2,0},{3,1},{4,6},{5,7},{6,4},{7,5},{8,10},{9,11},{10,... | collective-permute-start | bytes 786440 | tf_op jit(solution)/shard_map/ppermute | solution.py:18
  81.5 9.1 %collective-permute-start.6 = (bf16[256,512]{1,0:T(8,128)(2,1)S(1)}, bf16[256,512]{1,0:T(8,128)(2,1)S(1)}, u32[]{:S(2)}, u32[]{:S(2)}) collective-permute-start(bf16[256,512]{1,0:T(8,128)(2,1)S(1)} %fusion.own_ref), channel_id=1, source_target_pairs={{0,3},{1,0},{2,1},{3,2},{4,7},{5,4},{6,5},{7,6},{8,11},{9,8},{10,9... | collective-permute-start | bytes 786440 | tf_op jit(solution)/shard_map/ppermute | solution.py:18
  81.5 4.8 %collective-permute-start.7 = (f32[16,128]{1,0:T(8,128)S(1)}, f32[16,128]{1,0:T(8,128)S(1)}, u32[]{:S(2)}, u32[]{:S(2)}) collective-permute-start(f32[16,128]{1,0:T(8,128)S(1)} %select_bitcast_fusion), channel_id=1, source_target_pairs={{0,64},{64,0},{1,65},{65,1},{2,66},{66,2},{3,67},{67,3},{4,68},{68... | collective-permute-start | bytes 24584 | tf_op jit(solution)/shard_map/ppermute | solution.py:22
  99.8 1.9 collective-permute-start.9
  103.5 27.6 %all-to-all-start.2 = ((bf16[16,256,128]{2,1,0:T(8,128)(2,1)}), bf16[16,256,128]{2,1,0:T(8,128)(2,1)S(1)}, u32[]{:S(2)}, u32[]{:S(2)}) async-start(bf16[16,256,128]{2,1,0:T(8,128)(2,1)} %broadcast_in_dim.53), calls=%async_computation.2 | async-start | bytes 2097152 | tf_op jit(solution)/shard_map/all_to_all | solution.py:57
  112.0 22.2 %collective-permute-start.10 = (f32[256,512]{1,0:T(8,128)S(1)}, f32[256,512]{1,0:T(8,128)S(1)}, u32[]{:S(2)}, u32[]{:S(2)}) collective-permute-start(f32[256,512]{1,0:T(8,128)S(1)} %get-tuple-element.62), channel_id=1, source_target_pairs={{0,64},{64,0},{1,65},{65,1},{2,66},{66,2},{3,67},{67,3},{4,68},{68... | collective-permute-start | bytes 1572872 | tf_op jit(solution)/shard_map/ppermute | solution.py:22
  131.0 5.5 %collective-permute-start.11 = (bf16[16,4,64,128]{3,2,1,0:T(8,128)(2,1)S(1)}, bf16[16,4,64,128]{3,2,1,0:T(8,128)(2,1)}, u32[]{:S(2)}, u32[]{:S(2)}) collective-permute-start(bf16[16,4,64,128]{3,2,1,0:T(8,128)(2,1)S(1)} %bitcast.61), channel_id=1, source_target_pairs={{0,64},{64,0},{1,65},{65,1},{2,66},{66,2},{3,67},{67,3},{4,68},{68... | collective-permute-start | bytes 3145736 | tf_op jit(solution)/shard_map/ppermute | solution.py:22
  151.9 9.2 %collective-permute-start.13 = (bf16[256,512]{1,0:T(8,128)(2,1)S(1)}, bf16[256,512]{1,0:T(8,128)(2,1)S(1)}, u32[]{:S(2)}, u32[]{:S(2)}) collective-permute-start(bf16[256,512]{1,0:T(8,128)(2,1)S(1)} %get-tuple-element.67), channel_id=1, source_target_pairs={{0,2},{1,3},{2,0},{3,1},{4,6},{5,7},{6,4},{7,5},{8,10},{9,11},{10,... | collective-permute-start | bytes 786440 | tf_op jit(solution)/shard_map/ppermute | solution.py:18
  154.8 12.6 %collective-permute-start.14 = (bf16[256,512]{1,0:T(8,128)(2,1)S(1)}, bf16[256,512]{1,0:T(8,128)(2,1)S(1)}, u32[]{:S(2)}, u32[]{:S(2)}) collective-permute-start(bf16[256,512]{1,0:T(8,128)(2,1)S(1)} %get-tuple-element.68), channel_id=1, source_target_pairs={{0,1},{1,2},{2,3},{3,0},{4,5},{5,6},{6,7},{7,4},{8,9},{9,10},{10,1... | collective-permute-start | bytes 786440 | tf_op jit(solution)/shard_map/ppermute | solution.py:18
  155.2 12.2 %collective-permute-start.15 = (bf16[256,512]{1,0:T(8,128)(2,1)S(1)}, bf16[256,512]{1,0:T(8,128)(2,1)S(1)}, u32[]{:S(2)}, u32[]{:S(2)}) collective-permute-start(bf16[256,512]{1,0:T(8,128)(2,1)S(1)} %get-tuple-element.69), channel_id=1, source_target_pairs={{0,3},{1,0},{2,1},{3,2},{4,7},{5,4},{6,5},{7,6},{8,11},{9,8},{10,9... | collective-permute-start | bytes 786440 | tf_op jit(solution)/shard_map/ppermute | solution.py:18
  167.6 16.8 %collective-permute-start.17 = (bf16[256,512]{1,0:T(8,128)(2,1)S(1)}, bf16[256,512]{1,0:T(8,128)(2,1)S(1)}, u32[]{:S(2)}, u32[]{:S(2)}) collective-permute-start(bf16[256,512]{1,0:T(8,128)(2,1)S(1)} %add_convert_fusion.2.own_ref.first_ref), channel_id=1, source_target_pairs={{0,1},{1,2},{2,3},{3,0},{4,5},{5,6},{6,7},{7,4},{8,9},{9,10},{10,1... | collective-permute-start | bytes 786440 | tf_op jit(solution)/shard_map/ppermute | solution.py:18
  168.9 15.5 %collective-permute-start.18 = (bf16[256,512]{1,0:T(8,128)(2,1)S(1)}, bf16[256,512]{1,0:T(8,128)(2,1)S(1)}, u32[]{:S(2)}, u32[]{:S(2)}) collective-permute-start(bf16[256,512]{1,0:T(8,128)(2,1)S(1)} %add_convert_fusion.2.own_ref.first_ref), channel_id=1, source_target_pairs={{0,2},{1,3},{2,0},{3,1},{4,6},{5,7},{6,4},{7,5},{8,10},{9,11},{10,... | collective-permute-start | bytes 786440 | tf_op jit(solution)/shard_map/ppermute | solution.py:18
  171.5 12.9 %collective-permute-start.19 = (bf16[256,512]{1,0:T(8,128)(2,1)S(1)}, bf16[256,512]{1,0:T(8,128)(2,1)S(1)}, u32[]{:S(2)}, u32[]{:S(2)}) collective-permute-start(bf16[256,512]{1,0:T(8,128)(2,1)S(1)} %add_convert_fusion.2.own_ref.first_ref), channel_id=1, source_target_pairs={{0,3},{1,0},{2,1},{3,2},{4,7},{5,4},{6,5},{7,6},{8,11},{9,8},{10,9... | collective-permute-start | bytes 786440 | tf_op jit(solution)/shard_map/ppermute | solution.py:18
  187.1 1.9 collective-permute-start.20
  190.7 21.3 %all-to-all-start.3 = ((bf16[16,256,128]{2,1,0:T(8,128)(2,1)}), bf16[16,256,128]{2,1,0:T(8,128)(2,1)S(1)}, u32[]{:S(2)}, u32[]{:S(2)}) async-start(bf16[16,256,128]{2,1,0:T(8,128)(2,1)} %broadcast_in_dim.54), calls=%async_computation.3 | async-start | bytes 2097152 | tf_op jit(solution)/shard_map/all_to_all | solution.py:57
  198.9 15.2 %collective-permute-start.21 = (f32[256,512]{1,0:T(8,128)S(1)}, f32[256,512]{1,0:T(8,128)S(1)}, u32[]{:S(2)}, u32[]{:S(2)}) collective-permute-start(f32[256,512]{1,0:T(8,128)S(1)} %get-tuple-element.77), channel_id=1, source_target_pairs={{0,64},{64,0},{1,65},{65,1},{2,66},{66,2},{3,67},{67,3},{4,68},{68... | collective-permute-start | bytes 1572872 | tf_op jit(solution)/shard_map/ppermute | solution.py:22
  212.0 4.5 %collective-permute-start.22 = (bf16[16,4,64,128]{3,2,1,0:T(8,128)(2,1)S(1)}, bf16[16,4,64,128]{3,2,1,0:T(8,128)(2,1)}, u32[]{:S(2)}, u32[]{:S(2)}) collective-permute-start(bf16[16,4,64,128]{3,2,1,0:T(8,128)(2,1)S(1)} %bitcast.59), channel_id=1, source_target_pairs={{0,64},{64,0},{1,65},{65,1},{2,66},{66,2},{3,67},{67,3},{4,68},{68... | collective-permute-start | bytes 3145736 | tf_op jit(solution)/shard_map/ppermute | solution.py:22
  231.8 9.1 %collective-permute-start.24 = (bf16[256,512]{1,0:T(8,128)(2,1)S(1)}, bf16[256,512]{1,0:T(8,128)(2,1)S(1)}, u32[]{:S(2)}, u32[]{:S(2)}) collective-permute-start(bf16[256,512]{1,0:T(8,128)(2,1)S(1)} %get-tuple-element.80), channel_id=1, source_target_pairs={{0,2},{1,3},{2,0},{3,1},{4,6},{5,7},{6,4},{7,5},{8,10},{9,11},{10,... | collective-permute-start | bytes 786440 | tf_op jit(solution)/shard_map/ppermute | solution.py:18
  234.8 12.5 %collective-permute-start.25 = (bf16[256,512]{1,0:T(8,128)(2,1)S(1)}, bf16[256,512]{1,0:T(8,128)(2,1)S(1)}, u32[]{:S(2)}, u32[]{:S(2)}) collective-permute-start(bf16[256,512]{1,0:T(8,128)(2,1)S(1)} %get-tuple-element.81), channel_id=1, source_target_pairs={{0,1},{1,2},{2,3},{3,0},{4,5},{5,6},{6,7},{7,4},{8,9},{9,10},{10,1... | collective-permute-start | bytes 786440 | tf_op jit(solution)/shard_map/ppermute | solution.py:18
  235.2 12.1 %collective-permute-start.26 = (bf16[256,512]{1,0:T(8,128)(2,1)S(1)}, bf16[256,512]{1,0:T(8,128)(2,1)S(1)}, u32[]{:S(2)}, u32[]{:S(2)}) collective-permute-start(bf16[256,512]{1,0:T(8,128)(2,1)S(1)} %get-tuple-element.82), channel_id=1, source_target_pairs={{0,3},{1,0},{2,1},{3,2},{4,7},{5,4},{6,5},{7,6},{8,11},{9,8},{10,9... | collective-permute-start | bytes 786440 | tf_op jit(solution)/shard_map/ppermute | solution.py:18
  237.5 10.9 %collective-permute-start.16 = (bf16[256,512]{1,0:T(8,128)(2,1)S(1)}, bf16[256,512]{1,0:T(8,128)(2,1)S(1)}, u32[]{:S(2)}, u32[]{:S(2)}) collective-permute-start(bf16[256,512]{1,0:T(8,128)(2,1)S(1)} %add_convert_fusion.2.own_ref.first_ref), channel_id=1, source_target_pairs={{0,64},{64,0},{1,65},{65,1},{2,66},{66,2},{3,67},{67,3},{4,68},{68... | collective-permute-start | bytes 786440 | tf_op jit(solution)/shard_map/ppermute | solution.py:22
  247.5 2.1 collective-permute-start.27
  (24 other events, 367.2 us)
Sparse Core Ops, SparseCore 0:
  13.8 83.3 all-gather.2
  99.3 85.0 all-gather.4

commit v8 on v7

--- a/solution.py
+++ b/solution.py
@@ -142,6 +142,7 @@
             bytes_accessed=2 * (2 * query.size + 2 * mine.size),
             transcendentals=0,
         ),
+        compiler_params=pltpu.CompilerParams(vmem_limit_bytes=16 << 20),
         name="attention",
     )(scalars, query, mine, other)
 
@@ -173,6 +174,7 @@
             bytes_accessed=2 * (patches.size + merge_first.size),
             transcendentals=0,
         ),
+        compiler_params=pltpu.CompilerParams(vmem_limit_bytes=12 << 20),
         name="merger_inner",
     )(patches, merge_gain.reshape(1, -1), merge_first)
 
@@ -208,6 +210,7 @@
         out_shape=[shape] * n_mp,
         in_specs=[pl.BlockSpec(memory_space=pltpu.SMEM), whole, whole, whole],
         out_specs=[whole] * n_mp,
+        compiler_params=pltpu.CompilerParams(vmem_limit_bytes=12 << 20),
         name="merger_outer",
     )(place, mine, other, merge_second)
 
@@ -379,6 +382,7 @@
         out_shape=jax.ShapeDtypeStruct((first.shape[0], 2 * first.shape[1]), first.dtype),
         in_specs=[pl.BlockSpec(memory_space=pltpu.SMEM)] + [whole] * 4,
         out_specs=whole,
+        compiler_params=pltpu.CompilerParams(vmem_limit_bytes=8 << 20),
         name="joined",
     )(place, first, first_other, second, second_other)
 

time: 259 us -> 254 us (0.981)
  Pallas kernels: 45.2 us -> 38.8 us
  waiting for transfers between devices: 112 us -> 116 us
  local copies, waits for them, and re-layouts: 14.4 us -> 11.4 us
    all_gather x2, waiting for transfers between devices: 19.5 us -> 26.7 us  [local(): weight_full.append(lax.all_gather(mine, 'blk', axis=0, tiled=True))]
    unnamed x56 -> x38, local copies, waits for them, and re-layouts: 6.87 us -> 2.41 us
    mul x2, other arithmetic: 0.23 us -> 3.9 us  [local(): query = ((kept + swapped(sent)) * shrink).reshape(rows, -1, head_size)]
    pallas_call x2, Pallas kernels: 17.8 us -> 14.2 us  [attention(): pl.pallas_call(functools.partial(attention_kernel, chunk_runs=mine.shape[...]
    all_to_all x1, waiting for transfers between devices: 8.86 us -> 6.08 us  [local(): lax.all_to_all(total.astype(jnp.bfloat16).reshape(n_blk, -1, total.shape[...]
  transfers between devices with their start and end apart: 34 -> 34, of which waited for: 24 -> 22; matrix products, arithmetic and copies ran while one was open for 6% -> 7% of each run, Pallas kernels for 11% -> 9%
where the time goes in v8:
time: 254 us
  waiting for transfers between devices  116 us (46%)
  starting transfers between devices  61.3 us (24%)
  Pallas kernels  38.8 us (15%)
  between operations  14 us (6%)
  other arithmetic  12.4 us (5%)
  local copies, waits for them, and re-layouts  11.4 us (4%)
    all_to_all x3, waiting for transfers between devices, spread(): return lax.all_to_all(copies, 'blk', 0, 0, tiled=True)  39.9 us
    ppermute x15, waiting for transfers between devices, moved(): lax.ppermute(value, axis, [(i, (i + by) % size) for i in range(size)])  33.2 us
    all_gather x2, waiting for transfers between devices, local(): weight_full.append(lax.all_gather(mine, 'blk', axis=0, tiled=True))  26.7 us
    ppermute x15, starting transfers between devices, moved(): lax.ppermute(value, axis, [(i, (i + by) % size) for i in range(size)])  26.2 us
    ppermute x13, starting transfers between devices, swapped(): return lax.ppermute(value, 'section', [(0, 1), (1, 0)])  15.5 us
    pallas_call x2, Pallas kernels, attention(): pl.pallas_call(functools.partial(attention_kernel, chunk_runs=mine.shape[...  14.2 us
    pallas_call x4, Pallas kernels, project_in(): pl.pallas_call(functools.partial(project_in_kernel, at=at), out_shape=(ou...  13.6 us
    all_to_all x3, starting transfers between devices, spread(): return lax.all_to_all(copies, 'blk', 0, 0, tiled=True)  12.7 us
  transfers between devices with their start and end apart: 34, of which 22 were waited for; matrix products, arithmetic and copies ran while one was open for 7% of the time, Pallas kernels for 9%

profile of v8, /device:TPU:1, one launch (start us, length us, event | category | flops | bytes accessed | tf_op | source)
XLA Modules:
  0.0 253.7 jit_solution(12621054799714977212)
XLA Ops:
  21.3 3.8 %collective-permute-start.1 = (bf16[256,512]{1,0:T(8,128)(2,1)S(1)}, bf16[256,512]{1,0:T(8,128)(2,1)S(1)}, u32[]{:S(2)}, u32[]{:S(2)}) collective-permute-start(bf16[256,512]{1,0:T(8,128)(2,1)S(1)} %get-tuple-element.45), channel_id=1, source_target_pairs={{0,2},{1,3},{2,0},{3,1},{4,6},{5,7},{6,4},{7,5},{8,10},{9,11},{10,... | collective-permute-start | bytes 786440 | tf_op jit(solution)/shard_map/ppermute | solution.py:18
  28.7 3.0 %collective-permute-done.1 = bf16[256,512]{1,0:T(8,128)(2,1)S(1)} collective-permute-done((bf16[256,512]{1,0:T(8,128)(2,1)S(1)}, bf16[256,512]{1,0:T(8,128)(2,1)S(1)}, u32[]{:S(2)}, u32[]{:S(2)}) %collective-permute-start.1) | collective-permute-done | bytes 262176 | tf_op jit(solution)/shard_map/ppermute | solution.py:18
  31.7 5.9 %collective-permute-done.2 = bf16[256,512]{1,0:T(8,128)(2,1)S(1)} collective-permute-done((bf16[256,512]{1,0:T(8,128)(2,1)S(1)}, bf16[256,512]{1,0:T(8,128)(2,1)S(1)}, u32[]{:S(2)}, u32[]{:S(2)}) %collective-permute-start.2) | collective-permute-done | bytes 262176 | tf_op jit(solution)/shard_map/ppermute | solution.py:18
  38.7 6.9 %all-to-all-start = ((bf16[16,16,512]{2,1,0:T(8,128)(2,1)}), bf16[16,16,512]{2,1,0:T(8,128)(2,1)S(1)}, u32[]{:S(2)}, u32[]{:S(2)}) async-start(bf16[16,16,512]{2,1,0:T(8,128)(2,1)} %bitcast.3), calls=%async_computation | async-start | bytes 524288 | tf_op jit(solution)/shard_map/all_to_all | solution.py:457
  47.1 6.1 %all-to-all-done = bf16[16,16,512]{2,1,0:T(8,128)(2,1)S(1)} async-done(((bf16[16,16,512]{2,1,0:T(8,128)(2,1)}), bf16[16,16,512]{2,1,0:T(8,128)(2,1)S(1)}, u32[]{:S(2)}, u32[]{:S(2)}) %all-to-all-start) | async-done | bytes 262176 | tf_op jit(solution)/shard_map/all_to_all | solution.py:457
  54.0 3.5 %all-to-all-start.1 = ((bf16[16,16,512]{2,1,0:T(8,128)(2,1)}), bf16[16,16,512]{2,1,0:T(8,128)(2,1)S(1)}, u32[]{:S(2)}, u32[]{:S(2)}) async-start(bf16[16,16,512]{2,1,0:T(8,128)(2,1)} %broadcast_in_dim.52), calls=%async_computation.1 | async-start | bytes 524288 | tf_op jit(solution)/shard_map/all_to_all | solution.py:57
  57.6 10.7 %all-to-all-done.1 = bf16[16,16,512]{2,1,0:T(8,128)(2,1)S(1)} async-done(((bf16[16,16,512]{2,1,0:T(8,128)(2,1)}), bf16[16,16,512]{2,1,0:T(8,128)(2,1)S(1)}, u32[]{:S(2)}, u32[]{:S(2)}) %all-to-all-start.1) | async-done | bytes 262176 | tf_op jit(solution)/shard_map/all_to_all | solution.py:57
  69.3 3.7 %collective-permute-start.5 = (bf16[256,512]{1,0:T(8,128)(2,1)S(1)}, bf16[256,512]{1,0:T(8,128)(2,1)S(1)}, u32[]{:S(2)}, u32[]{:S(2)}) collective-permute-start(bf16[256,512]{1,0:T(8,128)(2,1)S(1)} %fusion.own_ref), channel_id=1, source_target_pairs={{0,2},{1,3},{2,0},{3,1},{4,6},{5,7},{6,4},{7,5},{8,10},{9,11},{10,... | collective-permute-start | bytes 786440 | tf_op jit(solution)/shard_map/ppermute | solution.py:18
  73.1 3.6 %collective-permute-start.7 = (f32[16,128]{1,0:T(8,128)S(1)}, f32[16,128]{1,0:T(8,128)S(1)}, u32[]{:S(2)}, u32[]{:S(2)}) collective-permute-start(f32[16,128]{1,0:T(8,128)S(1)} %select_bitcast_fusion), channel_id=1, source_target_pairs={{0,64},{64,0},{1,65},{65,1},{2,66},{66,2},{3,67},{67,3},{4,68},{68... | collective-permute-start | bytes 24584 | tf_op jit(solution)/shard_map/ppermute | solution.py:22
  77.5 4.5 %collective-permute-done.5.from_two = bf16[256,512]{1,0:T(8,128)(2,1)S(1)} collective-permute-done((bf16[256,512]{1,0:T(8,128)(2,1)S(1)}, bf16[256,512]{1,0:T(8,128)(2,1)S(1)}, u32[]{:S(2)}, u32[]{:S(2)}) %collective-permute-start.5) | collective-permute-done | bytes 262176 | tf_op jit(solution)/shard_map/ppermute | solution.py:18
  82.7 12.6 %all-gather.3.cloned.1.call-done.weight_hbm = bf16[2048,2304]{1,0:T(8,128)(2,1)} async-done(((bf16[128,2304]{1,0:T(8,128)(2,1)}), bf16[2048,2304]{1,0:T(8,128)(2,1)}) %all-gather.3.cloned.1.call-update) | async-done | bytes 9437200 | tf_op jit(solution)/shard_map/all_gather | solution.py:441
  95.4 2.6 %project_kv.2 = (f32[256,256]{1,0:T(8,128)S(1)}, f32[256,256]{1,0:T(8,128)S(1)}) custom-call(s32[3]{0:T(128)S(1)} %pad_add_fusion.place, bf16[256,512]{1,0:T(8,128)(2,1)S(1)} %fusion.own_ref, bf16[256,512]{1,0:T(8,128)(2,1)S(1)} %collective-permute-done.4.from_one, bf16[256,512]{1,0:T(8,128)(2,1)S(1)} %collective-permute-done.5.from_two, ...), custom_call_target="tpu_custom_call" | custom-call | flops 268435456 | bytes 1572864 | tf_op jit(solution)/shard_map/project_kv/pallas_call | solution.py:277
  101.4 4.2 %all-to-all-start.2 = ((bf16[16,256,128]{2,1,0:T(8,128)(2,1)}), bf16[16,256,128]{2,1,0:T(8,128)(2,1)S(1)}, u32[]{:S(2)}, u32[]{:S(2)}) async-start(bf16[16,256,128]{2,1,0:T(8,128)(2,1)} %broadcast_in_dim.53), calls=%async_computation.2 | async-start | bytes 2097152 | tf_op jit(solution)/shard_map/all_to_all | solution.py:57
  105.6 4.3 %project_q.2 = (f32[256,512]{1,0:T(8,128)S(1)}, f32[256,512]{1,0:T(8,128)}) custom-call(s32[3]{0:T(128)S(1)} %pad_add_fusion.place, bf16[256,512]{1,0:T(8,128)(2,1)S(1)} %fusion.own_ref, bf16[256,512]{1,0:T(8,128)(2,1)S(1)} %collective-permute-done.4.from_one, bf16[256,512]{1,0:T(8,128)(2,1)S(1)} %collective-permute-done.5.from_two, ...), custom_call_target="tpu_custom_call" | custom-call | flops 1073741824 | bytes 5242880 | tf_op jit(solution)/shard_map/project_q/pallas_call | solution.py:277
  110.6 17.6 %all-to-all-done.2 = bf16[16,256,128]{2,1,0:T(8,128)(2,1)S(1)} async-done(((bf16[16,256,128]{2,1,0:T(8,128)(2,1)}), bf16[16,256,128]{2,1,0:T(8,128)(2,1)S(1)}, u32[]{:S(2)}, u32[]{:S(2)}) %all-to-all-start.2) | async-done | bytes 1048608 | tf_op jit(solution)/shard_map/all_to_all | solution.py:57
  128.2 3.1 %collective-permute-start.11 = (bf16[16,4,64,128]{3,2,1,0:T(8,128)(2,1)S(1)}, bf16[16,4,64,128]{3,2,1,0:T(8,128)(2,1)S(1)}, u32[]{:S(2)}, u32[]{:S(2)}) collective-permute-start(bf16[16,4,64,128]{3,2,1,0:T(8,128)(2,1)S(1)} %bitcast.57), channel_id=1, source_target_pairs={{0,64},{64,0},{1,65},{65,1},{2,66},{66,2},{3,67},{67,3},{4,68},{68... | collective-permute-start | bytes 3145736 | tf_op jit(solution)/shard_map/ppermute | solution.py:22
  135.4 7.1 %attention.2.mine_ref = bf16[256,512]{1,0:T(8,128)(2,1)S(1)} custom-call(s32[4]{0:T(128)S(1)} %pad_add_fusion.1.scalars, bf16[256,512]{1,0:T(8,128)(2,1)S(1)} %bitcast.60, bf16[16,4,64,128]{3,2,1,0:T(8,128)(2,1)S(1)} %bitcast.58, bf16[16,4,64,128]{3,2,1,0:T(8,128)(2,1)S(1)} %collective-permute-done.11.other_ref), custom_call_target="tpu_custom_call" | custom-call | flops 134217728 | bytes 2621440 | tf_op jit(solution)/shard_map/attention/pallas_call | solution.py:135
  144.1 3.7 %project_out.2 = (bf16[256,512]{1,0:T(8,128)(2,1)S(1)}, bf16[256,512]{1,0:T(8,128)(2,1)S(1)}, bf16[256,512]{1,0:T(8,128)(2,1)S(1)}, bf16[256,512]{1,0:T(8,128)(2,1)S(1)}) custom-call(s32[3]{0:T(128)S(1)} %pad_add_fusion.place, bf16[256,512]{1,0:T(8,128)(2,1)S(1)} %attention.2.mine_ref, bf16[256,512]{1,0:T(8,128)(2,1)S(1)} %collective-permute-done.12.other_ref, ...), custom_call_target="tpu_custom_call" | custom-call | flops 1073741824 | bytes 5242880 | tf_op jit(solution)/shard_map/project_out/pallas_call | solution.py:336
  147.8 3.0 %collective-permute-start.13 = (bf16[256,512]{1,0:T(8,128)(2,1)S(1)}, bf16[256,512]{1,0:T(8,128)(2,1)S(1)}, u32[]{:S(2)}, u32[]{:S(2)}) collective-permute-start(bf16[256,512]{1,0:T(8,128)(2,1)S(1)} %get-tuple-element.67), channel_id=1, source_target_pairs={{0,2},{1,3},{2,0},{3,1},{4,6},{5,7},{6,4},{7,5},{8,10},{9,11},{10,... | collective-permute-start | bytes 786440 | tf_op jit(solution)/shard_map/ppermute | solution.py:18
  153.4 3.8 %collective-permute-done.13 = bf16[256,512]{1,0:T(8,128)(2,1)S(1)} collective-permute-done((bf16[256,512]{1,0:T(8,128)(2,1)S(1)}, bf16[256,512]{1,0:T(8,128)(2,1)S(1)}, u32[]{:S(2)}, u32[]{:S(2)}) %collective-permute-start.13) | collective-permute-done | bytes 262176 | tf_op jit(solution)/shard_map/ppermute | solution.py:18
  157.2 6.1 %collective-permute-done.14 = bf16[256,512]{1,0:T(8,128)(2,1)S(1)} collective-permute-done((bf16[256,512]{1,0:T(8,128)(2,1)S(1)}, bf16[256,512]{1,0:T(8,128)(2,1)S(1)}, u32[]{:S(2)}, u32[]{:S(2)}) %collective-permute-start.14) | collective-permute-done | bytes 262176 | tf_op jit(solution)/shard_map/ppermute | solution.py:18
  164.9 2.6 %collective-permute-start.18 = (bf16[256,512]{1,0:T(8,128)(2,1)S(1)}, bf16[256,512]{1,0:T(8,128)(2,1)S(1)}, u32[]{:S(2)}, u32[]{:S(2)}) collective-permute-start(bf16[256,512]{1,0:T(8,128)(2,1)S(1)} %add_convert_fusion.2.own_ref.first_ref), channel_id=1, source_target_pairs={{0,2},{1,3},{2,0},{3,1},{4,6},{5,7},{6,4},{7,5},{8,10},{9,11},{10,... | collective-permute-start | bytes 786440 | tf_op jit(solution)/shard_map/ppermute | solution.py:18
  167.4 14.1 %all-gather.5.cloned.1.call-done.weight_hbm = bf16[2048,2304]{1,0:T(8,128)(2,1)} async-done(((bf16[128,2304]{1,0:T(8,128)(2,1)}), bf16[2048,2304]{1,0:T(8,128)(2,1)}) %all-gather.5.cloned.1.call-update) | async-done | bytes 9437200 | tf_op jit(solution)/shard_map/all_gather | solution.py:441
  181.5 2.6 %project_kv.3 = (f32[256,256]{1,0:T(8,128)S(1)}, f32[256,256]{1,0:T(8,128)S(1)}) custom-call(s32[3]{0:T(128)S(1)} %pad_add_fusion.place, bf16[256,512]{1,0:T(8,128)(2,1)S(1)} %add_convert_fusion.2.own_ref.first_ref, bf16[256,512]{1,0:T(8,128)(2,1)S(1)} %collective-permute-done.17.from_one, bf16[256,512]{1,0:T(8,128)(2,1)S(1)} %collective-permute-done.18.from_two, ...), custom_call_target="tpu_custom_call" | custom-call | flops 268435456 | bytes 1572864 | tf_op jit(solution)/shard_map/project_kv/pallas_call | solution.py:277
  187.8 5.0 %all-to-all-start.3 = ((bf16[16,256,128]{2,1,0:T(8,128)(2,1)}), bf16[16,256,128]{2,1,0:T(8,128)(2,1)S(1)}, u32[]{:S(2)}, u32[]{:S(2)}) async-start(bf16[16,256,128]{2,1,0:T(8,128)(2,1)} %broadcast_in_dim.54), calls=%async_computation.3 | async-start | bytes 2097152 | tf_op jit(solution)/shard_map/all_to_all | solution.py:57
  192.8 4.0 %project_q.3 = (f32[256,512]{1,0:T(8,128)S(1)}, f32[256,512]{1,0:T(8,128)}) custom-call(s32[3]{0:T(128)S(1)} %pad_add_fusion.place, bf16[256,512]{1,0:T(8,128)(2,1)S(1)} %add_convert_fusion.2.own_ref.first_ref, bf16[256,512]{1,0:T(8,128)(2,1)S(1)} %collective-permute-done.17.from_one, bf16[256,512]{1,0:T(8,128)(2,1)S(1)} %collective-permute-done.18.from_two, ...), custom_call_target="tpu_custom_call" | custom-call | flops 1073741824 | bytes 5242880 | tf_op jit(solution)/shard_map/project_q/pallas_call | solution.py:277
  197.5 11.6 %all-to-all-done.3 = bf16[16,256,128]{2,1,0:T(8,128)(2,1)S(1)} async-done(((bf16[16,256,128]{2,1,0:T(8,128)(2,1)}), bf16[16,256,128]{2,1,0:T(8,128)(2,1)S(1)}, u32[]{:S(2)}, u32[]{:S(2)}) %all-to-all-start.3) | async-done | bytes 1048608 | tf_op jit(solution)/shard_map/all_to_all | solution.py:57
  215.3 7.1 %attention.3.mine_ref = bf16[256,512]{1,0:T(8,128)(2,1)S(1)} custom-call(s32[4]{0:T(128)S(1)} %pad_add_fusion.1.scalars, bf16[256,512]{1,0:T(8,128)(2,1)S(1)} %bitcast.59, bf16[16,4,64,128]{3,2,1,0:T(8,128)(2,1)S(1)} %bitcast.56, bf16[16,4,64,128]{3,2,1,0:T(8,128)(2,1)S(1)} %collective-permute-done.22.other_ref), custom_call_target="tpu_custom_call" | custom-call | flops 134217728 | bytes 2621440 | tf_op jit(solution)/shard_map/attention/pallas_call | solution.py:135
  224.0 3.7 %project_out.3 = (bf16[256,512]{1,0:T(8,128)(2,1)S(1)}, bf16[256,512]{1,0:T(8,128)(2,1)S(1)}, bf16[256,512]{1,0:T(8,128)(2,1)S(1)}, bf16[256,512]{1,0:T(8,128)(2,1)S(1)}) custom-call(s32[3]{0:T(128)S(1)} %pad_add_fusion.place, bf16[256,512]{1,0:T(8,128)(2,1)S(1)} %attention.3.mine_ref, bf16[256,512]{1,0:T(8,128)(2,1)S(1)} %collective-permute-done.23.other_ref, ...), custom_call_target="tpu_custom_call" | custom-call | flops 1073741824 | bytes 5242880 | tf_op jit(solution)/shard_map/project_out/pallas_call | solution.py:336
  227.7 3.0 %collective-permute-start.24 = (bf16[256,512]{1,0:T(8,128)(2,1)S(1)}, bf16[256,512]{1,0:T(8,128)(2,1)S(1)}, u32[]{:S(2)}, u32[]{:S(2)}) collective-permute-start(bf16[256,512]{1,0:T(8,128)(2,1)S(1)} %get-tuple-element.80), channel_id=1, source_target_pairs={{0,2},{1,3},{2,0},{3,1},{4,6},{5,7},{6,4},{7,5},{8,10},{9,11},{10,... | collective-permute-start | bytes 786440 | tf_op jit(solution)/shard_map/ppermute | solution.py:18
  234.4 2.8 %collective-permute-done.24 = bf16[256,512]{1,0:T(8,128)(2,1)S(1)} collective-permute-done((bf16[256,512]{1,0:T(8,128)(2,1)S(1)}, bf16[256,512]{1,0:T(8,128)(2,1)S(1)}, u32[]{:S(2)}, u32[]{:S(2)}) %collective-permute-start.24) | collective-permute-done | bytes 262176 | tf_op jit(solution)/shard_map/ppermute | solution.py:18
  237.1 6.0 %collective-permute-done.25 = bf16[256,512]{1,0:T(8,128)(2,1)S(1)} collective-permute-done((bf16[256,512]{1,0:T(8,128)(2,1)S(1)}, bf16[256,512]{1,0:T(8,128)(2,1)S(1)}, u32[]{:S(2)}, u32[]{:S(2)}) %collective-permute-start.25) | collective-permute-done | bytes 262176 | tf_op jit(solution)/shard_map/ppermute | solution.py:18
  (140 shorter events, 57.5 us)
Async XLA Ops:
  6.5 88.8 %all-gather.3.cloned.1.call-start = ((), (), s32[]{:S(2)}) async-start(), calls=%async_computation.4 | async-start | bytes 10027008 | tf_op jit(solution)/shard_map/all_gather | solution.py:441
  9.2 3.1 %collective-permute-start.8 = (bf16[128,2304]{1,0:T(8,128)(2,1)S(1)}, bf16[128,2304]{1,0:T(8,128)(2,1)S(1)}, u32[]{:S(2)}, u32[]{:S(2)}) collective-permute-start(bf16[128,2304]{1,0:T(8,128)(2,1)S(1)} %broadcast_select_fusion.2), channel_id=1, source_target_pairs={{0,64},{64,0},{1,65},{65,1},{2,66},{66,2},{3,67},{67,3},{4,68},{68... | collective-permute-start | bytes 1769480 | tf_op jit(solution)/shard_map/ppermute | solution.py:22
  13.7 167.9 %all-gather.5.cloned.1.call-start = ((), (), s32[]{:S(2)}) async-start(), calls=%async_computation.5 | async-start | bytes 10027008 | tf_op jit(solution)/shard_map/all_gather | solution.py:441
  17.3 2.7 %collective-permute-start = (bf16[128,80]{1,0:T(8,128)(2,1)S(1)}, bf16[128,80]{1,0:T(8,128)(2,1)S(1)}, u32[]{:S(2)}, u32[]{:S(2)}) collective-permute-start(bf16[128,80]{1,0:T(8,128)(2,1)S(1)} %merger_inner.1.mine_ref), channel_id=1, source_target_pairs={{0,64},{64,0},{1,65},{65,1},{2,66},{66,2},{3,67},{67,3},{4,68},{68... | collective-permute-start | bytes 61448 | tf_op jit(solution)/shard_map/ppermute | solution.py:22
  21.3 10.3 %collective-permute-start.1 = (bf16[256,512]{1,0:T(8,128)(2,1)S(1)}, bf16[256,512]{1,0:T(8,128)(2,1)S(1)}, u32[]{:S(2)}, u32[]{:S(2)}) collective-permute-start(bf16[256,512]{1,0:T(8,128)(2,1)S(1)} %get-tuple-element.45), channel_id=1, source_target_pairs={{0,2},{1,3},{2,0},{3,1},{4,6},{5,7},{6,4},{7,5},{8,10},{9,11},{10,... | collective-permute-start | bytes 786440 | tf_op jit(solution)/shard_map/ppermute | solution.py:18
  25.1 12.5 %collective-permute-start.2 = (bf16[256,512]{1,0:T(8,128)(2,1)S(1)}, bf16[256,512]{1,0:T(8,128)(2,1)S(1)}, u32[]{:S(2)}, u32[]{:S(2)}) collective-permute-start(bf16[256,512]{1,0:T(8,128)(2,1)S(1)} %get-tuple-element.46), channel_id=1, source_target_pairs={{0,1},{1,2},{2,3},{3,0},{4,5},{5,6},{6,7},{7,4},{8,9},{9,10},{10,1... | collective-permute-start | bytes 786440 | tf_op jit(solution)/shard_map/ppermute | solution.py:18
  25.8 12.1 %collective-permute-start.3 = (bf16[256,512]{1,0:T(8,128)(2,1)S(1)}, bf16[256,512]{1,0:T(8,128)(2,1)S(1)}, u32[]{:S(2)}, u32[]{:S(2)}) collective-permute-start(bf16[256,512]{1,0:T(8,128)(2,1)S(1)} %get-tuple-element.47), channel_id=1, source_target_pairs={{0,3},{1,0},{2,1},{3,2},{4,7},{5,4},{6,5},{7,6},{8,11},{9,8},{10,9... | collective-permute-start | bytes 786440 | tf_op jit(solution)/shard_map/ppermute | solution.py:18
  38.7 14.5 %all-to-all-start = ((bf16[16,16,512]{2,1,0:T(8,128)(2,1)}), bf16[16,16,512]{2,1,0:T(8,128)(2,1)S(1)}, u32[]{:S(2)}, u32[]{:S(2)}) async-start(bf16[16,16,512]{2,1,0:T(8,128)(2,1)} %bitcast.3), calls=%async_computation | async-start | bytes 524288 | tf_op jit(solution)/shard_map/all_to_all | solution.py:457
  54.0 14.3 %all-to-all-start.1 = ((bf16[16,16,512]{2,1,0:T(8,128)(2,1)}), bf16[16,16,512]{2,1,0:T(8,128)(2,1)S(1)}, u32[]{:S(2)}, u32[]{:S(2)}) async-start(bf16[16,16,512]{2,1,0:T(8,128)(2,1)} %broadcast_in_dim.52), calls=%async_computation.1 | async-start | bytes 524288 | tf_op jit(solution)/shard_map/all_to_all | solution.py:57
  68.5 9.0 %collective-permute-start.4 = (bf16[256,512]{1,0:T(8,128)(2,1)S(1)}, bf16[256,512]{1,0:T(8,128)(2,1)S(1)}, u32[]{:S(2)}, u32[]{:S(2)}) collective-permute-start(bf16[256,512]{1,0:T(8,128)(2,1)S(1)} %fusion.own_ref), channel_id=1, source_target_pairs={{0,1},{1,2},{2,3},{3,0},{4,5},{5,6},{6,7},{7,4},{8,9},{9,10},{10,1... | collective-permute-start | bytes 786440 | tf_op jit(solution)/shard_map/ppermute | solution.py:18
  69.3 12.6 %collective-permute-start.5 = (bf16[256,512]{1,0:T(8,128)(2,1)S(1)}, bf16[256,512]{1,0:T(8,128)(2,1)S(1)}, u32[]{:S(2)}, u32[]{:S(2)}) collective-permute-start(bf16[256,512]{1,0:T(8,128)(2,1)S(1)} %fusion.own_ref), channel_id=1, source_target_pairs={{0,2},{1,3},{2,0},{3,1},{4,6},{5,7},{6,4},{7,5},{8,10},{9,11},{10,... | collective-permute-start | bytes 786440 | tf_op jit(solution)/shard_map/ppermute | solution.py:18
  73.1 9.7 %collective-permute-start.6 = (bf16[256,512]{1,0:T(8,128)(2,1)S(1)}, bf16[256,512]{1,0:T(8,128)(2,1)S(1)}, u32[]{:S(2)}, u32[]{:S(2)}) collective-permute-start(bf16[256,512]{1,0:T(8,128)(2,1)S(1)} %fusion.own_ref), channel_id=1, source_target_pairs={{0,3},{1,0},{2,1},{3,2},{4,7},{5,4},{6,5},{7,6},{8,11},{9,8},{10,9... | collective-permute-start | bytes 786440 | tf_op jit(solution)/shard_map/ppermute | solution.py:18
  73.1 4.4 %collective-permute-start.7 = (f32[16,128]{1,0:T(8,128)S(1)}, f32[16,128]{1,0:T(8,128)S(1)}, u32[]{:S(2)}, u32[]{:S(2)}) collective-permute-start(f32[16,128]{1,0:T(8,128)S(1)} %select_bitcast_fusion), channel_id=1, source_target_pairs={{0,64},{64,0},{1,65},{65,1},{2,66},{66,2},{3,67},{67,3},{4,68},{68... | collective-permute-start | bytes 24584 | tf_op jit(solution)/shard_map/ppermute | solution.py:22
  98.0 1.7 collective-permute-start.9
  101.4 26.7 %all-to-all-start.2 = ((bf16[16,256,128]{2,1,0:T(8,128)(2,1)}), bf16[16,256,128]{2,1,0:T(8,128)(2,1)S(1)}, u32[]{:S(2)}, u32[]{:S(2)}) async-start(bf16[16,256,128]{2,1,0:T(8,128)(2,1)} %broadcast_in_dim.53), calls=%async_computation.2 | async-start | bytes 2097152 | tf_op jit(solution)/shard_map/all_to_all | solution.py:57
  109.9 21.4 %collective-permute-start.10 = (f32[256,512]{1,0:T(8,128)}, f32[256,512]{1,0:T(8,128)}, u32[]{:S(2)}, u32[]{:S(2)}) collective-permute-start(f32[256,512]{1,0:T(8,128)} %get-tuple-element.62), channel_id=1, source_target_pairs={{0,64},{64,0},{1,65},{65,1},{2,66},{66,2},{3,67},{67,3},{4,68},{68... | collective-permute-start | bytes 1572872 | tf_op jit(solution)/shard_map/ppermute | solution.py:22
  128.2 7.2 %collective-permute-start.11 = (bf16[16,4,64,128]{3,2,1,0:T(8,128)(2,1)S(1)}, bf16[16,4,64,128]{3,2,1,0:T(8,128)(2,1)S(1)}, u32[]{:S(2)}, u32[]{:S(2)}) collective-permute-start(bf16[16,4,64,128]{3,2,1,0:T(8,128)(2,1)S(1)} %bitcast.57), channel_id=1, source_target_pairs={{0,64},{64,0},{1,65},{65,1},{2,66},{66,2},{3,67},{67,3},{4,68},{68... | collective-permute-start | bytes 3145736 | tf_op jit(solution)/shard_map/ppermute | solution.py:22
  147.8 9.4 %collective-permute-start.13 = (bf16[256,512]{1,0:T(8,128)(2,1)S(1)}, bf16[256,512]{1,0:T(8,128)(2,1)S(1)}, u32[]{:S(2)}, u32[]{:S(2)}) collective-permute-start(bf16[256,512]{1,0:T(8,128)(2,1)S(1)} %get-tuple-element.67), channel_id=1, source_target_pairs={{0,2},{1,3},{2,0},{3,1},{4,6},{5,7},{6,4},{7,5},{8,10},{9,11},{10,... | collective-permute-start | bytes 786440 | tf_op jit(solution)/shard_map/ppermute | solution.py:18
  150.8 12.6 %collective-permute-start.14 = (bf16[256,512]{1,0:T(8,128)(2,1)S(1)}, bf16[256,512]{1,0:T(8,128)(2,1)S(1)}, u32[]{:S(2)}, u32[]{:S(2)}) collective-permute-start(bf16[256,512]{1,0:T(8,128)(2,1)S(1)} %get-tuple-element.68), channel_id=1, source_target_pairs={{0,1},{1,2},{2,3},{3,0},{4,5},{5,6},{6,7},{7,4},{8,9},{9,10},{10,1... | collective-permute-start | bytes 786440 | tf_op jit(solution)/shard_map/ppermute | solution.py:18
  151.1 12.2 %collective-permute-start.15 = (bf16[256,512]{1,0:T(8,128)(2,1)S(1)}, bf16[256,512]{1,0:T(8,128)(2,1)S(1)}, u32[]{:S(2)}, u32[]{:S(2)}) collective-permute-start(bf16[256,512]{1,0:T(8,128)(2,1)S(1)} %get-tuple-element.69), channel_id=1, source_target_pairs={{0,3},{1,0},{2,1},{3,2},{4,7},{5,4},{6,5},{7,6},{8,11},{9,8},{10,9... | collective-permute-start | bytes 786440 | tf_op jit(solution)/shard_map/ppermute | solution.py:18
  163.5 18.0 %collective-permute-start.17 = (bf16[256,512]{1,0:T(8,128)(2,1)S(1)}, bf16[256,512]{1,0:T(8,128)(2,1)S(1)}, u32[]{:S(2)}, u32[]{:S(2)}) collective-permute-start(bf16[256,512]{1,0:T(8,128)(2,1)S(1)} %add_convert_fusion.2.own_ref.first_ref), channel_id=1, source_target_pairs={{0,1},{1,2},{2,3},{3,0},{4,5},{5,6},{6,7},{7,4},{8,9},{9,10},{10,1... | collective-permute-start | bytes 786440 | tf_op jit(solution)/shard_map/ppermute | solution.py:18
  164.9 16.7 %collective-permute-start.18 = (bf16[256,512]{1,0:T(8,128)(2,1)S(1)}, bf16[256,512]{1,0:T(8,128)(2,1)S(1)}, u32[]{:S(2)}, u32[]{:S(2)}) collective-permute-start(bf16[256,512]{1,0:T(8,128)(2,1)S(1)} %add_convert_fusion.2.own_ref.first_ref), channel_id=1, source_target_pairs={{0,2},{1,3},{2,0},{3,1},{4,6},{5,7},{6,4},{7,5},{8,10},{9,11},{10,... | collective-permute-start | bytes 786440 | tf_op jit(solution)/shard_map/ppermute | solution.py:18
  167.4 14.1 %collective-permute-start.19 = (bf16[256,512]{1,0:T(8,128)(2,1)S(1)}, bf16[256,512]{1,0:T(8,128)(2,1)S(1)}, u32[]{:S(2)}, u32[]{:S(2)}) collective-permute-start(bf16[256,512]{1,0:T(8,128)(2,1)S(1)} %add_convert_fusion.2.own_ref.first_ref), channel_id=1, source_target_pairs={{0,3},{1,0},{2,1},{3,2},{4,7},{5,4},{6,5},{7,6},{8,11},{9,8},{10,9... | collective-permute-start | bytes 786440 | tf_op jit(solution)/shard_map/ppermute | solution.py:18
  184.2 1.9 collective-permute-start.20
  187.8 21.3 %all-to-all-start.3 = ((bf16[16,256,128]{2,1,0:T(8,128)(2,1)}), bf16[16,256,128]{2,1,0:T(8,128)(2,1)S(1)}, u32[]{:S(2)}, u32[]{:S(2)}) async-start(bf16[16,256,128]{2,1,0:T(8,128)(2,1)} %broadcast_in_dim.54), calls=%async_computation.3 | async-start | bytes 2097152 | tf_op jit(solution)/shard_map/all_to_all | solution.py:57
  196.8 14.4 %collective-permute-start.21 = (f32[256,512]{1,0:T(8,128)}, f32[256,512]{1,0:T(8,128)}, u32[]{:S(2)}, u32[]{:S(2)}) collective-permute-start(f32[256,512]{1,0:T(8,128)} %get-tuple-element.77), channel_id=1, source_target_pairs={{0,64},{64,0},{1,65},{65,1},{2,66},{66,2},{3,67},{67,3},{4,68},{68... | collective-permute-start | bytes 1572872 | tf_op jit(solution)/shard_map/ppermute | solution.py:22
  209.1 6.2 %collective-permute-start.22 = (bf16[16,4,64,128]{3,2,1,0:T(8,128)(2,1)S(1)}, bf16[16,4,64,128]{3,2,1,0:T(8,128)(2,1)S(1)}, u32[]{:S(2)}, u32[]{:S(2)}) collective-permute-start(bf16[16,4,64,128]{3,2,1,0:T(8,128)(2,1)S(1)} %bitcast.55), channel_id=1, source_target_pairs={{0,64},{64,0},{1,65},{65,1},{2,66},{66,2},{3,67},{67,3},{4,68},{68... | collective-permute-start | bytes 3145736 | tf_op jit(solution)/shard_map/ppermute | solution.py:22
  227.7 9.4 %collective-permute-start.24 = (bf16[256,512]{1,0:T(8,128)(2,1)S(1)}, bf16[256,512]{1,0:T(8,128)(2,1)S(1)}, u32[]{:S(2)}, u32[]{:S(2)}) collective-permute-start(bf16[256,512]{1,0:T(8,128)(2,1)S(1)} %get-tuple-element.80), channel_id=1, source_target_pairs={{0,2},{1,3},{2,0},{3,1},{4,6},{5,7},{6,4},{7,5},{8,10},{9,11},{10,... | collective-permute-start | bytes 786440 | tf_op jit(solution)/shard_map/ppermute | solution.py:18
  230.7 12.5 %collective-permute-start.25 = (bf16[256,512]{1,0:T(8,128)(2,1)S(1)}, bf16[256,512]{1,0:T(8,128)(2,1)S(1)}, u32[]{:S(2)}, u32[]{:S(2)}) collective-permute-start(bf16[256,512]{1,0:T(8,128)(2,1)S(1)} %get-tuple-element.81), channel_id=1, source_target_pairs={{0,1},{1,2},{2,3},{3,0},{4,5},{5,6},{6,7},{7,4},{8,9},{9,10},{10,1... | collective-permute-start | bytes 786440 | tf_op jit(solution)/shard_map/ppermute | solution.py:18
  231.0 12.1 %collective-permute-start.26 = (bf16[256,512]{1,0:T(8,128)(2,1)S(1)}, bf16[256,512]{1,0:T(8,128)(2,1)S(1)}, u32[]{:S(2)}, u32[]{:S(2)}) collective-permute-start(bf16[256,512]{1,0:T(8,128)(2,1)S(1)} %get-tuple-element.82), channel_id=1, source_target_pairs={{0,3},{1,0},{2,1},{3,2},{4,7},{5,4},{6,5},{7,6},{8,11},{9,8},{10,9... | collective-permute-start | bytes 786440 | tf_op jit(solution)/shard_map/ppermute | solution.py:18
  233.4 10.9 %collective-permute-start.16 = (bf16[256,512]{1,0:T(8,128)(2,1)S(1)}, bf16[256,512]{1,0:T(8,128)(2,1)S(1)}, u32[]{:S(2)}, u32[]{:S(2)}) collective-permute-start(bf16[256,512]{1,0:T(8,128)(2,1)S(1)} %add_convert_fusion.2.own_ref.first_ref), channel_id=1, source_target_pairs={{0,64},{64,0},{1,65},{65,1},{2,66},{66,2},{3,67},{67,3},{4,68},{68... | collective-permute-start | bytes 786440 | tf_op jit(solution)/shard_map/ppermute | solution.py:22
  243.3 2.0 collective-permute-start.27
  (15 other events, 135.0 us)
Sparse Core Ops, SparseCore 0:
  13.8 81.5 all-gather.2
  97.5 83.9 all-gather.4

commit v9 on v8

--- a/solution.py
+++ b/solution.py
@@ -27,15 +27,6 @@
     inverse = jnp.exp(-jnp.log(rope_base) * 2.0 * steps_half / head_size)
     angles = where_at.astype(jnp.float32)[:, None] * inverse[None, :]
     return (jnp.cos(angles), jnp.sin(angles))
-
-
-def rotate(values, cosine, sine):
-    half = values.shape[-1] // 2
-    first = values[..., :half]
-    second = values[..., half:]
-    return jnp.concatenate(
-        [first * cosine - second * sine, second * cosine + first * sine], axis=-1
-    )
 
 
 def my_half(value, axis, section_index):
@@ -225,13 +216,11 @@
     weight_hbm,
     kept_ref,
     sent_ref,
-    rows_ref,
-    weight_ref,
-    sums_ref,
-    semaphores,
-    *,
+    *rest,
     at,
 ):
+    later_ref = rest[0] if len(rest) > 4 else None
+    rows_ref, weight_ref, sums_ref, semaphores = rest[-4:]
     pieces, _, depth = gain_ref.shape
     half = weight_ref.shape[1] // 2
     copies = []
@@ -243,6 +232,19 @@
             )
         )
         copies[-1].start()
+    if later_ref is not None:
+        for by in range(pieces):
+            source = (place[2] + by) % pieces
+            copies.append(
+                pltpu.make_async_copy(
+                    weight_hbm.at[
+                        pl.ds(source * depth, depth), pl.ds(at + 2 * half, later_ref.shape[2])
+                    ],
+                    later_ref.at[by],
+                    semaphores.at[pieces + by],
+                )
+            )
+            copies[-1].start()
     squares = jnp.zeros((own_ref.shape[0], 1), jnp.float32)
     for by, part_ref in enumerate((own_ref, from_one, from_two, from_three)):
         source = (place[2] + pieces - by) % pieces
@@ -267,25 +269,31 @@
             sums_ref[...] = result
     kept_ref[:, :half] = result[:, :half]
     sent_ref[:, :half] = result[:, half:]
+    for copy in copies[pieces:]:
+        copy.wait()
 
 
 def project_in(place, parts, gain, weight, at, width, with_squares):
     rows, depth = parts[0].shape
     spare = lane if with_squares else 0
     out = jax.ShapeDtypeStruct((rows, width // 2 + spare), jnp.float32)
+    outs = [out, out]
+    if not with_squares:
+        later = weight.shape[1] - at - width
+        outs.append(jax.ShapeDtypeStruct((len(parts), depth, later), weight.dtype))
     whole = pl.BlockSpec(memory_space=pltpu.VMEM)
     return pl.pallas_call(
         functools.partial(project_in_kernel, at=at),
-        out_shape=(out, out),
+        out_shape=outs,
         in_specs=[pl.BlockSpec(memory_space=pltpu.SMEM)]
         + [whole] * 5
         + [pl.BlockSpec(memory_space=pltpu.HBM)],
-        out_specs=(whole, whole),
+        out_specs=[whole] * len(outs),
         scratch_shapes=[
             pltpu.VMEM((len(parts), rows, depth), jnp.bfloat16),
             pltpu.VMEM((weight.shape[0], width), jnp.bfloat16),
             pltpu.VMEM((rows, width), jnp.float32),
-            pltpu.SemaphoreType.DMA((len(parts),)),
+            pltpu.SemaphoreType.DMA((2 * len(parts),)),
         ],
         cost_estimate=pl.CostEstimate(
             flops=2 * rows * weight.shape[0] * width,
@@ -297,28 +305,58 @@
     )(place, *parts, gain, weight)
 
 
-def project_out_kernel(
-    place, mine_ref, other_ref, weight_hbm, own_ref, one_ref, two_ref, three_ref, weight_ref, semaphores
-):
+def keyval_rotate_kernel(kept_ref, arrived_ref, cosine_ref, sine_ref, out_ref, shrink_ref, *, features):
+    total = kept_ref[...] + arrived_ref[...]
+    shrink = lax.rsqrt(total[:, lane:] / features + epsilon)
+    shrink_ref[...] = shrink
+    values = total[:, :lane] * shrink
+    turned = pltpu.roll(values, lane // 2, 1)
+    result = (values * cosine_ref[...] + turned * sine_ref[...]).astype(out_ref.dtype)
+    for copy in range(out_ref.shape[0]):
+        out_ref[copy] = result
+
+
+def keyval_rotate(kept, arrived, cosine, sine, copies, features):
+    whole = pl.BlockSpec(memory_space=pltpu.VMEM)
+    rows = kept.shape[0]
+    return pl.pallas_call(
+        functools.partial(keyval_rotate_kernel, features=features),
+        out_shape=(
+            jax.ShapeDtypeStruct((copies, rows, lane), jnp.bfloat16),
+            jax.ShapeDtypeStruct((rows, lane), jnp.float32),
+        ),
+        in_specs=[whole] * 4,
+        out_specs=(whole, whole),
+        compiler_params=pltpu.CompilerParams(vmem_limit_bytes=8 << 20),
+        name="keyval_rotate",
+    )(kept, arrived, cosine, sine)
+
+
+def query_rotate_kernel(kept_ref, arrived_ref, shrink_ref, cosine_ref, sine_ref, out_ref):
+    for at in range(0, out_ref.shape[1], lane):
+        head = slice(at, at + lane)
+        values = (kept_ref[:, head] + arrived_ref[:, head]) * shrink_ref[...]
+        turned = pltpu.roll(values, lane // 2, 1)
+        out_ref[:, head] = (values * cosine_ref[...] + turned * sine_ref[...]).astype(out_ref.dtype)
+
+
+def query_rotate(kept, arrived, shrink, cosine, sine):
+    whole = pl.BlockSpec(memory_space=pltpu.VMEM)
+    return pl.pallas_call(
+        query_rotate_kernel,
+        out_shape=jax.ShapeDtypeStruct(kept.shape, jnp.bfloat16),
+        in_specs=[whole] * 5,
+        out_specs=whole,
+        cost_estimate=pl.CostEstimate(flops=0, bytes_accessed=12 * kept.size * 8, transcendentals=0),
+        compiler_params=pltpu.CompilerParams(vmem_limit_bytes=8 << 20),
+        name="query_rotate",
+    )(kept, arrived, shrink, cosine, sine)
+
+
+def project_out_kernel(mine_ref, other_ref, weight_ref, *outs):
     half = mine_ref.shape[1]
-    depth = own_ref.shape[1]
     over_last = (((1,), (1,)), ((), ()))
-    outs = (own_ref, one_ref, two_ref, three_ref)
-    copies = []
-    for by in range(len(outs)):
-        source = (place[2] + by) % len(outs)
-        copies.append(
-            pltpu.make_async_copy(
-                weight_hbm.at[
-                    pl.ds(source * depth, depth), pl.ds(weight_hbm.shape[1] - 2 * half, 2 * half)
-                ],
-                weight_ref.at[by],
-                semaphores.at[by],
-            )
-        )
-        copies[-1].start()
     for by, out_ref in enumerate(outs):
-        copies[by].wait()
         result = lax.dot_general(
             mine_ref[...], weight_ref[by, :, :half], over_last, preferred_element_type=jnp.float32
         ) + lax.dot_general(
@@ -327,34 +365,24 @@
         out_ref[...] = result.astype(out_ref.dtype)
 
 
-def project_out(place, mine, other, weight):
+def project_out(mine, other, weight):
     rows, half = mine.shape
-    pieces = lax.axis_size("mp")
-    depth = weight.shape[0] // pieces
+    pieces, depth, _ = weight.shape
     shape = jax.ShapeDtypeStruct((rows, depth), jnp.bfloat16)
     whole = pl.BlockSpec(memory_space=pltpu.VMEM)
     return pl.pallas_call(
         project_out_kernel,
         out_shape=[shape] * pieces,
-        in_specs=[
-            pl.BlockSpec(memory_space=pltpu.SMEM),
-            whole,
-            whole,
-            pl.BlockSpec(memory_space=pltpu.HBM),
-        ],
+        in_specs=[whole] * 3,
         out_specs=[whole] * pieces,
-        scratch_shapes=[
-            pltpu.VMEM((pieces, depth, 2 * half), jnp.bfloat16),
-            pltpu.SemaphoreType.DMA((pieces,)),
-        ],
         cost_estimate=pl.CostEstimate(
-            flops=4 * rows * half * weight.shape[0],
-            bytes_accessed=4 * half * weight.shape[0] + 2 * rows * weight.shape[0],
+            flops=2 * rows * weight.size,
+            bytes_accessed=2 * weight.size + 2 * rows * depth * pieces,
             transcendentals=0,
         ),
         compiler_params=pltpu.CompilerParams(vmem_limit_bytes=48 << 20),
         name="project_out",
-    )(place, mine, other, weight)
+    )(mine, other, weight)
 
 
 def joined_kernel(place, first_ref, first_other_ref, second_ref, second_other_ref, out_ref):
@@ -469,8 +497,10 @@
     has_visual = jnp.max(is_visual, axis=1, keepdims=True)
     text_rows = my_half(text_embeds.reshape(rows, slice_width), 1, section_index)
     cosine, sine = rope_tables(row_where, head_size)
-    keyval_cosine = jnp.where(first_core, jnp.concatenate([cosine, cosine], axis=1), 1.0)
-    keyval_sine = jnp.where(first_core, jnp.concatenate([-sine, sine], axis=1), 0.0)
+    cosine = jnp.concatenate([cosine, cosine], axis=1)
+    sine = jnp.concatenate([-sine, sine], axis=1)
+    keyval_cosine = jnp.where(first_core, cosine, 1.0)
+    keyval_sine = jnp.where(first_core, sine, 0.0)
     early = (scalars, is_visual, has_visual, text_rows, cosine, sine, keyval_cosine, keyval_sine)
     merged_terms, early = lax.optimization_barrier((merged_terms, early))
     scalars, is_visual, has_visual, text_rows, cosine, sine, keyval_cosine, keyval_sine = early
@@ -486,21 +516,20 @@
         gain = gain_layers[layer_index]
         weight = weight_full[layer_index]
         kept, sent = project_in(place, parts, gain, weight, 0, keyval_width, True)
-        total = kept + swapped(sent)
-        shrink = lax.rsqrt(total[:, head_size : head_size + 1] / (n_mp * slice_width) + epsilon)
-        keyval = total[:, :head_size] * shrink
-        half = head_size // 2
-        turned = jnp.concatenate([keyval[:, half:], keyval[:, :half]], axis=1)
-        keyval = (keyval * keyval_cosine + turned * keyval_sine).astype(jnp.bfloat16)
-        keyval, parts = lax.optimization_barrier((keyval, parts))
-        kept, sent = project_in(place, parts, gain, weight, keyval_width, 2 * heads_half, False)
-        query = ((kept + swapped(sent)) * shrink).reshape(rows, -1, head_size)
-        query = rotate(query, cosine[:, None, :], sine[:, None, :])
-        query = query.astype(jnp.bfloat16).reshape(rows, heads_half)
-        gathered = spread(keyval).reshape(n_blk, blocks, rows_here, head_size)
+        keyval_copies, shrink = keyval_rotate(
+            kept, swapped(sent), keyval_cosine, keyval_sine, n_blk, n_mp * slice_width
+        )
+        keyval_copies, parts = lax.optimization_barrier((keyval_copies, parts))
+        kept, sent, out_weight_here = project_in(
+            place, parts, gain, weight, keyval_width, 2 * heads_half, False
+        )
+        gathered = lax.all_to_all(keyval_copies, "blk", 0, 0, tiled=True)
+        gathered, kept, arrived = lax.optimization_barrier((gathered, kept, swapped(sent)))
+        query = query_rotate(kept, arrived, shrink, cosine, sine)
+        gathered = gathered.reshape(n_blk, blocks, rows_here, head_size)
         attended = attention(scalars, query, gathered, swapped(gathered))
         attended_other = swapped(attended)
-        own, *terms = project_out(place, attended, attended_other, weight)
+        own, *terms = project_out(attended, attended_other, out_weight_here)
         arrived = [moved(terms[by - 1], "mp", by) for by in (2, 1, 3)]
         total = state.astype(jnp.float32) + own.astype(jnp.float32)
         for part in arrived:

time: 254 us -> 250 us (0.984)
  waiting for transfers between devices: 116 us -> 126 us
  other arithmetic: 12.4 us -> 6.1 us
  starting transfers between devices: 61.3 us -> 57.9 us
  Pallas kernels: 38.8 us -> 35.8 us
    all_to_all x3 -> x1, waiting for transfers between devices: 39.9 us -> 10.2 us  [spread(): return lax.all_to_all(copies, 'blk', 0, 0, tiled=True)]
    all_to_all x0 -> x2, waiting for transfers between devices: none -> 23.6 us  [local(): gathered = lax.all_to_all(keyval_copies, 'blk', 0, 0, tiled=True)]
    all_to_all x0 -> x2, starting transfers between devices: none -> 9.47 us  [local(): gathered = lax.all_to_all(keyval_copies, 'blk', 0, 0, tiled=True)]
    all_to_all x3 -> x1, starting transfers between devices: 12.7 us -> 3.54 us  [spread(): return lax.all_to_all(copies, 'blk', 0, 0, tiled=True)]
    ppermute x15, starting transfers between devices: 26.2 us -> 19.1 us  [moved(): lax.ppermute(value, axis, [(i, (i + by) % size) for i in range(size)])]
    all_gather x2, waiting for transfers between devices: 26.7 us -> 33.7 us  [local(): weight_full.append(lax.all_gather(mine, 'blk', axis=0, tiled=True))]
    ppermute x13, waiting for transfers between devices: 9 us -> 15.4 us  [swapped(): return lax.ppermute(value, 'section', [(0, 1), (1, 0)])]
    pallas_call x4 -> x8, Pallas kernels: 13.6 us -> 18.5 us  [the longest x4 17.6 us: project_in(): pl.pallas_call(functools.partial(project_in_kernel, at=at), out_shape=out...]
  transfers between devices with their start and end apart: 34 -> 34, of which waited for: 22 -> 27; matrix products, arithmetic and copies ran while one was open for 7% -> 4% of each run, Pallas kernels for 9% -> 10%
where the time goes in v9:
time: 250 us; the launch traced here: 249 us
  waiting for transfers between devices  126 us (50%)
  starting transfers between devices  57.9 us (23%)
  Pallas kernels  35.8 us (14%)
  between operations  13.9 us (6%)
  local copies, waits for them, and re-layouts  9.44 us (4%)
  other arithmetic  6.1 us (2%)
    ppermute x15, waiting for transfers between devices, moved(): lax.ppermute(value, axis, [(i, (i + by) % size) for i in range(size)])  34.7 us
    all_gather x2, waiting for transfers between devices, local(): weight_full.append(lax.all_gather(mine, 'blk', axis=0, tiled=True))  33.7 us
    all_to_all x2, waiting for transfers between devices, local(): gathered = lax.all_to_all(keyval_copies, 'blk', 0, 0, tiled=True)  23.6 us
    ppermute x15, starting transfers between devices, moved(): lax.ppermute(value, axis, [(i, (i + by) % size) for i in range(size)])  19.1 us
    ppermute x13, starting transfers between devices, swapped(): return lax.ppermute(value, 'section', [(0, 1), (1, 0)])  19 us
    pallas_call x4, Pallas kernels, project_in(): pl.pallas_call(functools.partial(project_in_kernel, at=at), out_shape=out...  17.6 us
    ppermute x13, waiting for transfers between devices, swapped(): return lax.ppermute(value, 'section', [(0, 1), (1, 0)])  15.4 us
    pallas_call x2, Pallas kernels, attention(): pl.pallas_call(functools.partial(attention_kernel, chunk_runs=mine.shape[...  11.1 us
  transfers between devices with their start and end apart: 34, of which 27 were waited for; matrix products, arithmetic and copies ran while one was open for 4% of the time, Pallas kernels for 10%

profile of v9, /device:TPU:1, one launch (start us, length us, event | category | flops | bytes accessed | tf_op | source)
XLA Modules:
  0.0 249.1 jit_solution(9210557285358067719)
XLA Ops:
  14.5 1.8 copy.24.weight_ref
  22.5 3.9 %collective-permute-start.3 = (bf16[256,512]{1,0:T(8,128)(2,1)S(1)}, bf16[256,512]{1,0:T(8,128)(2,1)S(1)}, u32[]{:S(2)}, u32[]{:S(2)}) collective-permute-start(bf16[256,512]{1,0:T(8,128)(2,1)S(1)} %get-tuple-element.59), channel_id=1, source_target_pairs={{0,3},{1,0},{2,1},{3,2},{4,7},{5,4},{6,5},{7,6},{8,11},{9,8},{10,9... | collective-permute-start | bytes 786440 | tf_op jit(solution)/shard_map/ppermute | solution.py:18
  28.7 9.0 %collective-permute-done.3 = bf16[256,512]{1,0:T(8,128)(2,1)S(1)} collective-permute-done((bf16[256,512]{1,0:T(8,128)(2,1)S(1)}, bf16[256,512]{1,0:T(8,128)(2,1)S(1)}, u32[]{:S(2)}, u32[]{:S(2)}) %collective-permute-start.3) | collective-permute-done | bytes 262176 | tf_op jit(solution)/shard_map/ppermute | solution.py:18
  37.6 3.2 %collective-permute-done.2 = bf16[256,512]{1,0:T(8,128)(2,1)S(1)} collective-permute-done((bf16[256,512]{1,0:T(8,128)(2,1)S(1)}, bf16[256,512]{1,0:T(8,128)(2,1)S(1)}, u32[]{:S(2)}, u32[]{:S(2)}) %collective-permute-start.2) | collective-permute-done | bytes 262176 | tf_op jit(solution)/shard_map/ppermute | solution.py:18
  41.7 6.8 %all-to-all-start = ((bf16[16,16,512]{2,1,0:T(8,128)(2,1)}), bf16[16,16,512]{2,1,0:T(8,128)(2,1)S(1)}, u32[]{:S(2)}, u32[]{:S(2)}) async-start(bf16[16,16,512]{2,1,0:T(8,128)(2,1)} %bitcast.3), calls=%async_computation | async-start | bytes 524288 | tf_op jit(solution)/shard_map/all_to_all | solution.py:485
  49.9 7.3 %all-to-all-done = bf16[16,16,512]{2,1,0:T(8,128)(2,1)S(1)} async-done(((bf16[16,16,512]{2,1,0:T(8,128)(2,1)}), bf16[16,16,512]{2,1,0:T(8,128)(2,1)S(1)}, u32[]{:S(2)}, u32[]{:S(2)}) %all-to-all-start) | async-done | bytes 262176 | tf_op jit(solution)/shard_map/all_to_all | solution.py:485
  58.0 3.5 %all-to-all-start.1 = ((bf16[16,16,512]{2,1,0:T(8,128)(2,1)}), bf16[16,16,512]{2,1,0:T(8,128)(2,1)S(1)}, u32[]{:S(2)}, u32[]{:S(2)}) async-start(bf16[16,16,512]{2,1,0:T(8,128)(2,1)} %broadcast_in_dim.36), calls=%async_computation.1 | async-start | bytes 524288 | tf_op jit(solution)/shard_map/all_to_all | solution.py:48
  61.6 10.2 %all-to-all-done.1 = bf16[16,16,512]{2,1,0:T(8,128)(2,1)S(1)} async-done(((bf16[16,16,512]{2,1,0:T(8,128)(2,1)}), bf16[16,16,512]{2,1,0:T(8,128)(2,1)S(1)}, u32[]{:S(2)}, u32[]{:S(2)}) %all-to-all-start.1) | async-done | bytes 262176 | tf_op jit(solution)/shard_map/all_to_all | solution.py:48
  74.8 5.7 %collective-permute-start.7 = (f32[16,128]{1,0:T(8,128)S(1)}, f32[16,128]{1,0:T(8,128)S(1)}, u32[]{:S(2)}, u32[]{:S(2)}) collective-permute-start(f32[16,128]{1,0:T(8,128)S(1)} %select_bitcast_fusion), channel_id=1, source_target_pairs={{0,64},{64,0},{1,65},{65,1},{2,66},{66,2},{3,67},{67,3},{4,68},{68... | collective-permute-start | bytes 24584 | tf_op jit(solution)/shard_map/ppermute | solution.py:22
  82.4 14.5 %all-gather.3.cloned.1.call-done.weight_hbm = bf16[2048,2304]{1,0:T(8,128)(2,1)} async-done(((bf16[128,2304]{1,0:T(8,128)(2,1)}), bf16[2048,2304]{1,0:T(8,128)(2,1)}) %all-gather.3.cloned.1.call-update) | async-done | bytes 9437200 | tf_op jit(solution)/shard_map/all_gather | solution.py:469
  96.9 2.7 %project_kv.2 = (f32[256,256]{1,0:T(8,128)S(1)}, f32[256,256]{1,0:T(8,128)S(1)}) custom-call(s32[3]{0:T(128)S(1)} %pad_add_fusion.place, bf16[256,512]{1,0:T(8,128)(2,1)S(1)} %fusion.own_ref, bf16[256,512]{1,0:T(8,128)(2,1)S(1)} %collective-permute-done.4.from_one, bf16[256,512]{1,0:T(8,128)(2,1)S(1)} %collective-permute-done.5.from_two, ...), custom_call_target="tpu_custom_call" | custom-call | flops 268435456 | bytes 1572864 | tf_op jit(solution)/shard_map/project_kv/pallas_call | solution.py:285
  102.7 4.5 %all-to-all-start.2 = ((bf16[16,256,128]{2,1,0:T(8,128)(2,1)}), bf16[16,256,128]{2,1,0:T(8,128)(2,1)S(1)}, u32[]{:S(2)}, u32[]{:S(2)}) async-start(bf16[16,256,128]{2,1,0:T(8,128)(2,1)} %copy-done.4), calls=%async_computation.2 | async-start | bytes 2097152 | tf_op jit(solution)/shard_map/all_to_all | solution.py:526
  107.2 6.1 %project_q.2 = (f32[256,512]{1,0:T(8,128)S(1)}, f32[256,512]{1,0:T(8,128)S(1)}, bf16[4,512,1024]{2,1,0:T(8,128)(2,1)}) custom-call(s32[3]{0:T(128)S(1)} %pad_add_fusion.place, bf16[256,512]{1,0:T(8,128)(2,1)S(1)} %fusion.own_ref, bf16[256,512]{1,0:T(8,128)(2,1)S(1)} %collective-permute-done.4.from_one, bf16[256,512]{1,0:T(8,128)(2,1)S(1)} %collective-permute-done.5.from_two, ...), custom_call_target="tpu_custom_call" | custom-call | flops 1073741824 | bytes 5242880 | tf_op jit(solution)/shard_map/project_q/pallas_call | solution.py:285
  115.7 15.7 %all-to-all-done.2 = bf16[16,256,128]{2,1,0:T(8,128)(2,1)S(1)} async-done(((bf16[16,256,128]{2,1,0:T(8,128)(2,1)}), bf16[16,256,128]{2,1,0:T(8,128)(2,1)S(1)}, u32[]{:S(2)}, u32[]{:S(2)}) %all-to-all-start.2) | async-done | bytes 1048608 | tf_op jit(solution)/shard_map/all_to_all | solution.py:526
  133.0 2.0 collective-permute-done.11.other_ref
  135.1 5.6 %attention.2.mine_ref = bf16[256,512]{1,0:T(8,128)(2,1)S(1)} custom-call(s32[4]{0:T(128)S(1)} %pad_add_fusion.1.scalars, bf16[256,512]{1,0:T(8,128)(2,1)S(1)} %query_rotate.2.query_ref, bf16[16,4,64,128]{3,2,1,0:T(8,128)(2,1)S(1)} %bitcast.50, bf16[16,4,64,128]{3,2,1,0:T(8,128)(2,1)S(1)} %collective-permute-done.11.other_ref), custom_call_target="tpu_custom_call" | custom-call | flops 134217728 | bytes 2621440 | tf_op jit(solution)/shard_map/attention/pallas_call | solution.py:126
  146.5 4.8 %collective-permute-done.15 = bf16[256,512]{1,0:T(8,128)(2,1)S(1)} collective-permute-done((bf16[256,512]{1,0:T(8,128)(2,1)S(1)}, bf16[256,512]{1,0:T(8,128)(2,1)S(1)}, u32[]{:S(2)}, u32[]{:S(2)}) %collective-permute-start.15) | collective-permute-done | bytes 262176 | tf_op jit(solution)/shard_map/ppermute | solution.py:18
  151.3 2.9 %collective-permute-done.14 = bf16[256,512]{1,0:T(8,128)(2,1)S(1)} collective-permute-done((bf16[256,512]{1,0:T(8,128)(2,1)S(1)}, bf16[256,512]{1,0:T(8,128)(2,1)S(1)}, u32[]{:S(2)}, u32[]{:S(2)}) %collective-permute-start.14) | collective-permute-done | bytes 262176 | tf_op jit(solution)/shard_map/ppermute | solution.py:18
  154.2 3.7 %collective-permute-done.13 = bf16[256,512]{1,0:T(8,128)(2,1)S(1)} collective-permute-done((bf16[256,512]{1,0:T(8,128)(2,1)S(1)}, bf16[256,512]{1,0:T(8,128)(2,1)S(1)}, u32[]{:S(2)}, u32[]{:S(2)}) %collective-permute-start.13) | collective-permute-done | bytes 262176 | tf_op jit(solution)/shard_map/ppermute | solution.py:18
  158.1 2.5 %collective-permute-start.18 = (bf16[256,512]{1,0:T(8,128)(2,1)S(1)}, bf16[256,512]{1,0:T(8,128)(2,1)S(1)}, u32[]{:S(2)}, u32[]{:S(2)}) collective-permute-start(bf16[256,512]{1,0:T(8,128)(2,1)S(1)} %add_convert_fusion.1.own_ref.first_ref), channel_id=1, source_target_pairs={{0,2},{1,3},{2,0},{3,1},{4,6},{5,7},{6,4},{7,5},{8,10},{9,11},{10,... | collective-permute-start | bytes 786440 | tf_op jit(solution)/shard_map/ppermute | solution.py:18
  161.9 19.2 %all-gather.5.cloned.1.call-done.weight_hbm = bf16[2048,2304]{1,0:T(8,128)(2,1)} async-done(((bf16[128,2304]{1,0:T(8,128)(2,1)}), bf16[2048,2304]{1,0:T(8,128)(2,1)}) %all-gather.5.cloned.1.call-update) | async-done | bytes 9437200 | tf_op jit(solution)/shard_map/all_gather | solution.py:469
  181.1 2.7 %project_kv.3 = (f32[256,256]{1,0:T(8,128)S(1)}, f32[256,256]{1,0:T(8,128)S(1)}) custom-call(s32[3]{0:T(128)S(1)} %pad_add_fusion.place, bf16[256,512]{1,0:T(8,128)(2,1)S(1)} %add_convert_fusion.1.own_ref.first_ref, bf16[256,512]{1,0:T(8,128)(2,1)S(1)} %collective-permute-done.17.from_one, bf16[256,512]{1,0:T(8,128)(2,1)S(1)} %collective-permute-done.18.from_two, ...), custom_call_target="tpu_custom_call" | custom-call | flops 268435456 | bytes 1572864 | tf_op jit(solution)/shard_map/project_kv/pallas_call | solution.py:285
  186.9 5.0 %all-to-all-start.3 = ((bf16[16,256,128]{2,1,0:T(8,128)(2,1)}), bf16[16,256,128]{2,1,0:T(8,128)(2,1)S(1)}, u32[]{:S(2)}, u32[]{:S(2)}) async-start(bf16[16,256,128]{2,1,0:T(8,128)(2,1)} %copy-done.3), calls=%async_computation.3 | async-start | bytes 2097152 | tf_op jit(solution)/shard_map/all_to_all | solution.py:526
  191.8 6.1 %project_q.3 = (f32[256,512]{1,0:T(8,128)S(1)}, f32[256,512]{1,0:T(8,128)S(1)}, bf16[4,512,1024]{2,1,0:T(8,128)(2,1)}) custom-call(s32[3]{0:T(128)S(1)} %pad_add_fusion.place, bf16[256,512]{1,0:T(8,128)(2,1)S(1)} %add_convert_fusion.1.own_ref.first_ref, bf16[256,512]{1,0:T(8,128)(2,1)S(1)} %collective-permute-done.17.from_one, ...), custom_call_target="tpu_custom_call" | custom-call | flops 1073741824 | bytes 5242880 | tf_op jit(solution)/shard_map/project_q/pallas_call | solution.py:285
  200.2 7.9 %all-to-all-done.3 = bf16[16,256,128]{2,1,0:T(8,128)(2,1)S(1)} async-done(((bf16[16,256,128]{2,1,0:T(8,128)(2,1)}), bf16[16,256,128]{2,1,0:T(8,128)(2,1)S(1)}, u32[]{:S(2)}, u32[]{:S(2)}) %all-to-all-start.3) | async-done | bytes 1048608 | tf_op jit(solution)/shard_map/all_to_all | solution.py:526
  208.2 2.1 collective-permute-start.22
  210.5 2.0 collective-permute-done.22.other_ref
  212.6 5.6 %attention.3.mine_ref = bf16[256,512]{1,0:T(8,128)(2,1)S(1)} custom-call(s32[4]{0:T(128)S(1)} %pad_add_fusion.1.scalars, bf16[256,512]{1,0:T(8,128)(2,1)S(1)} %query_rotate.3.query_ref, bf16[16,4,64,128]{3,2,1,0:T(8,128)(2,1)S(1)} %bitcast.48, bf16[16,4,64,128]{3,2,1,0:T(8,128)(2,1)S(1)} %collective-permute-done.22.other_ref), custom_call_target="tpu_custom_call" | custom-call | flops 134217728 | bytes 2621440 | tf_op jit(solution)/shard_map/attention/pallas_call | solution.py:126
  221.1 2.7 %collective-permute-start.26 = (bf16[256,512]{1,0:T(8,128)(2,1)S(1)}, bf16[256,512]{1,0:T(8,128)(2,1)S(1)}, u32[]{:S(2)}, u32[]{:S(2)}) collective-permute-start(bf16[256,512]{1,0:T(8,128)(2,1)S(1)} %get-tuple-element.106), channel_id=1, source_target_pairs={{0,3},{1,0},{2,1},{3,2},{4,7},{5,4},{6,5},{7,6},{8,11},{9,8},{10,9... | collective-permute-start | bytes 786440 | tf_op jit(solution)/shard_map/ppermute | solution.py:18
  226.7 7.9 %collective-permute-done.26 = bf16[256,512]{1,0:T(8,128)(2,1)S(1)} collective-permute-done((bf16[256,512]{1,0:T(8,128)(2,1)S(1)}, bf16[256,512]{1,0:T(8,128)(2,1)S(1)}, u32[]{:S(2)}, u32[]{:S(2)}) %collective-permute-start.26) | collective-permute-done | bytes 262176 | tf_op jit(solution)/shard_map/ppermute | solution.py:18
  234.6 2.3 collective-permute-done.24
  237.1 2.6 %collective-permute-start.27 = (bf16[256,512]{1,0:T(8,128)(2,1)S(1)}, bf16[256,512]{1,0:T(8,128)(2,1)S(1)}, u32[]{:S(2)}, u32[]{:S(2)}) collective-permute-start(bf16[256,512]{1,0:T(8,128)(2,1)S(1)} %add_convert_fusion.second_ref), channel_id=1, source_target_pairs={{0,64},{64,0},{1,65},{65,1},{2,66},{66,2},{3,67},{67,3},{4,68},{68... | collective-permute-start | bytes 786440 | tf_op jit(solution)/shard_map/ppermute | solution.py:22
  (118 shorter events, 52.7 us)
Async XLA Ops:
  6.5 90.4 %all-gather.3.cloned.1.call-start = ((), (), s32[]{:S(2)}) async-start(), calls=%async_computation.4 | async-start | bytes 10027008 | tf_op jit(solution)/shard_map/all_gather | solution.py:469
  9.2 3.1 %collective-permute-start.8 = (bf16[128,2304]{1,0:T(8,128)(2,1)S(1)}, bf16[128,2304]{1,0:T(8,128)(2,1)S(1)}, u32[]{:S(2)}, u32[]{:S(2)}) collective-permute-start(bf16[128,2304]{1,0:T(8,128)(2,1)S(1)} %broadcast_select_fusion.2), channel_id=1, source_target_pairs={{0,64},{64,0},{1,65},{65,1},{2,66},{66,2},{3,67},{67,3},{4,68},{68... | collective-permute-start | bytes 1769480 | tf_op jit(solution)/shard_map/ppermute | solution.py:22
  13.7 167.4 %all-gather.5.cloned.1.call-start = ((), (), s32[]{:S(2)}) async-start(), calls=%async_computation.5 | async-start | bytes 10027008 | tf_op jit(solution)/shard_map/all_gather | solution.py:469
  17.5 3.8 %collective-permute-start = (bf16[128,80]{1,0:T(8,128)(2,1)S(1)}, bf16[128,80]{1,0:T(8,128)(2,1)S(1)}, u32[]{:S(2)}, u32[]{:S(2)}) collective-permute-start(bf16[128,80]{1,0:T(8,128)(2,1)S(1)} %merger_inner.1.mine_ref), channel_id=1, source_target_pairs={{0,64},{64,0},{1,65},{65,1},{2,66},{66,2},{3,67},{67,3},{4,68},{68... | collective-permute-start | bytes 61448 | tf_op jit(solution)/shard_map/ppermute | solution.py:22
  22.5 15.1 %collective-permute-start.3 = (bf16[256,512]{1,0:T(8,128)(2,1)S(1)}, bf16[256,512]{1,0:T(8,128)(2,1)S(1)}, u32[]{:S(2)}, u32[]{:S(2)}) collective-permute-start(bf16[256,512]{1,0:T(8,128)(2,1)S(1)} %get-tuple-element.59), channel_id=1, source_target_pairs={{0,3},{1,0},{2,1},{3,2},{4,7},{5,4},{6,5},{7,6},{8,11},{9,8},{10,9... | collective-permute-start | bytes 786440 | tf_op jit(solution)/shard_map/ppermute | solution.py:18
  26.4 14.4 %collective-permute-start.2 = (bf16[256,512]{1,0:T(8,128)(2,1)S(1)}, bf16[256,512]{1,0:T(8,128)(2,1)S(1)}, u32[]{:S(2)}, u32[]{:S(2)}) collective-permute-start(bf16[256,512]{1,0:T(8,128)(2,1)S(1)} %get-tuple-element.58), channel_id=1, source_target_pairs={{0,1},{1,2},{2,3},{3,0},{4,5},{5,6},{6,7},{7,4},{8,9},{9,10},{10,1... | collective-permute-start | bytes 786440 | tf_op jit(solution)/shard_map/ppermute | solution.py:18
  26.4 14.4 %collective-permute-start.1 = (bf16[256,512]{1,0:T(8,128)(2,1)S(1)}, bf16[256,512]{1,0:T(8,128)(2,1)S(1)}, u32[]{:S(2)}, u32[]{:S(2)}) collective-permute-start(bf16[256,512]{1,0:T(8,128)(2,1)S(1)} %get-tuple-element.57), channel_id=1, source_target_pairs={{0,2},{1,3},{2,0},{3,1},{4,6},{5,7},{6,4},{7,5},{8,10},{9,11},{10,... | collective-permute-start | bytes 786440 | tf_op jit(solution)/shard_map/ppermute | solution.py:18
  41.7 15.5 %all-to-all-start = ((bf16[16,16,512]{2,1,0:T(8,128)(2,1)}), bf16[16,16,512]{2,1,0:T(8,128)(2,1)S(1)}, u32[]{:S(2)}, u32[]{:S(2)}) async-start(bf16[16,16,512]{2,1,0:T(8,128)(2,1)} %bitcast.3), calls=%async_computation | async-start | bytes 524288 | tf_op jit(solution)/shard_map/all_to_all | solution.py:485
  58.0 13.8 %all-to-all-start.1 = ((bf16[16,16,512]{2,1,0:T(8,128)(2,1)}), bf16[16,16,512]{2,1,0:T(8,128)(2,1)S(1)}, u32[]{:S(2)}, u32[]{:S(2)}) async-start(bf16[16,16,512]{2,1,0:T(8,128)(2,1)} %broadcast_in_dim.36), calls=%async_computation.1 | async-start | bytes 524288 | tf_op jit(solution)/shard_map/all_to_all | solution.py:48
  72.0 9.5 %collective-permute-start.4 = (bf16[256,512]{1,0:T(8,128)(2,1)S(1)}, bf16[256,512]{1,0:T(8,128)(2,1)S(1)}, u32[]{:S(2)}, u32[]{:S(2)}) collective-permute-start(bf16[256,512]{1,0:T(8,128)(2,1)S(1)} %fusion.own_ref), channel_id=1, source_target_pairs={{0,1},{1,2},{2,3},{3,0},{4,5},{5,6},{6,7},{7,4},{8,9},{9,10},{10,1... | collective-permute-start | bytes 786440 | tf_op jit(solution)/shard_map/ppermute | solution.py:18
  72.1 9.5 %collective-permute-start.5 = (bf16[256,512]{1,0:T(8,128)(2,1)S(1)}, bf16[256,512]{1,0:T(8,128)(2,1)S(1)}, u32[]{:S(2)}, u32[]{:S(2)}) collective-permute-start(bf16[256,512]{1,0:T(8,128)(2,1)S(1)} %fusion.own_ref), channel_id=1, source_target_pairs={{0,2},{1,3},{2,0},{3,1},{4,6},{5,7},{6,4},{7,5},{8,10},{9,11},{10,... | collective-permute-start | bytes 786440 | tf_op jit(solution)/shard_map/ppermute | solution.py:18
  73.2 9.2 %collective-permute-start.6 = (bf16[256,512]{1,0:T(8,128)(2,1)S(1)}, bf16[256,512]{1,0:T(8,128)(2,1)S(1)}, u32[]{:S(2)}, u32[]{:S(2)}) collective-permute-start(bf16[256,512]{1,0:T(8,128)(2,1)S(1)} %fusion.own_ref), channel_id=1, source_target_pairs={{0,3},{1,0},{2,1},{3,2},{4,7},{5,4},{6,5},{7,6},{8,11},{9,8},{10,9... | collective-permute-start | bytes 786440 | tf_op jit(solution)/shard_map/ppermute | solution.py:18
  74.8 6.6 %collective-permute-start.7 = (f32[16,128]{1,0:T(8,128)S(1)}, f32[16,128]{1,0:T(8,128)S(1)}, u32[]{:S(2)}, u32[]{:S(2)}) collective-permute-start(f32[16,128]{1,0:T(8,128)S(1)} %select_bitcast_fusion), channel_id=1, source_target_pairs={{0,64},{64,0},{1,65},{65,1},{2,66},{66,2},{3,67},{67,3},{4,68},{68... | collective-permute-start | bytes 24584 | tf_op jit(solution)/shard_map/ppermute | solution.py:22
  99.6 1.9 collective-permute-start.9
  102.7 28.8 %all-to-all-start.2 = ((bf16[16,256,128]{2,1,0:T(8,128)(2,1)}), bf16[16,256,128]{2,1,0:T(8,128)(2,1)S(1)}, u32[]{:S(2)}, u32[]{:S(2)}) async-start(bf16[16,256,128]{2,1,0:T(8,128)(2,1)} %copy-done.4), calls=%async_computation.2 | async-start | bytes 2097152 | tf_op jit(solution)/shard_map/all_to_all | solution.py:526
  113.3 2.4 collective-permute-start.10
  131.4 3.6 %collective-permute-start.11 = (bf16[16,4,64,128]{3,2,1,0:T(8,128)(2,1)S(1)}, bf16[16,4,64,128]{3,2,1,0:T(8,128)(2,1)S(1)}, u32[]{:S(2)}, u32[]{:S(2)}) collective-permute-start(bf16[16,4,64,128]{3,2,1,0:T(8,128)(2,1)S(1)} %bitcast.49), channel_id=1, source_target_pairs={{0,64},{64,0},{1,65},{65,1},{2,66},{66,2},{3,67},{67,3},{4,68},{68... | collective-permute-start | bytes 3145736 | tf_op jit(solution)/shard_map/ppermute | solution.py:22
  143.6 7.7 %collective-permute-start.15 = (bf16[256,512]{1,0:T(8,128)(2,1)S(1)}, bf16[256,512]{1,0:T(8,128)(2,1)S(1)}, u32[]{:S(2)}, u32[]{:S(2)}) collective-permute-start(bf16[256,512]{1,0:T(8,128)(2,1)S(1)} %get-tuple-element.87), channel_id=1, source_target_pairs={{0,3},{1,0},{2,1},{3,2},{4,7},{5,4},{6,5},{7,6},{8,11},{9,8},{10,9... | collective-permute-start | bytes 786440 | tf_op jit(solution)/shard_map/ppermute | solution.py:18
  144.7 9.4 %collective-permute-start.14 = (bf16[256,512]{1,0:T(8,128)(2,1)S(1)}, bf16[256,512]{1,0:T(8,128)(2,1)S(1)}, u32[]{:S(2)}, u32[]{:S(2)}) collective-permute-start(bf16[256,512]{1,0:T(8,128)(2,1)S(1)} %get-tuple-element.86), channel_id=1, source_target_pairs={{0,1},{1,2},{2,3},{3,0},{4,5},{5,6},{6,7},{7,4},{8,9},{9,10},{10,1... | collective-permute-start | bytes 786440 | tf_op jit(solution)/shard_map/ppermute | solution.py:18
  145.1 12.7 %collective-permute-start.13 = (bf16[256,512]{1,0:T(8,128)(2,1)S(1)}, bf16[256,512]{1,0:T(8,128)(2,1)S(1)}, u32[]{:S(2)}, u32[]{:S(2)}) collective-permute-start(bf16[256,512]{1,0:T(8,128)(2,1)S(1)} %get-tuple-element.85), channel_id=1, source_target_pairs={{0,2},{1,3},{2,0},{3,1},{4,6},{5,7},{6,4},{7,5},{8,10},{9,11},{10,... | collective-permute-start | bytes 786440 | tf_op jit(solution)/shard_map/ppermute | solution.py:18
  158.0 23.0 %collective-permute-start.17 = (bf16[256,512]{1,0:T(8,128)(2,1)S(1)}, bf16[256,512]{1,0:T(8,128)(2,1)S(1)}, u32[]{:S(2)}, u32[]{:S(2)}) collective-permute-start(bf16[256,512]{1,0:T(8,128)(2,1)S(1)} %add_convert_fusion.1.own_ref.first_ref), channel_id=1, source_target_pairs={{0,1},{1,2},{2,3},{3,0},{4,5},{5,6},{6,7},{7,4},{8,9},{9,10},{10,1... | collective-permute-start | bytes 786440 | tf_op jit(solution)/shard_map/ppermute | solution.py:18
  158.1 23.0 %collective-permute-start.18 = (bf16[256,512]{1,0:T(8,128)(2,1)S(1)}, bf16[256,512]{1,0:T(8,128)(2,1)S(1)}, u32[]{:S(2)}, u32[]{:S(2)}) collective-permute-start(bf16[256,512]{1,0:T(8,128)(2,1)S(1)} %add_convert_fusion.1.own_ref.first_ref), channel_id=1, source_target_pairs={{0,2},{1,3},{2,0},{3,1},{4,6},{5,7},{6,4},{7,5},{8,10},{9,11},{10,... | collective-permute-start | bytes 786440 | tf_op jit(solution)/shard_map/ppermute | solution.py:18
  160.6 20.5 %collective-permute-start.19 = (bf16[256,512]{1,0:T(8,128)(2,1)S(1)}, bf16[256,512]{1,0:T(8,128)(2,1)S(1)}, u32[]{:S(2)}, u32[]{:S(2)}) collective-permute-start(bf16[256,512]{1,0:T(8,128)(2,1)S(1)} %add_convert_fusion.1.own_ref.first_ref), channel_id=1, source_target_pairs={{0,3},{1,0},{2,1},{3,2},{4,7},{5,4},{6,5},{7,6},{8,11},{9,8},{10,9... | collective-permute-start | bytes 786440 | tf_op jit(solution)/shard_map/ppermute | solution.py:18
  183.8 1.9 collective-permute-start.20
  186.9 21.3 %all-to-all-start.3 = ((bf16[16,256,128]{2,1,0:T(8,128)(2,1)}), bf16[16,256,128]{2,1,0:T(8,128)(2,1)S(1)}, u32[]{:S(2)}, u32[]{:S(2)}) async-start(bf16[16,256,128]{2,1,0:T(8,128)(2,1)} %copy-done.3), calls=%async_computation.3 | async-start | bytes 2097152 | tf_op jit(solution)/shard_map/all_to_all | solution.py:526
  198.0 2.3 collective-permute-start.21
  208.2 4.4 %collective-permute-start.22 = (bf16[16,4,64,128]{3,2,1,0:T(8,128)(2,1)S(1)}, bf16[16,4,64,128]{3,2,1,0:T(8,128)(2,1)S(1)}, u32[]{:S(2)}, u32[]{:S(2)}) collective-permute-start(bf16[16,4,64,128]{3,2,1,0:T(8,128)(2,1)S(1)} %bitcast.47), channel_id=1, source_target_pairs={{0,64},{64,0},{1,65},{65,1},{2,66},{66,2},{3,67},{67,3},{4,68},{68... | collective-permute-start | bytes 3145736 | tf_op jit(solution)/shard_map/ppermute | solution.py:22
  221.1 13.5 %collective-permute-start.26 = (bf16[256,512]{1,0:T(8,128)(2,1)S(1)}, bf16[256,512]{1,0:T(8,128)(2,1)S(1)}, u32[]{:S(2)}, u32[]{:S(2)}) collective-permute-start(bf16[256,512]{1,0:T(8,128)(2,1)S(1)} %get-tuple-element.106), channel_id=1, source_target_pairs={{0,3},{1,0},{2,1},{3,2},{4,7},{5,4},{6,5},{7,6},{8,11},{9,8},{10,9... | collective-permute-start | bytes 786440 | tf_op jit(solution)/shard_map/ppermute | solution.py:18
  223.8 10.8 %collective-permute-start.25 = (bf16[256,512]{1,0:T(8,128)(2,1)S(1)}, bf16[256,512]{1,0:T(8,128)(2,1)S(1)}, u32[]{:S(2)}, u32[]{:S(2)}) collective-permute-start(bf16[256,512]{1,0:T(8,128)(2,1)S(1)} %get-tuple-element.105), channel_id=1, source_target_pairs={{0,1},{1,2},{2,3},{3,0},{4,5},{5,6},{6,7},{7,4},{8,9},{9,10},{10,1... | collective-permute-start | bytes 786440 | tf_op jit(solution)/shard_map/ppermute | solution.py:18
  223.8 13.1 %collective-permute-start.24 = (bf16[256,512]{1,0:T(8,128)(2,1)S(1)}, bf16[256,512]{1,0:T(8,128)(2,1)S(1)}, u32[]{:S(2)}, u32[]{:S(2)}) collective-permute-start(bf16[256,512]{1,0:T(8,128)(2,1)S(1)} %get-tuple-element.104), channel_id=1, source_target_pairs={{0,2},{1,3},{2,0},{3,1},{4,6},{5,7},{6,4},{7,5},{8,10},{9,11},{10,... | collective-permute-start | bytes 786440 | tf_op jit(solution)/shard_map/ppermute | solution.py:18
  225.5 14.1 %collective-permute-start.16 = (bf16[256,512]{1,0:T(8,128)(2,1)S(1)}, bf16[256,512]{1,0:T(8,128)(2,1)S(1)}, u32[]{:S(2)}, u32[]{:S(2)}) collective-permute-start(bf16[256,512]{1,0:T(8,128)(2,1)S(1)} %add_convert_fusion.1.own_ref.first_ref), channel_id=1, source_target_pairs={{0,64},{64,0},{1,65},{65,1},{2,66},{66,2},{3,67},{67,3},{4,68},{68... | collective-permute-start | bytes 786440 | tf_op jit(solution)/shard_map/ppermute | solution.py:22
  237.1 3.7 %collective-permute-start.27 = (bf16[256,512]{1,0:T(8,128)(2,1)S(1)}, bf16[256,512]{1,0:T(8,128)(2,1)S(1)}, u32[]{:S(2)}, u32[]{:S(2)}) collective-permute-start(bf16[256,512]{1,0:T(8,128)(2,1)S(1)} %add_convert_fusion.second_ref), channel_id=1, source_target_pairs={{0,64},{64,0},{1,65},{65,1},{2,66},{66,2},{3,67},{67,3},{4,68},{68... | collective-permute-start | bytes 786440 | tf_op jit(solution)/shard_map/ppermute | solution.py:22
  (13 other events, 60.5 us)
Sparse Core Ops, SparseCore 0:
  13.8 83.0 all-gather.2
  99.0 81.9 all-gather.4

commit v10 on v9

--- a/solution.py
+++ b/solution.py
@@ -48,8 +48,9 @@
     return lax.all_to_all(copies, "blk", 0, 0, tiled=True)
 
 
-def attention_kernel(scalars, query_ref, mine_ref, other_ref, out_ref, *, chunk_runs):
-    runs, blocks, run, head_size = mine_ref.shape
+def attention_kernel(scalars, query_ref, mine_ref, other_ref, out_ref, *, chunk_runs, blocks_from):
+    runs, _, run, head_size = mine_ref.shape
+    blocks = out_ref.shape[0] // run
     heads = query_ref.shape[1] // head_size
     rows = heads * run
     chunk = chunk_runs * run
@@ -59,10 +60,11 @@
     factor = 1.0 / head_size**0.5 * math.log2(math.e)
 
     def stripes(key_ref, value_ref):
-        def stripe(block, carry):
-            row_from = pl.multiple_of(block * run, run)
+        def stripe(at, carry):
+            block = blocks_from + at
+            row_from = pl.multiple_of(at * run, run)
             first = block * block_len + cycle * run
-            here = query_ref[pl.ds(row_from, run), :]
+            here = query_ref[pl.ds(pl.multiple_of(block * run, run), run), :]
             stacked = jnp.concatenate(
                 [here[:, h * head_size : (h + 1) * head_size] for h in range(heads)], axis=0
             )
@@ -121,16 +123,19 @@
         stripes(other_ref, mine_ref)
 
 
-def attention(scalars, query, mine, other):
-    whole = pl.BlockSpec(memory_space=pltpu.VMEM)
-    return pl.pallas_call(
-        functools.partial(attention_kernel, chunk_runs=mine.shape[0]),
-        out_shape=jax.ShapeDtypeStruct(query.shape, query.dtype),
+def attention(scalars, query, mine, other, blocks_from, blocks):
+    whole = pl.BlockSpec(memory_space=pltpu.VMEM)
+    rows = blocks * mine.shape[2]
+    return pl.pallas_call(
+        functools.partial(
+            attention_kernel, chunk_runs=mine.shape[0], blocks_from=blocks_from
+        ),
+        out_shape=jax.ShapeDtypeStruct((rows, query.shape[1]), query.dtype),
         in_specs=[pl.BlockSpec(memory_space=pltpu.SMEM), whole, whole, whole],
         out_specs=whole,
         cost_estimate=pl.CostEstimate(
-            flops=4 * query.size * mine.size // query.shape[1] // 4,
-            bytes_accessed=2 * (2 * query.size + 2 * mine.size),
+            flops=rows * query.shape[1] * mine.size // mine.shape[3],
+            bytes_accessed=2 * (2 * rows * query.shape[1] + 2 * mine.size),
             transcendentals=0,
         ),
         compiler_params=pltpu.CompilerParams(vmem_limit_bytes=16 << 20),
@@ -305,15 +310,23 @@
     )(place, *parts, gain, weight)
 
 
-def keyval_rotate_kernel(kept_ref, arrived_ref, cosine_ref, sine_ref, out_ref, shrink_ref, *, features):
+def keyval_rotate_kernel(
+    kept_ref, arrived_ref, cosine_ref, sine_ref, out_hbm, shrink_ref, result_ref, semaphores, *, features
+):
     total = kept_ref[...] + arrived_ref[...]
     shrink = lax.rsqrt(total[:, lane:] / features + epsilon)
     shrink_ref[...] = shrink
     values = total[:, :lane] * shrink
     turned = pltpu.roll(values, lane // 2, 1)
-    result = (values * cosine_ref[...] + turned * sine_ref[...]).astype(out_ref.dtype)
-    for copy in range(out_ref.shape[0]):
-        out_ref[copy] = result
+    result_ref[...] = (values * cosine_ref[...] + turned * sine_ref[...]).astype(result_ref.dtype)
+    copies = [
+        pltpu.make_async_copy(result_ref, out_hbm.at[index], semaphores.at[index])
+        for index in range(out_hbm.shape[0])
+    ]
+    for copy in copies:
+        copy.start()
+    for copy in copies:
+        copy.wait()
 
 
 def keyval_rotate(kept, arrived, cosine, sine, copies, features):
@@ -326,7 +339,11 @@
             jax.ShapeDtypeStruct((rows, lane), jnp.float32),
         ),
         in_specs=[whole] * 4,
-        out_specs=(whole, whole),
+        out_specs=(pl.BlockSpec(memory_space=pltpu.HBM), whole),
+        scratch_shapes=[
+            pltpu.VMEM((rows, lane), jnp.bfloat16),
+            pltpu.SemaphoreType.DMA((copies,)),
+        ],
         compiler_params=pltpu.CompilerParams(vmem_limit_bytes=8 << 20),
         name="keyval_rotate",
     )(kept, arrived, cosine, sine)
@@ -385,22 +402,26 @@
     )(mine, other, weight)
 
 
-def joined_kernel(place, first_ref, first_other_ref, second_ref, second_other_ref, out_ref):
+def joined_kernel(place, first_ref, first_other_ref, *refs):
+    *seconds, out_ref = refs
+    half = len(seconds) // 2
     runs = first_ref.shape[1] // lane
 
-    def write(even_ref, odd_ref):
+    def write(even_ref, odd_ref, at):
+        here = slice(at, at + even_ref.shape[0])
         for run in range(runs):
-            here = slice(run * lane, (run + 1) * lane)
-            out_ref[:, 2 * run * lane : (2 * run + 1) * lane] = even_ref[:, here]
-            out_ref[:, (2 * run + 1) * lane : (2 * run + 2) * lane] = odd_ref[:, here]
+            columns = slice(run * lane, (run + 1) * lane)
+            out_ref[here, 2 * run * lane : (2 * run + 1) * lane] = even_ref[:, columns]
+            out_ref[here, (2 * run + 1) * lane : (2 * run + 2) * lane] = odd_ref[:, columns]
 
     @pl.when(place[0] == 0)
     def _():
-        write(first_ref, first_other_ref)
+        write(first_ref, first_other_ref, 0)
 
     @pl.when(place[0] != 0)
     def _():
-        write(second_other_ref, second_ref)
+        for part in range(half):
+            write(seconds[half + part], seconds[part], part * seconds[part].shape[0])
 
 
 def joined(place, first, first_other, second, second_other):
@@ -408,11 +429,11 @@
     return pl.pallas_call(
         joined_kernel,
         out_shape=jax.ShapeDtypeStruct((first.shape[0], 2 * first.shape[1]), first.dtype),
-        in_specs=[pl.BlockSpec(memory_space=pltpu.SMEM)] + [whole] * 4,
+        in_specs=[pl.BlockSpec(memory_space=pltpu.SMEM)] + [whole] * (2 + 2 * len(second)),
         out_specs=whole,
         compiler_params=pltpu.CompilerParams(vmem_limit_bytes=8 << 20),
         name="joined",
-    )(place, first, first_other, second, second_other)
+    )(place, first, first_other, *second, *second_other)
 
 
 def local(
@@ -527,19 +548,29 @@
         gathered, kept, arrived = lax.optimization_barrier((gathered, kept, swapped(sent)))
         query = query_rotate(kept, arrived, shrink, cosine, sine)
         gathered = gathered.reshape(n_blk, blocks, rows_here, head_size)
-        attended = attention(scalars, query, gathered, swapped(gathered))
-        attended_other = swapped(attended)
-        own, *terms = project_out(attended, attended_other, out_weight_here)
-        arrived = [moved(terms[by - 1], "mp", by) for by in (2, 1, 3)]
-        total = state.astype(jnp.float32) + own.astype(jnp.float32)
-        for part in arrived:
-            total = total + part.astype(jnp.float32)
-        state = total.astype(jnp.bfloat16)
+        gathered_other = swapped(gathered)
+        parts_of = 1 if layer_index + 1 < layers else 2
+        here = blocks // parts_of
+        states = []
+        for part_index in range(parts_of):
+            attended = attention(
+                scalars, query, gathered, gathered_other, part_index * here, here
+            )
+            own, *terms = project_out(attended, swapped(attended), out_weight_here)
+            arrived = [moved(terms[by - 1], "mp", by) for by in (2, 1, 3)]
+            size = here * rows_here
+            total = state[part_index * size : (part_index + 1) * size].astype(jnp.float32)
+            total = total + own.astype(jnp.float32)
+            for part in arrived:
+                total = total + part.astype(jnp.float32)
+            states.append(total.astype(jnp.bfloat16))
+        state = states[0] if parts_of == 1 else states
         results.append(state)
 
     first_other = swapped(results[0])
-    second_other = swapped(results[1])
-    hidden = joined(place, results[0], first_other, results[1], second_other)
+    second = results[1]
+    second_other = [swapped(part) for part in second]
+    hidden = joined(place, results[0], first_other, second, second_other)
     return hidden.reshape(1, blocks, rows_here, slice_width)
 
 

time: 250 us -> 254 us (1.016)
  waiting for transfers between devices: 126 us -> 119 us
  starting transfers between devices: 57.9 us -> 64.3 us
  Pallas kernels: 35.8 us -> 41 us
    ppermute x15 -> x18, waiting for transfers between devices: 34.7 us -> 28.3 us  [moved(): lax.ppermute(value, axis, [(i, (i + by) % size) for i in range(size)])]
    ppermute x15 -> x18, starting transfers between devices: 19.1 us -> 24.1 us  [moved(): lax.ppermute(value, axis, [(i, (i + by) % size) for i in range(size)])]
    pallas_call x2, Pallas kernels: 0.35 us -> 3.27 us  [keyval_rotate(): pl.pallas_call(functools.partial(keyval_rotate_kernel, features=features)...]
    ppermute x13 -> x15, starting transfers between devices: 19 us -> 20.8 us  [swapped(): return lax.ppermute(value, 'section', [(0, 1), (1, 0)])]
    ppermute x13 -> x15, waiting for transfers between devices: 15.4 us -> 14.4 us  [swapped(): return lax.ppermute(value, 'section', [(0, 1), (1, 0)])]
    pallas_call x2 -> x3, Pallas kernels: 11.1 us -> 11.9 us  [attention(): pl.pallas_call(functools.partial(attention_kernel, chunk_runs=mine.shape[...]
  transfers between devices with their start and end apart: 34 -> 39, of which waited for: 27 -> 25; matrix products, arithmetic and copies ran while one was open for 4% -> 3% of each run, Pallas kernels for 10% -> 13%
where the time goes in v10:
time: 254 us; the launch traced here: 252 us
  waiting for transfers between devices  119 us (47%)
  starting transfers between devices  64.3 us (25%)
  Pallas kernels  41 us (16%)
  between operations  13.9 us (5%)
  local copies, waits for them, and re-layouts  8 us (3%)
  other arithmetic  5.99 us (2%)
    all_gather x2, waiting for transfers between devices, local(): weight_full.append(lax.all_gather(mine, 'blk', axis=0, tiled=True))  35.8 us
    ppermute x18, waiting for transfers between devices, moved(): lax.ppermute(value, axis, [(i, (i + by) % size) for i in range(size)])  28.3 us
    ppermute x18, starting transfers between devices, moved(): lax.ppermute(value, axis, [(i, (i + by) % size) for i in range(size)])  24.1 us
    all_to_all x2, waiting for transfers between devices, local(): gathered = lax.all_to_all(keyval_copies, 'blk', 0, 0, tiled=True)  23.3 us
    ppermute x15, starting transfers between devices, swapped(): return lax.ppermute(value, 'section', [(0, 1), (1, 0)])  20.8 us
    pallas_call x4, Pallas kernels, project_in(): pl.pallas_call(functools.partial(project_in_kernel, at=at), out_shape=out...  17.5 us
    ppermute x15, waiting for transfers between devices, swapped(): return lax.ppermute(value, 'section', [(0, 1), (1, 0)])  14.4 us
    pallas_call x3, Pallas kernels, attention(): pl.pallas_call(functools.partial(attention_kernel, chunk_runs=mine.shape[...  11.9 us
  transfers between devices with their start and end apart: 39, of which 25 were waited for; matrix products, arithmetic and copies ran while one was open for 3% of the time, Pallas kernels for 13%

profile of v10, /device:TPU:1, one launch (start us, length us, event | category | flops | bytes accessed | tf_op | source)
XLA Modules:
  0.0 252.4 jit_solution(16423406777549693097)
XLA Ops:
  21.0 3.9 %collective-permute-start.3 = (bf16[256,512]{1,0:T(8,128)(2,1)S(1)}, bf16[256,512]{1,0:T(8,128)(2,1)S(1)}, u32[]{:S(2)}, u32[]{:S(2)}) collective-permute-start(bf16[256,512]{1,0:T(8,128)(2,1)S(1)} %get-tuple-element.63), channel_id=1, source_target_pairs={{0,3},{1,0},{2,1},{3,2},{4,7},{5,4},{6,5},{7,6},{8,11},{9,8},{10,9... | collective-permute-start | bytes 786440 | tf_op jit(solution)/shard_map/ppermute | solution.py:18
  27.1 9.0 %collective-permute-done.3 = bf16[256,512]{1,0:T(8,128)(2,1)S(1)} collective-permute-done((bf16[256,512]{1,0:T(8,128)(2,1)S(1)}, bf16[256,512]{1,0:T(8,128)(2,1)S(1)}, u32[]{:S(2)}, u32[]{:S(2)}) %collective-permute-start.3) | collective-permute-done | bytes 262176 | tf_op jit(solution)/shard_map/ppermute | solution.py:18
  36.1 3.2 %collective-permute-done.2 = bf16[256,512]{1,0:T(8,128)(2,1)S(1)} collective-permute-done((bf16[256,512]{1,0:T(8,128)(2,1)S(1)}, bf16[256,512]{1,0:T(8,128)(2,1)S(1)}, u32[]{:S(2)}, u32[]{:S(2)}) %collective-permute-start.2) | collective-permute-done | bytes 262176 | tf_op jit(solution)/shard_map/ppermute | solution.py:18
  40.1 6.8 %all-to-all-start = ((bf16[16,16,512]{2,1,0:T(8,128)(2,1)}), bf16[16,16,512]{2,1,0:T(8,128)(2,1)S(1)}, u32[]{:S(2)}, u32[]{:S(2)}) async-start(bf16[16,16,512]{2,1,0:T(8,128)(2,1)} %bitcast.3), calls=%async_computation | async-start | bytes 524288 | tf_op jit(solution)/shard_map/all_to_all | solution.py:506
  48.3 6.2 %all-to-all-done = bf16[16,16,512]{2,1,0:T(8,128)(2,1)S(1)} async-done(((bf16[16,16,512]{2,1,0:T(8,128)(2,1)}), bf16[16,16,512]{2,1,0:T(8,128)(2,1)S(1)}, u32[]{:S(2)}, u32[]{:S(2)}) %all-to-all-start) | async-done | bytes 262176 | tf_op jit(solution)/shard_map/all_to_all | solution.py:506
  55.3 3.5 %all-to-all-start.1 = ((bf16[16,16,512]{2,1,0:T(8,128)(2,1)}), bf16[16,16,512]{2,1,0:T(8,128)(2,1)S(1)}, u32[]{:S(2)}, u32[]{:S(2)}) async-start(bf16[16,16,512]{2,1,0:T(8,128)(2,1)} %broadcast_in_dim.36), calls=%async_computation.1 | async-start | bytes 524288 | tf_op jit(solution)/shard_map/all_to_all | solution.py:48
  58.9 10.2 %all-to-all-done.1 = bf16[16,16,512]{2,1,0:T(8,128)(2,1)S(1)} async-done(((bf16[16,16,512]{2,1,0:T(8,128)(2,1)}), bf16[16,16,512]{2,1,0:T(8,128)(2,1)S(1)}, u32[]{:S(2)}, u32[]{:S(2)}) %all-to-all-start.1) | async-done | bytes 262176 | tf_op jit(solution)/shard_map/all_to_all | solution.py:48
  72.7 5.7 %collective-permute-start.7 = (f32[16,128]{1,0:T(8,128)S(1)}, f32[16,128]{1,0:T(8,128)S(1)}, u32[]{:S(2)}, u32[]{:S(2)}) collective-permute-start(f32[16,128]{1,0:T(8,128)S(1)} %select_bitcast_fusion), channel_id=1, source_target_pairs={{0,64},{64,0},{1,65},{65,1},{2,66},{66,2},{3,67},{67,3},{4,68},{68... | collective-permute-start | bytes 24584 | tf_op jit(solution)/shard_map/ppermute | solution.py:22
  79.9 16.5 %all-gather.3.cloned.1.call-done.weight_hbm = bf16[2048,2304]{1,0:T(8,128)(2,1)} async-done(((bf16[128,2304]{1,0:T(8,128)(2,1)}), bf16[2048,2304]{1,0:T(8,128)(2,1)}) %all-gather.3.cloned.1.call-update) | async-done | bytes 9437200 | tf_op jit(solution)/shard_map/all_gather | solution.py:490
  96.4 2.7 %project_kv.2 = (f32[256,256]{1,0:T(8,128)S(1)}, f32[256,256]{1,0:T(8,128)S(1)}) custom-call(s32[3]{0:T(128)S(1)} %pad_add_fusion.place, bf16[256,512]{1,0:T(8,128)(2,1)S(1)} %fusion.own_ref, bf16[256,512]{1,0:T(8,128)(2,1)S(1)} %collective-permute-done.4.from_one, bf16[256,512]{1,0:T(8,128)(2,1)S(1)} %collective-permute-done.5.from_two, ...), custom_call_target="tpu_custom_call" | custom-call | flops 268435456 | bytes 1572864 | tf_op jit(solution)/shard_map/project_kv/pallas_call | solution.py:290
  103.4 4.1 %all-to-all-start.2 = ((bf16[16,256,128]{2,1,0:T(8,128)(2,1)}), bf16[16,256,128]{2,1,0:T(8,128)(2,1)S(1)}, u32[]{:S(2)}, u32[]{:S(2)}) async-start(bf16[16,256,128]{2,1,0:T(8,128)(2,1)} %copy-done.4), calls=%async_computation.2 | async-start | bytes 2097152 | tf_op jit(solution)/shard_map/all_to_all | solution.py:547
  107.5 6.1 %project_q.2 = (f32[256,512]{1,0:T(8,128)S(1)}, f32[256,512]{1,0:T(8,128)S(1)}, bf16[4,512,1024]{2,1,0:T(8,128)(2,1)}) custom-call(s32[3]{0:T(128)S(1)} %pad_add_fusion.place, bf16[256,512]{1,0:T(8,128)(2,1)S(1)} %fusion.own_ref, bf16[256,512]{1,0:T(8,128)(2,1)S(1)} %collective-permute-done.4.from_one, bf16[256,512]{1,0:T(8,128)(2,1)S(1)} %collective-permute-done.5.from_two, ...), custom_call_target="tpu_custom_call" | custom-call | flops 1073741824 | bytes 5242880 | tf_op jit(solution)/shard_map/project_q/pallas_call | solution.py:290
  116.0 15.4 %all-to-all-done.2 = bf16[16,256,128]{2,1,0:T(8,128)(2,1)S(1)} async-done(((bf16[16,256,128]{2,1,0:T(8,128)(2,1)}), bf16[16,256,128]{2,1,0:T(8,128)(2,1)S(1)}, u32[]{:S(2)}, u32[]{:S(2)}) %all-to-all-start.2) | async-done | bytes 1048608 | tf_op jit(solution)/shard_map/all_to_all | solution.py:547
  133.4 2.1 collective-permute-done.11.other_ref
  135.5 5.5 %attention.3.mine_ref = bf16[256,512]{1,0:T(8,128)(2,1)S(1)} custom-call(s32[4]{0:T(128)S(1)} %pad_add_fusion.1.scalars, bf16[256,512]{1,0:T(8,128)(2,1)S(1)} %query_rotate.2.query_ref, bf16[16,4,64,128]{3,2,1,0:T(8,128)(2,1)S(1)} %bitcast.51, bf16[16,4,64,128]{3,2,1,0:T(8,128)(2,1)S(1)} %collective-permute-done.11.other_ref), custom_call_target="tpu_custom_call" | custom-call | flops 536870912 | bytes 2621440 | tf_op jit(solution)/shard_map/attention/pallas_call | solution.py:129
  144.0 2.2 collective-permute-start.15
  147.8 4.2 %collective-permute-done.15 = bf16[256,512]{1,0:T(8,128)(2,1)S(1)} collective-permute-done((bf16[256,512]{1,0:T(8,128)(2,1)S(1)}, bf16[256,512]{1,0:T(8,128)(2,1)S(1)}, u32[]{:S(2)}, u32[]{:S(2)}) %collective-permute-start.15) | collective-permute-done | bytes 262176 | tf_op jit(solution)/shard_map/ppermute | solution.py:18
  152.0 3.8 %collective-permute-done.14 = bf16[256,512]{1,0:T(8,128)(2,1)S(1)} collective-permute-done((bf16[256,512]{1,0:T(8,128)(2,1)S(1)}, bf16[256,512]{1,0:T(8,128)(2,1)S(1)}, u32[]{:S(2)}, u32[]{:S(2)}) %collective-permute-start.14) | collective-permute-done | bytes 262176 | tf_op jit(solution)/shard_map/ppermute | solution.py:18
  155.8 3.4 %collective-permute-done.13 = bf16[256,512]{1,0:T(8,128)(2,1)S(1)} collective-permute-done((bf16[256,512]{1,0:T(8,128)(2,1)S(1)}, bf16[256,512]{1,0:T(8,128)(2,1)S(1)}, u32[]{:S(2)}, u32[]{:S(2)}) %collective-permute-start.13) | collective-permute-done | bytes 262176 | tf_op jit(solution)/shard_map/ppermute | solution.py:18
  159.5 2.6 %collective-permute-start.18 = (bf16[256,512]{1,0:T(8,128)(2,1)S(1)}, bf16[256,512]{1,0:T(8,128)(2,1)S(1)}, u32[]{:S(2)}, u32[]{:S(2)}) collective-permute-start(bf16[256,512]{1,0:T(8,128)(2,1)S(1)} %add_convert_fusion.own_ref.first_ref), channel_id=1, source_target_pairs={{0,2},{1,3},{2,0},{3,1},{4,6},{5,7},{6,4},{7,5},{8,10},{9,11},{10,... | collective-permute-start | bytes 786440 | tf_op jit(solution)/shard_map/ppermute | solution.py:18
  163.3 19.3 %all-gather.5.cloned.1.call-done.weight_hbm = bf16[2048,2304]{1,0:T(8,128)(2,1)} async-done(((bf16[128,2304]{1,0:T(8,128)(2,1)}), bf16[2048,2304]{1,0:T(8,128)(2,1)}) %all-gather.5.cloned.1.call-update) | async-done | bytes 9437200 | tf_op jit(solution)/shard_map/all_gather | solution.py:490
  182.6 2.7 %project_kv.3 = (f32[256,256]{1,0:T(8,128)S(1)}, f32[256,256]{1,0:T(8,128)S(1)}) custom-call(s32[3]{0:T(128)S(1)} %pad_add_fusion.place, bf16[256,512]{1,0:T(8,128)(2,1)S(1)} %add_convert_fusion.own_ref.first_ref, bf16[256,512]{1,0:T(8,128)(2,1)S(1)} %collective-permute-done.17.from_one, bf16[256,512]{1,0:T(8,128)(2,1)S(1)} %collective-permute-done.18.from_two, ...), custom_call_target="tpu_custom_call" | custom-call | flops 268435456 | bytes 1572864 | tf_op jit(solution)/shard_map/project_kv/pallas_call | solution.py:290
  189.9 5.0 %all-to-all-start.3 = ((bf16[16,256,128]{2,1,0:T(8,128)(2,1)}), bf16[16,256,128]{2,1,0:T(8,128)(2,1)S(1)}, u32[]{:S(2)}, u32[]{:S(2)}) async-start(bf16[16,256,128]{2,1,0:T(8,128)(2,1)} %copy-done.3), calls=%async_computation.3 | async-start | bytes 2097152 | tf_op jit(solution)/shard_map/all_to_all | solution.py:547
  194.9 6.1 %project_q.3 = (f32[256,512]{1,0:T(8,128)S(1)}, f32[256,512]{1,0:T(8,128)S(1)}, bf16[4,512,1024]{2,1,0:T(8,128)(2,1)}) custom-call(s32[3]{0:T(128)S(1)} %pad_add_fusion.place, bf16[256,512]{1,0:T(8,128)(2,1)S(1)} %add_convert_fusion.own_ref.first_ref, bf16[256,512]{1,0:T(8,128)(2,1)S(1)} %collective-permute-done.17.from_one, ...), custom_call_target="tpu_custom_call" | custom-call | flops 1073741824 | bytes 5242880 | tf_op jit(solution)/shard_map/project_q/pallas_call | solution.py:290
  203.3 7.9 %all-to-all-done.3 = bf16[16,256,128]{2,1,0:T(8,128)(2,1)S(1)} async-done(((bf16[16,256,128]{2,1,0:T(8,128)(2,1)}), bf16[16,256,128]{2,1,0:T(8,128)(2,1)S(1)}, u32[]{:S(2)}, u32[]{:S(2)}) %all-to-all-start.3) | async-done | bytes 1048608 | tf_op jit(solution)/shard_map/all_to_all | solution.py:547
  211.2 2.1 collective-permute-start.22
  213.6 2.1 collective-permute-done.22.other_ref
  215.6 3.0 %attention.5.mine_ref = bf16[128,512]{1,0:T(8,128)(2,1)S(1)} custom-call(s32[4]{0:T(128)S(1)} %pad_add_fusion.1.scalars, bf16[256,512]{1,0:T(8,128)(2,1)S(1)} %query_rotate.3.query_ref, bf16[16,4,64,128]{3,2,1,0:T(8,128)(2,1)S(1)} %bitcast.48, bf16[16,4,64,128]{3,2,1,0:T(8,128)(2,1)S(1)} %collective-permute-done.22.other_ref), custom_call_target="tpu_custom_call" | custom-call | flops 268435456 | bytes 2359296 | tf_op jit(solution)/shard_map/attention/pallas_call | solution.py:129
  219.2 3.3 %attention.4.mine_ref = bf16[128,512]{1,0:T(8,128)(2,1)S(1)} custom-call(s32[4]{0:T(128)S(1)} %pad_add_fusion.1.scalars, bf16[256,512]{1,0:T(8,128)(2,1)S(1)} %query_rotate.3.query_ref, bf16[16,4,64,128]{3,2,1,0:T(8,128)(2,1)S(1)} %bitcast.49, bf16[16,4,64,128]{3,2,1,0:T(8,128)(2,1)S(1)} %collective-permute-done.22.other_ref), custom_call_target="tpu_custom_call" | custom-call | flops 268435456 | bytes 2359296 | tf_op jit(solution)/shard_map/attention/pallas_call | solution.py:129
  224.2 2.7 %collective-permute-start.30 = (bf16[128,512]{1,0:T(8,128)(2,1)S(1)}, bf16[128,512]{1,0:T(8,128)(2,1)S(1)}, u32[]{:S(2)}, u32[]{:S(2)}) collective-permute-start(bf16[128,512]{1,0:T(8,128)(2,1)S(1)} %get-tuple-element.114), channel_id=1, source_target_pairs={{0,3},{1,0},{2,1},{3,2},{4,7},{5,4},{6,5},{7,6},{8,11},{9,8},{10,9... | collective-permute-start | bytes 393224 | tf_op jit(solution)/shard_map/ppermute | solution.py:18
  233.9 3.8 %collective-permute-start.16 = (bf16[256,512]{1,0:T(8,128)(2,1)S(1)}, bf16[256,512]{1,0:T(8,128)(2,1)S(1)}, u32[]{:S(2)}, u32[]{:S(2)}) collective-permute-start(bf16[256,512]{1,0:T(8,128)(2,1)S(1)} %add_convert_fusion.own_ref.first_ref), channel_id=1, source_target_pairs={{0,64},{64,0},{1,65},{65,1},{2,66},{66,2},{3,67},{67,3},{4,68},{68... | collective-permute-start | bytes 786440 | tf_op jit(solution)/shard_map/ppermute | solution.py:22
  237.6 3.7 %collective-permute-done.25 = bf16[128,512]{1,0:T(8,128)(2,1)S(1)} collective-permute-done((bf16[128,512]{1,0:T(8,128)(2,1)S(1)}, bf16[128,512]{1,0:T(8,128)(2,1)S(1)}, u32[]{:S(2)}, u32[]{:S(2)}) %collective-permute-start.25) | collective-permute-done | bytes 131104 | tf_op jit(solution)/shard_map/ppermute | solution.py:18
  (134 shorter events, 59.7 us)
Async XLA Ops:
  6.5 89.8 %all-gather.3.cloned.1.call-start = ((), (), s32[]{:S(2)}) async-start(), calls=%async_computation.4 | async-start | bytes 10027008 | tf_op jit(solution)/shard_map/all_gather | solution.py:490
  9.2 3.1 %collective-permute-start.8 = (bf16[128,2304]{1,0:T(8,128)(2,1)S(1)}, bf16[128,2304]{1,0:T(8,128)(2,1)S(1)}, u32[]{:S(2)}, u32[]{:S(2)}) collective-permute-start(bf16[128,2304]{1,0:T(8,128)(2,1)S(1)} %broadcast_select_fusion.2), channel_id=1, source_target_pairs={{0,64},{64,0},{1,65},{65,1},{2,66},{66,2},{3,67},{67,3},{4,68},{68... | collective-permute-start | bytes 1769480 | tf_op jit(solution)/shard_map/ppermute | solution.py:22
  13.7 168.9 %all-gather.5.cloned.1.call-start = ((), (), s32[]{:S(2)}) async-start(), calls=%async_computation.5 | async-start | bytes 10027008 | tf_op jit(solution)/shard_map/all_gather | solution.py:490
  17.0 2.7 %collective-permute-start = (bf16[128,80]{1,0:T(8,128)(2,1)S(1)}, bf16[128,80]{1,0:T(8,128)(2,1)S(1)}, u32[]{:S(2)}, u32[]{:S(2)}) collective-permute-start(bf16[128,80]{1,0:T(8,128)(2,1)S(1)} %merger_inner.1.mine_ref), channel_id=1, source_target_pairs={{0,64},{64,0},{1,65},{65,1},{2,66},{66,2},{3,67},{67,3},{4,68},{68... | collective-permute-start | bytes 61448 | tf_op jit(solution)/shard_map/ppermute | solution.py:22
  21.0 15.1 %collective-permute-start.3 = (bf16[256,512]{1,0:T(8,128)(2,1)S(1)}, bf16[256,512]{1,0:T(8,128)(2,1)S(1)}, u32[]{:S(2)}, u32[]{:S(2)}) collective-permute-start(bf16[256,512]{1,0:T(8,128)(2,1)S(1)} %get-tuple-element.63), channel_id=1, source_target_pairs={{0,3},{1,0},{2,1},{3,2},{4,7},{5,4},{6,5},{7,6},{8,11},{9,8},{10,9... | collective-permute-start | bytes 786440 | tf_op jit(solution)/shard_map/ppermute | solution.py:18
  24.9 14.4 %collective-permute-start.2 = (bf16[256,512]{1,0:T(8,128)(2,1)S(1)}, bf16[256,512]{1,0:T(8,128)(2,1)S(1)}, u32[]{:S(2)}, u32[]{:S(2)}) collective-permute-start(bf16[256,512]{1,0:T(8,128)(2,1)S(1)} %get-tuple-element.62), channel_id=1, source_target_pairs={{0,1},{1,2},{2,3},{3,0},{4,5},{5,6},{6,7},{7,4},{8,9},{9,10},{10,1... | collective-permute-start | bytes 786440 | tf_op jit(solution)/shard_map/ppermute | solution.py:18
  24.9 14.4 %collective-permute-start.1 = (bf16[256,512]{1,0:T(8,128)(2,1)S(1)}, bf16[256,512]{1,0:T(8,128)(2,1)S(1)}, u32[]{:S(2)}, u32[]{:S(2)}) collective-permute-start(bf16[256,512]{1,0:T(8,128)(2,1)S(1)} %get-tuple-element.61), channel_id=1, source_target_pairs={{0,2},{1,3},{2,0},{3,1},{4,6},{5,7},{6,4},{7,5},{8,10},{9,11},{10,... | collective-permute-start | bytes 786440 | tf_op jit(solution)/shard_map/ppermute | solution.py:18
  40.1 14.4 %all-to-all-start = ((bf16[16,16,512]{2,1,0:T(8,128)(2,1)}), bf16[16,16,512]{2,1,0:T(8,128)(2,1)S(1)}, u32[]{:S(2)}, u32[]{:S(2)}) async-start(bf16[16,16,512]{2,1,0:T(8,128)(2,1)} %bitcast.3), calls=%async_computation | async-start | bytes 524288 | tf_op jit(solution)/shard_map/all_to_all | solution.py:506
  55.3 13.8 %all-to-all-start.1 = ((bf16[16,16,512]{2,1,0:T(8,128)(2,1)}), bf16[16,16,512]{2,1,0:T(8,128)(2,1)S(1)}, u32[]{:S(2)}, u32[]{:S(2)}) async-start(bf16[16,16,512]{2,1,0:T(8,128)(2,1)} %broadcast_in_dim.36), calls=%async_computation.1 | async-start | bytes 524288 | tf_op jit(solution)/shard_map/all_to_all | solution.py:48
  69.4 9.8 %collective-permute-start.4 = (bf16[256,512]{1,0:T(8,128)(2,1)S(1)}, bf16[256,512]{1,0:T(8,128)(2,1)S(1)}, u32[]{:S(2)}, u32[]{:S(2)}) collective-permute-start(bf16[256,512]{1,0:T(8,128)(2,1)S(1)} %fusion.own_ref), channel_id=1, source_target_pairs={{0,1},{1,2},{2,3},{3,0},{4,5},{5,6},{6,7},{7,4},{8,9},{9,10},{10,1... | collective-permute-start | bytes 786440 | tf_op jit(solution)/shard_map/ppermute | solution.py:18
  69.5 10.4 %collective-permute-start.5 = (bf16[256,512]{1,0:T(8,128)(2,1)S(1)}, bf16[256,512]{1,0:T(8,128)(2,1)S(1)}, u32[]{:S(2)}, u32[]{:S(2)}) collective-permute-start(bf16[256,512]{1,0:T(8,128)(2,1)S(1)} %fusion.own_ref), channel_id=1, source_target_pairs={{0,2},{1,3},{2,0},{3,1},{4,6},{5,7},{6,4},{7,5},{8,10},{9,11},{10,... | collective-permute-start | bytes 786440 | tf_op jit(solution)/shard_map/ppermute | solution.py:18
  71.5 8.4 %collective-permute-start.6 = (bf16[256,512]{1,0:T(8,128)(2,1)S(1)}, bf16[256,512]{1,0:T(8,128)(2,1)S(1)}, u32[]{:S(2)}, u32[]{:S(2)}) collective-permute-start(bf16[256,512]{1,0:T(8,128)(2,1)S(1)} %fusion.own_ref), channel_id=1, source_target_pairs={{0,3},{1,0},{2,1},{3,2},{4,7},{5,4},{6,5},{7,6},{8,11},{9,8},{10,9... | collective-permute-start | bytes 786440 | tf_op jit(solution)/shard_map/ppermute | solution.py:18
  72.7 6.5 %collective-permute-start.7 = (f32[16,128]{1,0:T(8,128)S(1)}, f32[16,128]{1,0:T(8,128)S(1)}, u32[]{:S(2)}, u32[]{:S(2)}) collective-permute-start(f32[16,128]{1,0:T(8,128)S(1)} %select_bitcast_fusion), channel_id=1, source_target_pairs={{0,64},{64,0},{1,65},{65,1},{2,66},{66,2},{3,67},{67,3},{4,68},{68... | collective-permute-start | bytes 24584 | tf_op jit(solution)/shard_map/ppermute | solution.py:22
  103.4 28.0 %all-to-all-start.2 = ((bf16[16,256,128]{2,1,0:T(8,128)(2,1)}), bf16[16,256,128]{2,1,0:T(8,128)(2,1)S(1)}, u32[]{:S(2)}, u32[]{:S(2)}) async-start(bf16[16,256,128]{2,1,0:T(8,128)(2,1)} %copy-done.4), calls=%async_computation.2 | async-start | bytes 2097152 | tf_op jit(solution)/shard_map/all_to_all | solution.py:547
  131.4 4.1 %collective-permute-start.11 = (bf16[16,4,64,128]{3,2,1,0:T(8,128)(2,1)S(1)}, bf16[16,4,64,128]{3,2,1,0:T(8,128)(2,1)S(1)}, u32[]{:S(2)}, u32[]{:S(2)}) collective-permute-start(bf16[16,4,64,128]{3,2,1,0:T(8,128)(2,1)S(1)} %bitcast.50), channel_id=1, source_target_pairs={{0,64},{64,0},{1,65},{65,1},{2,66},{66,2},{3,67},{67,3},{4,68},{68... | collective-permute-start | bytes 3145736 | tf_op jit(solution)/shard_map/ppermute | solution.py:22
  144.0 8.1 %collective-permute-start.15 = (bf16[256,512]{1,0:T(8,128)(2,1)S(1)}, bf16[256,512]{1,0:T(8,128)(2,1)S(1)}, u32[]{:S(2)}, u32[]{:S(2)}) collective-permute-start(bf16[256,512]{1,0:T(8,128)(2,1)S(1)} %get-tuple-element.91), channel_id=1, source_target_pairs={{0,3},{1,0},{2,1},{3,2},{4,7},{5,4},{6,5},{7,6},{8,11},{9,8},{10,9... | collective-permute-start | bytes 786440 | tf_op jit(solution)/shard_map/ppermute | solution.py:18
  146.2 9.6 %collective-permute-start.14 = (bf16[256,512]{1,0:T(8,128)(2,1)S(1)}, bf16[256,512]{1,0:T(8,128)(2,1)S(1)}, u32[]{:S(2)}, u32[]{:S(2)}) collective-permute-start(bf16[256,512]{1,0:T(8,128)(2,1)S(1)} %get-tuple-element.90), channel_id=1, source_target_pairs={{0,1},{1,2},{2,3},{3,0},{4,5},{5,6},{6,7},{7,4},{8,9},{9,10},{10,1... | collective-permute-start | bytes 786440 | tf_op jit(solution)/shard_map/ppermute | solution.py:18
  146.2 13.0 %collective-permute-start.13 = (bf16[256,512]{1,0:T(8,128)(2,1)S(1)}, bf16[256,512]{1,0:T(8,128)(2,1)S(1)}, u32[]{:S(2)}, u32[]{:S(2)}) collective-permute-start(bf16[256,512]{1,0:T(8,128)(2,1)S(1)} %get-tuple-element.89), channel_id=1, source_target_pairs={{0,2},{1,3},{2,0},{3,1},{4,6},{5,7},{6,4},{7,5},{8,10},{9,11},{10,... | collective-permute-start | bytes 786440 | tf_op jit(solution)/shard_map/ppermute | solution.py:18
  159.4 23.2 %collective-permute-start.17 = (bf16[256,512]{1,0:T(8,128)(2,1)S(1)}, bf16[256,512]{1,0:T(8,128)(2,1)S(1)}, u32[]{:S(2)}, u32[]{:S(2)}) collective-permute-start(bf16[256,512]{1,0:T(8,128)(2,1)S(1)} %add_convert_fusion.own_ref.first_ref), channel_id=1, source_target_pairs={{0,1},{1,2},{2,3},{3,0},{4,5},{5,6},{6,7},{7,4},{8,9},{9,10},{10,1... | collective-permute-start | bytes 786440 | tf_op jit(solution)/shard_map/ppermute | solution.py:18
  159.5 23.2 %collective-permute-start.18 = (bf16[256,512]{1,0:T(8,128)(2,1)S(1)}, bf16[256,512]{1,0:T(8,128)(2,1)S(1)}, u32[]{:S(2)}, u32[]{:S(2)}) collective-permute-start(bf16[256,512]{1,0:T(8,128)(2,1)S(1)} %add_convert_fusion.own_ref.first_ref), channel_id=1, source_target_pairs={{0,2},{1,3},{2,0},{3,1},{4,6},{5,7},{6,4},{7,5},{8,10},{9,11},{10,... | collective-permute-start | bytes 786440 | tf_op jit(solution)/shard_map/ppermute | solution.py:18
  162.1 20.5 %collective-permute-start.19 = (bf16[256,512]{1,0:T(8,128)(2,1)S(1)}, bf16[256,512]{1,0:T(8,128)(2,1)S(1)}, u32[]{:S(2)}, u32[]{:S(2)}) collective-permute-start(bf16[256,512]{1,0:T(8,128)(2,1)S(1)} %add_convert_fusion.own_ref.first_ref), channel_id=1, source_target_pairs={{0,3},{1,0},{2,1},{3,2},{4,7},{5,4},{6,5},{7,6},{8,11},{9,8},{10,9... | collective-permute-start | bytes 786440 | tf_op jit(solution)/shard_map/ppermute | solution.py:18
  189.9 21.3 %all-to-all-start.3 = ((bf16[16,256,128]{2,1,0:T(8,128)(2,1)}), bf16[16,256,128]{2,1,0:T(8,128)(2,1)S(1)}, u32[]{:S(2)}, u32[]{:S(2)}) async-start(bf16[16,256,128]{2,1,0:T(8,128)(2,1)} %copy-done.3), calls=%async_computation.3 | async-start | bytes 2097152 | tf_op jit(solution)/shard_map/all_to_all | solution.py:547
  211.2 4.4 %collective-permute-start.22 = (bf16[16,4,64,128]{3,2,1,0:T(8,128)(2,1)S(1)}, bf16[16,4,64,128]{3,2,1,0:T(8,128)(2,1)S(1)}, u32[]{:S(2)}, u32[]{:S(2)}) collective-permute-start(bf16[16,4,64,128]{3,2,1,0:T(8,128)(2,1)S(1)} %bitcast.47), channel_id=1, source_target_pairs={{0,64},{64,0},{1,65},{65,1},{2,66},{66,2},{3,67},{67,3},{4,68},{68... | collective-permute-start | bytes 3145736 | tf_op jit(solution)/shard_map/ppermute | solution.py:22
  218.7 3.9 %collective-permute-start.27 = (bf16[128,512]{1,0:T(8,128)(2,1)S(1)}, bf16[128,512]{1,0:T(8,128)(2,1)S(1)}, u32[]{:S(2)}, u32[]{:S(2)}) collective-permute-start(bf16[128,512]{1,0:T(8,128)(2,1)S(1)} %attention.5.mine_ref), channel_id=1, source_target_pairs={{0,64},{64,0},{1,65},{65,1},{2,66},{66,2},{3,67},{67,3},{4,68},{68... | collective-permute-start | bytes 393224 | tf_op jit(solution)/shard_map/ppermute | solution.py:22
  222.4 6.2 %collective-permute-start.23 = (bf16[128,512]{1,0:T(8,128)(2,1)S(1)}, bf16[128,512]{1,0:T(8,128)(2,1)S(1)}, u32[]{:S(2)}, u32[]{:S(2)}) collective-permute-start(bf16[128,512]{1,0:T(8,128)(2,1)S(1)} %attention.4.mine_ref), channel_id=1, source_target_pairs={{0,64},{64,0},{1,65},{65,1},{2,66},{66,2},{3,67},{67,3},{4,68},{68... | collective-permute-start | bytes 393224 | tf_op jit(solution)/shard_map/ppermute | solution.py:22
  224.2 7.6 %collective-permute-start.30 = (bf16[128,512]{1,0:T(8,128)(2,1)S(1)}, bf16[128,512]{1,0:T(8,128)(2,1)S(1)}, u32[]{:S(2)}, u32[]{:S(2)}) collective-permute-start(bf16[128,512]{1,0:T(8,128)(2,1)S(1)} %get-tuple-element.114), channel_id=1, source_target_pairs={{0,3},{1,0},{2,1},{3,2},{4,7},{5,4},{6,5},{7,6},{8,11},{9,8},{10,9... | collective-permute-start | bytes 393224 | tf_op jit(solution)/shard_map/ppermute | solution.py:18
  226.9 6.9 %collective-permute-start.29 = (bf16[128,512]{1,0:T(8,128)(2,1)S(1)}, bf16[128,512]{1,0:T(8,128)(2,1)S(1)}, u32[]{:S(2)}, u32[]{:S(2)}) collective-permute-start(bf16[128,512]{1,0:T(8,128)(2,1)S(1)} %get-tuple-element.113), channel_id=1, source_target_pairs={{0,1},{1,2},{2,3},{3,0},{4,5},{5,6},{6,7},{7,4},{8,9},{9,10},{10,1... | collective-permute-start | bytes 393224 | tf_op jit(solution)/shard_map/ppermute | solution.py:18
  226.9 10.7 %collective-permute-start.28 = (bf16[128,512]{1,0:T(8,128)(2,1)S(1)}, bf16[128,512]{1,0:T(8,128)(2,1)S(1)}, u32[]{:S(2)}, u32[]{:S(2)}) collective-permute-start(bf16[128,512]{1,0:T(8,128)(2,1)S(1)} %get-tuple-element.112), channel_id=1, source_target_pairs={{0,2},{1,3},{2,0},{3,1},{4,6},{5,7},{6,4},{7,5},{8,10},{9,11},{10,... | collective-permute-start | bytes 393224 | tf_op jit(solution)/shard_map/ppermute | solution.py:18
  230.1 7.5 %collective-permute-start.26 = (bf16[128,512]{1,0:T(8,128)(2,1)S(1)}, bf16[128,512]{1,0:T(8,128)(2,1)S(1)}, u32[]{:S(2)}, u32[]{:S(2)}) collective-permute-start(bf16[128,512]{1,0:T(8,128)(2,1)S(1)} %get-tuple-element.110), channel_id=1, source_target_pairs={{0,3},{1,0},{2,1},{3,2},{4,7},{5,4},{6,5},{7,6},{8,11},{9,8},{10,9... | collective-permute-start | bytes 393224 | tf_op jit(solution)/shard_map/ppermute | solution.py:18
  231.2 10.1 %collective-permute-start.25 = (bf16[128,512]{1,0:T(8,128)(2,1)S(1)}, bf16[128,512]{1,0:T(8,128)(2,1)S(1)}, u32[]{:S(2)}, u32[]{:S(2)}) collective-permute-start(bf16[128,512]{1,0:T(8,128)(2,1)S(1)} %get-tuple-element.109), channel_id=1, source_target_pairs={{0,1},{1,2},{2,3},{3,0},{4,5},{5,6},{6,7},{7,4},{8,9},{9,10},{10,1... | collective-permute-start | bytes 393224 | tf_op jit(solution)/shard_map/ppermute | solution.py:18
  231.8 9.5 %collective-permute-start.24 = (bf16[128,512]{1,0:T(8,128)(2,1)S(1)}, bf16[128,512]{1,0:T(8,128)(2,1)S(1)}, u32[]{:S(2)}, u32[]{:S(2)}) collective-permute-start(bf16[128,512]{1,0:T(8,128)(2,1)S(1)} %get-tuple-element.108), channel_id=1, source_target_pairs={{0,2},{1,3},{2,0},{3,1},{4,6},{5,7},{6,4},{7,5},{8,10},{9,11},{10,... | collective-permute-start | bytes 393224 | tf_op jit(solution)/shard_map/ppermute | solution.py:18
  233.9 9.0 %collective-permute-start.16 = (bf16[256,512]{1,0:T(8,128)(2,1)S(1)}, bf16[256,512]{1,0:T(8,128)(2,1)S(1)}, u32[]{:S(2)}, u32[]{:S(2)}) collective-permute-start(bf16[256,512]{1,0:T(8,128)(2,1)S(1)} %add_convert_fusion.own_ref.first_ref), channel_id=1, source_target_pairs={{0,64},{64,0},{1,65},{65,1},{2,66},{66,2},{3,67},{67,3},{4,68},{68... | collective-permute-start | bytes 786440 | tf_op jit(solution)/shard_map/ppermute | solution.py:22
  (20 other events, 68.7 us)
Sparse Core Ops, SparseCore 0:
  13.8 82.5 all-gather.2
  98.5 84.0 all-gather.4

commit v11 on v9

--- a/solution.py
+++ b/solution.py
@@ -136,6 +136,64 @@
         compiler_params=pltpu.CompilerParams(vmem_limit_bytes=16 << 20),
         name="attention",
     )(scalars, query, mine, other)
+
+
+def weight_packed_kernel(place, query_ref, keyval_ref, out_weight_ref, keep_ref, send_ref):
+    rows = keep_ref.shape[0]
+    heads, head = query_ref.shape[1] // 2, keyval_ref.shape[1] // 2
+
+    def write(ref, core):
+        here = slice(core * rows, (core + 1) * rows)
+        turned = out_weight_ref[:, here].T
+        at = 0
+        for source, width in ((keyval_ref[here, :], head), (query_ref[here, :], heads), (turned, heads)):
+            for half in (core, 1 - core):
+                ref[:, at : at + width] = source[:, half * width : (half + 1) * width]
+                at += width
+
+    for core in range(2):
+
+        @pl.when(place[0] == core)
+        def _():
+            write(keep_ref, core)
+            write(send_ref, 1 - core)
+
+
+def weight_packed(place, query, keyval, out_weight):
+    whole = pl.BlockSpec(memory_space=pltpu.VMEM)
+    shard = jax.ShapeDtypeStruct(
+        (query.shape[0] // 2, query.shape[1] + keyval.shape[1] + out_weight.shape[0]), query.dtype
+    )
+    return pl.pallas_call(
+        weight_packed_kernel,
+        out_shape=(shard, shard),
+        in_specs=[pl.BlockSpec(memory_space=pltpu.SMEM)] + [whole] * 3,
+        out_specs=(whole, whole),
+        compiler_params=pltpu.CompilerParams(vmem_limit_bytes=12 << 20),
+        name="weight_packed",
+    )(place, query, keyval, out_weight)
+
+
+def weight_picked_kernel(place, keep_ref, other_ref, out_ref, *, home):
+    @pl.when(place[0] == home)
+    def _():
+        out_ref[...] = keep_ref[...]
+
+    @pl.when(place[0] != home)
+    def _():
+        out_ref[...] = other_ref[...]
+
+
+def weight_picked(place, keep, other, home):
+    whole = pl.BlockSpec(memory_space=pltpu.VMEM)
+    return pl.pallas_call(
+        functools.partial(weight_picked_kernel, home=home),
+        out_shape=jax.ShapeDtypeStruct(keep.shape, keep.dtype),
+        in_specs=[pl.BlockSpec(memory_space=pltpu.SMEM), whole, whole],
+        out_specs=whole,
+        compiler_params=pltpu.CompilerParams(vmem_limit_bytes=8 << 20),
+        name="weight_picked",
+    )(place, keep, other)
 
 
 def merger_kernel(patches_ref, gain_ref, weight_ref, out_ref):
@@ -447,25 +505,14 @@
     keyval_own = keyval_weight[0].reshape(keyval_weight.shape[1], 2 * head_size)
     out_own = out_weight[0]
     heads_half = query_own.shape[1] // 2
-    weight_half = query_own.shape[0] // 2
-
-    def packed(core):
-        keep_rows = slice(core * weight_half, (core + 1) * weight_half)
-        query_rows, keyval_rows = query_own[keep_rows], keyval_own[keep_rows]
-        out_rows = out_own[:, keep_rows].T
-        halves = (core, 1 - core)
-        parts = [keyval_rows[:, half * head_size : (half + 1) * head_size] for half in halves]
-        parts += [query_rows[:, half * heads_half : (half + 1) * heads_half] for half in halves]
-        parts += [out_rows[:, half * heads_half : (half + 1) * heads_half] for half in halves]
-        return jnp.concatenate(parts, axis=1)
-
-    for_first, for_second = packed(0), packed(1)
-    weight_keep = jnp.where(first_core, for_first, for_second)
-    weight_other = swapped(jnp.where(first_core, for_second, for_first))
+
+    place = jnp.stack([section_index, cycle_index, model_index]).astype(jnp.int32)
+    weight_keep, weight_send = weight_packed(place, query_own, keyval_own, out_own)
+    weight_other = swapped(weight_send)
     keyval_width = 2 * head_size
     weight_full = []
     for home in range(layers):
-        mine = jnp.where(section_index == home, weight_keep, weight_other)
+        mine = weight_picked(place, weight_keep, weight_other, home)
         weight_full.append(lax.all_gather(mine, "blk", axis=0, tiled=True))
     gain_half = norm_gain[0].reshape(-1, 2, lane)
     gain_keep = jnp.where(first_core, gain_half[:, 0], gain_half[:, 1])
@@ -477,7 +524,6 @@
     ]
 
     inner = merger_inner(patches, merge_gain, merge_first)
-    place = jnp.stack([section_index, cycle_index, model_index]).astype(jnp.int32)
     own, *terms = merger_outer(place, inner, swapped(inner), merge_second, n_mp)
     total = own.astype(jnp.float32)
     for part in [moved(terms[by - 1], "mp", by) for by in (2, 1, 3)]:

time: 250 us -> 252 us (level)
  Pallas kernels: 35.8 us -> 42.6 us
    all_gather x2, waiting for transfers between devices: 33.7 us -> 30.1 us  [local(): weight_full.append(lax.all_gather(mine, 'blk', axis=0, tiled=True))]
    pallas_call x0 -> x3, Pallas kernels: none -> 3.62 us  [the longest x2 2.88 us: weight_picked(): pl.pallas_call(functools.partial(weight_picked_kernel, home=home), out_sh...]
    pallas_call x2, Pallas kernels: 11.1 us -> 14.2 us  [attention(): pl.pallas_call(functools.partial(attention_kernel, chunk_runs=mine.shape[...]
    unnamed x32 -> x27, local copies, waits for them, and re-layouts: 4.33 us -> 6.86 us
  transfers between devices with their start and end apart: 34 -> 34, of which waited for: 27 -> 26; matrix products, arithmetic and copies ran while one was open for 4% -> 4% of each run, Pallas kernels for 10% -> 11%
where the time goes in v11:
time: 252 us
  waiting for transfers between devices  124 us (49%)
  starting transfers between devices  56.9 us (23%)
  Pallas kernels  42.6 us (17%)
  between operations  13.8 us (5%)
  local copies, waits for them, and re-layouts  9.83 us (4%)
  other arithmetic  4.59 us (2%)
    ppermute x15, waiting for transfers between devices, moved(): lax.ppermute(value, axis, [(i, (i + by) % size) for i in range(size)])  36 us
    all_gather x2, waiting for transfers between devices, local(): weight_full.append(lax.all_gather(mine, 'blk', axis=0, tiled=True))  30.1 us
    all_to_all x2, waiting for transfers between devices, local(): gathered = lax.all_to_all(keyval_copies, 'blk', 0, 0, tiled=True)  24 us
    ppermute x15, starting transfers between devices, moved(): lax.ppermute(value, axis, [(i, (i + by) % size) for i in range(size)])  19.1 us
    ppermute x13, starting transfers between devices, swapped(): return lax.ppermute(value, 'section', [(0, 1), (1, 0)])  17.9 us
    pallas_call x4, Pallas kernels, project_in(): pl.pallas_call(functools.partial(project_in_kernel, at=at), out_shape=out...  17.6 us
    ppermute x13, waiting for transfers between devices, swapped(): return lax.ppermute(value, 'section', [(0, 1), (1, 0)])  15.4 us
    pallas_call x2, Pallas kernels, attention(): pl.pallas_call(functools.partial(attention_kernel, chunk_runs=mine.shape[...  14.2 us
  transfers between devices with their start and end apart: 34, of which 26 were waited for; matrix products, arithmetic and copies ran while one was open for 4% of the time, Pallas kernels for 11%

profile of v11, /device:TPU:1, one launch (start us, length us, event | category | flops | bytes accessed | tf_op | source)
XLA Modules:
  0.0 252.2 jit_solution(16106456919073203329)
XLA Ops:
  24.3 3.9 %collective-permute-start.3 = (bf16[256,512]{1,0:T(8,128)(2,1)S(1)}, bf16[256,512]{1,0:T(8,128)(2,1)S(1)}, u32[]{:S(2)}, u32[]{:S(2)}) collective-permute-start(bf16[256,512]{1,0:T(8,128)(2,1)S(1)} %get-tuple-element.61), channel_id=1, source_target_pairs={{0,3},{1,0},{2,1},{3,2},{4,7},{5,4},{6,5},{7,6},{8,11},{9,8},{10,9... | collective-permute-start | bytes 786440 | tf_op jit(solution)/shard_map/ppermute | solution.py:18
  30.4 9.0 %collective-permute-done.3 = bf16[256,512]{1,0:T(8,128)(2,1)S(1)} collective-permute-done((bf16[256,512]{1,0:T(8,128)(2,1)S(1)}, bf16[256,512]{1,0:T(8,128)(2,1)S(1)}, u32[]{:S(2)}, u32[]{:S(2)}) %collective-permute-start.3) | collective-permute-done | bytes 262176 | tf_op jit(solution)/shard_map/ppermute | solution.py:18
  39.4 3.1 %collective-permute-done.2 = bf16[256,512]{1,0:T(8,128)(2,1)S(1)} collective-permute-done((bf16[256,512]{1,0:T(8,128)(2,1)S(1)}, bf16[256,512]{1,0:T(8,128)(2,1)S(1)}, u32[]{:S(2)}, u32[]{:S(2)}) %collective-permute-start.2) | collective-permute-done | bytes 262176 | tf_op jit(solution)/shard_map/ppermute | solution.py:18
  43.4 6.7 %all-to-all-start = ((bf16[16,16,512]{2,1,0:T(8,128)(2,1)}), bf16[16,16,512]{2,1,0:T(8,128)(2,1)S(1)}, u32[]{:S(2)}, u32[]{:S(2)}) async-start(bf16[16,16,512]{2,1,0:T(8,128)(2,1)} %bitcast.3), calls=%async_computation | async-start | bytes 524288 | tf_op jit(solution)/shard_map/all_to_all | solution.py:531
  51.6 8.2 %all-to-all-done = bf16[16,16,512]{2,1,0:T(8,128)(2,1)S(1)} async-done(((bf16[16,16,512]{2,1,0:T(8,128)(2,1)}), bf16[16,16,512]{2,1,0:T(8,128)(2,1)S(1)}, u32[]{:S(2)}, u32[]{:S(2)}) %all-to-all-start) | async-done | bytes 262176 | tf_op jit(solution)/shard_map/all_to_all | solution.py:531
  60.5 3.5 %all-to-all-start.1 = ((bf16[16,16,512]{2,1,0:T(8,128)(2,1)}), bf16[16,16,512]{2,1,0:T(8,128)(2,1)S(1)}, u32[]{:S(2)}, u32[]{:S(2)}) async-start(bf16[16,16,512]{2,1,0:T(8,128)(2,1)} %broadcast_in_dim.36), calls=%async_computation.1 | async-start | bytes 524288 | tf_op jit(solution)/shard_map/all_to_all | solution.py:48
  64.1 10.6 %all-to-all-done.1 = bf16[16,16,512]{2,1,0:T(8,128)(2,1)S(1)} async-done(((bf16[16,16,512]{2,1,0:T(8,128)(2,1)}), bf16[16,16,512]{2,1,0:T(8,128)(2,1)S(1)}, u32[]{:S(2)}, u32[]{:S(2)}) %all-to-all-start.1) | async-done | bytes 262176 | tf_op jit(solution)/shard_map/all_to_all | solution.py:48
  75.2 2.6 %collective-permute-start.6 = (bf16[256,512]{1,0:T(8,128)(2,1)S(1)}, bf16[256,512]{1,0:T(8,128)(2,1)S(1)}, u32[]{:S(2)}, u32[]{:S(2)}) collective-permute-start(bf16[256,512]{1,0:T(8,128)(2,1)S(1)} %fusion.own_ref), channel_id=1, source_target_pairs={{0,3},{1,0},{2,1},{3,2},{4,7},{5,4},{6,5},{7,6},{8,11},{9,8},{10,9... | collective-permute-start | bytes 786440 | tf_op jit(solution)/shard_map/ppermute | solution.py:18
  77.7 4.9 %collective-permute-start.7 = (f32[16,128]{1,0:T(8,128)S(1)}, f32[16,128]{1,0:T(8,128)S(1)}, u32[]{:S(2)}, u32[]{:S(2)}) collective-permute-start(f32[16,128]{1,0:T(8,128)S(1)} %select_bitcast_fusion), channel_id=1, source_target_pairs={{0,64},{64,0},{1,65},{65,1},{2,66},{66,2},{3,67},{67,3},{4,68},{68... | collective-permute-start | bytes 24584 | tf_op jit(solution)/shard_map/ppermute | solution.py:22
  85.8 12.4 %all-gather.3.cloned.1.call-done.weight_hbm = bf16[2048,2304]{1,0:T(8,128)(2,1)} async-done(((bf16[128,2304]{1,0:T(8,128)(2,1)}), bf16[2048,2304]{1,0:T(8,128)(2,1)}) %all-gather.3.cloned.1.call-update) | async-done | bytes 9437200 | tf_op jit(solution)/shard_map/all_gather | solution.py:516
  98.3 2.7 %project_kv.2 = (f32[256,256]{1,0:T(8,128)S(1)}, f32[256,256]{1,0:T(8,128)S(1)}) custom-call(s32[3]{0:T(128)S(1)} %pad_add_fusion.place, bf16[256,512]{1,0:T(8,128)(2,1)S(1)} %fusion.own_ref, bf16[256,512]{1,0:T(8,128)(2,1)S(1)} %collective-permute-done.4.from_one, bf16[256,512]{1,0:T(8,128)(2,1)S(1)} %collective-permute-done.5.from_two, ...), custom_call_target="tpu_custom_call" | custom-call | flops 268435456 | bytes 1572864 | tf_op jit(solution)/shard_map/project_kv/pallas_call | solution.py:343
  104.0 4.6 %all-to-all-start.2 = ((bf16[16,256,128]{2,1,0:T(8,128)(2,1)}), bf16[16,256,128]{2,1,0:T(8,128)(2,1)S(1)}, u32[]{:S(2)}, u32[]{:S(2)}) async-start(bf16[16,256,128]{2,1,0:T(8,128)(2,1)} %copy-done.4), calls=%async_computation.2 | async-start | bytes 2097152 | tf_op jit(solution)/shard_map/all_to_all | solution.py:572
  108.7 6.1 %project_q.2 = (f32[256,512]{1,0:T(8,128)S(1)}, f32[256,512]{1,0:T(8,128)S(1)}, bf16[4,512,1024]{2,1,0:T(8,128)(2,1)}) custom-call(s32[3]{0:T(128)S(1)} %pad_add_fusion.place, bf16[256,512]{1,0:T(8,128)(2,1)S(1)} %fusion.own_ref, bf16[256,512]{1,0:T(8,128)(2,1)S(1)} %collective-permute-done.4.from_one, bf16[256,512]{1,0:T(8,128)(2,1)S(1)} %collective-permute-done.5.from_two, ...), custom_call_target="tpu_custom_call" | custom-call | flops 1073741824 | bytes 5242880 | tf_op jit(solution)/shard_map/project_q/pallas_call | solution.py:343
  117.0 16.1 %all-to-all-done.2 = bf16[16,256,128]{2,1,0:T(8,128)(2,1)S(1)} async-done(((bf16[16,256,128]{2,1,0:T(8,128)(2,1)}), bf16[16,256,128]{2,1,0:T(8,128)(2,1)S(1)}, u32[]{:S(2)}, u32[]{:S(2)}) %all-to-all-start.2) | async-done | bytes 1048608 | tf_op jit(solution)/shard_map/all_to_all | solution.py:572
  134.6 2.0 collective-permute-done.11.other_ref
  136.6 7.1 %attention.2.mine_ref = bf16[256,512]{1,0:T(8,128)(2,1)S(1)} custom-call(s32[4]{0:T(128)S(1)} %pad_add_fusion.1.scalars, bf16[256,512]{1,0:T(8,128)(2,1)S(1)} %query_rotate.2.query_ref, bf16[16,4,64,128]{3,2,1,0:T(8,128)(2,1)S(1)} %bitcast.38, bf16[16,4,64,128]{3,2,1,0:T(8,128)(2,1)S(1)} %collective-permute-done.11.other_ref), custom_call_target="tpu_custom_call" | custom-call | flops 134217728 | bytes 2621440 | tf_op jit(solution)/shard_map/attention/pallas_call | solution.py:126
  149.6 4.8 %collective-permute-done.15 = bf16[256,512]{1,0:T(8,128)(2,1)S(1)} collective-permute-done((bf16[256,512]{1,0:T(8,128)(2,1)S(1)}, bf16[256,512]{1,0:T(8,128)(2,1)S(1)}, u32[]{:S(2)}, u32[]{:S(2)}) %collective-permute-start.15) | collective-permute-done | bytes 262176 | tf_op jit(solution)/shard_map/ppermute | solution.py:18
  154.4 3.1 %collective-permute-done.14 = bf16[256,512]{1,0:T(8,128)(2,1)S(1)} collective-permute-done((bf16[256,512]{1,0:T(8,128)(2,1)S(1)}, bf16[256,512]{1,0:T(8,128)(2,1)S(1)}, u32[]{:S(2)}, u32[]{:S(2)}) %collective-permute-start.14) | collective-permute-done | bytes 262176 | tf_op jit(solution)/shard_map/ppermute | solution.py:18
  157.4 3.6 %collective-permute-done.13 = bf16[256,512]{1,0:T(8,128)(2,1)S(1)} collective-permute-done((bf16[256,512]{1,0:T(8,128)(2,1)S(1)}, bf16[256,512]{1,0:T(8,128)(2,1)S(1)}, u32[]{:S(2)}, u32[]{:S(2)}) %collective-permute-start.13) | collective-permute-done | bytes 262176 | tf_op jit(solution)/shard_map/ppermute | solution.py:18
  161.3 2.5 collective-permute-start.18
  165.0 17.7 %all-gather.5.cloned.1.call-done.weight_hbm = bf16[2048,2304]{1,0:T(8,128)(2,1)} async-done(((bf16[128,2304]{1,0:T(8,128)(2,1)}), bf16[2048,2304]{1,0:T(8,128)(2,1)}) %all-gather.5.cloned.1.call-update) | async-done | bytes 9437200 | tf_op jit(solution)/shard_map/all_gather | solution.py:516
  182.6 2.7 %project_kv.3 = (f32[256,256]{1,0:T(8,128)S(1)}, f32[256,256]{1,0:T(8,128)S(1)}) custom-call(s32[3]{0:T(128)S(1)} %pad_add_fusion.place, bf16[256,512]{1,0:T(8,128)(2,1)S(1)} %add_convert_fusion.1.own_ref.first_ref, bf16[256,512]{1,0:T(8,128)(2,1)S(1)} %collective-permute-done.17.from_one, bf16[256,512]{1,0:T(8,128)(2,1)S(1)} %collective-permute-done.18.from_two, ...), custom_call_target="tpu_custom_call" | custom-call | flops 268435456 | bytes 1572864 | tf_op jit(solution)/shard_map/project_kv/pallas_call | solution.py:343
  188.4 5.0 %all-to-all-start.3 = ((bf16[16,256,128]{2,1,0:T(8,128)(2,1)}), bf16[16,256,128]{2,1,0:T(8,128)(2,1)S(1)}, u32[]{:S(2)}, u32[]{:S(2)}) async-start(bf16[16,256,128]{2,1,0:T(8,128)(2,1)} %copy-done.3), calls=%async_computation.3 | async-start | bytes 2097152 | tf_op jit(solution)/shard_map/all_to_all | solution.py:572
  193.4 6.1 %project_q.3 = (f32[256,512]{1,0:T(8,128)S(1)}, f32[256,512]{1,0:T(8,128)S(1)}, bf16[4,512,1024]{2,1,0:T(8,128)(2,1)}) custom-call(s32[3]{0:T(128)S(1)} %pad_add_fusion.place, bf16[256,512]{1,0:T(8,128)(2,1)S(1)} %add_convert_fusion.1.own_ref.first_ref, bf16[256,512]{1,0:T(8,128)(2,1)S(1)} %collective-permute-done.17.from_one, ...), custom_call_target="tpu_custom_call" | custom-call | flops 1073741824 | bytes 5242880 | tf_op jit(solution)/shard_map/project_q/pallas_call | solution.py:343
  201.8 7.9 %all-to-all-done.3 = bf16[16,256,128]{2,1,0:T(8,128)(2,1)S(1)} async-done(((bf16[16,256,128]{2,1,0:T(8,128)(2,1)}), bf16[16,256,128]{2,1,0:T(8,128)(2,1)S(1)}, u32[]{:S(2)}, u32[]{:S(2)}) %all-to-all-start.3) | async-done | bytes 1048608 | tf_op jit(solution)/shard_map/all_to_all | solution.py:572
  209.7 2.1 collective-permute-start.22
  212.1 2.0 collective-permute-done.22.other_ref
  214.1 7.1 %attention.3.mine_ref = bf16[256,512]{1,0:T(8,128)(2,1)S(1)} custom-call(s32[4]{0:T(128)S(1)} %pad_add_fusion.1.scalars, bf16[256,512]{1,0:T(8,128)(2,1)S(1)} %query_rotate.3.query_ref, bf16[16,4,64,128]{3,2,1,0:T(8,128)(2,1)S(1)} %bitcast.36, bf16[16,4,64,128]{3,2,1,0:T(8,128)(2,1)S(1)} %collective-permute-done.22.other_ref), custom_call_target="tpu_custom_call" | custom-call | flops 134217728 | bytes 2621440 | tf_op jit(solution)/shard_map/attention/pallas_call | solution.py:126
  224.2 2.7 %collective-permute-start.26 = (bf16[256,512]{1,0:T(8,128)(2,1)S(1)}, bf16[256,512]{1,0:T(8,128)(2,1)S(1)}, u32[]{:S(2)}, u32[]{:S(2)}) collective-permute-start(bf16[256,512]{1,0:T(8,128)(2,1)S(1)} %get-tuple-element.110), channel_id=1, source_target_pairs={{0,3},{1,0},{2,1},{3,2},{4,7},{5,4},{6,5},{7,6},{8,11},{9,8},{10,9... | collective-permute-start | bytes 786440 | tf_op jit(solution)/shard_map/ppermute | solution.py:18
  229.8 7.9 %collective-permute-done.26 = bf16[256,512]{1,0:T(8,128)(2,1)S(1)} collective-permute-done((bf16[256,512]{1,0:T(8,128)(2,1)S(1)}, bf16[256,512]{1,0:T(8,128)(2,1)S(1)}, u32[]{:S(2)}, u32[]{:S(2)}) %collective-permute-start.26) | collective-permute-done | bytes 262176 | tf_op jit(solution)/shard_map/ppermute | solution.py:18
  237.7 2.3 collective-permute-done.24
  240.2 2.6 %collective-permute-start.27 = (bf16[256,512]{1,0:T(8,128)(2,1)S(1)}, bf16[256,512]{1,0:T(8,128)(2,1)S(1)}, u32[]{:S(2)}, u32[]{:S(2)}) collective-permute-start(bf16[256,512]{1,0:T(8,128)(2,1)S(1)} %add_convert_fusion.second_ref), channel_id=1, source_target_pairs={{0,64},{64,0},{1,65},{65,1},{2,66},{66,2},{3,67},{67,3},{4,68},{68... | collective-permute-start | bytes 786440 | tf_op jit(solution)/shard_map/ppermute | solution.py:22
  (110 shorter events, 54.9 us)
Async XLA Ops:
  6.5 91.7 %all-gather.3.cloned.1.call-start = ((), (), s32[]{:S(2)}) async-start(), calls=%async_computation.4 | async-start | bytes 10027008 | tf_op jit(solution)/shard_map/all_gather | solution.py:516
  10.5 3.1 %collective-permute-start.8 = (bf16[128,2304]{1,0:T(8,128)(2,1)S(1)}, bf16[128,2304]{1,0:T(8,128)(2,1)S(1)}, u32[]{:S(2)}, u32[]{:S(2)}) collective-permute-start(bf16[128,2304]{1,0:T(8,128)(2,1)S(1)} %get-tuple-element.68), channel_id=1, source_target_pairs={{0,64},{64,0},{1,65},{65,1},{2,66},{66,2},{3,67},{67,3},{4,68},{68... | collective-permute-start | bytes 1769480 | tf_op jit(solution)/shard_map/ppermute | solution.py:22
  15.0 167.6 %all-gather.5.cloned.1.call-start = ((), (), s32[]{:S(2)}) async-start(), calls=%async_computation.5 | async-start | bytes 10027008 | tf_op jit(solution)/shard_map/all_gather | solution.py:516
  19.6 3.7 %collective-permute-start = (bf16[128,80]{1,0:T(8,128)(2,1)S(1)}, bf16[128,80]{1,0:T(8,128)(2,1)S(1)}, u32[]{:S(2)}, u32[]{:S(2)}) collective-permute-start(bf16[128,80]{1,0:T(8,128)(2,1)S(1)} %merger_inner.1.mine_ref), channel_id=1, source_target_pairs={{0,64},{64,0},{1,65},{65,1},{2,66},{66,2},{3,67},{67,3},{4,68},{68... | collective-permute-start | bytes 61448 | tf_op jit(solution)/shard_map/ppermute | solution.py:22
  24.3 15.1 %collective-permute-start.3 = (bf16[256,512]{1,0:T(8,128)(2,1)S(1)}, bf16[256,512]{1,0:T(8,128)(2,1)S(1)}, u32[]{:S(2)}, u32[]{:S(2)}) collective-permute-start(bf16[256,512]{1,0:T(8,128)(2,1)S(1)} %get-tuple-element.61), channel_id=1, source_target_pairs={{0,3},{1,0},{2,1},{3,2},{4,7},{5,4},{6,5},{7,6},{8,11},{9,8},{10,9... | collective-permute-start | bytes 786440 | tf_op jit(solution)/shard_map/ppermute | solution.py:18
  28.2 14.3 %collective-permute-start.2 = (bf16[256,512]{1,0:T(8,128)(2,1)S(1)}, bf16[256,512]{1,0:T(8,128)(2,1)S(1)}, u32[]{:S(2)}, u32[]{:S(2)}) collective-permute-start(bf16[256,512]{1,0:T(8,128)(2,1)S(1)} %get-tuple-element.60), channel_id=1, source_target_pairs={{0,1},{1,2},{2,3},{3,0},{4,5},{5,6},{6,7},{7,4},{8,9},{9,10},{10,1... | collective-permute-start | bytes 786440 | tf_op jit(solution)/shard_map/ppermute | solution.py:18
  28.2 14.3 %collective-permute-start.1 = (bf16[256,512]{1,0:T(8,128)(2,1)S(1)}, bf16[256,512]{1,0:T(8,128)(2,1)S(1)}, u32[]{:S(2)}, u32[]{:S(2)}) collective-permute-start(bf16[256,512]{1,0:T(8,128)(2,1)S(1)} %get-tuple-element.59), channel_id=1, source_target_pairs={{0,2},{1,3},{2,0},{3,1},{4,6},{5,7},{6,4},{7,5},{8,10},{9,11},{10,... | collective-permute-start | bytes 786440 | tf_op jit(solution)/shard_map/ppermute | solution.py:18
  43.4 16.4 %all-to-all-start = ((bf16[16,16,512]{2,1,0:T(8,128)(2,1)}), bf16[16,16,512]{2,1,0:T(8,128)(2,1)S(1)}, u32[]{:S(2)}, u32[]{:S(2)}) async-start(bf16[16,16,512]{2,1,0:T(8,128)(2,1)} %bitcast.3), calls=%async_computation | async-start | bytes 524288 | tf_op jit(solution)/shard_map/all_to_all | solution.py:531
  60.5 14.2 %all-to-all-start.1 = ((bf16[16,16,512]{2,1,0:T(8,128)(2,1)}), bf16[16,16,512]{2,1,0:T(8,128)(2,1)S(1)}, u32[]{:S(2)}, u32[]{:S(2)}) async-start(bf16[16,16,512]{2,1,0:T(8,128)(2,1)} %broadcast_in_dim.36), calls=%async_computation.1 | async-start | bytes 524288 | tf_op jit(solution)/shard_map/all_to_all | solution.py:48
  75.0 10.1 %collective-permute-start.4 = (bf16[256,512]{1,0:T(8,128)(2,1)S(1)}, bf16[256,512]{1,0:T(8,128)(2,1)S(1)}, u32[]{:S(2)}, u32[]{:S(2)}) collective-permute-start(bf16[256,512]{1,0:T(8,128)(2,1)S(1)} %fusion.own_ref), channel_id=1, source_target_pairs={{0,1},{1,2},{2,3},{3,0},{4,5},{5,6},{6,7},{7,4},{8,9},{9,10},{10,1... | collective-permute-start | bytes 786440 | tf_op jit(solution)/shard_map/ppermute | solution.py:18
  75.1 10.0 %collective-permute-start.5 = (bf16[256,512]{1,0:T(8,128)(2,1)S(1)}, bf16[256,512]{1,0:T(8,128)(2,1)S(1)}, u32[]{:S(2)}, u32[]{:S(2)}) collective-permute-start(bf16[256,512]{1,0:T(8,128)(2,1)S(1)} %fusion.own_ref), channel_id=1, source_target_pairs={{0,2},{1,3},{2,0},{3,1},{4,6},{5,7},{6,4},{7,5},{8,10},{9,11},{10,... | collective-permute-start | bytes 786440 | tf_op jit(solution)/shard_map/ppermute | solution.py:18
  75.2 10.7 %collective-permute-start.6 = (bf16[256,512]{1,0:T(8,128)(2,1)S(1)}, bf16[256,512]{1,0:T(8,128)(2,1)S(1)}, u32[]{:S(2)}, u32[]{:S(2)}) collective-permute-start(bf16[256,512]{1,0:T(8,128)(2,1)S(1)} %fusion.own_ref), channel_id=1, source_target_pairs={{0,3},{1,0},{2,1},{3,2},{4,7},{5,4},{6,5},{7,6},{8,11},{9,8},{10,9... | collective-permute-start | bytes 786440 | tf_op jit(solution)/shard_map/ppermute | solution.py:18
  77.7 5.7 %collective-permute-start.7 = (f32[16,128]{1,0:T(8,128)S(1)}, f32[16,128]{1,0:T(8,128)S(1)}, u32[]{:S(2)}, u32[]{:S(2)}) collective-permute-start(f32[16,128]{1,0:T(8,128)S(1)} %select_bitcast_fusion), channel_id=1, source_target_pairs={{0,64},{64,0},{1,65},{65,1},{2,66},{66,2},{3,67},{67,3},{4,68},{68... | collective-permute-start | bytes 24584 | tf_op jit(solution)/shard_map/ppermute | solution.py:22
  100.9 1.9 collective-permute-start.9
  104.0 29.1 %all-to-all-start.2 = ((bf16[16,256,128]{2,1,0:T(8,128)(2,1)}), bf16[16,256,128]{2,1,0:T(8,128)(2,1)S(1)}, u32[]{:S(2)}, u32[]{:S(2)}) async-start(bf16[16,256,128]{2,1,0:T(8,128)(2,1)} %copy-done.4), calls=%async_computation.2 | async-start | bytes 2097152 | tf_op jit(solution)/shard_map/all_to_all | solution.py:572
  114.8 2.2 collective-permute-start.10
  133.1 3.5 %collective-permute-start.11 = (bf16[16,4,64,128]{3,2,1,0:T(8,128)(2,1)S(1)}, bf16[16,4,64,128]{3,2,1,0:T(8,128)(2,1)S(1)}, u32[]{:S(2)}, u32[]{:S(2)}) collective-permute-start(bf16[16,4,64,128]{3,2,1,0:T(8,128)(2,1)S(1)} %bitcast.37), channel_id=1, source_target_pairs={{0,64},{64,0},{1,65},{65,1},{2,66},{66,2},{3,67},{67,3},{4,68},{68... | collective-permute-start | bytes 3145736 | tf_op jit(solution)/shard_map/ppermute | solution.py:22
  146.7 7.7 %collective-permute-start.15 = (bf16[256,512]{1,0:T(8,128)(2,1)S(1)}, bf16[256,512]{1,0:T(8,128)(2,1)S(1)}, u32[]{:S(2)}, u32[]{:S(2)}) collective-permute-start(bf16[256,512]{1,0:T(8,128)(2,1)S(1)} %get-tuple-element.91), channel_id=1, source_target_pairs={{0,3},{1,0},{2,1},{3,2},{4,7},{5,4},{6,5},{7,6},{8,11},{9,8},{10,9... | collective-permute-start | bytes 786440 | tf_op jit(solution)/shard_map/ppermute | solution.py:18
  147.9 9.5 %collective-permute-start.14 = (bf16[256,512]{1,0:T(8,128)(2,1)S(1)}, bf16[256,512]{1,0:T(8,128)(2,1)S(1)}, u32[]{:S(2)}, u32[]{:S(2)}) collective-permute-start(bf16[256,512]{1,0:T(8,128)(2,1)S(1)} %get-tuple-element.90), channel_id=1, source_target_pairs={{0,1},{1,2},{2,3},{3,0},{4,5},{5,6},{6,7},{7,4},{8,9},{9,10},{10,1... | collective-permute-start | bytes 786440 | tf_op jit(solution)/shard_map/ppermute | solution.py:18
  148.2 12.8 %collective-permute-start.13 = (bf16[256,512]{1,0:T(8,128)(2,1)S(1)}, bf16[256,512]{1,0:T(8,128)(2,1)S(1)}, u32[]{:S(2)}, u32[]{:S(2)}) collective-permute-start(bf16[256,512]{1,0:T(8,128)(2,1)S(1)} %get-tuple-element.89), channel_id=1, source_target_pairs={{0,2},{1,3},{2,0},{3,1},{4,6},{5,7},{6,4},{7,5},{8,10},{9,11},{10,... | collective-permute-start | bytes 786440 | tf_op jit(solution)/shard_map/ppermute | solution.py:18
  161.2 21.5 %collective-permute-start.17 = (bf16[256,512]{1,0:T(8,128)(2,1)S(1)}, bf16[256,512]{1,0:T(8,128)(2,1)S(1)}, u32[]{:S(2)}, u32[]{:S(2)}) collective-permute-start(bf16[256,512]{1,0:T(8,128)(2,1)S(1)} %add_convert_fusion.1.own_ref.first_ref), channel_id=1, source_target_pairs={{0,1},{1,2},{2,3},{3,0},{4,5},{5,6},{6,7},{7,4},{8,9},{9,10},{10,1... | collective-permute-start | bytes 786440 | tf_op jit(solution)/shard_map/ppermute | solution.py:18
  161.3 21.4 %collective-permute-start.18 = (bf16[256,512]{1,0:T(8,128)(2,1)S(1)}, bf16[256,512]{1,0:T(8,128)(2,1)S(1)}, u32[]{:S(2)}, u32[]{:S(2)}) collective-permute-start(bf16[256,512]{1,0:T(8,128)(2,1)S(1)} %add_convert_fusion.1.own_ref.first_ref), channel_id=1, source_target_pairs={{0,2},{1,3},{2,0},{3,1},{4,6},{5,7},{6,4},{7,5},{8,10},{9,11},{10,... | collective-permute-start | bytes 786440 | tf_op jit(solution)/shard_map/ppermute | solution.py:18
  163.7 18.9 %collective-permute-start.19 = (bf16[256,512]{1,0:T(8,128)(2,1)S(1)}, bf16[256,512]{1,0:T(8,128)(2,1)S(1)}, u32[]{:S(2)}, u32[]{:S(2)}) collective-permute-start(bf16[256,512]{1,0:T(8,128)(2,1)S(1)} %add_convert_fusion.1.own_ref.first_ref), channel_id=1, source_target_pairs={{0,3},{1,0},{2,1},{3,2},{4,7},{5,4},{6,5},{7,6},{8,11},{9,8},{10,9... | collective-permute-start | bytes 786440 | tf_op jit(solution)/shard_map/ppermute | solution.py:18
  185.3 1.9 collective-permute-start.20
  188.4 21.3 %all-to-all-start.3 = ((bf16[16,256,128]{2,1,0:T(8,128)(2,1)}), bf16[16,256,128]{2,1,0:T(8,128)(2,1)S(1)}, u32[]{:S(2)}, u32[]{:S(2)}) async-start(bf16[16,256,128]{2,1,0:T(8,128)(2,1)} %copy-done.3), calls=%async_computation.3 | async-start | bytes 2097152 | tf_op jit(solution)/shard_map/all_to_all | solution.py:572
  199.5 2.3 collective-permute-start.21
  209.7 4.4 %collective-permute-start.22 = (bf16[16,4,64,128]{3,2,1,0:T(8,128)(2,1)S(1)}, bf16[16,4,64,128]{3,2,1,0:T(8,128)(2,1)S(1)}, u32[]{:S(2)}, u32[]{:S(2)}) collective-permute-start(bf16[16,4,64,128]{3,2,1,0:T(8,128)(2,1)S(1)} %bitcast.35), channel_id=1, source_target_pairs={{0,64},{64,0},{1,65},{65,1},{2,66},{66,2},{3,67},{67,3},{4,68},{68... | collective-permute-start | bytes 3145736 | tf_op jit(solution)/shard_map/ppermute | solution.py:22
  224.2 13.5 %collective-permute-start.26 = (bf16[256,512]{1,0:T(8,128)(2,1)S(1)}, bf16[256,512]{1,0:T(8,128)(2,1)S(1)}, u32[]{:S(2)}, u32[]{:S(2)}) collective-permute-start(bf16[256,512]{1,0:T(8,128)(2,1)S(1)} %get-tuple-element.110), channel_id=1, source_target_pairs={{0,3},{1,0},{2,1},{3,2},{4,7},{5,4},{6,5},{7,6},{8,11},{9,8},{10,9... | collective-permute-start | bytes 786440 | tf_op jit(solution)/shard_map/ppermute | solution.py:18
  226.9 10.8 %collective-permute-start.25 = (bf16[256,512]{1,0:T(8,128)(2,1)S(1)}, bf16[256,512]{1,0:T(8,128)(2,1)S(1)}, u32[]{:S(2)}, u32[]{:S(2)}) collective-permute-start(bf16[256,512]{1,0:T(8,128)(2,1)S(1)} %get-tuple-element.109), channel_id=1, source_target_pairs={{0,1},{1,2},{2,3},{3,0},{4,5},{5,6},{6,7},{7,4},{8,9},{9,10},{10,1... | collective-permute-start | bytes 786440 | tf_op jit(solution)/shard_map/ppermute | solution.py:18
  226.9 13.1 %collective-permute-start.24 = (bf16[256,512]{1,0:T(8,128)(2,1)S(1)}, bf16[256,512]{1,0:T(8,128)(2,1)S(1)}, u32[]{:S(2)}, u32[]{:S(2)}) collective-permute-start(bf16[256,512]{1,0:T(8,128)(2,1)S(1)} %get-tuple-element.108), channel_id=1, source_target_pairs={{0,2},{1,3},{2,0},{3,1},{4,6},{5,7},{6,4},{7,5},{8,10},{9,11},{10,... | collective-permute-start | bytes 786440 | tf_op jit(solution)/shard_map/ppermute | solution.py:18
  228.6 14.1 %collective-permute-start.16 = (bf16[256,512]{1,0:T(8,128)(2,1)S(1)}, bf16[256,512]{1,0:T(8,128)(2,1)S(1)}, u32[]{:S(2)}, u32[]{:S(2)}) collective-permute-start(bf16[256,512]{1,0:T(8,128)(2,1)S(1)} %add_convert_fusion.1.own_ref.first_ref), channel_id=1, source_target_pairs={{0,64},{64,0},{1,65},{65,1},{2,66},{66,2},{3,67},{67,3},{4,68},{68... | collective-permute-start | bytes 786440 | tf_op jit(solution)/shard_map/ppermute | solution.py:22
  240.2 3.7 %collective-permute-start.27 = (bf16[256,512]{1,0:T(8,128)(2,1)S(1)}, bf16[256,512]{1,0:T(8,128)(2,1)S(1)}, u32[]{:S(2)}, u32[]{:S(2)}) collective-permute-start(bf16[256,512]{1,0:T(8,128)(2,1)S(1)} %add_convert_fusion.second_ref), channel_id=1, source_target_pairs={{0,64},{64,0},{1,65},{65,1},{2,66},{66,2},{3,67},{67,3},{4,68},{68... | collective-permute-start | bytes 786440 | tf_op jit(solution)/shard_map/ppermute | solution.py:22
  (14 other events, 117.7 us)
Sparse Core Ops, SparseCore 0:
  15.2 83.0 all-gather.2
  100.4 82.2 all-gather.4

commit v12 on v9

--- a/solution.py
+++ b/solution.py
@@ -463,8 +463,13 @@
     weight_keep = jnp.where(first_core, for_first, for_second)
     weight_other = swapped(jnp.where(first_core, for_second, for_first))
     keyval_width = 2 * head_size
+    inner = merger_inner(patches, merge_gain, merge_first)
     weight_full = []
     for home in range(layers):
+        if home > 0:
+            inner, weight_keep, weight_other = lax.optimization_barrier(
+                (inner, weight_keep, weight_other)
+            )
         mine = jnp.where(section_index == home, weight_keep, weight_other)
         weight_full.append(lax.all_gather(mine, "blk", axis=0, tiled=True))
     gain_half = norm_gain[0].reshape(-1, 2, lane)
@@ -476,7 +481,6 @@
         jnp.where(first_core, gain_other, gain_keep).reshape(n_mp, 1, -1),
     ]
 
-    inner = merger_inner(patches, merge_gain, merge_first)
     place = jnp.stack([section_index, cycle_index, model_index]).astype(jnp.int32)
     own, *terms = merger_outer(place, inner, swapped(inner), merge_second, n_mp)
     total = own.astype(jnp.float32)

time: 250 us -> 250 us (level)
  transfers between devices with their start and end apart: 34 -> 34, of which waited for: 27 -> 25; matrix products, arithmetic and copies ran while one was open for 4% -> 4% of each run, Pallas kernels for 10% -> 10%
where the time goes in v12:
time: 250 us; the launch traced here: 249 us
  waiting for transfers between devices  125 us (50%)
  starting transfers between devices  58.7 us (23%)
  Pallas kernels  35.8 us (14%)
  between operations  13.9 us (6%)
  local copies, waits for them, and re-layouts  8.27 us (3%)
  other arithmetic  6.95 us (3%)
    all_gather x2, waiting for transfers between devices, local(): weight_full.append(lax.all_gather(mine, 'blk', axis=0, tiled=True))  35.3 us
    ppermute x15, waiting for transfers between devices, moved(): lax.ppermute(value, axis, [(i, (i + by) % size) for i in range(size)])  33.6 us
    all_to_all x2, waiting for transfers between devices, local(): gathered = lax.all_to_all(keyval_copies, 'blk', 0, 0, tiled=True)  23.7 us
    ppermute x13, starting transfers between devices, swapped(): return lax.ppermute(value, 'section', [(0, 1), (1, 0)])  19.6 us
    ppermute x15, starting transfers between devices, moved(): lax.ppermute(value, axis, [(i, (i + by) % size) for i in range(size)])  19.6 us
    pallas_call x4, Pallas kernels, project_in(): pl.pallas_call(functools.partial(project_in_kernel, at=at), out_shape=out...  17.7 us
    ppermute x13, waiting for transfers between devices, swapped(): return lax.ppermute(value, 'section', [(0, 1), (1, 0)])  16.2 us
    pallas_call x2, Pallas kernels, attention(): pl.pallas_call(functools.partial(attention_kernel, chunk_runs=mine.shape[...  11.1 us
  transfers between devices with their start and end apart: 34, of which 25 were waited for; matrix products, arithmetic and copies ran while one was open for 4% of the time, Pallas kernels for 10%

profile of v12, /device:TPU:1, one launch (start us, length us, event | category | flops | bytes accessed | tf_op | source)
XLA Modules:
  0.0 248.9 jit_solution(1879224522629173059)
XLA Ops:
  22.3 3.9 %collective-permute-start.4 = (bf16[256,512]{1,0:T(8,128)(2,1)S(1)}, bf16[256,512]{1,0:T(8,128)(2,1)S(1)}, u32[]{:S(2)}, u32[]{:S(2)}) collective-permute-start(bf16[256,512]{1,0:T(8,128)(2,1)S(1)} %get-tuple-element.63), channel_id=1, source_target_pairs={{0,3},{1,0},{2,1},{3,2},{4,7},{5,4},{6,5},{7,6},{8,11},{9,8},{10,9... | collective-permute-start | bytes 786440 | tf_op jit(solution)/shard_map/ppermute | solution.py:18
  28.5 8.7 %collective-permute-done.4 = bf16[256,512]{1,0:T(8,128)(2,1)S(1)} collective-permute-done((bf16[256,512]{1,0:T(8,128)(2,1)S(1)}, bf16[256,512]{1,0:T(8,128)(2,1)S(1)}, u32[]{:S(2)}, u32[]{:S(2)}) %collective-permute-start.4) | collective-permute-done | bytes 262176 | tf_op jit(solution)/shard_map/ppermute | solution.py:18
  37.2 3.2 %collective-permute-done.3 = bf16[256,512]{1,0:T(8,128)(2,1)S(1)} collective-permute-done((bf16[256,512]{1,0:T(8,128)(2,1)S(1)}, bf16[256,512]{1,0:T(8,128)(2,1)S(1)}, u32[]{:S(2)}, u32[]{:S(2)}) %collective-permute-start.3) | collective-permute-done | bytes 262176 | tf_op jit(solution)/shard_map/ppermute | solution.py:18
  41.2 6.8 %all-to-all-start = ((bf16[16,16,512]{2,1,0:T(8,128)(2,1)}), bf16[16,16,512]{2,1,0:T(8,128)(2,1)S(1)}, u32[]{:S(2)}, u32[]{:S(2)}) async-start(bf16[16,16,512]{2,1,0:T(8,128)(2,1)} %bitcast.8), calls=%async_computation | async-start | bytes 524288 | tf_op jit(solution)/shard_map/all_to_all | solution.py:489
  49.5 6.1 %all-to-all-done = bf16[16,16,512]{2,1,0:T(8,128)(2,1)S(1)} async-done(((bf16[16,16,512]{2,1,0:T(8,128)(2,1)}), bf16[16,16,512]{2,1,0:T(8,128)(2,1)S(1)}, u32[]{:S(2)}, u32[]{:S(2)}) %all-to-all-start) | async-done | bytes 262176 | tf_op jit(solution)/shard_map/all_to_all | solution.py:489
  56.4 3.5 %all-to-all-start.1 = ((bf16[16,16,512]{2,1,0:T(8,128)(2,1)}), bf16[16,16,512]{2,1,0:T(8,128)(2,1)S(1)}, u32[]{:S(2)}, u32[]{:S(2)}) async-start(bf16[16,16,512]{2,1,0:T(8,128)(2,1)} %broadcast_in_dim.36), calls=%async_computation.1 | async-start | bytes 524288 | tf_op jit(solution)/shard_map/all_to_all | solution.py:48
  60.0 10.2 %all-to-all-done.1 = bf16[16,16,512]{2,1,0:T(8,128)(2,1)S(1)} async-done(((bf16[16,16,512]{2,1,0:T(8,128)(2,1)}), bf16[16,16,512]{2,1,0:T(8,128)(2,1)S(1)}, u32[]{:S(2)}, u32[]{:S(2)}) %all-to-all-start.1) | async-done | bytes 262176 | tf_op jit(solution)/shard_map/all_to_all | solution.py:48
  70.5 2.0 collective-permute-start.6
  73.7 6.5 %collective-permute-start.8 = (f32[16,128]{1,0:T(8,128)S(1)}, f32[16,128]{1,0:T(8,128)S(1)}, u32[]{:S(2)}, u32[]{:S(2)}) collective-permute-start(f32[16,128]{1,0:T(8,128)S(1)} %select_bitcast_fusion), channel_id=1, source_target_pairs={{0,64},{64,0},{1,65},{65,1},{2,66},{66,2},{3,67},{67,3},{4,68},{68... | collective-permute-start | bytes 24584 | tf_op jit(solution)/shard_map/ppermute | solution.py:22
  81.1 16.0 %all-gather.3.cloned.1.call-done.weight_hbm = bf16[2048,2304]{1,0:T(8,128)(2,1)} async-done(((bf16[128,2304]{1,0:T(8,128)(2,1)}), bf16[2048,2304]{1,0:T(8,128)(2,1)}) %all-gather.3.cloned.1.call-update) | async-done | bytes 9437200 | tf_op jit(solution)/shard_map/all_gather | solution.py:474
  97.1 2.7 %project_kv.2 = (f32[256,256]{1,0:T(8,128)S(1)}, f32[256,256]{1,0:T(8,128)S(1)}) custom-call(s32[3]{0:T(128)S(1)} %pad_add_fusion.place, bf16[256,512]{1,0:T(8,128)(2,1)S(1)} %fusion.own_ref, bf16[256,512]{1,0:T(8,128)(2,1)S(1)} %collective-permute-done.5.from_one, bf16[256,512]{1,0:T(8,128)(2,1)S(1)} %collective-permute-done.6.from_two, ...), custom_call_target="tpu_custom_call" | custom-call | flops 268435456 | bytes 1572864 | tf_op jit(solution)/shard_map/project_kv/pallas_call | solution.py:285
  102.7 4.1 %all-to-all-start.2 = ((bf16[16,256,128]{2,1,0:T(8,128)(2,1)}), bf16[16,256,128]{2,1,0:T(8,128)(2,1)S(1)}, u32[]{:S(2)}, u32[]{:S(2)}) async-start(bf16[16,256,128]{2,1,0:T(8,128)(2,1)} %copy-done.4), calls=%async_computation.2 | async-start | bytes 2097152 | tf_op jit(solution)/shard_map/all_to_all | solution.py:530
  106.8 6.2 %project_q.2 = (f32[256,512]{1,0:T(8,128)S(1)}, f32[256,512]{1,0:T(8,128)S(1)}, bf16[4,512,1024]{2,1,0:T(8,128)(2,1)}) custom-call(s32[3]{0:T(128)S(1)} %pad_add_fusion.place, bf16[256,512]{1,0:T(8,128)(2,1)S(1)} %fusion.own_ref, bf16[256,512]{1,0:T(8,128)(2,1)S(1)} %collective-permute-done.5.from_one, bf16[256,512]{1,0:T(8,128)(2,1)S(1)} %collective-permute-done.6.from_two, ...), custom_call_target="tpu_custom_call" | custom-call | flops 1073741824 | bytes 5242880 | tf_op jit(solution)/shard_map/project_q/pallas_call | solution.py:285
  115.4 15.7 %all-to-all-done.2 = bf16[16,256,128]{2,1,0:T(8,128)(2,1)S(1)} async-done(((bf16[16,256,128]{2,1,0:T(8,128)(2,1)}), bf16[16,256,128]{2,1,0:T(8,128)(2,1)S(1)}, u32[]{:S(2)}, u32[]{:S(2)}) %all-to-all-start.2) | async-done | bytes 1048608 | tf_op jit(solution)/shard_map/all_to_all | solution.py:530
  132.8 2.1 collective-permute-done.11.other_ref
  134.8 5.5 %attention.2.mine_ref = bf16[256,512]{1,0:T(8,128)(2,1)S(1)} custom-call(s32[4]{0:T(128)S(1)} %pad_add_fusion.1.scalars, bf16[256,512]{1,0:T(8,128)(2,1)S(1)} %query_rotate.2.query_ref, bf16[16,4,64,128]{3,2,1,0:T(8,128)(2,1)S(1)} %bitcast.50, bf16[16,4,64,128]{3,2,1,0:T(8,128)(2,1)S(1)} %collective-permute-done.11.other_ref), custom_call_target="tpu_custom_call" | custom-call | flops 134217728 | bytes 2621440 | tf_op jit(solution)/shard_map/attention/pallas_call | solution.py:126
  146.2 4.8 %collective-permute-done.15 = bf16[256,512]{1,0:T(8,128)(2,1)S(1)} collective-permute-done((bf16[256,512]{1,0:T(8,128)(2,1)S(1)}, bf16[256,512]{1,0:T(8,128)(2,1)S(1)}, u32[]{:S(2)}, u32[]{:S(2)}) %collective-permute-start.15) | collective-permute-done | bytes 262176 | tf_op jit(solution)/shard_map/ppermute | solution.py:18
  151.0 3.1 %collective-permute-done.14 = bf16[256,512]{1,0:T(8,128)(2,1)S(1)} collective-permute-done((bf16[256,512]{1,0:T(8,128)(2,1)S(1)}, bf16[256,512]{1,0:T(8,128)(2,1)S(1)}, u32[]{:S(2)}, u32[]{:S(2)}) %collective-permute-start.14) | collective-permute-done | bytes 262176 | tf_op jit(solution)/shard_map/ppermute | solution.py:18
  154.1 3.5 %collective-permute-done.13 = bf16[256,512]{1,0:T(8,128)(2,1)S(1)} collective-permute-done((bf16[256,512]{1,0:T(8,128)(2,1)S(1)}, bf16[256,512]{1,0:T(8,128)(2,1)S(1)}, u32[]{:S(2)}, u32[]{:S(2)}) %collective-permute-start.13) | collective-permute-done | bytes 262176 | tf_op jit(solution)/shard_map/ppermute | solution.py:18
  157.9 2.4 collective-permute-start.18
  161.6 19.3 %all-gather.5.cloned.1.call-done.weight_hbm = bf16[2048,2304]{1,0:T(8,128)(2,1)} async-done(((bf16[128,2304]{1,0:T(8,128)(2,1)}), bf16[2048,2304]{1,0:T(8,128)(2,1)}) %all-gather.5.cloned.1.call-update) | async-done | bytes 9437200 | tf_op jit(solution)/shard_map/all_gather | solution.py:474
  180.9 2.7 %project_kv.3 = (f32[256,256]{1,0:T(8,128)S(1)}, f32[256,256]{1,0:T(8,128)S(1)}) custom-call(s32[3]{0:T(128)S(1)} %pad_add_fusion.place, bf16[256,512]{1,0:T(8,128)(2,1)S(1)} %add_convert_fusion.1.own_ref.first_ref, bf16[256,512]{1,0:T(8,128)(2,1)S(1)} %collective-permute-done.17.from_one, bf16[256,512]{1,0:T(8,128)(2,1)S(1)} %collective-permute-done.18.from_two, ...), custom_call_target="tpu_custom_call" | custom-call | flops 268435456 | bytes 1572864 | tf_op jit(solution)/shard_map/project_kv/pallas_call | solution.py:285
  186.7 5.0 %all-to-all-start.3 = ((bf16[16,256,128]{2,1,0:T(8,128)(2,1)}), bf16[16,256,128]{2,1,0:T(8,128)(2,1)S(1)}, u32[]{:S(2)}, u32[]{:S(2)}) async-start(bf16[16,256,128]{2,1,0:T(8,128)(2,1)} %copy-done.3), calls=%async_computation.3 | async-start | bytes 2097152 | tf_op jit(solution)/shard_map/all_to_all | solution.py:530
  191.7 6.1 %project_q.3 = (f32[256,512]{1,0:T(8,128)S(1)}, f32[256,512]{1,0:T(8,128)S(1)}, bf16[4,512,1024]{2,1,0:T(8,128)(2,1)}) custom-call(s32[3]{0:T(128)S(1)} %pad_add_fusion.place, bf16[256,512]{1,0:T(8,128)(2,1)S(1)} %add_convert_fusion.1.own_ref.first_ref, bf16[256,512]{1,0:T(8,128)(2,1)S(1)} %collective-permute-done.17.from_one, ...), custom_call_target="tpu_custom_call" | custom-call | flops 1073741824 | bytes 5242880 | tf_op jit(solution)/shard_map/project_q/pallas_call | solution.py:285
  200.1 7.9 %all-to-all-done.3 = bf16[16,256,128]{2,1,0:T(8,128)(2,1)S(1)} async-done(((bf16[16,256,128]{2,1,0:T(8,128)(2,1)}), bf16[16,256,128]{2,1,0:T(8,128)(2,1)S(1)}, u32[]{:S(2)}, u32[]{:S(2)}) %all-to-all-start.3) | async-done | bytes 1048608 | tf_op jit(solution)/shard_map/all_to_all | solution.py:530
  208.0 2.1 collective-permute-start.22
  210.4 2.1 collective-permute-done.22.other_ref
  212.4 5.5 %attention.3.mine_ref = bf16[256,512]{1,0:T(8,128)(2,1)S(1)} custom-call(s32[4]{0:T(128)S(1)} %pad_add_fusion.1.scalars, bf16[256,512]{1,0:T(8,128)(2,1)S(1)} %query_rotate.3.query_ref, bf16[16,4,64,128]{3,2,1,0:T(8,128)(2,1)S(1)} %bitcast.48, bf16[16,4,64,128]{3,2,1,0:T(8,128)(2,1)S(1)} %collective-permute-done.22.other_ref), custom_call_target="tpu_custom_call" | custom-call | flops 134217728 | bytes 2621440 | tf_op jit(solution)/shard_map/attention/pallas_call | solution.py:126
  220.9 2.7 %collective-permute-start.26 = (bf16[256,512]{1,0:T(8,128)(2,1)S(1)}, bf16[256,512]{1,0:T(8,128)(2,1)S(1)}, u32[]{:S(2)}, u32[]{:S(2)}) collective-permute-start(bf16[256,512]{1,0:T(8,128)(2,1)S(1)} %get-tuple-element.112), channel_id=1, source_target_pairs={{0,3},{1,0},{2,1},{3,2},{4,7},{5,4},{6,5},{7,6},{8,11},{9,8},{10,9... | collective-permute-start | bytes 786440 | tf_op jit(solution)/shard_map/ppermute | solution.py:18
  226.5 7.9 %collective-permute-done.26 = bf16[256,512]{1,0:T(8,128)(2,1)S(1)} collective-permute-done((bf16[256,512]{1,0:T(8,128)(2,1)S(1)}, bf16[256,512]{1,0:T(8,128)(2,1)S(1)}, u32[]{:S(2)}, u32[]{:S(2)}) %collective-permute-start.26) | collective-permute-done | bytes 262176 | tf_op jit(solution)/shard_map/ppermute | solution.py:18
  234.4 2.3 collective-permute-done.24
  236.8 2.6 %collective-permute-start.27 = (bf16[256,512]{1,0:T(8,128)(2,1)S(1)}, bf16[256,512]{1,0:T(8,128)(2,1)S(1)}, u32[]{:S(2)}, u32[]{:S(2)}) collective-permute-start(bf16[256,512]{1,0:T(8,128)(2,1)S(1)} %add_convert_fusion.second_ref), channel_id=1, source_target_pairs={{0,64},{64,0},{1,65},{65,1},{2,66},{66,2},{3,67},{67,3},{4,68},{68... | collective-permute-start | bytes 786440 | tf_op jit(solution)/shard_map/ppermute | solution.py:22
  (123 shorter events, 51.6 us)
Async XLA Ops:
  6.5 90.6 %all-gather.3.cloned.1.call-start = ((), (), s32[]{:S(2)}) async-start(), calls=%async_computation.4 | async-start | bytes 10027008 | tf_op jit(solution)/shard_map/all_gather | solution.py:474
  9.2 3.1 %collective-permute-start = (bf16[128,2304]{1,0:T(8,128)(2,1)S(1)}, bf16[128,2304]{1,0:T(8,128)(2,1)S(1)}, u32[]{:S(2)}, u32[]{:S(2)}) collective-permute-start(bf16[128,2304]{1,0:T(8,128)(2,1)S(1)} %broadcast_select_fusion.2), channel_id=1, source_target_pairs={{0,64},{64,0},{1,65},{65,1},{2,66},{66,2},{3,67},{67,3},{4,68},{68... | collective-permute-start | bytes 1769480 | tf_op jit(solution)/shard_map/ppermute | solution.py:22
  13.7 167.2 %all-gather.5.cloned.1.call-start = ((), (), s32[]{:S(2)}) async-start(), calls=%async_computation.5 | async-start | bytes 10027008 | tf_op jit(solution)/shard_map/all_gather | solution.py:474
  22.3 14.9 %collective-permute-start.4 = (bf16[256,512]{1,0:T(8,128)(2,1)S(1)}, bf16[256,512]{1,0:T(8,128)(2,1)S(1)}, u32[]{:S(2)}, u32[]{:S(2)}) collective-permute-start(bf16[256,512]{1,0:T(8,128)(2,1)S(1)} %get-tuple-element.63), channel_id=1, source_target_pairs={{0,3},{1,0},{2,1},{3,2},{4,7},{5,4},{6,5},{7,6},{8,11},{9,8},{10,9... | collective-permute-start | bytes 786440 | tf_op jit(solution)/shard_map/ppermute | solution.py:18
  26.2 14.2 %collective-permute-start.3 = (bf16[256,512]{1,0:T(8,128)(2,1)S(1)}, bf16[256,512]{1,0:T(8,128)(2,1)S(1)}, u32[]{:S(2)}, u32[]{:S(2)}) collective-permute-start(bf16[256,512]{1,0:T(8,128)(2,1)S(1)} %get-tuple-element.62), channel_id=1, source_target_pairs={{0,1},{1,2},{2,3},{3,0},{4,5},{5,6},{6,7},{7,4},{8,9},{9,10},{10,1... | collective-permute-start | bytes 786440 | tf_op jit(solution)/shard_map/ppermute | solution.py:18
  26.2 14.2 %collective-permute-start.2 = (bf16[256,512]{1,0:T(8,128)(2,1)S(1)}, bf16[256,512]{1,0:T(8,128)(2,1)S(1)}, u32[]{:S(2)}, u32[]{:S(2)}) collective-permute-start(bf16[256,512]{1,0:T(8,128)(2,1)S(1)} %get-tuple-element.61), channel_id=1, source_target_pairs={{0,2},{1,3},{2,0},{3,1},{4,6},{5,7},{6,4},{7,5},{8,10},{9,11},{10,... | collective-permute-start | bytes 786440 | tf_op jit(solution)/shard_map/ppermute | solution.py:18
  41.2 14.4 %all-to-all-start = ((bf16[16,16,512]{2,1,0:T(8,128)(2,1)}), bf16[16,16,512]{2,1,0:T(8,128)(2,1)S(1)}, u32[]{:S(2)}, u32[]{:S(2)}) async-start(bf16[16,16,512]{2,1,0:T(8,128)(2,1)} %bitcast.8), calls=%async_computation | async-start | bytes 524288 | tf_op jit(solution)/shard_map/all_to_all | solution.py:489
  56.4 13.8 %all-to-all-start.1 = ((bf16[16,16,512]{2,1,0:T(8,128)(2,1)}), bf16[16,16,512]{2,1,0:T(8,128)(2,1)S(1)}, u32[]{:S(2)}, u32[]{:S(2)}) async-start(bf16[16,16,512]{2,1,0:T(8,128)(2,1)} %broadcast_in_dim.36), calls=%async_computation.1 | async-start | bytes 524288 | tf_op jit(solution)/shard_map/all_to_all | solution.py:48
  70.4 10.7 %collective-permute-start.5 = (bf16[256,512]{1,0:T(8,128)(2,1)S(1)}, bf16[256,512]{1,0:T(8,128)(2,1)S(1)}, u32[]{:S(2)}, u32[]{:S(2)}) collective-permute-start(bf16[256,512]{1,0:T(8,128)(2,1)S(1)} %fusion.own_ref), channel_id=1, source_target_pairs={{0,1},{1,2},{2,3},{3,0},{4,5},{5,6},{6,7},{7,4},{8,9},{9,10},{10,1... | collective-permute-start | bytes 786440 | tf_op jit(solution)/shard_map/ppermute | solution.py:18
  70.5 10.6 %collective-permute-start.6 = (bf16[256,512]{1,0:T(8,128)(2,1)S(1)}, bf16[256,512]{1,0:T(8,128)(2,1)S(1)}, u32[]{:S(2)}, u32[]{:S(2)}) collective-permute-start(bf16[256,512]{1,0:T(8,128)(2,1)S(1)} %fusion.own_ref), channel_id=1, source_target_pairs={{0,2},{1,3},{2,0},{3,1},{4,6},{5,7},{6,4},{7,5},{8,10},{9,11},{10,... | collective-permute-start | bytes 786440 | tf_op jit(solution)/shard_map/ppermute | solution.py:18
  72.5 8.6 %collective-permute-start.7 = (bf16[256,512]{1,0:T(8,128)(2,1)S(1)}, bf16[256,512]{1,0:T(8,128)(2,1)S(1)}, u32[]{:S(2)}, u32[]{:S(2)}) collective-permute-start(bf16[256,512]{1,0:T(8,128)(2,1)S(1)} %fusion.own_ref), channel_id=1, source_target_pairs={{0,3},{1,0},{2,1},{3,2},{4,7},{5,4},{6,5},{7,6},{8,11},{9,8},{10,9... | collective-permute-start | bytes 786440 | tf_op jit(solution)/shard_map/ppermute | solution.py:18
  73.7 7.4 %collective-permute-start.8 = (f32[16,128]{1,0:T(8,128)S(1)}, f32[16,128]{1,0:T(8,128)S(1)}, u32[]{:S(2)}, u32[]{:S(2)}) collective-permute-start(f32[16,128]{1,0:T(8,128)S(1)} %select_bitcast_fusion), channel_id=1, source_target_pairs={{0,64},{64,0},{1,65},{65,1},{2,66},{66,2},{3,67},{67,3},{4,68},{68... | collective-permute-start | bytes 24584 | tf_op jit(solution)/shard_map/ppermute | solution.py:22
  99.8 1.7 collective-permute-start.9
  102.7 28.5 %all-to-all-start.2 = ((bf16[16,256,128]{2,1,0:T(8,128)(2,1)}), bf16[16,256,128]{2,1,0:T(8,128)(2,1)S(1)}, u32[]{:S(2)}, u32[]{:S(2)}) async-start(bf16[16,256,128]{2,1,0:T(8,128)(2,1)} %copy-done.4), calls=%async_computation.2 | async-start | bytes 2097152 | tf_op jit(solution)/shard_map/all_to_all | solution.py:530
  113.0 2.4 collective-permute-start.10
  131.1 3.7 %collective-permute-start.11 = (bf16[16,4,64,128]{3,2,1,0:T(8,128)(2,1)S(1)}, bf16[16,4,64,128]{3,2,1,0:T(8,128)(2,1)S(1)}, u32[]{:S(2)}, u32[]{:S(2)}) collective-permute-start(bf16[16,4,64,128]{3,2,1,0:T(8,128)(2,1)S(1)} %bitcast.49), channel_id=1, source_target_pairs={{0,64},{64,0},{1,65},{65,1},{2,66},{66,2},{3,67},{67,3},{4,68},{68... | collective-permute-start | bytes 3145736 | tf_op jit(solution)/shard_map/ppermute | solution.py:22
  140.4 1.6 collective-permute-start.12
  143.3 7.7 %collective-permute-start.15 = (bf16[256,512]{1,0:T(8,128)(2,1)S(1)}, bf16[256,512]{1,0:T(8,128)(2,1)S(1)}, u32[]{:S(2)}, u32[]{:S(2)}) collective-permute-start(bf16[256,512]{1,0:T(8,128)(2,1)S(1)} %get-tuple-element.91), channel_id=1, source_target_pairs={{0,3},{1,0},{2,1},{3,2},{4,7},{5,4},{6,5},{7,6},{8,11},{9,8},{10,9... | collective-permute-start | bytes 786440 | tf_op jit(solution)/shard_map/ppermute | solution.py:18
  144.6 9.5 %collective-permute-start.14 = (bf16[256,512]{1,0:T(8,128)(2,1)S(1)}, bf16[256,512]{1,0:T(8,128)(2,1)S(1)}, u32[]{:S(2)}, u32[]{:S(2)}) collective-permute-start(bf16[256,512]{1,0:T(8,128)(2,1)S(1)} %get-tuple-element.90), channel_id=1, source_target_pairs={{0,1},{1,2},{2,3},{3,0},{4,5},{5,6},{6,7},{7,4},{8,9},{9,10},{10,1... | collective-permute-start | bytes 786440 | tf_op jit(solution)/shard_map/ppermute | solution.py:18
  144.8 12.8 %collective-permute-start.13 = (bf16[256,512]{1,0:T(8,128)(2,1)S(1)}, bf16[256,512]{1,0:T(8,128)(2,1)S(1)}, u32[]{:S(2)}, u32[]{:S(2)}) collective-permute-start(bf16[256,512]{1,0:T(8,128)(2,1)S(1)} %get-tuple-element.89), channel_id=1, source_target_pairs={{0,2},{1,3},{2,0},{3,1},{4,6},{5,7},{6,4},{7,5},{8,10},{9,11},{10,... | collective-permute-start | bytes 786440 | tf_op jit(solution)/shard_map/ppermute | solution.py:18
  157.8 23.1 %collective-permute-start.17 = (bf16[256,512]{1,0:T(8,128)(2,1)S(1)}, bf16[256,512]{1,0:T(8,128)(2,1)S(1)}, u32[]{:S(2)}, u32[]{:S(2)}) collective-permute-start(bf16[256,512]{1,0:T(8,128)(2,1)S(1)} %add_convert_fusion.1.own_ref.first_ref), channel_id=1, source_target_pairs={{0,1},{1,2},{2,3},{3,0},{4,5},{5,6},{6,7},{7,4},{8,9},{9,10},{10,1... | collective-permute-start | bytes 786440 | tf_op jit(solution)/shard_map/ppermute | solution.py:18
  157.9 23.0 %collective-permute-start.18 = (bf16[256,512]{1,0:T(8,128)(2,1)S(1)}, bf16[256,512]{1,0:T(8,128)(2,1)S(1)}, u32[]{:S(2)}, u32[]{:S(2)}) collective-permute-start(bf16[256,512]{1,0:T(8,128)(2,1)S(1)} %add_convert_fusion.1.own_ref.first_ref), channel_id=1, source_target_pairs={{0,2},{1,3},{2,0},{3,1},{4,6},{5,7},{6,4},{7,5},{8,10},{9,11},{10,... | collective-permute-start | bytes 786440 | tf_op jit(solution)/shard_map/ppermute | solution.py:18
  160.3 20.6 %collective-permute-start.19 = (bf16[256,512]{1,0:T(8,128)(2,1)S(1)}, bf16[256,512]{1,0:T(8,128)(2,1)S(1)}, u32[]{:S(2)}, u32[]{:S(2)}) collective-permute-start(bf16[256,512]{1,0:T(8,128)(2,1)S(1)} %add_convert_fusion.1.own_ref.first_ref), channel_id=1, source_target_pairs={{0,3},{1,0},{2,1},{3,2},{4,7},{5,4},{6,5},{7,6},{8,11},{9,8},{10,9... | collective-permute-start | bytes 786440 | tf_op jit(solution)/shard_map/ppermute | solution.py:18
  183.6 1.9 collective-permute-start.20
  186.7 21.3 %all-to-all-start.3 = ((bf16[16,256,128]{2,1,0:T(8,128)(2,1)}), bf16[16,256,128]{2,1,0:T(8,128)(2,1)S(1)}, u32[]{:S(2)}, u32[]{:S(2)}) async-start(bf16[16,256,128]{2,1,0:T(8,128)(2,1)} %copy-done.3), calls=%async_computation.3 | async-start | bytes 2097152 | tf_op jit(solution)/shard_map/all_to_all | solution.py:530
  197.8 2.3 collective-permute-start.21
  208.0 4.4 %collective-permute-start.22 = (bf16[16,4,64,128]{3,2,1,0:T(8,128)(2,1)S(1)}, bf16[16,4,64,128]{3,2,1,0:T(8,128)(2,1)S(1)}, u32[]{:S(2)}, u32[]{:S(2)}) collective-permute-start(bf16[16,4,64,128]{3,2,1,0:T(8,128)(2,1)S(1)} %bitcast.47), channel_id=1, source_target_pairs={{0,64},{64,0},{1,65},{65,1},{2,66},{66,2},{3,67},{67,3},{4,68},{68... | collective-permute-start | bytes 3145736 | tf_op jit(solution)/shard_map/ppermute | solution.py:22
  220.9 13.5 %collective-permute-start.26 = (bf16[256,512]{1,0:T(8,128)(2,1)S(1)}, bf16[256,512]{1,0:T(8,128)(2,1)S(1)}, u32[]{:S(2)}, u32[]{:S(2)}) collective-permute-start(bf16[256,512]{1,0:T(8,128)(2,1)S(1)} %get-tuple-element.112), channel_id=1, source_target_pairs={{0,3},{1,0},{2,1},{3,2},{4,7},{5,4},{6,5},{7,6},{8,11},{9,8},{10,9... | collective-permute-start | bytes 786440 | tf_op jit(solution)/shard_map/ppermute | solution.py:18
  223.6 10.8 %collective-permute-start.25 = (bf16[256,512]{1,0:T(8,128)(2,1)S(1)}, bf16[256,512]{1,0:T(8,128)(2,1)S(1)}, u32[]{:S(2)}, u32[]{:S(2)}) collective-permute-start(bf16[256,512]{1,0:T(8,128)(2,1)S(1)} %get-tuple-element.111), channel_id=1, source_target_pairs={{0,1},{1,2},{2,3},{3,0},{4,5},{5,6},{6,7},{7,4},{8,9},{9,10},{10,1... | collective-permute-start | bytes 786440 | tf_op jit(solution)/shard_map/ppermute | solution.py:18
  223.6 13.1 %collective-permute-start.24 = (bf16[256,512]{1,0:T(8,128)(2,1)S(1)}, bf16[256,512]{1,0:T(8,128)(2,1)S(1)}, u32[]{:S(2)}, u32[]{:S(2)}) collective-permute-start(bf16[256,512]{1,0:T(8,128)(2,1)S(1)} %get-tuple-element.110), channel_id=1, source_target_pairs={{0,2},{1,3},{2,0},{3,1},{4,6},{5,7},{6,4},{7,5},{8,10},{9,11},{10,... | collective-permute-start | bytes 786440 | tf_op jit(solution)/shard_map/ppermute | solution.py:18
  225.3 14.1 %collective-permute-start.16 = (bf16[256,512]{1,0:T(8,128)(2,1)S(1)}, bf16[256,512]{1,0:T(8,128)(2,1)S(1)}, u32[]{:S(2)}, u32[]{:S(2)}) collective-permute-start(bf16[256,512]{1,0:T(8,128)(2,1)S(1)} %add_convert_fusion.1.own_ref.first_ref), channel_id=1, source_target_pairs={{0,64},{64,0},{1,65},{65,1},{2,66},{66,2},{3,67},{67,3},{4,68},{68... | collective-permute-start | bytes 786440 | tf_op jit(solution)/shard_map/ppermute | solution.py:22
  236.8 3.7 %collective-permute-start.27 = (bf16[256,512]{1,0:T(8,128)(2,1)S(1)}, bf16[256,512]{1,0:T(8,128)(2,1)S(1)}, u32[]{:S(2)}, u32[]{:S(2)}) collective-permute-start(bf16[256,512]{1,0:T(8,128)(2,1)S(1)} %add_convert_fusion.second_ref), channel_id=1, source_target_pairs={{0,64},{64,0},{1,65},{65,1},{2,66},{66,2},{3,67},{67,3},{4,68},{68... | collective-permute-start | bytes 786440 | tf_op jit(solution)/shard_map/ppermute | solution.py:22
  (15 other events, 64.5 us)
Sparse Core Ops, SparseCore 0:
  13.8 83.2 all-gather.2
  99.3 81.5 all-gather.4
